TPU v7x, 32 devices: a whole 2x2x4 slice. The times are simulated.
32 devices in a mesh: dp: 8 (over z, x), fsdp: 4 (over y, core).
Axes of the slice: x: 2, y: 2, z: 4, core: 2. Of those that a mesh axis runs over, the one named last changes fastest.
Arguments:
- acts: bfloat16 [1024, 3072], P('dp'), may hold values from -6 to 6
- weight: bfloat16 [3072, 3072], P('dp', 'fsdp'), may hold values from -0.15625 to 0.15625
- block_mask: int32 [4, 12, 12], replicated, may hold values 0 or 1
- out_grad: bfloat16 [4, 1024, 3072], P(None, 'dp', 'fsdp'), may hold values from -6 to 6
Outputs:
- outputs: bfloat16 [4, 1024, 3072], P(None, 'dp', 'fsdp')
- grad_w: float32 [3072, 3072], P('dp', 'fsdp')
- grad_x: bfloat16 [1024, 3072], P('dp', 'fsdp')
All inputs are finite; a program needn't handle non-finite values.
Results may differ from a plain program's by a relative error of at most 0.001.
Values may be sent and summed in bfloat16 or wider, within the bound.
No kernel may reach another device: no remote copies, remote signals or barrier semaphores. Data moves between devices by JAX's collectives and lax.ppermute only.
A program may use at most 128 MiB of HBM per device.

v0:
```python
import jax
import jax.numpy as jnp
from jax import lax
from jax.sharding import PartitionSpec as P

BS = 256
TOK_G = 128


def on_device(acts, weight, block_mask, out_grad):
    width = weight.shape[1]
    kblocks = block_mask.shape[1]
    oblocks = block_mask.shape[2]
    first_col = lax.axis_index("fsdp") * width
    col_ids = (first_col + jnp.arange(width, dtype=jnp.int32)) // BS
    col_select = (col_ids[None, :] == jnp.arange(oblocks, dtype=jnp.int32)[:, None]).astype(
        jnp.float32
    )
    col_mask = jnp.einsum("skb,bc->skc", block_mask.astype(jnp.float32), col_select)

    def piece_mask(count):
        row_ids = jnp.arange(count, dtype=jnp.int32) // BS
        row_select = (row_ids[:, None] == jnp.arange(kblocks, dtype=jnp.int32)[None, :]).astype(
            jnp.float32
        )
        return jnp.einsum("nk,skc->snc", row_select, col_mask)

    def masked_piece(piece):
        return piece_mask(piece.shape[0]).astype(jnp.bfloat16) * piece[None]

    cols = acts
    forward = jnp.einsum(
        "tn,snc->stc",
        cols,
        masked_piece(lax.all_gather(weight, "dp", axis=0, tiled=True)),
        preferred_element_type=jnp.float32,
    )
    input_part = jnp.einsum(
        "stc,snc->tn",
        out_grad,
        masked_piece(lax.all_gather(weight, "dp", axis=0, tiled=True)),
        preferred_element_type=jnp.float32,
    )
    outputs = forward.astype(jnp.bfloat16)
    cols = acts
    products = jnp.einsum("tn,stc->snc", cols, out_grad, preferred_element_type=jnp.float32)
    grad_w = lax.psum_scatter(
        jnp.sum(piece_mask(lax.axis_size("dp") * weight.shape[0]) * products, axis=0)
        * (1.0 / TOK_G),
        "dp",
        scatter_dimension=0,
        tiled=True,
    )
    grad_x = lax.psum_scatter(input_part, "fsdp", scatter_dimension=1, tiled=True).astype(
        jnp.bfloat16
    )
    return (outputs, grad_w, grad_x)


def solution(mesh):
    in_specs = (P("dp", None), P("dp", "fsdp"), P(), P(None, "dp", "fsdp"))
    out_specs = (P(None, "dp", "fsdp"), P("dp", "fsdp"), P("dp", "fsdp"))
    return jax.shard_map(
        on_device, mesh=mesh, in_specs=in_specs, out_specs=out_specs, check_vma=False
    )
```

profile of v0, /device:TPU:0, one launch (start us, length us, event | category | flops | bytes accessed | tf_op | source)
XLA Modules:
  0.0 319.4 jit_solution(12060055116255987593)
XLA Ops:
  7.2 0.0 copy-start
  7.2 0.0 all-gather.2.cloned.1.call-start
  7.2 0.7 all-gather.2.cloned.1.call-update
  7.9 0.0 reduce-scatter.5.cloned.1.call-start
  8.0 0.7 convert_element_type.23
  8.7 15.5 %fusion.5 = f32[4,768,3072]{2,1,0:T(8,128)} fusion(s32[3072]{0:T(1024)S(1)} %add_select_fusion, bf16[4,12,12]{2,0,1:T(4,128)(2,1)S(1)} %convert_element_type.23, s32[768]{0:T(1024)S(1)} %add_select_fusion.1), kind=kOutput, calls=%fused_computation.9 | convolution fusion | flops 227423232 | bytes 37765248 | tf_op jit(solution)/shard_map/nk,skc->snc/dot_general | solution.py:26
  24.2 68.6 %all-gather.2.cloned.1.call-done = bf16[3072,768]{1,0:T(8,128)(2,1)} async-done(((bf16[384,768]{1,0:T(8,128)(2,1)}), bf16[3072,768]{1,0:T(8,128)(2,1)}) %all-gather.2.cloned.1.call-update) | async-done | bytes 4718608 | tf_op jit(solution)/shard_map/all_gather | solution.py:35
  92.8 6.6 %copy.12 = bf16[3072,768]{0,1:T(8,128)(2,1)} copy(bf16[3072,768]{1,0:T(8,128)(2,1)} %all-gather.2.cloned.1.call-done) | data formatting | bytes 9437184 | tf_op jit(solution)/shard_map/all_gather | solution.py:35
  99.5 0.0 copy-done
  99.5 0.0 copy-start.1
  99.5 16.7 %fusion.2 = f32[128,3072]{0,1:T(8,128)} fusion(bf16[4,128,768]{2,1,0:T(8,128)(2,1)S(1)} %copy-done, f32[4,768,3072]{2,1,0:T(8,128)} %fusion.5, bf16[3072,768]{0,1:T(8,128)(2,1)} %copy.12), kind=kOutput, calls=%fused_computation.5 | convolution fusion | flops 2434793472 | bytes 44826624 | tf_op jit(solution)/shard_map/stc,snc->tn/dot_general | solution.py:38
  116.2 0.0 reduce-scatter.5.cloned.1.call-update
  116.2 0.0 reduce-scatter.3.cloned.1.call-start
  116.3 0.0 copy-done.1
  116.3 18.9 %multiply_reduce_fusion = f32[768,3072]{1,0:T(8,128)} fusion(f32[4,768,3072]{2,1,0:T(8,128)} %fusion.5, bf16[4,128,768]{2,1,0:T(8,128)(2,1)S(1)} %copy-done, bf16[128,3072]{1,0:T(8,128)(2,1)S(1)} %copy-done.1), kind=kOutput, calls=%fused_computation | convolution fusion | flops 2432434176 | bytes 48758784 | tf_op jit(solution)/shard_map/tn,stc->snc/dot_general | solution.py:46
  135.2 9.0 %multiply_bitcast_fusion = f32[3072,768]{0,1:T(8,128)} fusion(f32[768,3072]{1,0:T(8,128)} %multiply_reduce_fusion), kind=kLoop, calls=%fused_computation.2 | loop fusion | flops 2359296 | bytes 18874368 | tf_op jit(solution)/shard_map/mul | solution.py:48
  144.2 0.0 reduce-scatter.3.cloned.1.call-update
  144.2 16.1 %fusion.4 = bf16[4,128,768]{1,2,0:T(8,128)(2,1)S(1)} fusion(f32[4,768,3072]{2,1,0:T(8,128)} %fusion.5, bf16[3072,768]{0,1:T(8,128)(2,1)} %copy.12, bf16[128,3072]{1,0:T(8,128)(2,1)S(1)} %copy-done.1), kind=kOutput, calls=%fused_computation.7 | convolution fusion | flops 2435186688 | bytes 44040192 | tf_op jit(solution)/shard_map/tn,snc->stc/dot_general | solution.py:32
  160.3 1.2 copy.15
  161.4 0.0 reduce-scatter.5.cloned.1.call-done
  161.4 1.0 convert_element_type.28
  162.5 0.8 copy.17
  163.3 146.9 %reduce-scatter.3.cloned.1.call-done = f32[384,768]{0,1:T(8,128)} async-done(((f32[3072,768]{0,1:T(8,128)}), f32[384,768]{0,1:T(8,128)}) %reduce-scatter.3.cloned.1.call-update) | async-done | bytes 1179664 | tf_op jit(solution)/shard_map/reduce_scatter | solution.py:47
  310.2 2.7 copy.16
  (2 shorter events, 0.0 us)
Async XLA Ops:
  7.2 92.3 %copy-start = (bf16[4,128,768]{2,1,0:T(8,128)(2,1)S(1)}, bf16[4,128,768]{2,1,0:T(8,128)(2,1)}, u32[]{:S(2)}) copy-start(bf16[4,128,768]{2,1,0:T(8,128)(2,1)} %param.7) | copy-start | bytes 2359300
  7.2 85.6 %all-gather.2.cloned.1.call-start = ((), (), s32[]{:S(2)}) async-start(), calls=%async_computation.2 | async-start | bytes 5308416 | tf_op jit(solution)/shard_map/all_gather | solution.py:35
  7.9 153.5 %reduce-scatter.5.cloned.1.call-start = ((), (), s32[]{:S(2)}) async-start(), calls=%async_computation.4 | async-start | bytes 1966080 | tf_op jit(solution)/shard_map/reduce_scatter | solution.py:54
  99.5 16.8 %copy-start.1 = (bf16[128,3072]{1,0:T(8,128)(2,1)S(1)}, bf16[128,3072]{1,0:T(8,128)(2,1)}, u32[]{:S(2)}) copy-start(bf16[128,3072]{1,0:T(8,128)(2,1)} %param.4) | copy-start | bytes 2359300
  116.2 194.0 %reduce-scatter.3.cloned.1.call-start = ((), (), s32[]{:S(2)}) async-start(), calls=%async_computation.3 | async-start | bytes 10616832 | tf_op jit(solution)/shard_map/reduce_scatter | solution.py:47
Sparse Core Ops, SparseCore 0:
  10.2 82.5 all-gather.1
  116.3 26.2 reduce-scatter.4
  146.7 163.4 reduce-scatter.2
where the time goes:
time: 320 us; the launch traced here: 319 us
  waiting for transfers between devices  216 us (68%)
  matrix products  67.2 us (21%)
  between operations  13.8 us (4%)
  local copies, waits for them, and re-layouts  11.3 us (4%)
  other arithmetic  10.8 us (3%)
    reduce_scatter x1, waiting for transfers between devices, on_device(): lax.psum_scatter(jnp.sum(piece_mask(lax.axis_size('dp') * weight.shape[0]...  147 us
    all_gather x1, waiting for transfers between devices, on_device(): lax.all_gather(weight, 'dp', axis=0, tiled=True)  68.6 us
    dot_general x1, matrix products, on_device(): jnp.einsum('tn,stc->snc', cols, out_grad, preferred_element_type=jnp.floa...  18.9 us
    dot_general x1, matrix products, on_device(): jnp.einsum('stc,snc->tn', out_grad, masked_piece(lax.all_gather(weight, '...  16.7 us
    dot_general x1, matrix products, on_device(): jnp.einsum('tn,snc->stc', cols, masked_piece(lax.all_gather(weight, 'dp',...  16.1 us
    dot_general x1, matrix products, piece_mask(): return jnp.einsum('nk,skc->snc', row_select, col_mask)  15.5 us
    mul x1, other arithmetic, on_device(): jnp.sum(piece_mask(lax.axis_size('dp') * weight.shape[0]) * products, axi...  8.99 us
    all_gather x1, local copies, waits for them, and re-layouts, on_device(): lax.all_gather(weight, 'dp', axis=0, tiled=True)  6.65 us
  transfers between devices with their start and end apart: 3, of which 2 were waited for; matrix products, arithmetic and copies ran while one was open for 20% of the time, Pallas kernels for 0%

commit v1 on v0

v1 whole, which is shorter than its diff:
```python
import math

import jax
import jax.numpy as jnp
from jax import lax
from jax.sharding import PartitionSpec as P

BS = 256
TOK_G = 128
F32 = jnp.float32
BF16 = jnp.bfloat16


def on_device(acts, weight, block_mask, out_grad):
    nsub = block_mask.shape[0]
    rows, width = weight.shape
    tokens, depth = acts.shape
    dp = lax.axis_size("dp")
    nx = 2 if dp % 2 == 0 else 1
    nz = dp // nx
    me = lax.axis_index("dp")
    z, x = me // nx, me % nx
    first_col = lax.axis_index("fsdp") * width
    cw = math.gcd(width, BS)
    nch = width // cw

    def swap_x(a):
        return lax.ppermute(a, "dp", [(d, d ^ 1) for d in range(dp)])

    def shift_z(a, step, senders):
        pairs = [(i * nx + j, (i + step) * nx + j) for i in senders for j in range(nx)]
        return lax.ppermute(a, "dp", pairs)

    acts_by = acts.reshape(tokens, nz, nx, rows)
    mine = lax.dynamic_index_in_dim(acts_by, x, 2, keepdims=False)
    other = lax.dynamic_index_in_dim(acts_by, 1 - x, 2, keepdims=False)

    col_blocks = (first_col + jnp.arange(nch, dtype=jnp.int32) * cw) // BS
    chunk_mask = jnp.take(block_mask, col_blocks, axis=2)
    row_mask = jnp.repeat(chunk_mask, BS, axis=1).reshape(nsub, nz, nx, rows, nch).astype(BF16)
    row_mask_mine = lax.dynamic_index_in_dim(row_mask, x, 2, keepdims=False)
    row_mask_other = lax.dynamic_index_in_dim(row_mask, 1 - x, 2, keepdims=False)

    groups = [[i * nx + j for i in range(nz)] for j in range(nx)]
    halves = 2
    hr = rows // halves
    weight_own = [
        lax.all_gather(weight[h * hr : (h + 1) * hr], "dp", axis_index_groups=groups, axis=0)
        for h in range(halves)
    ]

    acts_pair = jnp.concatenate([mine, swap_x(other)], axis=0).reshape(2 * tokens, nz * rows)
    grads = []
    for j in range(nch):
        og = out_grad[:, :, j * cw : (j + 1) * cw]
        og_pair = jnp.concatenate([og, swap_x(og)], axis=1)
        lhs = acts_pair[None] * row_mask_mine[..., j].reshape(nsub, 1, nz * rows)
        part = jnp.einsum("stn,stc->nc", lhs, og_pair, preferred_element_type=F32)
        part = part.reshape(nz, rows, cw)
        up = None
        down = None
        for i in range(1, nz):
            send = lax.dynamic_index_in_dim(part, jnp.minimum(z + nz - i, nz - 1), 0, keepdims=False)
            up = shift_z(send if up is None else send + up, 1, range(0, i))
            send = lax.dynamic_index_in_dim(part, jnp.maximum(z - nz + i, 0), 0, keepdims=False)
            down = shift_z(send if down is None else send + down, -1, range(nz - i, nz))
        own = lax.dynamic_index_in_dim(part, z, 0, keepdims=False)
        if nz > 1:
            own = own + up + down
        grads.append(own * (1.0 / TOK_G))
    grad_w = jnp.concatenate(grads, axis=1)

    forward = jnp.zeros((nsub, tokens, width), F32)
    parts = []
    for h in range(halves):
        own = weight_own[h]
        peer = swap_x(own)
        pair = []
        for w, a, m in ((own, mine, row_mask_mine), (peer, other, row_mask_other)):
            m_h = m[:, :, h * hr : (h + 1) * hr]
            full = jnp.repeat(m_h, cw, axis=3)
            masked = (full * w[None]).reshape(nsub, nz * hr, width)
            a_h = a[:, :, h * hr : (h + 1) * hr].reshape(tokens, nz * hr)
            forward = forward + jnp.einsum("tn,snc->stc", a_h, masked, preferred_element_type=F32)
            pair.append(
                jnp.einsum("stc,snc->tn", out_grad, masked, preferred_element_type=F32).reshape(
                    tokens, nz, hr
                )
            )
        lo = jnp.where(x == 0, pair[0], pair[1])
        hi = jnp.where(x == 0, pair[1], pair[0])
        parts.append(jnp.stack([lo, hi], axis=2))
    outputs = forward.astype(BF16)
    input_part = jnp.stack(parts, axis=3).reshape(tokens, depth)
    grad_x = lax.psum_scatter(input_part, "fsdp", scatter_dimension=1, tiled=True).astype(BF16)
    return (outputs, grad_w, grad_x)


def solution(mesh):
    in_specs = (P("dp", None), P("dp", "fsdp"), P(), P(None, "dp", "fsdp"))
    out_specs = (P(None, "dp", "fsdp"), P("dp", "fsdp"), P("dp", "fsdp"))
    return jax.shard_map(
        on_device, mesh=mesh, in_specs=in_specs, out_specs=out_specs, check_vma=False
    )
```

time: 320 us -> 307 us (0.959)
  waiting for transfers between devices: 216 us -> 61.7 us
  local copies, waits for them, and re-layouts: 11.3 us -> 139 us
  starting transfers between devices: 0.12 us -> 49.5 us
  matrix products: 67.2 us -> 26.2 us
    reduce_scatter x1 -> x0, waiting for transfers between devices: 147 us -> none  [on_device(): lax.psum_scatter(jnp.sum(piece_mask(lax.axis_size('dp') * weight.shape[0]...]
    reshape x0 -> x9, local copies, waits for them, and re-layouts: none -> 105 us  [the longest x8 104 us: on_device(): full = jnp.repeat(m_h, cw, axis=3)]
    all_gather x1 -> x2, waiting for transfers between devices: 68.6 us -> 0.01 us  [on_device(): lax.all_gather(weight[h * hr:(h + 1) * hr], 'dp', axis_index_groups=group...]
    ppermute x0 -> x24, waiting for transfers between devices: none -> 61.7 us  [the longest x6 36.8 us: swap_x(): return lax.ppermute(a, 'dp', [(d, d ^ 1) for d in range(dp)])]
    ppermute x0 -> x24, starting transfers between devices: none -> 49.2 us  [the longest x18 42 us: shift_z(): return lax.ppermute(a, 'dp', pairs)]
    dot_general x4 -> x11, matrix products: 67.2 us -> 26.2 us  [the longest x4 11.5 us: on_device(): jnp.einsum('tn,snc->stc', a_h, masked, preferred_element_type=F32)]
    broadcast_in_dim x0 -> x5, local copies, waits for them, and re-layouts: none -> 22.1 us  [the longest x4 22 us: on_device(): full = jnp.repeat(m_h, cw, axis=3)]
    all_gather x1 -> x0, local copies, waits for them, and re-layouts: 6.65 us -> none  [on_device(): lax.all_gather(weight, 'dp', axis=0, tiled=True)]
  transfers between devices with their start and end apart: 3 -> 27, of which waited for: 2 -> 10; matrix products, arithmetic and copies ran while one was open for 20% -> 57% of each run, Pallas kernels for 0% -> 0%
where the time goes in v1:
time: 307 us; the launch traced here: 304 us
  local copies, waits for them, and re-layouts  139 us (45%)
  waiting for transfers between devices  61.7 us (20%)
  starting transfers between devices  49.5 us (16%)
  matrix products  26.2 us (9%)
  between operations  14.6 us (5%)
  other arithmetic  13.5 us (4%)
    reshape x8, local copies, waits for them, and re-layouts, on_device(): full = jnp.repeat(m_h, cw, axis=3)  104 us
    ppermute x18, starting transfers between devices, shift_z(): return lax.ppermute(a, 'dp', pairs)  42 us
    ppermute x6, waiting for transfers between devices, swap_x(): return lax.ppermute(a, 'dp', [(d, d ^ 1) for d in range(dp)])  36.8 us
    ppermute x18, waiting for transfers between devices, shift_z(): return lax.ppermute(a, 'dp', pairs)  24.8 us
    broadcast_in_dim x4, local copies, waits for them, and re-layouts, on_device(): full = jnp.repeat(m_h, cw, axis=3)  22 us
    dot_general x4, matrix products, on_device(): jnp.einsum('tn,snc->stc', a_h, masked, preferred_element_type=F32)  11.5 us
    dot_general x4, matrix products, on_device(): jnp.einsum('stc,snc->tn', out_grad, masked, preferred_element_type=F32)  8.68 us
    ppermute x6, starting transfers between devices, swap_x(): return lax.ppermute(a, 'dp', [(d, d ^ 1) for d in range(dp)])  7.19 us
  transfers between devices with their start and end apart: 27, of which 10 were waited for; matrix products, arithmetic and copies ran while one was open for 57% of the time, Pallas kernels for 0%

profile of v1, /device:TPU:0, one launch (start us, length us, event | category | flops | bytes accessed | tf_op | source)
XLA Modules:
  0.0 304.1 jit_solution(6278973375161865933)
XLA Ops:
  7.2 2.0 fusion.75
  9.9 1.6 constant_dynamic-slice_fusion
  11.5 1.1 copy.45
  12.6 3.0 collective-permute-start.2
  15.6 0.9 fusion.74
  16.6 2.0 collective-permute-start.17
  20.8 5.5 %broadcast_in_dim.35 = bf16[4,4,192,3,256]{4,3,2,1,0:T(4,128)(2,1)} broadcast(bf16[4,4,192,3]{3,2,1,0:T(8,128)(2,1)S(1)} %copy.31), dimensions={0,1,2,3} | broadcast | bytes 4737024 | tf_op jit(solution)/shard_map/broadcast_in_dim | solution.py:81
  26.3 13.0 %reshape.228 = bf16[4,768,768]{2,1,0:T(8,128)(2,1)} reshape(bf16[4,4,192,3,256]{4,3,2,1,0:T(4,128)(2,1)} %broadcast_in_dim.35) | data formatting | bytes 9437184 | tf_op jit(solution)/shard_map/reshape | solution.py:81
  39.3 13.0 %reshape.221 = bf16[4,4,192,768]{3,2,1,0:T(8,128)(2,1)} reshape(bf16[4,4,192,3,256]{4,3,2,1,0:T(4,128)(2,1)} %broadcast_in_dim.35) | data formatting | bytes 9437184 | tf_op jit(solution)/shard_map/reshape | solution.py:81
  52.8 5.5 %broadcast_in_dim.34 = bf16[4,4,192,3,256]{4,3,2,1,0:T(4,128)(2,1)} broadcast(bf16[4,4,192,3]{3,2,1,0:T(8,128)(2,1)S(1)} %copy.30), dimensions={0,1,2,3} | broadcast | bytes 4737024 | tf_op jit(solution)/shard_map/broadcast_in_dim | solution.py:81
  58.3 13.0 %reshape.227 = bf16[4,768,768]{2,1,0:T(8,128)(2,1)} reshape(bf16[4,4,192,3,256]{4,3,2,1,0:T(4,128)(2,1)} %broadcast_in_dim.34) | data formatting | bytes 9437184 | tf_op jit(solution)/shard_map/reshape | solution.py:81
  71.3 13.0 %reshape.220 = bf16[4,4,192,768]{3,2,1,0:T(8,128)(2,1)} reshape(bf16[4,4,192,3,256]{4,3,2,1,0:T(4,128)(2,1)} %broadcast_in_dim.34) | data formatting | bytes 9437184 | tf_op jit(solution)/shard_map/reshape | solution.py:81
  84.8 5.5 %broadcast_in_dim.33 = bf16[4,4,192,3,256]{4,3,2,1,0:T(4,128)(2,1)} broadcast(bf16[4,4,192,3]{3,2,1,0:T(8,128)(2,1)S(1)} %copy.28), dimensions={0,1,2,3} | broadcast | bytes 4737024 | tf_op jit(solution)/shard_map/broadcast_in_dim | solution.py:81
  90.2 13.0 %reshape.226 = bf16[4,768,768]{2,1,0:T(8,128)(2,1)} reshape(bf16[4,4,192,3,256]{4,3,2,1,0:T(4,128)(2,1)} %broadcast_in_dim.33) | data formatting | bytes 9437184 | tf_op jit(solution)/shard_map/reshape | solution.py:81
  103.2 13.0 %reshape.219 = bf16[4,4,192,768]{3,2,1,0:T(8,128)(2,1)} reshape(bf16[4,4,192,3,256]{4,3,2,1,0:T(4,128)(2,1)} %broadcast_in_dim.33) | data formatting | bytes 9437184 | tf_op jit(solution)/shard_map/reshape | solution.py:81
  116.7 5.5 %broadcast_in_dim.32 = bf16[4,4,192,3,256]{4,3,2,1,0:T(4,128)(2,1)} broadcast(bf16[4,4,192,3]{3,2,1,0:T(8,128)(2,1)S(1)} %copy.26), dimensions={0,1,2,3} | broadcast | bytes 4737024 | tf_op jit(solution)/shard_map/broadcast_in_dim | solution.py:81
  122.2 13.0 %reshape.225 = bf16[4,768,768]{2,1,0:T(8,128)(2,1)} reshape(bf16[4,4,192,3,256]{4,3,2,1,0:T(4,128)(2,1)} %broadcast_in_dim.32) | data formatting | bytes 9437184 | tf_op jit(solution)/shard_map/reshape | solution.py:81
  135.2 13.0 %reshape.217 = bf16[4,4,192,768]{3,2,1,0:T(8,128)(2,1)} reshape(bf16[4,4,192,3,256]{4,3,2,1,0:T(4,128)(2,1)} %broadcast_in_dim.32) | data formatting | bytes 9437184 | tf_op jit(solution)/shard_map/reshape | solution.py:81
  148.3 1.1 copy.44
  149.5 2.0 fusion.18
  151.6 4.0 %collective-permute-start.11 = (f32[384,256]{1,0:T(8,128)S(1)}, f32[384,256]{1,0:T(8,128)S(1)}, u32[]{:S(2)}, u32[]{:S(2)}) collective-permute-start(f32[384,256]{1,0:T(8,128)S(1)} %get-tuple-element.18), channel_id=1, source_target_pairs={{0,8},{4,12},{1,9},{5,13},{2,10},{6,14},{3,11},{7,15}} | collective-permute-start | bytes 1179656 | tf_op jit(solution)/shard_map/ppermute | solution.py:32
  156.3 2.0 fusion.20
  158.4 1.3 collective-permute-start.4
  160.4 2.0 fusion.16
  162.5 1.3 collective-permute-start.18
  163.8 1.3 collective-permute-done.11
  165.9 7.7 %collective-permute-done.4 = f32[384,256]{1,0:T(8,128)S(1)} collective-permute-done((f32[384,256]{1,0:T(8,128)S(1)}, f32[384,256]{1,0:T(8,128)S(1)}, u32[]{:S(2)}, u32[]{:S(2)}) %collective-permute-start.4) | collective-permute-done | bytes 393248 | tf_op jit(solution)/shard_map/ppermute | solution.py:32
  173.6 4.4 %collective-permute-start.12 = (f32[384,256]{1,0:T(8,128)S(1)}, f32[384,256]{1,0:T(8,128)S(1)}, u32[]{:S(2)}, u32[]{:S(2)}) collective-permute-start(f32[384,256]{1,0:T(8,128)S(1)} %bitcast_add_fusion.10), channel_id=1, source_target_pairs={{0,8},{4,12},{8,16},{12,20},{1,9},{5,13},{9,17},{13,21},{2,10},{6,... | collective-permute-start | bytes 1179656 | tf_op jit(solution)/shard_map/ppermute | solution.py:32
  178.0 4.0 %collective-permute-done.18 = f32[384,256]{1,0:T(8,128)S(1)} collective-permute-done((f32[384,256]{1,0:T(8,128)S(1)}, f32[384,256]{1,0:T(8,128)S(1)}, u32[]{:S(2)}, u32[]{:S(2)}) %collective-permute-start.18) | collective-permute-done | bytes 393248 | tf_op jit(solution)/shard_map/ppermute | solution.py:32
  182.0 4.4 %collective-permute-start.5 = (f32[384,256]{1,0:T(8,128)S(1)}, f32[384,256]{1,0:T(8,128)S(1)}, u32[]{:S(2)}, u32[]{:S(2)}) collective-permute-start(f32[384,256]{1,0:T(8,128)S(1)} %bitcast_add_fusion.15), channel_id=1, source_target_pairs={{0,8},{4,12},{8,16},{12,20},{1,9},{5,13},{9,17},{13,21},{2,10},{6,... | collective-permute-start | bytes 1179656 | tf_op jit(solution)/shard_map/ppermute | solution.py:32
  186.5 2.1 collective-permute-start.19
  188.6 1.8 collective-permute-done.12
  190.4 0.9 bitcast_add_fusion.11
  191.3 5.1 %collective-permute-start.13 = (f32[384,256]{1,0:T(8,128)}, f32[384,256]{1,0:T(8,128)}, u32[]{:S(2)}, u32[]{:S(2)}) collective-permute-start(f32[384,256]{1,0:T(8,128)} %get-tuple-element.16), channel_id=1, source_target_pairs={{0,8},{4,12},{8,16},{12,20},{16,24},{20,28},{1,9},{5,13},{9,17},{1... | collective-permute-start | bytes 1179656 | tf_op jit(solution)/shard_map/ppermute | solution.py:32
  197.2 1.7 collective-permute-done.5
  198.8 0.9 bitcast_add_fusion.16
  199.7 5.1 %collective-permute-start.6 = (f32[384,256]{1,0:T(8,128)}, f32[384,256]{1,0:T(8,128)}, u32[]{:S(2)}, u32[]{:S(2)}) collective-permute-start(f32[384,256]{1,0:T(8,128)} %get-tuple-element.12), channel_id=1, source_target_pairs={{0,8},{4,12},{8,16},{12,20},{16,24},{20,28},{1,9},{5,13},{9,17},{1... | collective-permute-start | bytes 1179656 | tf_op jit(solution)/shard_map/ppermute | solution.py:32
  205.6 1.7 collective-permute-done.19
  207.3 1.0 bitcast_add_fusion.6
  208.3 5.1 %collective-permute-start.20 = (f32[384,256]{1,0:T(8,128)}, f32[384,256]{1,0:T(8,128)}, u32[]{:S(2)}, u32[]{:S(2)}) collective-permute-start(f32[384,256]{1,0:T(8,128)} %get-tuple-element.20), channel_id=1, source_target_pairs={{0,8},{4,12},{8,16},{12,20},{16,24},{20,28},{1,9},{5,13},{9,17},{1... | collective-permute-start | bytes 1179656 | tf_op jit(solution)/shard_map/ppermute | solution.py:32
  214.2 1.5 collective-permute-start.1
  217.1 4.6 %fusion.48 = f32[768,128]{1,0:T(8,128)S(1)} fusion(bf16[4,128,768]{2,1,0:T(8,128)(2,1)} %param.7, bf16[4,768,768]{2,1,0:T(8,128)(2,1)} %reshape.227, bf16[768,768]{1,0:T(8,128)(2,1)} %all-gather.7.cloned.1.call-done), kind=kOutput, calls=%fused_computation.45 | convolution fusion | flops 606339072 | bytes 7077888 | tf_op jit(solution)/shard_map/stc,snc->tn/dot_general | solution.py:86
  221.8 1.4 fusion.42
  223.1 20.2 %collective-permute-done.1 = bf16[4,192,768]{2,1,0:T(8,128)(2,1)S(1)} collective-permute-done((bf16[4,192,768]{2,1,0:T(8,128)(2,1)}, bf16[4,192,768]{2,1,0:T(8,128)(2,1)S(1)}, u32[]{:S(2)}, u32[]{:S(2)}) %collective-permute-start.1) | collective-permute-done | bytes 1179680 | tf_op jit(solution)/shard_map/ppermute | solution.py:28
  243.3 1.4 collective-permute-start.22
  244.8 1.4 broadcast_select_fusion.1
  246.1 16.6 %collective-permute-done = bf16[4,192,768]{2,1,0:T(8,128)(2,1)S(1)} collective-permute-done((bf16[4,192,768]{2,1,0:T(8,128)(2,1)}, bf16[4,192,768]{2,1,0:T(8,128)(2,1)S(1)}, u32[]{:S(2)}, u32[]{:S(2)}) %collective-permute-start) | collective-permute-done | bytes 1179680 | tf_op jit(solution)/shard_map/ppermute | solution.py:28
  262.8 1.3 collective-permute-start.16
  264.1 1.4 broadcast_select_fusion.3
  265.6 1.3 pad_maximum_fusion
  266.9 1.4 collective-permute-start.9
  268.4 1.2 bitcast_add_fusion.4
  269.6 4.0 %fusion.10 = f32[4,768,128,1]{2,1,3,0:T(8,128)S(1)} fusion(bf16[4,4,192,768]{3,2,1,0:T(8,128)(2,1)} %reshape.220, bf16[4,192,768]{2,1,0:T(8,128)(2,1)S(1)} %bitcast.180, bf16[128,4,384]{0,2,1:T(8,128)(2,1)} %bitcast.208), kind=kOutput, calls=%fused_computation.11 | convolution fusion | flops 606339072 | bytes 7667712 | tf_op jit(solution)/shard_map/tn,snc->stc/dot_general | solution.py:84
  273.6 4.3 %fusion.14 = f32[4,768,128,1]{2,1,3,0:T(8,128)S(1)} fusion(bf16[4,4,192,768]{3,2,1,0:T(8,128)(2,1)} %reshape.217, bf16[4,192,768]{2,1,0:T(8,128)(2,1)S(1)} %bitcast.182, bf16[128,4,384]{0,2,1:T(8,128)(2,1)S(1)} %bitcast.209), kind=kOutput, calls=%fused_computation.15 | convolution fusion | flops 606339072 | bytes 7667712 | tf_op jit(solution)/shard_map/tn,snc->stc/dot_general | solution.py:84
  277.9 1.6 collective-permute-start.23
  279.5 1.3 fusion.66
  281.1 1.3 fusion.68
  282.4 6.4 %collective-permute-done.23 = f32[384,256]{1,0:T(8,128)S(1)} collective-permute-done((f32[384,256]{1,0:T(8,128)S(1)}, f32[384,256]{1,0:T(8,128)S(1)}, u32[]{:S(2)}, u32[]{:S(2)}) %collective-permute-start.23) | collective-permute-done | bytes 393248 | tf_op jit(solution)/shard_map/ppermute | solution.py:32
  288.8 1.4 fusion.64
  290.2 1.1 pad_maximum_fusion.1
  291.3 1.6 fusion.12
  292.9 1.7 fusion.39
  294.6 1.2 copy.36
  295.7 1.0 convert_element_type.20
  (121 shorter events, 11.7 us)
Async XLA Ops:
  7.2 2.1 copy-start.11
  7.2 207.0 %all-gather.7.cloned.1.call-start = ((), (), s32[]{:S(2)}) async-start(), calls=%async_computation.3 | async-start | bytes 1474560 | tf_op jit(solution)/shard_map/all_gather | solution.py:48
  9.2 207.3 %all-gather.5.cloned.1.call-start = ((), (), s32[]{:S(2)}) async-start(), calls=%async_computation.2 | async-start | bytes 1474560 | tf_op jit(solution)/shard_map/all_gather | solution.py:48
  9.9 5.7 %copy-start.12 = (bf16[4,128,768]{2,1,0:T(8,128)(2,1)S(1)}, bf16[4,128,768]{2,1,0:T(8,128)(2,1)}, u32[]{:S(2)}) copy-start(bf16[4,128,768]{2,1,0:T(8,128)(2,1)} %param.7) | copy-start | bytes 2359300
  11.5 7.4 %copy-start.14 = (s32[4,12,12]{2,0,1:T(4,128)S(1)}, s32[4,12,12]{2,0,1:T(4,128)}, u32[]{:S(2)}) copy-start(s32[4,12,12]{2,0,1:T(4,128)} %param.6) | copy-start | bytes 6916
  12.6 7.7 %copy-start.9 = (bf16[128,4,1,384]{0,3,1,2:T(8,128)(2,1)}, bf16[128,4,1,384]{0,3,1,2:T(8,128)(2,1)S(1)}, u32[]{:S(2)}) copy-start(bf16[128,4,1,384]{0,3,1,2:T(8,128)(2,1)S(1)} %copy.45) | copy-start | bytes 1179652
  12.6 136.8 %collective-permute-start.2 = (bf16[128,4,384]{0,2,1:T(8,128)(2,1)S(1)}, bf16[128,4,384]{0,2,1:T(8,128)(2,1)S(1)}, u32[]{:S(2)}, u32[]{:S(2)}) collective-permute-start(bf16[128,4,384]{0,2,1:T(8,128)(2,1)S(1)} %bitcast.210), channel_id=1, source_target_pairs={{0,4},{4,0},{8,12},{12,8},{16,20},{20,16},{24,28},{28,24},{1,5},{5... | collective-permute-start | bytes 1179656 | tf_op jit(solution)/shard_map/ppermute | solution.py:28
  16.5 139.8 %collective-permute-start.3 = (bf16[4,128,256]{2,1,0:T(8,128)(2,1)}, bf16[4,128,256]{2,1,0:T(8,128)(2,1)S(1)}, u32[]{:S(2)}, u32[]{:S(2)}) collective-permute-start(bf16[4,128,256]{2,1,0:T(8,128)(2,1)} %get-tuple-element.28), channel_id=1, source_target_pairs={{0,4},{4,0},{8,12},{12,8},{16,20},{20,16},{24,28},{28,24},{1,5},{5... | collective-permute-start | bytes 786440 | tf_op jit(solution)/shard_map/ppermute | solution.py:28
  16.6 143.8 %collective-permute-start.17 = (bf16[4,128,256]{2,1,0:T(8,128)(2,1)}, bf16[4,128,256]{2,1,0:T(8,128)(2,1)S(1)}, u32[]{:S(2)}, u32[]{:S(2)}) collective-permute-start(bf16[4,128,256]{2,1,0:T(8,128)(2,1)} %get-tuple-element.29), channel_id=1, source_target_pairs={{0,4},{4,0},{8,12},{12,8},{16,20},{20,16},{24,28},{28,24},{1,5},{5... | collective-permute-start | bytes 786440 | tf_op jit(solution)/shard_map/ppermute | solution.py:28
  18.5 131.0 %collective-permute-start.10 = (bf16[4,128,256]{2,1,0:T(8,128)(2,1)}, bf16[4,128,256]{2,1,0:T(8,128)(2,1)S(1)}, u32[]{:S(2)}, u32[]{:S(2)}) collective-permute-start(bf16[4,128,256]{2,1,0:T(8,128)(2,1)} %get-tuple-element.30), channel_id=1, source_target_pairs={{0,4},{4,0},{8,12},{12,8},{16,20},{20,16},{24,28},{28,24},{1,5},{5... | collective-permute-start | bytes 786440 | tf_op jit(solution)/shard_map/ppermute | solution.py:28
  18.6 277.1 %reduce-scatter.2.cloned.1.call-start = ((), (), s32[]{:S(2)}) async-start(), calls=%async_computation.1 | async-start | bytes 1966080 | tf_op jit(solution)/shard_map/reduce_scatter | solution.py:95
  149.3 2.2 copy-start.7
  151.5 61.9 %copy-start.4 = (f32[1536,256,1]{1,0,2:T(8,128)}, f32[1536,256,1]{1,0,2:T(8,128)S(1)}, u32[]{:S(2)}) copy-start(f32[1536,256,1]{1,0,2:T(8,128)S(1)} %fusion.18) | copy-start | bytes 4718596
  151.6 13.5 %collective-permute-start.11 = (f32[384,256]{1,0:T(8,128)S(1)}, f32[384,256]{1,0:T(8,128)S(1)}, u32[]{:S(2)}, u32[]{:S(2)}) collective-permute-start(f32[384,256]{1,0:T(8,128)S(1)} %get-tuple-element.18), channel_id=1, source_target_pairs={{0,8},{4,12},{1,9},{5,13},{2,10},{6,14},{3,11},{7,15}} | collective-permute-start | bytes 1179656 | tf_op jit(solution)/shard_map/ppermute | solution.py:32
  155.6 30.9 %collective-permute-start.14 = (f32[384,256]{1,0:T(8,128)S(1)}, f32[384,256]{1,0:T(8,128)S(1)}, u32[]{:S(2)}, u32[]{:S(2)}) collective-permute-start(f32[384,256]{1,0:T(8,128)S(1)} %get-tuple-element.19), channel_id=1, source_target_pairs={{24,16},{28,20},{25,17},{29,21},{26,18},{30,22},{27,19},{31,23}} | collective-permute-start | bytes 1179656 | tf_op jit(solution)/shard_map/ppermute | solution.py:32
  158.3 57.4 %copy-start.5 = (f32[1536,256,1]{1,0,2:T(8,128)}, f32[1536,256,1]{1,0,2:T(8,128)S(1)}, u32[]{:S(2)}) copy-start(f32[1536,256,1]{1,0,2:T(8,128)S(1)} %fusion.20) | copy-start | bytes 4718596
  158.4 15.2 %collective-permute-start.4 = (f32[384,256]{1,0:T(8,128)S(1)}, f32[384,256]{1,0:T(8,128)S(1)}, u32[]{:S(2)}, u32[]{:S(2)}) collective-permute-start(f32[384,256]{1,0:T(8,128)S(1)} %get-tuple-element.14), channel_id=1, source_target_pairs={{0,8},{4,12},{1,9},{5,13},{2,10},{6,14},{3,11},{7,15}} | collective-permute-start | bytes 1179656 | tf_op jit(solution)/shard_map/ppermute | solution.py:32
  159.7 36.8 %collective-permute-start.7 = (f32[384,256]{1,0:T(8,128)S(1)}, f32[384,256]{1,0:T(8,128)S(1)}, u32[]{:S(2)}, u32[]{:S(2)}) collective-permute-start(f32[384,256]{1,0:T(8,128)S(1)} %get-tuple-element.15), channel_id=1, source_target_pairs={{24,16},{28,20},{25,17},{29,21},{26,18},{30,22},{27,19},{31,23}} | collective-permute-start | bytes 1179656 | tf_op jit(solution)/shard_map/ppermute | solution.py:32
  162.4 44.9 %copy-start.6 = (f32[1536,256,1]{1,0,2:T(8,128)}, f32[1536,256,1]{1,0,2:T(8,128)S(1)}, u32[]{:S(2)}) copy-start(f32[1536,256,1]{1,0,2:T(8,128)S(1)} %fusion.16) | copy-start | bytes 4718596
  162.5 19.5 %collective-permute-start.18 = (f32[384,256]{1,0:T(8,128)S(1)}, f32[384,256]{1,0:T(8,128)S(1)}, u32[]{:S(2)}, u32[]{:S(2)}) collective-permute-start(f32[384,256]{1,0:T(8,128)S(1)} %get-tuple-element.22), channel_id=1, source_target_pairs={{0,8},{4,12},{1,9},{5,13},{2,10},{6,14},{3,11},{7,15}} | collective-permute-start | bytes 1179656 | tf_op jit(solution)/shard_map/ppermute | solution.py:32
  165.1 39.7 %collective-permute-start.21 = (f32[384,256]{1,0:T(8,128)S(1)}, f32[384,256]{1,0:T(8,128)S(1)}, u32[]{:S(2)}, u32[]{:S(2)}) collective-permute-start(f32[384,256]{1,0:T(8,128)S(1)} %get-tuple-element.23), channel_id=1, source_target_pairs={{24,16},{28,20},{25,17},{29,21},{26,18},{30,22},{27,19},{31,23}} | collective-permute-start | bytes 1179656 | tf_op jit(solution)/shard_map/ppermute | solution.py:32
  173.6 16.9 %collective-permute-start.12 = (f32[384,256]{1,0:T(8,128)S(1)}, f32[384,256]{1,0:T(8,128)S(1)}, u32[]{:S(2)}, u32[]{:S(2)}) collective-permute-start(f32[384,256]{1,0:T(8,128)S(1)} %bitcast_add_fusion.10), channel_id=1, source_target_pairs={{0,8},{4,12},{8,16},{12,20},{1,9},{5,13},{9,17},{13,21},{2,10},{6,... | collective-permute-start | bytes 1179656 | tf_op jit(solution)/shard_map/ppermute | solution.py:32
  182.0 16.9 %collective-permute-start.5 = (f32[384,256]{1,0:T(8,128)S(1)}, f32[384,256]{1,0:T(8,128)S(1)}, u32[]{:S(2)}, u32[]{:S(2)}) collective-permute-start(f32[384,256]{1,0:T(8,128)S(1)} %bitcast_add_fusion.15), channel_id=1, source_target_pairs={{0,8},{4,12},{8,16},{12,20},{1,9},{5,13},{9,17},{13,21},{2,10},{6,... | collective-permute-start | bytes 1179656 | tf_op jit(solution)/shard_map/ppermute | solution.py:32
  186.5 20.8 %collective-permute-start.19 = (f32[384,256]{1,0:T(8,128)S(1)}, f32[384,256]{1,0:T(8,128)S(1)}, u32[]{:S(2)}, u32[]{:S(2)}) collective-permute-start(f32[384,256]{1,0:T(8,128)S(1)} %bitcast_add_fusion.5), channel_id=1, source_target_pairs={{0,8},{4,12},{8,16},{12,20},{1,9},{5,13},{9,17},{13,21},{2,10},{6,... | collective-permute-start | bytes 1179656 | tf_op jit(solution)/shard_map/ppermute | solution.py:32
  191.3 86.5 %collective-permute-start.13 = (f32[384,256]{1,0:T(8,128)}, f32[384,256]{1,0:T(8,128)}, u32[]{:S(2)}, u32[]{:S(2)}) collective-permute-start(f32[384,256]{1,0:T(8,128)} %get-tuple-element.16), channel_id=1, source_target_pairs={{0,8},{4,12},{8,16},{12,20},{16,24},{20,28},{1,9},{5,13},{9,17},{1... | collective-permute-start | bytes 1179656 | tf_op jit(solution)/shard_map/ppermute | solution.py:32
  196.5 16.9 %collective-permute-start.15 = (f32[384,256]{1,0:T(8,128)S(1)}, f32[384,256]{1,0:T(8,128)S(1)}, u32[]{:S(2)}, u32[]{:S(2)}) collective-permute-start(f32[384,256]{1,0:T(8,128)S(1)} %get-tuple-element.17), channel_id=1, source_target_pairs={{16,8},{20,12},{24,16},{28,20},{17,9},{21,13},{25,17},{29,21},{18,... | collective-permute-start | bytes 1179656 | tf_op jit(solution)/shard_map/ppermute | solution.py:32
  199.7 81.0 %collective-permute-start.6 = (f32[384,256]{1,0:T(8,128)}, f32[384,256]{1,0:T(8,128)}, u32[]{:S(2)}, u32[]{:S(2)}) collective-permute-start(f32[384,256]{1,0:T(8,128)} %get-tuple-element.12), channel_id=1, source_target_pairs={{0,8},{4,12},{8,16},{12,20},{16,24},{20,28},{1,9},{5,13},{9,17},{1... | collective-permute-start | bytes 1179656 | tf_op jit(solution)/shard_map/ppermute | solution.py:32
  204.9 10.8 %collective-permute-start.8 = (f32[384,256]{1,0:T(8,128)S(1)}, f32[384,256]{1,0:T(8,128)S(1)}, u32[]{:S(2)}, u32[]{:S(2)}) collective-permute-start(f32[384,256]{1,0:T(8,128)S(1)} %get-tuple-element.13), channel_id=1, source_target_pairs={{16,8},{20,12},{24,16},{28,20},{17,9},{21,13},{25,17},{29,21},{18,... | collective-permute-start | bytes 1179656 | tf_op jit(solution)/shard_map/ppermute | solution.py:32
  208.3 74.1 %collective-permute-start.20 = (f32[384,256]{1,0:T(8,128)}, f32[384,256]{1,0:T(8,128)}, u32[]{:S(2)}, u32[]{:S(2)}) collective-permute-start(f32[384,256]{1,0:T(8,128)} %get-tuple-element.20), channel_id=1, source_target_pairs={{0,8},{4,12},{8,16},{12,20},{16,24},{20,28},{1,9},{5,13},{9,17},{1... | collective-permute-start | bytes 1179656 | tf_op jit(solution)/shard_map/ppermute | solution.py:32
  214.2 29.1 %collective-permute-start.1 = (bf16[4,192,768]{2,1,0:T(8,128)(2,1)}, bf16[4,192,768]{2,1,0:T(8,128)(2,1)S(1)}, u32[]{:S(2)}, u32[]{:S(2)}) collective-permute-start(bf16[4,192,768]{2,1,0:T(8,128)(2,1)} %bitcast.179), channel_id=1, source_target_pairs={{0,4},{4,0},{8,12},{12,8},{16,20},{20,16},{24,28},{28,24},{1,5},{5... | collective-permute-start | bytes 3538952 | tf_op jit(solution)/shard_map/ppermute | solution.py:28
  216.5 5.2 %slice-start.8 = ((s8[4718592]{0:T(1024)(128)(4,1)}), s8[4194304]{0:T(1024)(128)(4,1)S(1)}, s32[]{:S(2)}) async-start(s8[4718592]{0:T(1024)(128)(4,1)} %bitcast.205), calls=%async_computation.12 | async-start | bytes 8388608
  216.5 5.2 %copy-start.1 = (bf16[768,768]{1,0:T(8,128)(2,1)S(1)}, bf16[768,768]{1,0:T(8,128)(2,1)}, u32[]{:S(2)}) copy-start(bf16[768,768]{1,0:T(8,128)(2,1)} %all-gather.5.cloned.1.call-done) | copy-start | bytes 3538948
  216.5 5.2 %slice-start.9 = ((s8[4718592]{0:T(1024)(128)(4,1)}), s8[524288]{0:T(1024)(128)(4,1)S(1)}, s32[]{:S(2)}) async-start(s8[4718592]{0:T(1024)(128)(4,1)} %bitcast.205), calls=%async_computation.13 | async-start | bytes 1048576
  216.5 5.2 %copy-start.13 = (bf16[4,128,768]{2,1,0:T(8,128)(2,1)S(1)}, bf16[4,128,768]{2,1,0:T(8,128)(2,1)}, u32[]{:S(2)}) copy-start(bf16[4,128,768]{2,1,0:T(8,128)(2,1)} %param.7) | copy-start | bytes 2359300
  216.5 46.3 %collective-permute-start = (bf16[4,192,768]{2,1,0:T(8,128)(2,1)}, bf16[4,192,768]{2,1,0:T(8,128)(2,1)S(1)}, u32[]{:S(2)}, u32[]{:S(2)}) collective-permute-start(bf16[4,192,768]{2,1,0:T(8,128)(2,1)} %bitcast.181), channel_id=1, source_target_pairs={{0,4},{4,0},{8,12},{12,8},{16,20},{20,16},{24,28},{28,24},{1,5},{5... | collective-permute-start | bytes 3538952 | tf_op jit(solution)/shard_map/ppermute | solution.py:28
  217.1 27.6 %slice-start.4 = ((s8[4718592]{0:T(1024)(128)(4,1)}), s8[4194304]{0:T(1024)(128)(4,1)S(1)}, s32[]{:S(2)}) async-start(s8[4718592]{0:T(1024)(128)(4,1)} %bitcast.201), calls=%async_computation.8 | async-start | bytes 8388608
  221.7 23.0 %slice-start.5 = ((s8[4718592]{0:T(1024)(128)(4,1)}), s8[524288]{0:T(1024)(128)(4,1)S(1)}, s32[]{:S(2)}) async-start(s8[4718592]{0:T(1024)(128)(4,1)} %bitcast.201), calls=%async_computation.9 | async-start | bytes 1048576
  221.7 42.3 %slice-start.6 = ((s8[4718592]{0:T(1024)(128)(4,1)}), s8[4194304]{0:T(1024)(128)(4,1)S(1)}, s32[]{:S(2)}) async-start(s8[4718592]{0:T(1024)(128)(4,1)} %bitcast.203), calls=%async_computation.10 | async-start | bytes 8388608
  243.3 23.6 %collective-permute-start.22 = (f32[384,256]{1,0:T(8,128)}, f32[384,256]{1,0:T(8,128)}, u32[]{:S(2)}, u32[]{:S(2)}) collective-permute-start(f32[384,256]{1,0:T(8,128)} %get-tuple-element.21), channel_id=1, source_target_pairs={{16,8},{20,12},{24,16},{28,20},{17,9},{21,13},{25,17},{29,21},{18,... | collective-permute-start | bytes 1179656 | tf_op jit(solution)/shard_map/ppermute | solution.py:32
  244.8 19.3 %slice-start.7 = ((s8[4718592]{0:T(1024)(128)(4,1)}), s8[524288]{0:T(1024)(128)(4,1)S(1)}, s32[]{:S(2)}) async-start(s8[4718592]{0:T(1024)(128)(4,1)} %bitcast.203), calls=%async_computation.11 | async-start | bytes 1048576
  262.8 2.7 copy-start.2
  262.8 16.7 %collective-permute-start.16 = (f32[384,256]{1,0:T(8,128)}, f32[384,256]{1,0:T(8,128)}, u32[]{:S(2)}, u32[]{:S(2)}) collective-permute-start(f32[384,256]{1,0:T(8,128)} %bitcast_add_fusion.9), channel_id=1, source_target_pairs={{8,0},{12,4},{16,8},{20,12},{24,16},{28,20},{9,1},{13,5},{17,9},{2... | collective-permute-start | bytes 1179656 | tf_op jit(solution)/shard_map/ppermute | solution.py:32
  266.9 2.6 copy-start
  266.9 14.1 %collective-permute-start.9 = (f32[384,256]{1,0:T(8,128)}, f32[384,256]{1,0:T(8,128)S(1)}, u32[]{:S(2)}, u32[]{:S(2)}) collective-permute-start(f32[384,256]{1,0:T(8,128)} %bitcast_add_fusion.14), channel_id=1, source_target_pairs={{8,0},{12,4},{16,8},{20,12},{24,16},{28,20},{9,1},{13,5},{17,9},{2... | collective-permute-start | bytes 1179656 | tf_op jit(solution)/shard_map/ppermute | solution.py:32
  269.6 4.0 %copy-start.8 = (bf16[128,4,1,384]{0,3,1,2:T(8,128)(2,1)S(1)}, bf16[128,4,1,384]{0,3,1,2:T(8,128)(2,1)}, u32[]{:S(2)}) copy-start(bf16[128,4,1,384]{0,3,1,2:T(8,128)(2,1)} %copy-done.7) | copy-start | bytes 1179652
  269.6 21.7 %slice-start.2 = ((s8[4718592]{0:T(1024)(128)(4,1)}), s8[4194304]{0:T(1024)(128)(4,1)S(1)}, s32[]{:S(2)}) async-start(s8[4718592]{0:T(1024)(128)(4,1)} %bitcast.177), calls=%async_computation.6 | async-start | bytes 8388608
  273.6 17.7 %slice-start.3 = ((s8[4718592]{0:T(1024)(128)(4,1)}), s8[524288]{0:T(1024)(128)(4,1)S(1)}, s32[]{:S(2)}) async-start(s8[4718592]{0:T(1024)(128)(4,1)} %bitcast.177), calls=%async_computation.7 | async-start | bytes 1048576
  277.9 10.9 %collective-permute-start.23 = (f32[384,256]{1,0:T(8,128)S(1)}, f32[384,256]{1,0:T(8,128)S(1)}, u32[]{:S(2)}, u32[]{:S(2)}) collective-permute-start(f32[384,256]{1,0:T(8,128)S(1)} %bitcast_add_fusion.4), channel_id=1, source_target_pairs={{8,0},{12,4},{16,8},{20,12},{24,16},{28,20},{9,1},{13,5},{17,9},{2... | collective-permute-start | bytes 1179656 | tf_op jit(solution)/shard_map/ppermute | solution.py:32
  281.1 10.2 %copy-start.3 = (bf16[4,192,768]{2,1,0:T(8,128)(2,1)S(1)}, bf16[4,192,768]{2,1,0:T(8,128)(2,1)}, u32[]{:S(2)}) copy-start(bf16[4,192,768]{2,1,0:T(8,128)(2,1)} %copy-done.2) | copy-start | bytes 3538948
  281.1 10.2 %copy-start.10 = (bf16[128,4,1,384]{0,3,1,2:T(8,128)(2,1)S(1)}, bf16[128,4,1,384]{0,3,1,2:T(8,128)(2,1)}, u32[]{:S(2)}) copy-start(bf16[128,4,1,384]{0,3,1,2:T(8,128)(2,1)} %copy-done.9) | copy-start | bytes 1179652
  288.8 4.0 %slice-start = ((s8[4718592]{0:T(1024)(128)(4,1)}), s8[4194304]{0:T(1024)(128)(4,1)S(1)}, s32[]{:S(2)}) async-start(s8[4718592]{0:T(1024)(128)(4,1)} %bitcast.175), calls=%async_computation.4 | async-start | bytes 8388608
  291.3 1.6 slice-start.1
Sparse Core Ops, SparseCore 0:
  9.6 33.1 all-gather.6
  44.3 29.5 all-gather.4
  267.1 28.4 reduce-scatter.1

commit v2 on v1

v2 whole, which is shorter than its diff:
```python
import math

import jax
import jax.numpy as jnp
from jax import lax
from jax.experimental import pallas as pl
from jax.experimental.pallas import tpu as pltpu
from jax.sharding import PartitionSpec as P

BS = 256
TOK_G = 128
LANES = 128
F32 = jnp.float32
BF16 = jnp.bfloat16
VMEM_BYTES = 40 * 1024 * 1024


def plain(acts, weight, block_mask, out_grad):
    width = weight.shape[1]
    kblocks = block_mask.shape[1]
    oblocks = block_mask.shape[2]
    first_col = lax.axis_index("fsdp") * width
    col_ids = (first_col + jnp.arange(width, dtype=jnp.int32)) // BS
    col_select = (col_ids[None, :] == jnp.arange(oblocks, dtype=jnp.int32)[:, None]).astype(F32)
    col_mask = jnp.einsum("skb,bc->skc", block_mask.astype(F32), col_select)
    full = lax.all_gather(weight, "dp", axis=0, tiled=True)
    row_ids = jnp.arange(full.shape[0], dtype=jnp.int32) // BS
    row_select = (row_ids[:, None] == jnp.arange(kblocks, dtype=jnp.int32)[None, :]).astype(F32)
    mask = jnp.einsum("nk,skc->snc", row_select, col_mask)
    masked = mask.astype(BF16) * full[None]
    forward = jnp.einsum("tn,snc->stc", acts, masked, preferred_element_type=F32)
    input_part = jnp.einsum("stc,snc->tn", out_grad, masked, preferred_element_type=F32)
    products = jnp.einsum("tn,stc->snc", acts, out_grad, preferred_element_type=F32)
    grad_w = lax.psum_scatter(
        jnp.sum(mask * products, axis=0) * (1.0 / TOK_G), "dp", scatter_dimension=0, tiled=True
    )
    grad_x = lax.psum_scatter(input_part, "fsdp", scatter_dimension=1, tiled=True).astype(BF16)
    return (forward.astype(BF16), grad_w, grad_x)


def weight_grad_part(acts_mine, acts_peer, og_mine, og_peer, block_mask, where, nx, rows, chunk):
    nsub, tokens, cw = og_mine.shape
    total = acts_mine.shape[1]

    def kernel(where_ref, mask_ref, am_ref, ap_ref, om_ref, op_ref, out_ref):
        x = where_ref[0]
        col = where_ref[1] + chunk
        rhs_m = om_ref[...].reshape(nsub * tokens, cw)
        rhs_p = op_ref[...].reshape(nsub * tokens, cw)
        for g in range(total // LANES):
            piece, inside = divmod(g * LANES, rows)
            block = ((piece * nx + x) * rows + inside) // BS
            at = slice(g * LANES, (g + 1) * LANES)
            tm = am_ref[:, at].T
            tp = ap_ref[:, at].T
            keep = [mask_ref[s, block, col].astype(F32) for s in range(nsub)]
            keep = [jnp.full(tm.shape, k).astype(BF16) for k in keep]
            lhs_m = jnp.concatenate([tm * k for k in keep], axis=1)
            lhs_p = jnp.concatenate([tp * k for k in keep], axis=1)
            out_ref[at, :] = jnp.dot(lhs_m, rhs_m, preferred_element_type=F32) + jnp.dot(
                lhs_p, rhs_p, preferred_element_type=F32
            )

    smem = pl.BlockSpec(memory_space=pltpu.SMEM)
    vmem = pl.BlockSpec(memory_space=pltpu.VMEM)
    return pl.pallas_call(
        kernel,
        out_shape=jax.ShapeDtypeStruct((total, cw), F32),
        in_specs=[smem, smem, vmem, vmem, vmem, vmem],
        out_specs=vmem,
        compiler_params=pltpu.CompilerParams(vmem_limit_bytes=VMEM_BYTES),
        cost_estimate=pl.CostEstimate(
            flops=4 * total * cw * nsub * tokens, bytes_accessed=6 * total * cw, transcendentals=0
        ),
        name="weight_grad_part",
    )(where, block_mask, acts_mine, acts_peer, og_mine, og_peer)


def forward_and_input(acts, w_mine, w_peer, og, so_far, block_mask, where, nx, chunk):
    nsub, tokens, cw = og.shape
    depth = acts.shape[1]
    nz, rows, _ = w_mine.shape
    per = rows // LANES

    def kernel(where_ref, mask_ref, acts_ref, wm_ref, wp_ref, og_ref, *rest):
        prev_ref = rest[0] if so_far is not None else None
        out_ref, gx_ref, acc, hilo = rest[-4:]
        x = where_ref[0]
        col = where_ref[1] + chunk
        acc[...] = jnp.zeros_like(acc)
        for b in range(depth // BS):
            total = jnp.zeros((tokens, cw), F32)
            for s in range(nsub):
                total = total + mask_ref[s, b, col].astype(F32) * og_ref[s].astype(F32)
            hi = total.astype(BF16)
            hilo[b, :tokens] = hi
            hilo[b, tokens:] = (total - hi.astype(F32)).astype(BF16)

        for side in range(2):
            w_ref = wm_ref if side == 0 else wp_ref
            xs = x if side == 0 else 1 - x
            for piece in range(nz):
                for g in range(per):
                    start = (piece * nx + xs) * rows + g * LANES
                    block = start // BS
                    at = pl.ds(pl.multiple_of(start, LANES), LANES)
                    w = w_ref[piece, g * LANES : (g + 1) * LANES, :]
                    prod = jnp.dot(acts_ref[:, at], w, preferred_element_type=F32)
                    for s in range(nsub):
                        acc[s] += mask_ref[s, block, col].astype(F32) * prod
                    two = lax.dot_general(
                        hilo[block], w, (((1,), (1,)), ((), ())), preferred_element_type=F32
                    )
                    gx = two[:tokens] + two[tokens:]
                    if prev_ref is not None:
                        gx = gx + prev_ref[:, at]
                    gx_ref[:, at] = gx
        out_ref[...] = acc[...].astype(BF16)

    smem = pl.BlockSpec(memory_space=pltpu.SMEM)
    vmem = pl.BlockSpec(memory_space=pltpu.VMEM)
    args = [where, block_mask, acts, w_mine, w_peer, og]
    if so_far is not None:
        args.append(so_far)
    return pl.pallas_call(
        kernel,
        out_shape=(
            jax.ShapeDtypeStruct((nsub, tokens, cw), BF16),
            jax.ShapeDtypeStruct((tokens, depth), F32),
        ),
        in_specs=[smem, smem] + [vmem] * (len(args) - 2),
        out_specs=(vmem, vmem),
        scratch_shapes=[
            pltpu.VMEM((nsub, tokens, cw), F32),
            pltpu.VMEM((depth // BS, 2 * tokens, cw), BF16),
        ],
        compiler_params=pltpu.CompilerParams(vmem_limit_bytes=VMEM_BYTES),
        cost_estimate=pl.CostEstimate(
            flops=6 * tokens * depth * cw, bytes_accessed=4 * depth * cw, transcendentals=0
        ),
        name="forward_and_input",
    )(*args)


def on_device(acts, weight, block_mask, out_grad):
    rows, width = weight.shape
    tokens, depth = acts.shape
    dp = lax.axis_size("dp")
    fsdp = lax.axis_size("fsdp")
    if rows % LANES or width % BS or dp % 2 or fsdp != 4 or tokens % LANES:
        return plain(acts, weight, block_mask, out_grad)
    nx = 2
    nz = dp // nx
    me = lax.axis_index("dp")
    z, x = me // nx, me % nx
    col0 = lax.axis_index("fsdp") * (width // BS)
    cw = BS
    nch = width // cw
    where = jnp.stack([x, col0]).astype(jnp.int32)

    def swap_x(a):
        return lax.ppermute(a, "dp", [(d, d ^ 1) for d in range(dp)])

    def swap_f(a, bit):
        return lax.ppermute(a, "fsdp", [(d, d ^ bit) for d in range(fsdp)])

    def shift_z(a, step, senders):
        pairs = [(i * nx + j, (i + step) * nx + j) for i in senders for j in range(nx)]
        return lax.ppermute(a, "dp", pairs)

    groups = [[i * nx + j for i in range(nz)] for j in range(nx)]
    weight_mine = [
        lax.all_gather(weight[:, j * cw : (j + 1) * cw], "dp", axis_index_groups=groups, axis=0)
        for j in range(nch)
    ]

    acts_by = acts.reshape(tokens, nz, nx, rows)
    mine = lax.dynamic_index_in_dim(acts_by, x, 2, keepdims=False).reshape(tokens, nz * rows)
    other = lax.dynamic_index_in_dim(acts_by, 1 - x, 2, keepdims=False).reshape(tokens, nz * rows)
    peer = swap_x(other)
    grads = []
    for j in range(nch):
        og = out_grad[:, :, j * cw : (j + 1) * cw]
        part = weight_grad_part(mine, peer, og, swap_x(og), block_mask, where, nx, rows, j)
        part = part.reshape(nz, rows, cw)
        up = None
        down = None
        for i in range(1, nz):
            send = lax.dynamic_index_in_dim(part, jnp.minimum(z + nz - i, nz - 1), 0, keepdims=False)
            up = shift_z(send if up is None else send + up, 1, range(0, i))
            send = lax.dynamic_index_in_dim(part, jnp.maximum(z - nz + i, 0), 0, keepdims=False)
            down = shift_z(send if down is None else send + down, -1, range(nz - i, nz))
        own = lax.dynamic_index_in_dim(part, z, 0, keepdims=False)
        if nz > 1:
            own = own + up + down
        grads.append(own * (1.0 / TOK_G))
    grad_w = jnp.concatenate(grads, axis=1)

    outs = []
    gx = None
    for j in range(nch):
        og = out_grad[:, :, j * cw : (j + 1) * cw]
        out, gx = forward_and_input(
            acts, weight_mine[j], swap_x(weight_mine[j]), og, gx, block_mask, where, nx, j
        )
        outs.append(out)
    outputs = jnp.concatenate(outs, axis=2)

    f = lax.axis_index("fsdp")
    y, c = f // 2, f % 2
    by = gx.reshape(tokens, 2, 2, depth // 4)
    half = lax.dynamic_index_in_dim(by, c, 2, keepdims=False) + swap_f(
        lax.dynamic_index_in_dim(by, 1 - c, 2, keepdims=False), 1
    )
    grad_x = lax.dynamic_index_in_dim(half, y, 1, keepdims=False) + swap_f(
        lax.dynamic_index_in_dim(half, 1 - y, 1, keepdims=False), 2
    )
    return (outputs, grad_w, grad_x.astype(BF16))


def solution(mesh):
    in_specs = (P("dp", None), P("dp", "fsdp"), P(), P(None, "dp", "fsdp"))
    out_specs = (P(None, "dp", "fsdp"), P("dp", "fsdp"), P("dp", "fsdp"))
    return jax.shard_map(
        on_device, mesh=mesh, in_specs=in_specs, out_specs=out_specs, check_vma=False
    )
```

time: 307 us -> 200 us (0.65)
  the two profiles are of different devices: /device:TPU:0 before, /device:TPU:12 now
where the time goes in v2:
time: 200 us; the launch traced here: 199 us
  blocking collectives  54.3 us (27%)
  waiting for transfers between devices  47.2 us (24%)
  starting transfers between devices  44.1 us (22%)
  local copies, waits for them, and re-layouts  26.4 us (13%)
  Pallas kernels  17.3 us (9%)
  other arithmetic  8.94 us (4%)
    all_gather x3, blocking collectives, on_device(): lax.all_gather(weight[:, j * cw:(j + 1) * cw], 'dp', axis_index_groups=gr...  54.3 us
    ppermute x18, starting transfers between devices, shift_z(): return lax.ppermute(a, 'dp', pairs)  35.9 us
    ppermute x18, waiting for transfers between devices, shift_z(): return lax.ppermute(a, 'dp', pairs)  33 us
    ppermute x7, waiting for transfers between devices, swap_x(): return lax.ppermute(a, 'dp', [(d, d ^ 1) for d in range(dp)])  14.2 us
    unnamed x54, local copies, waits for them, and re-layouts  11.9 us
    pallas_call x3, Pallas kernels, forward_and_input(): pl.pallas_call(kernel, out_shape=(jax.ShapeDtypeStruct((nsub, tokens, cw)...  11.1 us
    ppermute x7, starting transfers between devices, swap_x(): return lax.ppermute(a, 'dp', [(d, d ^ 1) for d in range(dp)])  7.57 us
    pallas_call x3, Pallas kernels, weight_grad_part(): pl.pallas_call(kernel, out_shape=jax.ShapeDtypeStruct((total, cw), F32),...  6.26 us
  transfers between devices with their start and end apart: 27, of which 10 were waited for; matrix products, arithmetic and copies ran while one was open for 12% of the time, Pallas kernels for 9%

profile of v2, /device:TPU:12, one launch (start us, length us, event | category | flops | bytes accessed | tf_op | source)
XLA Modules:
  0.0 199.4 jit_solution(17018943691170801549)
XLA Ops:
  0.6 1.2 fusion.9
  1.9 18.7 %all-gather = bf16[1536,256]{1,0:T(8,128)(2,1)} all-gather(bf16[384,256]{1,0:T(8,128)(2,1)S(1)} %get-tuple-element.34), channel_id=2, replica_groups={{0,8,16,24},{4,12,20,28},{1,9,17,25},{5,13,21,29},{2,10,18,26},{6,14,22..., dimensions={0}, use_global_device_ids=true | all-gather | bytes 983040 | tf_op jit(solution)/shard_map/all_gather | solution.py:173
  20.5 1.5 collective-permute-start
  22.0 17.4 %all-gather.1 = bf16[1536,256]{1,0:T(8,128)(2,1)S(1)} all-gather(bf16[384,256]{1,0:T(8,128)(2,1)S(1)} %get-tuple-element.36), channel_id=3, replica_groups={{0,8,16,24},{4,12,20,28},{1,9,17,25},{5,13,21,29},{2,10,18,26},{6,14,22..., dimensions={0}, use_global_device_ids=true | all-gather | bytes 983040 | tf_op jit(solution)/shard_map/all_gather | solution.py:173
  40.6 4.9 %dynamic-slice_reduce_fusion = (bf16[128,4,384]{2,1,0:T(4,128)(2,1)S(1)}, bf16[128,4,384]{2,1,0:T(4,128)(2,1)S(1)}) fusion(bf16[128,4,2,384]{3,2,1,0:T(2,128)(2,1)S(1)} %reshape.29, s32[]{:T(128)S(6)} %select_n.71, s32[]{:T(128)S(6)} %select_n.70), kind=kLoop, calls=%fused_computation.5 | loop fusion | bytes 1572872 | tf_op jit(solution)/shard_map/jit(dynamic_index_in_dim)/dynamic_slice | solution.py:179
  45.5 0.8 copy.30
  46.3 1.5 collective-permute-start.3
  47.8 0.8 fusion.8
  49.1 18.2 %all-gather.2 = bf16[1536,256]{1,0:T(8,128)(2,1)} all-gather(bf16[384,256]{1,0:T(8,128)(2,1)S(1)} %get-tuple-element.35), channel_id=4, replica_groups={{0,8,16,24},{4,12,20,28},{1,9,17,25},{5,13,21,29},{2,10,18,26},{6,14,22..., dimensions={0}, use_global_device_ids=true | all-gather | bytes 983040 | tf_op jit(solution)/shard_map/all_gather | solution.py:173
  67.3 1.5 collective-permute-start.2
  68.8 5.1 %collective-permute-done.4.op_ref = bf16[4,128,256]{2,1,0:T(8,128)(2,1)S(1)} collective-permute-done((bf16[4,128,256]{2,1,0:T(8,128)(2,1)S(1)}, bf16[4,128,256]{2,1,0:T(8,128)(2,1)S(1)}, u32[]{:S(2)}, u32[]{:S(2)}) %collective-permute-start.4) | collective-permute-done | bytes 262176 | tf_op jit(solution)/shard_map/ppermute | solution.py:162
  74.6 0.8 copy.29
  75.4 0.7 copy-done.17
  76.1 1.5 collective-permute-start.18
  77.6 0.9 copy-done.7
  78.5 1.0 copy-done.9
  79.5 1.0 copy-done.18
  80.5 0.9 copy-done.21
  81.5 2.1 %weight_grad_part.3 = f32[1536,256]{1,0:T(8,128)S(1)} custom-call(s32[2]{0:T(128)S(1)} %pad_add_fusion.where_ref, s32[4,12,12]{2,1,0:T(8,128)S(1)} %copy.15.mask_ref, bf16[128,1536]{1,0:T(8,128)(2,1)S(1)} %bitcast.96, bf16[128,1536]{1,0:T(8,128)(2,1)S(1)} %copy-done.18, bf16[4,128,256]{2,1,0:T(8,128)(2,1)S(1)} %copy-done.7, bf16[4,128,256]{2,1,0:T(8,128)(2,1)S(1)} %copy-done.21), custom_call_target="tpu_custom_call" | custom-call | flops 805306368 | bytes 2359296 | tf_op jit(solution)/shard_map/weight_grad_part/pallas_call | solution.py:66
  83.6 1.0 dynamic-slice_bitcast_fusion.6
  84.6 9.0 %collective-permute-done.11.op_ref = bf16[4,128,256]{2,1,0:T(8,128)(2,1)} collective-permute-done((bf16[4,128,256]{2,1,0:T(8,128)(2,1)}, bf16[4,128,256]{2,1,0:T(8,128)(2,1)}, u32[]{:S(2)}, u32[]{:S(2)}) %collective-permute-start.11) | collective-permute-done | bytes 262176 | tf_op jit(solution)/shard_map/ppermute | solution.py:162
  93.6 1.3 collective-permute-start.5
  94.9 2.1 %weight_grad_part.4 = f32[1536,256]{1,0:T(8,128)S(1)} custom-call(s32[2]{0:T(128)S(1)} %pad_add_fusion.where_ref, s32[4,12,12]{2,1,0:T(8,128)S(1)} %copy.15.mask_ref, bf16[128,1536]{1,0:T(8,128)(2,1)S(1)} %bitcast.97, bf16[128,1536]{1,0:T(8,128)(2,1)S(1)} %copy-done.19, bf16[4,128,256]{2,1,0:T(8,128)(2,1)} %get-tuple-element.33.og_ref.om_ref, ...), custom_call_target="tpu_custom_call" | custom-call | flops 805306368 | bytes 2359296 | tf_op jit(solution)/shard_map/weight_grad_part/pallas_call | solution.py:66
  97.0 1.2 copy-done.1
  98.2 1.0 dynamic-slice_bitcast_fusion.4
  99.2 1.6 collective-permute-start.8
  100.8 2.1 %weight_grad_part.5 = f32[1536,256]{1,0:T(8,128)S(1)} custom-call(s32[2]{0:T(128)S(1)} %pad_add_fusion.where_ref, s32[4,12,12]{2,1,0:T(8,128)S(1)} %copy.15.mask_ref, bf16[128,1536]{1,0:T(8,128)(2,1)S(1)} %bitcast.98, bf16[128,1536]{1,0:T(8,128)(2,1)S(1)} %copy-done.19, bf16[4,128,256]{2,1,0:T(8,128)(2,1)S(1)} %get-tuple-element.32.og_ref.om_ref, ...), custom_call_target="tpu_custom_call" | custom-call | flops 805306368 | bytes 2359296 | tf_op jit(solution)/shard_map/weight_grad_part/pallas_call | solution.py:66
  102.9 1.1 copy-done.3
  104.0 0.9 dynamic-slice_bitcast_fusion.2
  104.9 1.5 collective-permute-start.12
  106.4 3.7 %forward_and_input.3 = (bf16[4,128,256]{2,1,0:T(8,128)(2,1)S(1)}, f32[128,3072]{1,0:T(8,128)S(1)}) custom-call(s32[2]{0:T(128)S(1)} %pad_add_fusion.where_ref, s32[4,12,12]{2,1,0:T(8,128)S(1)} %copy.15.mask_ref, bf16[128,3072]{1,0:T(8,128)(2,1)S(1)} %copy-done, bf16[4,384,256]{2,1,0:T(8,128)(2,1)} %bitcast.2.wm_ref, ...), custom_call_target="tpu_custom_call" | custom-call | flops 603979776 | bytes 3145728 | tf_op jit(solution)/shard_map/forward_and_input/pallas_call | solution.py:125
  110.8 1.4 collective-permute-start.15
  112.2 3.6 %forward_and_input.4 = (bf16[4,128,256]{2,1,0:T(8,128)(2,1)S(1)}, f32[128,3072]{1,0:T(8,128)S(1)}) custom-call(s32[2]{0:T(128)S(1)} %pad_add_fusion.where_ref, s32[4,12,12]{2,1,0:T(8,128)S(1)} %copy.15.mask_ref, bf16[128,3072]{1,0:T(8,128)(2,1)S(1)} %copy-done, bf16[4,384,256]{2,1,0:T(8,128)(2,1)S(1)} %bitcast.95, ...), custom_call_target="tpu_custom_call" | custom-call | flops 603979776 | bytes 3145728 | tf_op jit(solution)/shard_map/forward_and_input/pallas_call | solution.py:125
  116.5 1.3 collective-permute-start.19
  117.8 3.8 %forward_and_input.5 = (bf16[4,128,256]{2,1,0:T(8,128)(2,1)S(1)}, f32[128,3072]{1,0:T(8,128)S(1)}) custom-call(s32[2]{0:T(128)S(1)} %pad_add_fusion.where_ref, s32[4,12,12]{2,1,0:T(8,128)S(1)} %copy.15.mask_ref, bf16[128,3072]{1,0:T(8,128)(2,1)S(1)} %copy-done, bf16[4,384,256]{2,1,0:T(8,128)(2,1)} %bitcast.4.wm_ref, ...), custom_call_target="tpu_custom_call" | custom-call | flops 603979776 | bytes 3145728 | tf_op jit(solution)/shard_map/forward_and_input/pallas_call | solution.py:125
  121.6 1.2 copy-done.5
  123.5 2.7 %reshape.35 = f32[128,2,2,768]{3,2,1,0:T(2,128)S(1)} reshape(f32[128,3072]{1,0:T(8,128)} %copy-done.5) | data formatting | bytes 3145728 | tf_op jit(solution)/shard_map/reshape | solution.py:211
  126.9 1.1 bitcast_add_fusion.13
  128.0 4.2 %collective-permute-start.6 = (f32[384,256]{1,0:T(8,128)S(1)}, f32[384,256]{1,0:T(8,128)S(1)}, u32[]{:S(2)}, u32[]{:S(2)}) collective-permute-start(f32[384,256]{1,0:T(8,128)S(1)} %bitcast_add_fusion.13), channel_id=1, source_target_pairs={{0,8},{4,12},{8,16},{12,20},{1,9},{5,13},{9,17},{13,21},{2,10},{6,... | collective-permute-start | bytes 1179656 | tf_op jit(solution)/shard_map/ppermute | solution.py:169
  132.2 1.2 bitcast_add_fusion.8
  133.4 1.4 constant_dynamic-slice_fusion.1
  134.8 2.1 %collective-permute-start.13 = (f32[384,256]{1,0:T(8,128)S(1)}, f32[384,256]{1,0:T(8,128)S(1)}, u32[]{:S(2)}, u32[]{:S(2)}) collective-permute-start(f32[384,256]{1,0:T(8,128)S(1)} %bitcast_add_fusion.8), channel_id=1, source_target_pairs={{0,8},{4,12},{8,16},{12,20},{1,9},{5,13},{9,17},{13,21},{2,10},{6,... | collective-permute-start | bytes 1179656 | tf_op jit(solution)/shard_map/ppermute | solution.py:169
  136.9 1.1 bitcast_add_fusion.3
  138.0 0.9 pad_maximum_fusion.1
  138.9 1.4 collective-permute-done.6
  140.3 1.9 collective-permute-start.20
  142.3 1.1 bitcast_add_fusion.14
  143.4 1.3 collective-permute-start.9
  145.3 4.0 %collective-permute-start.7 = (f32[384,256]{1,0:T(8,128)S(1)}, f32[384,256]{1,0:T(8,128)S(1)}, u32[]{:S(2)}, u32[]{:S(2)}) collective-permute-start(f32[384,256]{1,0:T(8,128)S(1)} %get-tuple-element.19), channel_id=1, source_target_pairs={{0,8},{4,12},{8,16},{12,20},{16,24},{20,28},{1,9},{5,13},{9,17},{1... | collective-permute-start | bytes 1179656 | tf_op jit(solution)/shard_map/ppermute | solution.py:169
  149.3 1.1 bitcast_add_fusion.9
  150.4 1.3 collective-permute-start.16
  151.7 2.6 %collective-permute-done.20 = f32[384,256]{1,0:T(8,128)S(1)} collective-permute-done((f32[384,256]{1,0:T(8,128)S(1)}, f32[384,256]{1,0:T(8,128)S(1)}, u32[]{:S(2)}, u32[]{:S(2)}) %collective-permute-start.20) | collective-permute-done | bytes 393248 | tf_op jit(solution)/shard_map/ppermute | solution.py:169
  154.3 2.0 collective-permute-start.14
  156.4 1.3 collective-permute-start.23
  157.8 4.6 %collective-permute-start.21 = (f32[384,256]{1,0:T(8,128)S(1)}, f32[384,256]{1,0:T(8,128)S(1)}, u32[]{:S(2)}, u32[]{:S(2)}) collective-permute-start(f32[384,256]{1,0:T(8,128)S(1)} %get-tuple-element.27), channel_id=1, source_target_pairs={{0,8},{4,12},{8,16},{12,20},{16,24},{20,28},{1,9},{5,13},{9,17},{1... | collective-permute-start | bytes 1179656 | tf_op jit(solution)/shard_map/ppermute | solution.py:169
  162.4 3.3 %collective-permute-done.16 = f32[384,256]{1,0:T(8,128)S(1)} collective-permute-done((f32[384,256]{1,0:T(8,128)S(1)}, f32[384,256]{1,0:T(8,128)S(1)}, u32[]{:S(2)}, u32[]{:S(2)}) %collective-permute-start.16) | collective-permute-done | bytes 393248 | tf_op jit(solution)/shard_map/ppermute | solution.py:169
  165.7 1.9 collective-permute-start.10
  167.7 6.4 %collective-permute-done.23 = f32[384,256]{1,0:T(8,128)S(1)} collective-permute-done((f32[384,256]{1,0:T(8,128)S(1)}, f32[384,256]{1,0:T(8,128)S(1)}, u32[]{:S(2)}, u32[]{:S(2)}) %collective-permute-start.23) | collective-permute-done | bytes 393248 | tf_op jit(solution)/shard_map/ppermute | solution.py:169
  174.2 1.9 collective-permute-start.17
  176.8 5.8 %collective-permute-done.10 = f32[384,256]{1,0:T(8,128)S(1)} collective-permute-done((f32[384,256]{1,0:T(8,128)S(1)}, f32[384,256]{1,0:T(8,128)S(1)}, u32[]{:S(2)}, u32[]{:S(2)}) %collective-permute-start.10) | collective-permute-done | bytes 393248 | tf_op jit(solution)/shard_map/ppermute | solution.py:169
  182.6 1.9 collective-permute-start.24
  184.6 6.4 %collective-permute-done.17 = f32[384,256]{1,0:T(8,128)S(1)} collective-permute-done((f32[384,256]{1,0:T(8,128)S(1)}, f32[384,256]{1,0:T(8,128)S(1)}, u32[]{:S(2)}, u32[]{:S(2)}) %collective-permute-start.17) | collective-permute-done | bytes 393248 | tf_op jit(solution)/shard_map/ppermute | solution.py:169
  191.1 6.4 %collective-permute-done.24 = f32[384,256]{1,0:T(8,128)S(1)} collective-permute-done((f32[384,256]{1,0:T(8,128)S(1)}, f32[384,256]{1,0:T(8,128)S(1)}, u32[]{:S(2)}, u32[]{:S(2)}) %collective-permute-start.24) | collective-permute-done | bytes 393248 | tf_op jit(solution)/shard_map/ppermute | solution.py:169
  197.6 1.1 pad_maximum_fusion
  (80 shorter events, 7.8 us)
Async XLA Ops:
  0.6 39.3 %copy-start = (bf16[128,3072]{1,0:T(8,128)(2,1)S(1)}, bf16[128,3072]{1,0:T(8,128)(2,1)}, u32[]{:S(2)}) copy-start(bf16[128,3072]{1,0:T(8,128)(2,1)} %acts_ref.5) | copy-start | bytes 2359300
  20.5 84.4 %collective-permute-start = (bf16[4,384,256]{2,1,0:T(8,128)(2,1)}, bf16[4,384,256]{2,1,0:T(8,128)(2,1)}, u32[]{:S(2)}, u32[]{:S(2)}) collective-permute-start(bf16[4,384,256]{2,1,0:T(8,128)(2,1)} %bitcast.2.wm_ref), channel_id=1, source_target_pairs={{0,4},{4,0},{8,12},{12,8},{16,20},{20,16},{24,28},{28,24},{1,5},{5... | collective-permute-start | bytes 2359304 | tf_op jit(solution)/shard_map/ppermute | solution.py:162
  39.4 71.4 %collective-permute-start.1 = (bf16[4,384,256]{2,1,0:T(8,128)(2,1)S(1)}, bf16[4,384,256]{2,1,0:T(8,128)(2,1)}, u32[]{:S(2)}, u32[]{:S(2)}) collective-permute-start(bf16[4,384,256]{2,1,0:T(8,128)(2,1)S(1)} %bitcast.94), channel_id=1, source_target_pairs={{0,4},{4,0},{8,12},{12,8},{16,20},{20,16},{24,28},{28,24},{1,5},{5... | collective-permute-start | bytes 2359304 | tf_op jit(solution)/shard_map/ppermute | solution.py:162
  40.5 7.2 %copy-start.22 = (bf16[4,128,768]{2,1,0:T(8,128)(2,1)S(1)}, bf16[4,128,768]{2,1,0:T(8,128)(2,1)}, u32[]{:S(2)}) copy-start(bf16[4,128,768]{2,1,0:T(8,128)(2,1)} %param.7) | copy-start | bytes 2359300
  45.5 29.1 %copy-start.24 = (s32[4,12,12]{2,0,1:T(4,128)S(1)}, s32[4,12,12]{2,0,1:T(4,128)}, u32[]{:S(2)}) copy-start(s32[4,12,12]{2,0,1:T(4,128)} %param.6) | copy-start | bytes 6916
  46.3 29.1 %collective-permute-start.3 = (bf16[128,1536]{1,0:T(8,128)(2,1)}, bf16[128,1536]{1,0:T(8,128)(2,1)S(1)}, u32[]{:S(2)}, u32[]{:S(2)}) collective-permute-start(bf16[128,1536]{1,0:T(8,128)(2,1)} %bitcast.36), channel_id=1, source_target_pairs={{0,4},{4,0},{8,12},{12,8},{16,20},{20,16},{24,28},{28,24},{1,5},{5... | collective-permute-start | bytes 1179656 | tf_op jit(solution)/shard_map/ppermute | solution.py:162
  48.5 29.1 %copy-start.6 = (bf16[4,128,256]{2,1,0:T(8,128)(2,1)}, bf16[4,128,256]{2,1,0:T(8,128)(2,1)S(1)}, u32[]{:S(2)}) copy-start(bf16[4,128,256]{2,1,0:T(8,128)(2,1)S(1)} %get-tuple-element.31.og_ref.om_ref) | copy-start | bytes 786436
  48.5 25.4 %collective-permute-start.4 = (bf16[4,128,256]{2,1,0:T(8,128)(2,1)S(1)}, bf16[4,128,256]{2,1,0:T(8,128)(2,1)S(1)}, u32[]{:S(2)}, u32[]{:S(2)}) collective-permute-start(bf16[4,128,256]{2,1,0:T(8,128)(2,1)S(1)} %get-tuple-element.31.og_ref.om_ref), channel_id=1, source_target_pairs={{0,4},{4,0},{8,12},{12,8},{16,20},{20,16},{24,28},{28,24},{1,5},{5... | collective-permute-start | bytes 786440 | tf_op jit(solution)/shard_map/ppermute | solution.py:162
  67.3 49.2 %collective-permute-start.2 = (bf16[4,384,256]{2,1,0:T(8,128)(2,1)}, bf16[4,384,256]{2,1,0:T(8,128)(2,1)}, u32[]{:S(2)}, u32[]{:S(2)}) collective-permute-start(bf16[4,384,256]{2,1,0:T(8,128)(2,1)} %bitcast.4.wm_ref), channel_id=1, source_target_pairs={{0,4},{4,0},{8,12},{12,8},{16,20},{20,16},{24,28},{28,24},{1,5},{5... | collective-permute-start | bytes 2359304 | tf_op jit(solution)/shard_map/ppermute | solution.py:162
  73.9 3.7 %copy-start.20 = (bf16[4,128,256]{2,1,0:T(8,128)(2,1)}, bf16[4,128,256]{2,1,0:T(8,128)(2,1)S(1)}, u32[]{:S(2)}) copy-start(bf16[4,128,256]{2,1,0:T(8,128)(2,1)S(1)} %collective-permute-done.4.op_ref) | copy-start | bytes 786436
  73.9 19.6 %collective-permute-start.11 = (bf16[4,128,256]{2,1,0:T(8,128)(2,1)}, bf16[4,128,256]{2,1,0:T(8,128)(2,1)}, u32[]{:S(2)}, u32[]{:S(2)}) collective-permute-start(bf16[4,128,256]{2,1,0:T(8,128)(2,1)} %get-tuple-element.33.og_ref.om_ref), channel_id=1, source_target_pairs={{0,4},{4,0},{8,12},{12,8},{16,20},{20,16},{24,28},{28,24},{1,5},{5... | collective-permute-start | bytes 786440 | tf_op jit(solution)/shard_map/ppermute | solution.py:162
  75.4 0.7 copy-start.17
  76.1 23.1 %collective-permute-start.18 = (bf16[4,128,256]{2,1,0:T(8,128)(2,1)S(1)}, bf16[4,128,256]{2,1,0:T(8,128)(2,1)S(1)}, u32[]{:S(2)}, u32[]{:S(2)}) collective-permute-start(bf16[4,128,256]{2,1,0:T(8,128)(2,1)S(1)} %get-tuple-element.32.og_ref.om_ref), channel_id=1, source_target_pairs={{0,4},{4,0},{8,12},{12,8},{16,20},{20,16},{24,28},{28,24},{1,5},{5... | collective-permute-start | bytes 786440 | tf_op jit(solution)/shard_map/ppermute | solution.py:162
  77.6 1.0 copy-start.7
  78.5 1.0 copy-start.9
  79.5 1.0 copy-start.18
  80.5 0.9 copy-start.21
  81.5 13.4 %copy-start.10 = (bf16[16,8,4,384]{3,1,2,0:T(8,128)(2,1)S(1)}, bf16[16,8,4,384]{3,1,2,0:T(8,128)(2,1)}, u32[]{:S(2)}) copy-start(bf16[16,8,4,384]{3,1,2,0:T(8,128)(2,1)} %copy.29) | copy-start | bytes 1179652
  81.5 13.4 %copy-start.19 = (bf16[128,1536]{1,0:T(8,128)(2,1)S(1)}, bf16[128,1536]{1,0:T(8,128)(2,1)}, u32[]{:S(2)}) copy-start(bf16[128,1536]{1,0:T(8,128)(2,1)} %copy-done.17) | copy-start | bytes 1179652
  93.6 32.6 %collective-permute-start.5 = (f32[384,256]{1,0:T(8,128)}, f32[384,256]{1,0:T(8,128)}, u32[]{:S(2)}, u32[]{:S(2)}) collective-permute-start(f32[384,256]{1,0:T(8,128)} %get-tuple-element.21), channel_id=1, source_target_pairs={{0,8},{4,12},{1,9},{5,13},{2,10},{6,14},{3,11},{7,15}} | collective-permute-start | bytes 1179656 | tf_op jit(solution)/shard_map/ppermute | solution.py:169
  97.0 1.2 copy-start.1
  99.2 7.2 %copy-start.8 = (bf16[4,128,256]{2,1,0:T(8,128)(2,1)S(1)}, bf16[4,128,256]{2,1,0:T(8,128)(2,1)}, u32[]{:S(2)}) copy-start(bf16[4,128,256]{2,1,0:T(8,128)(2,1)} %copy-done.6) | copy-start | bytes 786436
  99.2 39.7 %collective-permute-start.8 = (f32[384,256]{1,0:T(8,128)}, f32[384,256]{1,0:T(8,128)}, u32[]{:S(2)}, u32[]{:S(2)}) collective-permute-start(f32[384,256]{1,0:T(8,128)} %get-tuple-element.22), channel_id=1, source_target_pairs={{24,16},{28,20},{25,17},{29,21},{26,18},{30,22},{27,19},{31,23}} | collective-permute-start | bytes 1179656 | tf_op jit(solution)/shard_map/ppermute | solution.py:169
  102.9 1.1 copy-start.3
  104.9 23.0 %collective-permute-start.12 = (f32[384,256]{1,0:T(8,128)}, f32[384,256]{1,0:T(8,128)}, u32[]{:S(2)}, u32[]{:S(2)}) collective-permute-start(f32[384,256]{1,0:T(8,128)} %get-tuple-element.25), channel_id=1, source_target_pairs={{0,8},{4,12},{1,9},{5,13},{2,10},{6,14},{3,11},{7,15}} | collective-permute-start | bytes 1179656 | tf_op jit(solution)/shard_map/ppermute | solution.py:169
  110.1 0.7 copy-start.11
  110.8 32.6 %collective-permute-start.15 = (f32[384,256]{1,0:T(8,128)}, f32[384,256]{1,0:T(8,128)}, u32[]{:S(2)}, u32[]{:S(2)}) collective-permute-start(f32[384,256]{1,0:T(8,128)} %get-tuple-element.26), channel_id=1, source_target_pairs={{24,16},{28,20},{25,17},{29,21},{26,18},{30,22},{27,19},{31,23}} | collective-permute-start | bytes 1179656 | tf_op jit(solution)/shard_map/ppermute | solution.py:169
  115.8 0.7 copy-start.13
  116.5 18.3 %collective-permute-start.19 = (f32[384,256]{1,0:T(8,128)}, f32[384,256]{1,0:T(8,128)}, u32[]{:S(2)}, u32[]{:S(2)}) collective-permute-start(f32[384,256]{1,0:T(8,128)} %get-tuple-element.29), channel_id=1, source_target_pairs={{0,8},{4,12},{1,9},{5,13},{2,10},{6,14},{3,11},{7,15}} | collective-permute-start | bytes 1179656 | tf_op jit(solution)/shard_map/ppermute | solution.py:169
  121.6 1.2 copy-start.5
  122.8 0.7 copy-start.15
  123.5 2.7 %copy-start.23 = (f32[384,256]{1,0:T(8,128)S(1)}, f32[384,256]{1,0:T(8,128)}, u32[]{:S(2)}) copy-start(f32[384,256]{1,0:T(8,128)} %get-tuple-element.30) | copy-start | bytes 1179652
  126.2 24.1 %collective-permute-start.22 = (f32[384,256]{1,0:T(8,128)S(1)}, f32[384,256]{1,0:T(8,128)S(1)}, u32[]{:S(2)}, u32[]{:S(2)}) collective-permute-start(f32[384,256]{1,0:T(8,128)S(1)} %copy-done.23), channel_id=1, source_target_pairs={{24,16},{28,20},{25,17},{29,21},{26,18},{30,22},{27,19},{31,23}} | collective-permute-start | bytes 1179656 | tf_op jit(solution)/shard_map/ppermute | solution.py:169
  128.0 12.4 %collective-permute-start.6 = (f32[384,256]{1,0:T(8,128)S(1)}, f32[384,256]{1,0:T(8,128)S(1)}, u32[]{:S(2)}, u32[]{:S(2)}) collective-permute-start(f32[384,256]{1,0:T(8,128)S(1)} %bitcast_add_fusion.13), channel_id=1, source_target_pairs={{0,8},{4,12},{8,16},{12,20},{1,9},{5,13},{9,17},{13,21},{2,10},{6,... | collective-permute-start | bytes 1179656 | tf_op jit(solution)/shard_map/ppermute | solution.py:169
  134.7 2.2 %copy-start.4 = (f32[1536,256]{1,0:T(8,128)S(1)}, f32[1536,256]{1,0:T(8,128)}, u32[]{:S(2)}) copy-start(f32[1536,256]{1,0:T(8,128)} %copy-done.3) | copy-start | bytes 4718596
  134.7 3.2 %copy-start.12 = (bf16[4,128,256]{2,1,0:T(8,128)(2,1)S(1)}, bf16[4,128,256]{2,1,0:T(8,128)(2,1)}, u32[]{:S(2)}) copy-start(bf16[4,128,256]{2,1,0:T(8,128)(2,1)} %copy-done.11) | copy-start | bytes 786436
  134.7 3.2 %copy-start.14 = (bf16[4,128,256]{2,1,0:T(8,128)(2,1)S(1)}, bf16[4,128,256]{2,1,0:T(8,128)(2,1)}, u32[]{:S(2)}) copy-start(bf16[4,128,256]{2,1,0:T(8,128)(2,1)} %copy-done.13) | copy-start | bytes 786436
  134.7 3.2 %copy-start.16 = (bf16[4,128,256]{2,1,0:T(8,128)(2,1)S(1)}, bf16[4,128,256]{2,1,0:T(8,128)(2,1)}, u32[]{:S(2)}) copy-start(bf16[4,128,256]{2,1,0:T(8,128)(2,1)} %copy-done.15) | copy-start | bytes 786436
  134.8 10.4 %collective-permute-start.13 = (f32[384,256]{1,0:T(8,128)S(1)}, f32[384,256]{1,0:T(8,128)S(1)}, u32[]{:S(2)}, u32[]{:S(2)}) collective-permute-start(f32[384,256]{1,0:T(8,128)S(1)} %bitcast_add_fusion.8), channel_id=1, source_target_pairs={{0,8},{4,12},{8,16},{12,20},{1,9},{5,13},{9,17},{13,21},{2,10},{6,... | collective-permute-start | bytes 1179656 | tf_op jit(solution)/shard_map/ppermute | solution.py:169
  138.9 10.3 %copy-start.2 = (f32[1536,256]{1,0:T(8,128)S(1)}, f32[1536,256]{1,0:T(8,128)}, u32[]{:S(2)}) copy-start(f32[1536,256]{1,0:T(8,128)} %copy-done.1) | copy-start | bytes 4718596
  138.9 17.5 %collective-permute-start.25 = (f32[128,2,768]{2,0,1:T(8,128)S(1)}, f32[128,2,768]{2,0,1:T(8,128)S(1)}, u32[]{:S(2)}, u32[]{:S(2)}) collective-permute-start(f32[128,2,768]{2,0,1:T(8,128)S(1)} %bitcast.101), channel_id=1, source_target_pairs={{0,1},{1,0},{2,3},{3,2},{4,5},{5,4},{6,7},{7,6},{8,9},{9,8},{10,11... | collective-permute-start | bytes 2359304 | tf_op jit(solution)/shard_map/ppermute | solution.py:165
  140.3 13.9 %collective-permute-start.20 = (f32[384,256]{1,0:T(8,128)S(1)}, f32[384,256]{1,0:T(8,128)S(1)}, u32[]{:S(2)}, u32[]{:S(2)}) collective-permute-start(f32[384,256]{1,0:T(8,128)S(1)} %bitcast_add_fusion.3), channel_id=1, source_target_pairs={{0,8},{4,12},{8,16},{12,20},{1,9},{5,13},{9,17},{13,21},{2,10},{6,... | collective-permute-start | bytes 1179656 | tf_op jit(solution)/shard_map/ppermute | solution.py:169
  143.4 14.4 %collective-permute-start.9 = (f32[384,256]{1,0:T(8,128)S(1)}, f32[384,256]{1,0:T(8,128)S(1)}, u32[]{:S(2)}, u32[]{:S(2)}) collective-permute-start(f32[384,256]{1,0:T(8,128)S(1)} %get-tuple-element.20), channel_id=1, source_target_pairs={{16,8},{20,12},{24,16},{28,20},{17,9},{21,13},{25,17},{29,21},{18,... | collective-permute-start | bytes 1179656 | tf_op jit(solution)/shard_map/ppermute | solution.py:169
  145.3 30.9 %collective-permute-start.7 = (f32[384,256]{1,0:T(8,128)S(1)}, f32[384,256]{1,0:T(8,128)S(1)}, u32[]{:S(2)}, u32[]{:S(2)}) collective-permute-start(f32[384,256]{1,0:T(8,128)S(1)} %get-tuple-element.19), channel_id=1, source_target_pairs={{0,8},{4,12},{8,16},{12,20},{16,24},{20,28},{1,9},{5,13},{9,17},{1... | collective-permute-start | bytes 1179656 | tf_op jit(solution)/shard_map/ppermute | solution.py:169
  150.4 15.4 %collective-permute-start.16 = (f32[384,256]{1,0:T(8,128)S(1)}, f32[384,256]{1,0:T(8,128)S(1)}, u32[]{:S(2)}, u32[]{:S(2)}) collective-permute-start(f32[384,256]{1,0:T(8,128)S(1)} %get-tuple-element.24), channel_id=1, source_target_pairs={{16,8},{20,12},{24,16},{28,20},{17,9},{21,13},{25,17},{29,21},{18,... | collective-permute-start | bytes 1179656 | tf_op jit(solution)/shard_map/ppermute | solution.py:169
  154.3 30.3 %collective-permute-start.14 = (f32[384,256]{1,0:T(8,128)S(1)}, f32[384,256]{1,0:T(8,128)S(1)}, u32[]{:S(2)}, u32[]{:S(2)}) collective-permute-start(f32[384,256]{1,0:T(8,128)S(1)} %get-tuple-element.23), channel_id=1, source_target_pairs={{0,8},{4,12},{8,16},{12,20},{16,24},{20,28},{1,9},{5,13},{9,17},{1... | collective-permute-start | bytes 1179656 | tf_op jit(solution)/shard_map/ppermute | solution.py:169
  156.4 17.8 %collective-permute-start.23 = (f32[384,256]{1,0:T(8,128)S(1)}, f32[384,256]{1,0:T(8,128)S(1)}, u32[]{:S(2)}, u32[]{:S(2)}) collective-permute-start(f32[384,256]{1,0:T(8,128)S(1)} %get-tuple-element.28), channel_id=1, source_target_pairs={{16,8},{20,12},{24,16},{28,20},{17,9},{21,13},{25,17},{29,21},{18,... | collective-permute-start | bytes 1179656 | tf_op jit(solution)/shard_map/ppermute | solution.py:169
  157.8 33.3 %collective-permute-start.21 = (f32[384,256]{1,0:T(8,128)S(1)}, f32[384,256]{1,0:T(8,128)S(1)}, u32[]{:S(2)}, u32[]{:S(2)}) collective-permute-start(f32[384,256]{1,0:T(8,128)S(1)} %get-tuple-element.27), channel_id=1, source_target_pairs={{0,8},{4,12},{8,16},{12,20},{16,24},{20,28},{1,9},{5,13},{9,17},{1... | collective-permute-start | bytes 1179656 | tf_op jit(solution)/shard_map/ppermute | solution.py:169
  165.7 16.9 %collective-permute-start.10 = (f32[384,256]{1,0:T(8,128)S(1)}, f32[384,256]{1,0:T(8,128)S(1)}, u32[]{:S(2)}, u32[]{:S(2)}) collective-permute-start(f32[384,256]{1,0:T(8,128)S(1)} %bitcast_add_fusion.12), channel_id=1, source_target_pairs={{8,0},{12,4},{16,8},{20,12},{24,16},{28,20},{9,1},{13,5},{17,9},{2... | collective-permute-start | bytes 1179656 | tf_op jit(solution)/shard_map/ppermute | solution.py:169
  174.2 16.9 %collective-permute-start.17 = (f32[384,256]{1,0:T(8,128)S(1)}, f32[384,256]{1,0:T(8,128)S(1)}, u32[]{:S(2)}, u32[]{:S(2)}) collective-permute-start(f32[384,256]{1,0:T(8,128)S(1)} %bitcast_add_fusion.7), channel_id=1, source_target_pairs={{8,0},{12,4},{16,8},{20,12},{24,16},{28,20},{9,1},{13,5},{17,9},{2... | collective-permute-start | bytes 1179656 | tf_op jit(solution)/shard_map/ppermute | solution.py:169
  176.2 22.5 %collective-permute-start.26 = (f32[128,768]{1,0:T(8,128)S(1)}, f32[128,768]{1,0:T(8,128)S(1)}, u32[]{:S(2)}, u32[]{:S(2)}) collective-permute-start(f32[128,768]{1,0:T(8,128)S(1)} %dynamic-slice_bitcast_fusion), channel_id=1, source_target_pairs={{0,2},{1,3},{2,0},{3,1},{4,6},{5,7},{6,4},{7,5},{8,10},{9,11},{10,... | collective-permute-start | bytes 1179656 | tf_op jit(solution)/shard_map/ppermute | solution.py:165
  182.6 14.9 %collective-permute-start.24 = (f32[384,256]{1,0:T(8,128)S(1)}, f32[384,256]{1,0:T(8,128)S(1)}, u32[]{:S(2)}, u32[]{:S(2)}) collective-permute-start(f32[384,256]{1,0:T(8,128)S(1)} %bitcast_add_fusion.2), channel_id=1, source_target_pairs={{8,0},{12,4},{16,8},{20,12},{24,16},{28,20},{9,1},{13,5},{17,9},{2... | collective-permute-start | bytes 1179656 | tf_op jit(solution)/shard_map/ppermute | solution.py:169

commit v3 on v0

v3 whole, which is shorter than its diff:
```python
import jax
import jax.numpy as jnp
from jax import lax
from jax.experimental import pallas as pl
from jax.experimental.pallas import tpu as pltpu
from jax.sharding import PartitionSpec as P

BS = 256
TOK_G = 128
LANES = 128
F32 = jnp.float32
BF16 = jnp.bfloat16
VMEM_BYTES = 40 * 1024 * 1024


def plain(acts, weight, block_mask, out_grad):
    width = weight.shape[1]
    kblocks = block_mask.shape[1]
    oblocks = block_mask.shape[2]
    first_col = lax.axis_index("fsdp") * width
    col_ids = (first_col + jnp.arange(width, dtype=jnp.int32)) // BS
    col_select = (col_ids[None, :] == jnp.arange(oblocks, dtype=jnp.int32)[:, None]).astype(F32)
    col_mask = jnp.einsum("skb,bc->skc", block_mask.astype(F32), col_select)
    full = lax.all_gather(weight, "dp", axis=0, tiled=True)
    row_ids = jnp.arange(full.shape[0], dtype=jnp.int32) // BS
    row_select = (row_ids[:, None] == jnp.arange(kblocks, dtype=jnp.int32)[None, :]).astype(F32)
    mask = jnp.einsum("nk,skc->snc", row_select, col_mask)
    masked = mask.astype(BF16) * full[None]
    forward = jnp.einsum("tn,snc->stc", acts, masked, preferred_element_type=F32)
    input_part = jnp.einsum("stc,snc->tn", out_grad, masked, preferred_element_type=F32)
    products = jnp.einsum("tn,stc->snc", acts, out_grad, preferred_element_type=F32)
    grad_w = lax.psum_scatter(
        jnp.sum(mask * products, axis=0) * (1.0 / TOK_G), "dp", scatter_dimension=0, tiled=True
    )
    grad_x = lax.psum_scatter(input_part, "fsdp", scatter_dimension=1, tiled=True).astype(BF16)
    return (forward.astype(BF16), grad_w, grad_x)


def weight_grad_part(acts_own, acts_got, og_own, og_got, block_mask, where, rows, chunk):
    nsub, tokens, cw = og_own.shape
    cols = where_chunk(chunk, cw)
    got = len(og_got)

    def kernel(where_ref, mask_ref, *refs):
        acts_refs, og_refs = refs[: got + 1], refs[got + 1 : 2 * got + 2]
        outs = refs[2 * got + 2 :]
        z, x = where_ref[0], where_ref[1]
        col = where_ref[2] + cols
        rhs = [r[...].reshape(nsub * tokens, cw) for r in og_refs]
        for side in range(2):
            xs = x if side == 0 else 1 - x
            for g in range(rows // LANES):
                inside = xs * rows + g * LANES
                block = (z * 2 * rows + inside) // BS
                at = pl.ds(pl.multiple_of(inside, LANES), LANES)
                keep = [mask_ref[s, block, col].astype(F32) for s in range(nsub)]
                keep = [jnp.full((LANES, tokens), k).astype(BF16) for k in keep]
                total = None
                for a_ref, r in zip(acts_refs, rhs):
                    t = a_ref[:, at].T
                    lhs = jnp.concatenate([t * k for k in keep], axis=1)
                    term = jnp.dot(lhs, r, preferred_element_type=F32)
                    total = term if total is None else total + term
                outs[side][g * LANES : (g + 1) * LANES, :] = total * (1.0 / TOK_G)

    smem = pl.BlockSpec(memory_space=pltpu.SMEM)
    vmem = pl.BlockSpec(memory_space=pltpu.VMEM)
    shape = jax.ShapeDtypeStruct((rows, cw), F32)
    return pl.pallas_call(
        kernel,
        out_shape=(shape, shape),
        in_specs=[smem, smem] + [vmem] * (2 * got + 2),
        out_specs=(vmem, vmem),
        compiler_params=pltpu.CompilerParams(vmem_limit_bytes=VMEM_BYTES),
        cost_estimate=pl.CostEstimate(
            flops=4 * (got + 1) * rows * cw * nsub * tokens,
            bytes_accessed=8 * rows * cw,
            transcendentals=0,
        ),
        name="weight_grad_part",
    )(where, block_mask, acts_own, *acts_got, og_own, *og_got)


def where_chunk(first, cw):
    assert first // BS == (first + cw - 1) // BS
    return first // BS


def forward_and_input(acts, w_mine, w_peer, og, block_mask, where):
    nsub, tokens, width = og.shape
    depth = acts.shape[1]
    nz = len(w_mine)
    rows = w_mine[0].shape[0]
    per = rows // LANES

    def kernel(where_ref, mask_ref, acts_ref, og_ref, *rest):
        w_refs, (out_ref, gx_ref, acc, hilo) = rest[: 2 * nz], rest[2 * nz :]
        z, x = where_ref[0], where_ref[1]
        step = pl.program_id(0)
        col = where_ref[2] + step

        @pl.when(step == 0)
        def _():
            gx_ref[...] = jnp.zeros_like(gx_ref)

        acc[...] = jnp.zeros_like(acc)
        for b in range(depth // BS):
            total = jnp.zeros((tokens, BS), F32)
            for s in range(nsub):
                total = total + mask_ref[s, b, col].astype(F32) * og_ref[s].astype(F32)
            hi = total.astype(BF16)
            hilo[b, :tokens] = hi
            hilo[b, tokens:] = (total - hi.astype(F32)).astype(BF16)

        for i, w_ref in enumerate(w_refs):
            xs = x if i < nz else 1 - x
            owner = z ^ (i % nz)
            for g in range(per):
                start = (owner * 2 + xs) * rows + g * LANES
                block = start // BS
                at = pl.ds(pl.multiple_of(start, LANES), LANES)
                w = w_ref[g * LANES : (g + 1) * LANES, :]
                prod = jnp.dot(acts_ref[:, at], w, preferred_element_type=F32)
                for s in range(nsub):
                    acc[s] += mask_ref[s, block, col].astype(F32) * prod
                two = lax.dot_general(
                    hilo[block], w, (((1,), (1,)), ((), ())), preferred_element_type=F32
                )
                gx_ref[:, at] += two[:tokens] + two[tokens:]
        out_ref[...] = acc[...].astype(BF16)

    smem = pl.BlockSpec(memory_space=pltpu.SMEM)
    by_col = pl.BlockSpec((nsub, tokens, BS), lambda j: (0, 0, j))
    whole = pl.BlockSpec((tokens, depth), lambda j: (0, 0))
    return pl.pallas_call(
        kernel,
        grid=(width // BS,),
        out_shape=(
            jax.ShapeDtypeStruct((nsub, tokens, width), BF16),
            jax.ShapeDtypeStruct((tokens, depth), F32),
        ),
        in_specs=[smem, smem, whole, by_col]
        + [pl.BlockSpec((rows, BS), lambda j: (0, j))] * (2 * nz),
        out_specs=(by_col, whole),
        scratch_shapes=[
            pltpu.VMEM((nsub, tokens, BS), F32),
            pltpu.VMEM((depth // BS, 2 * tokens, BS), BF16),
        ],
        compiler_params=pltpu.CompilerParams(vmem_limit_bytes=VMEM_BYTES),
        cost_estimate=pl.CostEstimate(
            flops=6 * tokens * depth * width, bytes_accessed=4 * depth * width, transcendentals=0
        ),
        name="forward_and_input",
    )(where, block_mask, acts, og, *w_mine, *w_peer)


def on_device(acts, weight, block_mask, out_grad):
    rows, width = weight.shape
    tokens, depth = acts.shape
    dp = lax.axis_size("dp")
    fsdp = lax.axis_size("fsdp")
    if rows % LANES or width % BS or dp != 8 or fsdp != 4 or tokens % LANES:
        return plain(acts, weight, block_mask, out_grad)
    nx = 2
    me = lax.axis_index("dp")
    z, x = me // nx, me % nx
    f = lax.axis_index("fsdp")
    y, c = f // 2, f % 2
    where = jnp.stack([z, x, f * (width // BS)]).astype(jnp.int32)

    def swap_dp(a, bits):
        return lax.ppermute(a, "dp", [(d, d ^ bits) for d in range(dp)])

    def swap_x(a):
        return swap_dp(a, 1)

    def swap_z(a, k):
        return swap_dp(a, k * nx)

    def swap_f(a, bit):
        return lax.ppermute(a, "fsdp", [(d, d ^ bit) for d in range(fsdp)])

    def gather_z(a):
        two = swap_z(a, 2)
        one = swap_z(a, 1)
        return [a, one, two, swap_z(two, 1)]

    w_mine = gather_z(weight)
    w_peer = [swap_x(w) for w in w_mine]

    def acts_of(k):
        return lax.dynamic_slice_in_dim(acts, (z ^ k) * nx * rows, nx * rows, 1)

    acts_own = acts_of(0)
    acts_got = [swap_z(acts_of(k), k) for k in range(1, 4)]

    grads = []
    for first, cw in [(i * BS, BS) for i in range(width // BS)]:
        og = gather_z(out_grad[:, :, first : first + cw])
        keep, send = weight_grad_part(
            acts_own, acts_got, og[0], og[1:], block_mask, where, rows, first
        )
        grads.append(keep + swap_x(send))
    grad_w = jnp.concatenate(grads, axis=1)

    outputs, gx = forward_and_input(acts, w_mine, w_peer, out_grad, block_mask, where)

    by = gx.reshape(tokens, 2, 2, depth // 4)
    half = lax.dynamic_index_in_dim(by, c, 2, keepdims=False) + swap_f(
        lax.dynamic_index_in_dim(by, 1 - c, 2, keepdims=False), 1
    )
    grad_x = lax.dynamic_index_in_dim(half, y, 1, keepdims=False) + swap_f(
        lax.dynamic_index_in_dim(half, 1 - y, 1, keepdims=False), 2
    )
    return (outputs, grad_w, grad_x.astype(BF16))


def solution(mesh):
    in_specs = (P("dp", None), P("dp", "fsdp"), P(), P(None, "dp", "fsdp"))
    out_specs = (P(None, "dp", "fsdp"), P("dp", "fsdp"), P("dp", "fsdp"))
    return jax.shard_map(
        on_device, mesh=mesh, in_specs=in_specs, out_specs=out_specs, check_vma=False
    )
```

time: 320 us -> 171 us (0.53)
  waiting for transfers between devices: 216 us -> 86.3 us
  matrix products: 67.2 us -> 0 us
  starting transfers between devices: 0.12 us -> 42.7 us
  Pallas kernels: 0 us -> 16.7 us
  between operations: 13.8 us -> 0.76 us
  local copies, waits for them, and re-layouts: 11.3 us -> 16.5 us
  other arithmetic: 10.8 us -> 7.24 us
    reduce_scatter x2 -> x0, waiting for transfers between devices: 147 us -> none  [the longest x1 147 us: on_device(): lax.psum_scatter(jnp.sum(piece_mask(lax.axis_size('dp') * weight.shape[0]...]
    ppermute x0 -> x24, waiting for transfers between devices: none -> 86.3 us  [the longest x22 85 us: swap_dp(): return lax.ppermute(a, 'dp', [(d, d ^ bits) for d in range(dp)])]
    all_gather x1 -> x0, waiting for transfers between devices: 68.6 us -> none  [on_device(): lax.all_gather(weight, 'dp', axis=0, tiled=True)]
    dot_general x4 -> x0, matrix products: 67.2 us -> none  [the longest x1 18.9 us: on_device(): jnp.einsum('tn,stc->snc', cols, out_grad, preferred_element_type=jnp.floa...]
    ppermute x0 -> x24, starting transfers between devices: none -> 42.7 us  [the longest x22 41.2 us: swap_dp(): return lax.ppermute(a, 'dp', [(d, d ^ bits) for d in range(dp)])]
    pallas_call x0 -> x4, Pallas kernels: none -> 16.7 us  [the longest x1 9.75 us: forward_and_input(): pl.pallas_call(kernel, grid=(width // BS,), out_shape=(jax.ShapeDtypeStru...]
    mul x1 -> x0, other arithmetic: 8.99 us -> none  [on_device(): jnp.sum(piece_mask(lax.axis_size('dp') * weight.shape[0]) * products, axi...]
    all_gather x1 -> x0, local copies, waits for them, and re-layouts: 6.65 us -> none  [on_device(): lax.all_gather(weight, 'dp', axis=0, tiled=True)]
  transfers between devices with their start and end apart: 3 -> 24, of which waited for: 2 -> 12; matrix products, arithmetic and copies ran while one was open for 20% -> 8% of each run, Pallas kernels for 0% -> 10%
where the time goes in v3:
time: 171 us; the launch traced here: 170 us
  waiting for transfers between devices  86.3 us (50%)
  starting transfers between devices  42.7 us (25%)
  Pallas kernels  16.7 us (10%)
  local copies, waits for them, and re-layouts  16.5 us (10%)
  other arithmetic  7.24 us (4%)
    ppermute x22, waiting for transfers between devices, swap_dp(): return lax.ppermute(a, 'dp', [(d, d ^ bits) for d in range(dp)])  85 us
    ppermute x22, starting transfers between devices, swap_dp(): return lax.ppermute(a, 'dp', [(d, d ^ bits) for d in range(dp)])  41.2 us
    pallas_call x1, Pallas kernels, forward_and_input(): pl.pallas_call(kernel, grid=(width // BS,), out_shape=(jax.ShapeDtypeStru...  9.75 us
    unnamed x36, local copies, waits for them, and re-layouts  9.14 us
    pallas_call x3, Pallas kernels, weight_grad_part(): pl.pallas_call(kernel, out_shape=(shape, shape), in_specs=[smem, smem] +...  6.91 us
  transfers between devices with their start and end apart: 24, of which 12 were waited for; matrix products, arithmetic and copies ran while one was open for 8% of the time, Pallas kernels for 10%

profile of v3, /device:TPU:0, one launch (start us, length us, event | category | flops | bytes accessed | tf_op | source)
XLA Modules:
  0.0 170.1 jit_solution(5155213145844701076)
XLA Ops:
  0.7 4.1 %collective-permute-start.1 = (bf16[384,768]{1,0:T(8,128)(2,1)}, bf16[384,768]{1,0:T(8,128)(2,1)S(1)}, u32[]{:S(2)}, u32[]{:S(2)}) collective-permute-start(bf16[384,768]{1,0:T(8,128)(2,1)} %rest_0_.1), channel_id=1, source_target_pairs={{0,16},{4,20},{8,24},{12,28},{16,0},{20,4},{24,8},{28,12},{1,17},{... | collective-permute-start | bytes 1769480 | tf_op jit(solution)/shard_map/ppermute | solution.py:172
  4.8 1.6 collective-permute-start
  6.3 24.7 %collective-permute-done.1.rest_2_ = bf16[384,768]{1,0:T(8,128)(2,1)S(1)} collective-permute-done((bf16[384,768]{1,0:T(8,128)(2,1)}, bf16[384,768]{1,0:T(8,128)(2,1)S(1)}, u32[]{:S(2)}, u32[]{:S(2)}) %collective-permute-start.1) | collective-permute-done | bytes 589856 | tf_op jit(solution)/shard_map/ppermute | solution.py:172
  31.0 0.7 collective-permute-start.2
  31.8 1.5 collective-permute-start.3
  33.3 0.5 collective-permute-start.5
  33.8 1.5 collective-permute-start.4
  35.3 10.3 %collective-permute-done.2.rest_3_ = bf16[384,768]{1,0:T(8,128)(2,1)} collective-permute-done((bf16[384,768]{1,0:T(8,128)(2,1)S(1)}, bf16[384,768]{1,0:T(8,128)(2,1)}, u32[]{:S(2)}, u32[]{:S(2)}) %collective-permute-start.2) | collective-permute-done | bytes 589856 | tf_op jit(solution)/shard_map/ppermute | solution.py:172
  45.6 1.3 collective-permute-start.6
  46.9 2.1 %constant_dynamic-slice_fusion.2 = (bf16[128,768]{1,0:T(8,128)(2,1)}, bf16[128,768]{1,0:T(8,128)(2,1)}, bf16[128,768]{1,0:T(8,128)(2,1)}, bf16[128,768]{1,0:T(8,128)(2,1)}) fusion(bf16[128,3072]{1,0:T(8,128)(2,1)} %acts_ref.1, s32[]{:T(128)S(6)} %select_n.49, s32[]{:T(128)S(6)} %select_n.47, s32[]{:T(128)S(6)} %select_n.46, s32[]{:T(128)S(6)} %select_n.48), kind=kLoop, calls=%fused_computation.9 | loop fusion | bytes 1572880 | tf_op jit(solution)/shard_map/dynamic_slice | solution.py:192
  49.0 1.7 %collective-permute-start.7 = (bf16[128,768]{1,0:T(8,128)(2,1)}, bf16[128,768]{1,0:T(8,128)(2,1)}, u32[]{:S(2)}, u32[]{:S(2)}) collective-permute-start(bf16[128,768]{1,0:T(8,128)(2,1)} %get-tuple-element.25), channel_id=1, source_target_pairs={{0,8},{4,12},{8,0},{12,4},{16,24},{20,28},{24,16},{28,20},{1,9},{5... | collective-permute-start | bytes 589832 | tf_op jit(solution)/shard_map/ppermute | solution.py:172
  50.7 0.1 pad_add_fusion.where_ref
  50.8 0.8 fusion.2
  51.7 3.3 %collective-permute-start.8 = (bf16[128,768]{1,0:T(8,128)(2,1)}, bf16[128,768]{1,0:T(8,128)(2,1)}, u32[]{:S(2)}, u32[]{:S(2)}) collective-permute-start(bf16[128,768]{1,0:T(8,128)(2,1)} %get-tuple-element.27), channel_id=1, source_target_pairs={{0,16},{4,20},{8,24},{12,28},{16,0},{20,4},{24,8},{28,12},{1,17},{... | collective-permute-start | bytes 589832 | tf_op jit(solution)/shard_map/ppermute | solution.py:172
  55.0 5.9 %collective-permute-done.5.rest_6_ = bf16[384,768]{1,0:T(8,128)(2,1)} collective-permute-done((bf16[384,768]{1,0:T(8,128)(2,1)S(1)}, bf16[384,768]{1,0:T(8,128)(2,1)}, u32[]{:S(2)}, u32[]{:S(2)}) %collective-permute-start.5) | collective-permute-done | bytes 589856 | tf_op jit(solution)/shard_map/ppermute | solution.py:172
  60.9 2.7 %collective-permute-start.9 = (bf16[128,768]{1,0:T(8,128)(2,1)}, bf16[128,768]{1,0:T(8,128)(2,1)}, u32[]{:S(2)}, u32[]{:S(2)}) collective-permute-start(bf16[128,768]{1,0:T(8,128)(2,1)} %get-tuple-element.24), channel_id=1, source_target_pairs={{0,24},{4,28},{8,16},{12,20},{16,8},{20,12},{24,0},{28,4},{1,25},{... | collective-permute-start | bytes 589832 | tf_op jit(solution)/shard_map/ppermute | solution.py:172
  63.6 10.0 %collective-permute-done.4.rest_5_ = bf16[384,768]{1,0:T(8,128)(2,1)} collective-permute-done((bf16[384,768]{1,0:T(8,128)(2,1)S(1)}, bf16[384,768]{1,0:T(8,128)(2,1)}, u32[]{:S(2)}, u32[]{:S(2)}) %collective-permute-start.4) | collective-permute-done | bytes 589856 | tf_op jit(solution)/shard_map/ppermute | solution.py:172
  73.6 3.3 %collective-permute-start.11 = (bf16[4,128,256]{2,1,0:T(8,128)(2,1)}, bf16[4,128,256]{2,1,0:T(8,128)(2,1)}, u32[]{:S(2)}, u32[]{:S(2)}) collective-permute-start(bf16[4,128,256]{2,1,0:T(8,128)(2,1)} %get-tuple-element.21.refs_4_), channel_id=1, source_target_pairs={{0,16},{4,20},{8,24},{12,28},{16,0},{20,4},{24,8},{28,12},{1,17},{... | collective-permute-start | bytes 786440 | tf_op jit(solution)/shard_map/ppermute | solution.py:172
  76.9 8.1 %collective-permute-done.6.rest_7_ = bf16[384,768]{1,0:T(8,128)(2,1)} collective-permute-done((bf16[384,768]{1,0:T(8,128)(2,1)}, bf16[384,768]{1,0:T(8,128)(2,1)}, u32[]{:S(2)}, u32[]{:S(2)}) %collective-permute-start.6) | collective-permute-done | bytes 589856 | tf_op jit(solution)/shard_map/ppermute | solution.py:172
  85.0 1.1 copy-done.4
  86.0 1.1 copy-done.6
  87.1 1.1 copy-done.8
  88.2 9.8 %forward_and_input.1 = (bf16[4,128,768]{2,1,0:T(8,128)(2,1)}, f32[128,3072]{1,0:T(8,128)S(1)}) custom-call(s32[3]{0:T(128)S(1)} %pad_add_fusion.where_ref, s32[4,12,12]{2,1,0:T(8,128)S(1)} %copy.11.mask_ref, bf16[128,3072]{1,0:T(8,128)(2,1)S(1)} %copy-done, bf16[4,128,768]{2,1,0:T(8,128)(2,1)S(1)} %copy-done.1, bf16[384,768]{1,0:T(8,128)(2,1)S(1)} %copy-done.4, ...), custom_call_target="tpu_custom_call" | custom-call | flops 1811939328 | bytes 9437184 | tf_op jit(solution)/shard_map/forward_and_input/pallas_call | solution.py:135
  97.9 1.3 reshape.9
  99.3 2.2 %constant_dynamic-slice_fusion.1 = (f32[128,2,1,768]{3,2,1,0:T(1,128)}, f32[128,2,1,768]{3,2,1,0:T(1,128)S(1)}) fusion(f32[128,2,2,768]{3,2,1,0:T(2,128)S(1)} %reshape.9, s32[]{:T(128)S(6)} %select_n.51, s32[]{:T(128)S(6)} %select_n.52), kind=kLoop, calls=%fused_computation.8 | loop fusion | bytes 3145736 | tf_op jit(solution)/shard_map/jit(dynamic_index_in_dim)/dynamic_slice | solution.py:209
  101.5 1.0 copy.23
  102.5 0.0 collective-permute-start.22
  102.5 0.0 collective-permute-done.7.refs_1_
  102.5 0.5 collective-permute-start.10
  102.9 3.1 %collective-permute-start.15 = (bf16[4,128,256]{2,1,0:T(8,128)(2,1)S(1)}, bf16[4,128,256]{2,1,0:T(8,128)(2,1)S(1)}, u32[]{:S(2)}, u32[]{:S(2)}) collective-permute-start(bf16[4,128,256]{2,1,0:T(8,128)(2,1)S(1)} %copy-done.2), channel_id=1, source_target_pairs={{0,16},{4,20},{8,24},{12,28},{16,0},{20,4},{24,8},{28,12},{1,17},{... | collective-permute-start | bytes 786440 | tf_op jit(solution)/shard_map/ppermute | solution.py:172
  106.0 0.1 collective-permute-start.19
  106.1 0.0 collective-permute-done.11.refs_6_
  106.1 1.8 %collective-permute-start.12 = (bf16[4,128,256]{2,1,0:T(8,128)(2,1)}, bf16[4,128,256]{2,1,0:T(8,128)(2,1)S(1)}, u32[]{:S(2)}, u32[]{:S(2)}) collective-permute-start(bf16[4,128,256]{2,1,0:T(8,128)(2,1)} %collective-permute-done.11.refs_6_), channel_id=1, source_target_pairs={{0,8},{4,12},{8,0},{12,4},{16,24},{20,28},{24,16},{28,20},{1,9},{5... | collective-permute-start | bytes 786440 | tf_op jit(solution)/shard_map/ppermute | solution.py:172
  107.8 10.9 %collective-permute-done.10.refs_5_ = bf16[4,128,256]{2,1,0:T(8,128)(2,1)S(1)} collective-permute-done((bf16[4,128,256]{2,1,0:T(8,128)(2,1)}, bf16[4,128,256]{2,1,0:T(8,128)(2,1)S(1)}, u32[]{:S(2)}, u32[]{:S(2)}) %collective-permute-start.10) | collective-permute-done | bytes 262176 | tf_op jit(solution)/shard_map/ppermute | solution.py:172
  118.8 0.0 collective-permute-start.14
  118.8 7.0 %collective-permute-start.16 = (bf16[4,128,256]{2,1,0:T(8,128)(2,1)S(1)}, bf16[4,128,256]{2,1,0:T(8,128)(2,1)}, u32[]{:S(2)}, u32[]{:S(2)}) collective-permute-start(bf16[4,128,256]{2,1,0:T(8,128)(2,1)S(1)} %collective-permute-done.15.refs_6_), channel_id=1, source_target_pairs={{0,8},{4,12},{8,0},{12,4},{16,24},{20,28},{24,16},{28,20},{1,9},{5... | collective-permute-start | bytes 786440 | tf_op jit(solution)/shard_map/ppermute | solution.py:172
  125.7 4.0 %collective-permute-done.19.refs_6_ = bf16[4,128,256]{2,1,0:T(8,128)(2,1)S(1)} collective-permute-done((bf16[4,128,256]{2,1,0:T(8,128)(2,1)S(1)}, bf16[4,128,256]{2,1,0:T(8,128)(2,1)S(1)}, u32[]{:S(2)}, u32[]{:S(2)}) %collective-permute-start.19) | collective-permute-done | bytes 262176 | tf_op jit(solution)/shard_map/ppermute | solution.py:172
  129.8 0.9 collective-permute-start.18
  130.7 0.7 copy-done.13
  131.4 1.2 collective-permute-start.20
  132.5 0.9 copy-done.14
  133.5 2.3 %weight_grad_part.3 = (f32[384,256]{1,0:T(8,128)S(1)}, f32[384,256]{1,0:T(8,128)S(1)}) custom-call(s32[3]{0:T(128)S(1)} %pad_add_fusion.where_ref, s32[4,12,12]{2,1,0:T(8,128)S(1)} %copy.11.mask_ref, bf16[128,768]{1,0:T(8,128)(2,1)S(1)} %copy-done.3, bf16[128,768]{1,0:T(8,128)(2,1)} %collective-permute-done.7.refs_1_, ...), custom_call_target="tpu_custom_call" | custom-call | flops 805306368 | bytes 786432 | tf_op jit(solution)/shard_map/weight_grad_part/pallas_call | solution.py:69
  135.8 0.7 copy-done.11
  136.5 1.5 collective-permute-start.13
  138.0 2.0 %collective-permute-done.16.refs_7_ = bf16[4,128,256]{2,1,0:T(8,128)(2,1)} collective-permute-done((bf16[4,128,256]{2,1,0:T(8,128)(2,1)S(1)}, bf16[4,128,256]{2,1,0:T(8,128)(2,1)}, u32[]{:S(2)}, u32[]{:S(2)}) %collective-permute-start.16) | collective-permute-done | bytes 262176 | tf_op jit(solution)/shard_map/ppermute | solution.py:172
  140.0 0.9 copy-done.12
  140.9 2.3 %weight_grad_part.4 = (f32[384,256]{1,0:T(8,128)S(1)}, f32[384,256]{1,0:T(8,128)S(1)}) custom-call(s32[3]{0:T(128)S(1)} %pad_add_fusion.where_ref, s32[4,12,12]{2,1,0:T(8,128)S(1)} %copy.11.mask_ref, bf16[128,768]{1,0:T(8,128)(2,1)S(1)} %copy-done.3, bf16[128,768]{1,0:T(8,128)(2,1)} %collective-permute-done.7.refs_1_, ...), custom_call_target="tpu_custom_call" | custom-call | flops 805306368 | bytes 786432 | tf_op jit(solution)/shard_map/weight_grad_part/pallas_call | solution.py:69
  143.3 1.6 collective-permute-start.17
  144.8 0.7 collective-permute-done.18.refs_5_
  145.5 0.7 copy-done.9
  146.2 4.6 %collective-permute-done.20.refs_7_ = bf16[4,128,256]{2,1,0:T(8,128)(2,1)} collective-permute-done((bf16[4,128,256]{2,1,0:T(8,128)(2,1)S(1)}, bf16[4,128,256]{2,1,0:T(8,128)(2,1)}, u32[]{:S(2)}, u32[]{:S(2)}) %collective-permute-start.20) | collective-permute-done | bytes 262176 | tf_op jit(solution)/shard_map/ppermute | solution.py:172
  150.8 0.9 copy-done.10
  151.8 2.3 %weight_grad_part.5 = (f32[384,256]{1,0:T(8,128)S(1)}, f32[384,256]{1,0:T(8,128)S(1)}) custom-call(s32[3]{0:T(128)S(1)} %pad_add_fusion.where_ref, s32[4,12,12]{2,1,0:T(8,128)S(1)} %copy.11.mask_ref, bf16[128,768]{1,0:T(8,128)(2,1)S(1)} %copy-done.3, bf16[128,768]{1,0:T(8,128)(2,1)} %collective-permute-done.7.refs_1_, ...), custom_call_target="tpu_custom_call" | custom-call | flops 805306368 | bytes 786432 | tf_op jit(solution)/shard_map/weight_grad_part/pallas_call | solution.py:69
  154.0 1.6 collective-permute-start.21
  155.6 1.2 fusion
  156.8 0.8 dynamic-slice_bitcast_fusion
  157.6 1.5 collective-permute-start.23
  159.2 1.0 add.57
  160.2 1.0 add.58
  161.3 3.7 %collective-permute-done.21 = f32[384,256]{1,0:T(8,128)} collective-permute-done((f32[384,256]{1,0:T(8,128)S(1)}, f32[384,256]{1,0:T(8,128)}, u32[]{:S(2)}, u32[]{:S(2)}) %collective-permute-start.21) | collective-permute-done | bytes 393248 | tf_op jit(solution)/shard_map/ppermute | solution.py:172
  165.0 1.0 add.59
  166.0 1.1 pad_maximum_fusion
  167.1 1.3 collective-permute-done.23
  168.4 1.7 %fusion.1 = bf16[128,768]{1,0:T(8,128)(2,1)} fusion(f32[128,768]{1,0:T(8,128)} %collective-permute-done.23, f32[128,2,768]{2,0,1:T(8,128)S(1)} %fusion, s32[]{:T(128)S(6)} %select_n.54), kind=kLoop, calls=%fused_computation.5 | loop fusion | flops 196608 | bytes 983044 | tf_op jit(solution)/shard_map/convert_element_type | solution.py:215
  (36 shorter events, 0.1 us)
Async XLA Ops:
  0.6 50.1 %copy-start.16 = (s32[4,12,12]{2,0,1:T(4,128)S(1)}, s32[4,12,12]{2,0,1:T(4,128)}, u32[]{:S(2)}) copy-start(s32[4,12,12]{2,0,1:T(4,128)} %param.6) | copy-start | bytes 6916
  0.6 50.2 %copy-start.1 = (bf16[4,128,768]{2,1,0:T(8,128)(2,1)S(1)}, bf16[4,128,768]{2,1,0:T(8,128)(2,1)}, u32[]{:S(2)}) copy-start(bf16[4,128,768]{2,1,0:T(8,128)(2,1)} %og_ref.1) | copy-start | bytes 2359300
  0.7 30.4 %collective-permute-start.1 = (bf16[384,768]{1,0:T(8,128)(2,1)}, bf16[384,768]{1,0:T(8,128)(2,1)S(1)}, u32[]{:S(2)}, u32[]{:S(2)}) collective-permute-start(bf16[384,768]{1,0:T(8,128)(2,1)} %rest_0_.1), channel_id=1, source_target_pairs={{0,16},{4,20},{8,24},{12,28},{16,0},{20,4},{24,8},{28,12},{1,17},{... | collective-permute-start | bytes 1769480 | tf_op jit(solution)/shard_map/ppermute | solution.py:172
  4.8 29.0 %collective-permute-start = (bf16[384,768]{1,0:T(8,128)(2,1)}, bf16[384,768]{1,0:T(8,128)(2,1)S(1)}, u32[]{:S(2)}, u32[]{:S(2)}) collective-permute-start(bf16[384,768]{1,0:T(8,128)(2,1)} %rest_0_.1), channel_id=1, source_target_pairs={{0,8},{4,12},{8,0},{12,4},{16,24},{20,28},{24,16},{28,20},{1,9},{5... | collective-permute-start | bytes 1769480 | tf_op jit(solution)/shard_map/ppermute | solution.py:172
  31.0 20.6 %copy-start.5 = (bf16[384,768]{1,0:T(8,128)(2,1)}, bf16[384,768]{1,0:T(8,128)(2,1)S(1)}, u32[]{:S(2)}) copy-start(bf16[384,768]{1,0:T(8,128)(2,1)S(1)} %collective-permute-done.1.rest_2_) | copy-start | bytes 1769476
  31.0 14.6 %collective-permute-start.2 = (bf16[384,768]{1,0:T(8,128)(2,1)S(1)}, bf16[384,768]{1,0:T(8,128)(2,1)}, u32[]{:S(2)}, u32[]{:S(2)}) collective-permute-start(bf16[384,768]{1,0:T(8,128)(2,1)S(1)} %collective-permute-done.1.rest_2_), channel_id=1, source_target_pairs={{0,8},{4,12},{8,0},{12,4},{16,24},{20,28},{24,16},{28,20},{1,9},{5... | collective-permute-start | bytes 1769480 | tf_op jit(solution)/shard_map/ppermute | solution.py:172
  31.8 19.9 %collective-permute-start.3 = (bf16[384,768]{1,0:T(8,128)(2,1)}, bf16[384,768]{1,0:T(8,128)(2,1)}, u32[]{:S(2)}, u32[]{:S(2)}) collective-permute-start(bf16[384,768]{1,0:T(8,128)(2,1)} %rest_0_.1), channel_id=1, source_target_pairs={{0,4},{4,0},{8,12},{12,8},{16,20},{20,16},{24,28},{28,24},{1,5},{5... | collective-permute-start | bytes 1769480 | tf_op jit(solution)/shard_map/ppermute | solution.py:172
  33.3 27.7 %collective-permute-start.5 = (bf16[384,768]{1,0:T(8,128)(2,1)S(1)}, bf16[384,768]{1,0:T(8,128)(2,1)}, u32[]{:S(2)}, u32[]{:S(2)}) collective-permute-start(bf16[384,768]{1,0:T(8,128)(2,1)S(1)} %collective-permute-done.1.rest_2_), channel_id=1, source_target_pairs={{0,4},{4,0},{8,12},{12,8},{16,20},{20,16},{24,28},{28,24},{1,5},{5... | collective-permute-start | bytes 1769480 | tf_op jit(solution)/shard_map/ppermute | solution.py:172
  33.8 17.9 %copy-start.7 = (bf16[384,768]{1,0:T(8,128)(2,1)}, bf16[384,768]{1,0:T(8,128)(2,1)S(1)}, u32[]{:S(2)}) copy-start(bf16[384,768]{1,0:T(8,128)(2,1)S(1)} %collective-permute-done.rest_1_) | copy-start | bytes 1769476
  33.8 39.8 %collective-permute-start.4 = (bf16[384,768]{1,0:T(8,128)(2,1)S(1)}, bf16[384,768]{1,0:T(8,128)(2,1)}, u32[]{:S(2)}, u32[]{:S(2)}) collective-permute-start(bf16[384,768]{1,0:T(8,128)(2,1)S(1)} %collective-permute-done.rest_1_), channel_id=1, source_target_pairs={{0,4},{4,0},{8,12},{12,8},{16,20},{20,16},{24,28},{28,24},{1,5},{5... | collective-permute-start | bytes 1769480 | tf_op jit(solution)/shard_map/ppermute | solution.py:172
  45.6 39.4 %collective-permute-start.6 = (bf16[384,768]{1,0:T(8,128)(2,1)}, bf16[384,768]{1,0:T(8,128)(2,1)}, u32[]{:S(2)}, u32[]{:S(2)}) collective-permute-start(bf16[384,768]{1,0:T(8,128)(2,1)} %collective-permute-done.2.rest_3_), channel_id=1, source_target_pairs={{0,4},{4,0},{8,12},{12,8},{16,20},{20,16},{24,28},{28,24},{1,5},{5... | collective-permute-start | bytes 1769480 | tf_op jit(solution)/shard_map/ppermute | solution.py:172
  49.0 36.0 %copy-start = (bf16[128,3072]{1,0:T(8,128)(2,1)S(1)}, bf16[128,3072]{1,0:T(8,128)(2,1)}, u32[]{:S(2)}) copy-start(bf16[128,3072]{1,0:T(8,128)(2,1)} %acts_ref.1) | copy-start | bytes 2359300
  49.0 53.5 %collective-permute-start.7 = (bf16[128,768]{1,0:T(8,128)(2,1)}, bf16[128,768]{1,0:T(8,128)(2,1)}, u32[]{:S(2)}, u32[]{:S(2)}) collective-permute-start(bf16[128,768]{1,0:T(8,128)(2,1)} %get-tuple-element.25), channel_id=1, source_target_pairs={{0,8},{4,12},{8,0},{12,4},{16,24},{20,28},{24,16},{28,20},{1,9},{5... | collective-permute-start | bytes 589832 | tf_op jit(solution)/shard_map/ppermute | solution.py:172
  51.7 51.3 %collective-permute-start.8 = (bf16[128,768]{1,0:T(8,128)(2,1)}, bf16[128,768]{1,0:T(8,128)(2,1)}, u32[]{:S(2)}, u32[]{:S(2)}) collective-permute-start(bf16[128,768]{1,0:T(8,128)(2,1)} %get-tuple-element.27), channel_id=1, source_target_pairs={{0,16},{4,20},{8,24},{12,28},{16,0},{20,4},{24,8},{28,12},{1,17},{... | collective-permute-start | bytes 589832 | tf_op jit(solution)/shard_map/ppermute | solution.py:172
  60.9 45.1 %collective-permute-start.9 = (bf16[128,768]{1,0:T(8,128)(2,1)}, bf16[128,768]{1,0:T(8,128)(2,1)}, u32[]{:S(2)}, u32[]{:S(2)}) collective-permute-start(bf16[128,768]{1,0:T(8,128)(2,1)} %get-tuple-element.24), channel_id=1, source_target_pairs={{0,24},{4,28},{8,16},{12,20},{16,8},{20,12},{24,0},{28,4},{1,25},{... | collective-permute-start | bytes 589832 | tf_op jit(solution)/shard_map/ppermute | solution.py:172
  73.6 32.5 %collective-permute-start.11 = (bf16[4,128,256]{2,1,0:T(8,128)(2,1)}, bf16[4,128,256]{2,1,0:T(8,128)(2,1)}, u32[]{:S(2)}, u32[]{:S(2)}) collective-permute-start(bf16[4,128,256]{2,1,0:T(8,128)(2,1)} %get-tuple-element.21.refs_4_), channel_id=1, source_target_pairs={{0,16},{4,20},{8,24},{12,28},{16,0},{20,4},{24,8},{28,12},{1,17},{... | collective-permute-start | bytes 786440 | tf_op jit(solution)/shard_map/ppermute | solution.py:172
  85.0 1.1 copy-start.4
  86.0 1.1 copy-start.6
  87.1 1.1 copy-start.8
  101.5 1.4 copy-start.2
  101.5 31.0 %copy-start.3 = (bf16[128,768]{1,0:T(8,128)(2,1)S(1)}, bf16[128,768]{1,0:T(8,128)(2,1)}, u32[]{:S(2)}) copy-start(bf16[128,768]{1,0:T(8,128)(2,1)} %get-tuple-element.26.refs_0_) | copy-start | bytes 589828
  102.5 53.2 %collective-permute-start.22 = (f32[128,2,768]{2,0,1:T(8,128)}, f32[128,2,768]{2,0,1:T(8,128)}, u32[]{:S(2)}, u32[]{:S(2)}) collective-permute-start(f32[128,2,768]{2,0,1:T(8,128)} %bitcast.15), channel_id=1, source_target_pairs={{0,1},{1,0},{2,3},{3,2},{4,5},{5,4},{6,7},{7,6},{8,9},{9,8},{10,11... | collective-permute-start | bytes 2359304 | tf_op jit(solution)/shard_map/ppermute | solution.py:181
  102.5 16.3 %collective-permute-start.10 = (bf16[4,128,256]{2,1,0:T(8,128)(2,1)}, bf16[4,128,256]{2,1,0:T(8,128)(2,1)S(1)}, u32[]{:S(2)}, u32[]{:S(2)}) collective-permute-start(bf16[4,128,256]{2,1,0:T(8,128)(2,1)} %get-tuple-element.21.refs_4_), channel_id=1, source_target_pairs={{0,8},{4,12},{8,0},{12,4},{16,24},{20,28},{24,16},{28,20},{1,9},{5... | collective-permute-start | bytes 786440 | tf_op jit(solution)/shard_map/ppermute | solution.py:172
  102.9 15.8 %collective-permute-start.15 = (bf16[4,128,256]{2,1,0:T(8,128)(2,1)S(1)}, bf16[4,128,256]{2,1,0:T(8,128)(2,1)S(1)}, u32[]{:S(2)}, u32[]{:S(2)}) collective-permute-start(bf16[4,128,256]{2,1,0:T(8,128)(2,1)S(1)} %copy-done.2), channel_id=1, source_target_pairs={{0,16},{4,20},{8,24},{12,28},{16,0},{20,4},{24,8},{28,12},{1,17},{... | collective-permute-start | bytes 786440 | tf_op jit(solution)/shard_map/ppermute | solution.py:172
  106.0 23.8 %collective-permute-start.19 = (bf16[4,128,256]{2,1,0:T(8,128)(2,1)S(1)}, bf16[4,128,256]{2,1,0:T(8,128)(2,1)S(1)}, u32[]{:S(2)}, u32[]{:S(2)}) collective-permute-start(bf16[4,128,256]{2,1,0:T(8,128)(2,1)S(1)} %get-tuple-element.22.refs_4_), channel_id=1, source_target_pairs={{0,16},{4,20},{8,24},{12,28},{16,0},{20,4},{24,8},{28,12},{1,17},{... | collective-permute-start | bytes 786440 | tf_op jit(solution)/shard_map/ppermute | solution.py:172
  106.1 24.6 %collective-permute-start.12 = (bf16[4,128,256]{2,1,0:T(8,128)(2,1)}, bf16[4,128,256]{2,1,0:T(8,128)(2,1)S(1)}, u32[]{:S(2)}, u32[]{:S(2)}) collective-permute-start(bf16[4,128,256]{2,1,0:T(8,128)(2,1)} %collective-permute-done.11.refs_6_), channel_id=1, source_target_pairs={{0,8},{4,12},{8,0},{12,4},{16,24},{20,28},{24,16},{28,20},{1,9},{5... | collective-permute-start | bytes 786440 | tf_op jit(solution)/shard_map/ppermute | solution.py:172
  118.8 17.0 %collective-permute-start.14 = (bf16[4,128,256]{2,1,0:T(8,128)(2,1)S(1)}, bf16[4,128,256]{2,1,0:T(8,128)(2,1)S(1)}, u32[]{:S(2)}, u32[]{:S(2)}) collective-permute-start(bf16[4,128,256]{2,1,0:T(8,128)(2,1)S(1)} %copy-done.2), channel_id=1, source_target_pairs={{0,8},{4,12},{8,0},{12,4},{16,24},{20,28},{24,16},{28,20},{1,9},{5... | collective-permute-start | bytes 786440 | tf_op jit(solution)/shard_map/ppermute | solution.py:172
  118.8 21.2 %collective-permute-start.16 = (bf16[4,128,256]{2,1,0:T(8,128)(2,1)S(1)}, bf16[4,128,256]{2,1,0:T(8,128)(2,1)}, u32[]{:S(2)}, u32[]{:S(2)}) collective-permute-start(bf16[4,128,256]{2,1,0:T(8,128)(2,1)S(1)} %collective-permute-done.15.refs_6_), channel_id=1, source_target_pairs={{0,8},{4,12},{8,0},{12,4},{16,24},{20,28},{24,16},{28,20},{1,9},{5... | collective-permute-start | bytes 786440 | tf_op jit(solution)/shard_map/ppermute | solution.py:172
  129.8 15.7 %collective-permute-start.18 = (bf16[4,128,256]{2,1,0:T(8,128)(2,1)S(1)}, bf16[4,128,256]{2,1,0:T(8,128)(2,1)S(1)}, u32[]{:S(2)}, u32[]{:S(2)}) collective-permute-start(bf16[4,128,256]{2,1,0:T(8,128)(2,1)S(1)} %get-tuple-element.22.refs_4_), channel_id=1, source_target_pairs={{0,8},{4,12},{8,0},{12,4},{16,24},{20,28},{24,16},{28,20},{1,9},{5... | collective-permute-start | bytes 786440 | tf_op jit(solution)/shard_map/ppermute | solution.py:172
  130.7 0.7 copy-start.13
  131.4 19.5 %collective-permute-start.20 = (bf16[4,128,256]{2,1,0:T(8,128)(2,1)S(1)}, bf16[4,128,256]{2,1,0:T(8,128)(2,1)}, u32[]{:S(2)}, u32[]{:S(2)}) collective-permute-start(bf16[4,128,256]{2,1,0:T(8,128)(2,1)S(1)} %collective-permute-done.19.refs_6_), channel_id=1, source_target_pairs={{0,8},{4,12},{8,0},{12,4},{16,24},{20,28},{24,16},{28,20},{1,9},{5... | collective-permute-start | bytes 786440 | tf_op jit(solution)/shard_map/ppermute | solution.py:172
  132.5 1.0 copy-start.14
  135.8 0.7 copy-start.11
  136.5 22.6 %collective-permute-start.13 = (f32[384,256]{1,0:T(8,128)S(1)}, f32[384,256]{1,0:T(8,128)}, u32[]{:S(2)}, u32[]{:S(2)}) collective-permute-start(f32[384,256]{1,0:T(8,128)S(1)} %get-tuple-element.13), channel_id=1, source_target_pairs={{0,4},{4,0},{8,12},{12,8},{16,20},{20,16},{24,28},{28,24},{1,5},{5... | collective-permute-start | bytes 1179656 | tf_op jit(solution)/shard_map/ppermute | solution.py:172
  140.0 1.0 copy-start.12
  140.9 14.7 %copy-start.15 = (f32[128,2,1,768]{3,2,1,0:T(1,128)S(1)}, f32[128,2,1,768]{3,2,1,0:T(1,128)}, u32[]{:S(2)}) copy-start(f32[128,2,1,768]{3,2,1,0:T(1,128)} %get-tuple-element.19) | copy-start | bytes 2359300
  143.3 16.9 %collective-permute-start.17 = (f32[384,256]{1,0:T(8,128)S(1)}, f32[384,256]{1,0:T(8,128)}, u32[]{:S(2)}, u32[]{:S(2)}) collective-permute-start(f32[384,256]{1,0:T(8,128)S(1)} %get-tuple-element.15), channel_id=1, source_target_pairs={{0,4},{4,0},{8,12},{12,8},{16,20},{20,16},{24,28},{28,24},{1,5},{5... | collective-permute-start | bytes 1179656 | tf_op jit(solution)/shard_map/ppermute | solution.py:172
  145.5 0.7 copy-start.9
  150.8 1.0 copy-start.10
  154.0 10.9 %collective-permute-start.21 = (f32[384,256]{1,0:T(8,128)S(1)}, f32[384,256]{1,0:T(8,128)}, u32[]{:S(2)}, u32[]{:S(2)}) collective-permute-start(f32[384,256]{1,0:T(8,128)S(1)} %get-tuple-element.17), channel_id=1, source_target_pairs={{0,4},{4,0},{8,12},{12,8},{16,20},{20,16},{24,28},{28,24},{1,5},{5... | collective-permute-start | bytes 1179656 | tf_op jit(solution)/shard_map/ppermute | solution.py:172
  157.6 10.8 %collective-permute-start.23 = (f32[128,768]{1,0:T(8,128)}, f32[128,768]{1,0:T(8,128)}, u32[]{:S(2)}, u32[]{:S(2)}) collective-permute-start(f32[128,768]{1,0:T(8,128)} %dynamic-slice_bitcast_fusion), channel_id=1, source_target_pairs={{0,2},{1,3},{2,0},{3,1},{4,6},{5,7},{6,4},{7,5},{8,10},{9,11},{10,... | collective-permute-start | bytes 1179656 | tf_op jit(solution)/shard_map/ppermute | solution.py:181

commit v4 on v3

--- a/solution.py
+++ b/solution.py
@@ -36,54 +36,87 @@
     return (forward.astype(BF16), grad_w, grad_x)
 
 
-def weight_grad_part(acts_own, acts_got, og_own, og_got, block_mask, where, rows, chunk):
-    nsub, tokens, cw = og_own.shape
-    cols = where_chunk(chunk, cw)
-    got = len(og_got)
-
-    def kernel(where_ref, mask_ref, *refs):
-        acts_refs, og_refs = refs[: got + 1], refs[got + 1 : 2 * got + 2]
-        outs = refs[2 * got + 2 :]
-        z, x = where_ref[0], where_ref[1]
-        col = where_ref[2] + cols
-        rhs = [r[...].reshape(nsub * tokens, cw) for r in og_refs]
-        for side in range(2):
-            xs = x if side == 0 else 1 - x
-            for g in range(rows // LANES):
-                inside = xs * rows + g * LANES
-                block = (z * 2 * rows + inside) // BS
-                at = pl.ds(pl.multiple_of(inside, LANES), LANES)
+def pack_acts(a, lanes):
+    t = a.shape[0]
+    rest = a[:, lanes:].reshape(2, t // 2, 2, LANES)
+    return jnp.concatenate(
+        [a[:, :lanes]] + [jnp.concatenate([rest[h, :, i] for i in range(2) for h in range(2)], axis=1)]
+    )
+
+
+def unpack_acts(ref, first, t, g):
+    if g < 4:
+        return ref[first : first + t, g * LANES : (g + 1) * LANES]
+    at = 2 * (g - 4)
+    return jnp.concatenate(
+        [
+            ref[first + t : first + t + t // 2, (at + h) * LANES : (at + h + 1) * LANES]
+            for h in range(2)
+        ]
+    )
+
+
+def weight_grad_part(acts_own, acts_got, acts_swap, og, og_first, block_mask, where, rows, first):
+    nsub = block_mask.shape[0]
+    tokens = acts_own.shape[0]
+    half = tokens // 2
+    packed = half + half // 2
+    cw = og[0].shape[-1]
+    ng = len(og)
+
+    def kernel(where_ref, mask_ref, own_ref, swap_ref, *refs):
+        got_refs, og_refs = refs[: ng - 1], refs[ng - 1 : 2 * ng - 1]
+        keep_ref, send_ref = refs[2 * ng - 1 :]
+        z, x, core = where_ref[0], where_ref[1], where_ref[3]
+        for g in range(2 * rows // LANES):
+            side, inside = divmod(g * LANES, rows)
+            block = (z * 2 * rows + g * LANES) // BS
+            tiles = [own_ref[:, g * LANES : (g + 1) * LANES].T]
+            for k, r in enumerate(got_refs):
+                mine = unpack_acts(r, acts_first[k], half, g)
+                other = unpack_acts(swap_ref, k * packed, half, g)
+                low = jnp.where(core == 0, mine, other)
+                high = jnp.where(core == 0, other, mine)
+                tiles.append(jnp.concatenate([low, high]).T)
+            for b in range(cw // BS):
+                col = where_ref[2] + first // BS + b
+                lanes = slice(b * BS, (b + 1) * BS)
                 keep = [mask_ref[s, block, col].astype(F32) for s in range(nsub)]
                 keep = [jnp.full((LANES, tokens), k).astype(BF16) for k in keep]
                 total = None
-                for a_ref, r in zip(acts_refs, rhs):
-                    t = a_ref[:, at].T
+                for t, r, r0 in zip(tiles, og_refs, og_first):
                     lhs = jnp.concatenate([t * k for k in keep], axis=1)
-                    term = jnp.dot(lhs, r, preferred_element_type=F32)
+                    term = jnp.dot(
+                        lhs, r[r0 : r0 + nsub * tokens, lanes], preferred_element_type=F32
+                    )
                     total = term if total is None else total + term
-                outs[side][g * LANES : (g + 1) * LANES, :] = total * (1.0 / TOK_G)
-
+                total = total * (1.0 / TOK_G)
+
+                @pl.when(x == side)
+                def _():
+                    keep_ref[inside : inside + LANES, lanes] = total
+
+                @pl.when(x != side)
+                def _():
+                    send_ref[inside : inside + LANES, lanes] = total
+
+    acts_first = [nsub * tokens, 0, nsub * tokens]
     smem = pl.BlockSpec(memory_space=pltpu.SMEM)
     vmem = pl.BlockSpec(memory_space=pltpu.VMEM)
     shape = jax.ShapeDtypeStruct((rows, cw), F32)
     return pl.pallas_call(
         kernel,
         out_shape=(shape, shape),
-        in_specs=[smem, smem] + [vmem] * (2 * got + 2),
+        in_specs=[smem, smem] + [vmem] * (2 * ng + 1),
         out_specs=(vmem, vmem),
         compiler_params=pltpu.CompilerParams(vmem_limit_bytes=VMEM_BYTES),
         cost_estimate=pl.CostEstimate(
-            flops=4 * (got + 1) * rows * cw * nsub * tokens,
+            flops=4 * ng * rows * cw * nsub * tokens,
             bytes_accessed=8 * rows * cw,
             transcendentals=0,
         ),
         name="weight_grad_part",
-    )(where, block_mask, acts_own, *acts_got, og_own, *og_got)
-
-
-def where_chunk(first, cw):
-    assert first // BS == (first + cw - 1) // BS
-    return first // BS
+    )(where, block_mask, acts_own, acts_swap, *acts_got, *og)
 
 
 def forward_and_input(acts, w_mine, w_peer, og, block_mask, where):
@@ -159,14 +192,14 @@
     tokens, depth = acts.shape
     dp = lax.axis_size("dp")
     fsdp = lax.axis_size("fsdp")
-    if rows % LANES or width % BS or dp != 8 or fsdp != 4 or tokens % LANES:
+    if rows != 3 * LANES or width != 3 * BS or dp != 8 or fsdp != 4 or tokens != LANES:
         return plain(acts, weight, block_mask, out_grad)
     nx = 2
     me = lax.axis_index("dp")
     z, x = me // nx, me % nx
     f = lax.axis_index("fsdp")
     y, c = f // 2, f % 2
-    where = jnp.stack([z, x, f * (width // BS)]).astype(jnp.int32)
+    where = jnp.stack([z, x, f * (width // BS), c]).astype(jnp.int32)
 
     def swap_dp(a, bits):
         return lax.ppermute(a, "dp", [(d, d ^ bits) for d in range(dp)])
@@ -191,14 +224,32 @@
     def acts_of(k):
         return lax.dynamic_slice_in_dim(acts, (z ^ k) * nx * rows, nx * rows, 1)
 
+    half = tokens // 2
+    nsub = out_grad.shape[0]
+    flat = nsub * tokens
+    packed = half + half // 2
+    wide = 2 * BS
+    a1, a2, a3 = [
+        pack_acts(lax.dynamic_slice_in_dim(acts_of(k), c * half, half, 0), wide) for k in (1, 2, 3)
+    ]
+    og_a = out_grad[:, :, :wide].reshape(flat, wide)
+    og_b = out_grad[:, :, wide:].reshape(flat, width - wide)
+    two_a = swap_z(jnp.concatenate([a2, og_a, a3]), 2)
+    one_a = swap_z(jnp.concatenate([og_a, a1]), 1)
+    three_a = swap_z(two_a[packed:], 1)
+    b_own, b_one, b_two, b_three = gather_z(og_b)
+    acts_swap = swap_f(
+        jnp.concatenate([one_a[flat:], two_a[:packed], three_a[flat:]]), 1
+    )
     acts_own = acts_of(0)
-    acts_got = [swap_z(acts_of(k), k) for k in range(1, 4)]
-
+    acts_got = [one_a, two_a, three_a]
     grads = []
-    for first, cw in [(i * BS, BS) for i in range(width // BS)]:
-        og = gather_z(out_grad[:, :, first : first + cw])
+    for first, og, og_first in (
+        (0, [og_a, one_a, two_a, three_a], [0, 0, packed, 0]),
+        (wide, [b_own, b_one, b_two, b_three], [0, 0, 0, 0]),
+    ):
         keep, send = weight_grad_part(
-            acts_own, acts_got, og[0], og[1:], block_mask, where, rows, first
+            acts_own, acts_got, acts_swap, og, og_first, block_mask, where, rows, first
         )
         grads.append(keep + swap_x(send))
     grad_w = jnp.concatenate(grads, axis=1)

time: 171 us -> 156 us (0.912)
  starting transfers between devices: 42.7 us -> 21.4 us
  Pallas kernels: 16.7 us -> 22 us
  local copies, waits for them, and re-layouts: 16.5 us -> 21.4 us
  other arithmetic: 7.24 us -> 5.33 us
  waiting for transfers between devices: 86.3 us -> 84.4 us
    ppermute x22 -> x15, starting transfers between devices: 41.2 us -> 19.5 us  [swap_dp(): return lax.ppermute(a, 'dp', [(d, d ^ bits) for d in range(dp)])]
    pallas_call x3 -> x2, Pallas kernels: 6.91 us -> 12.3 us  [weight_grad_part(): pl.pallas_call(kernel, out_shape=(shape, shape), in_specs=[smem, smem] +...]
    slice x1 -> x11, local copies, waits for them, and re-layouts: 0.85 us -> 6.03 us  [the longest x1 1.08 us: on_device(): og_a = out_grad[:, :, :wide].reshape(flat, wide)]
    dynamic_slice x1, local copies, waits for them, and re-layouts: 2.23 us -> 4.38 us  [on_device(): lax.dynamic_index_in_dim(by, c, 2, keepdims=False)]
    add x3 -> x2, other arithmetic: 3.14 us -> 1.33 us  [on_device(): grads.append(keep + swap_x(send))]
    unnamed x36 -> x22, local copies, waits for them, and re-layouts: 9.14 us -> 7.45 us
    ppermute x22 -> x15, waiting for transfers between devices: 85 us -> 84.4 us  [swap_dp(): return lax.ppermute(a, 'dp', [(d, d ^ bits) for d in range(dp)])]
  transfers between devices with their start and end apart: 24 -> 18, of which waited for: 12 -> 6; matrix products, arithmetic and copies ran while one was open for 8% -> 13% of each run, Pallas kernels for 10% -> 14%
where the time goes in v4:
time: 156 us; the launch traced here: 155 us
  waiting for transfers between devices  84.4 us (54%)
  Pallas kernels  22 us (14%)
  starting transfers between devices  21.4 us (14%)
  local copies, waits for them, and re-layouts  21.4 us (14%)
  other arithmetic  5.33 us (3%)
    ppermute x15, waiting for transfers between devices, swap_dp(): return lax.ppermute(a, 'dp', [(d, d ^ bits) for d in range(dp)])  84.4 us
    ppermute x15, starting transfers between devices, swap_dp(): return lax.ppermute(a, 'dp', [(d, d ^ bits) for d in range(dp)])  19.5 us
    pallas_call x2, Pallas kernels, weight_grad_part(): pl.pallas_call(kernel, out_shape=(shape, shape), in_specs=[smem, smem] +...  12.3 us
    pallas_call x1, Pallas kernels, forward_and_input(): pl.pallas_call(kernel, grid=(width // BS,), out_shape=(jax.ShapeDtypeStru...  9.75 us
    unnamed x22, local copies, waits for them, and re-layouts  7.45 us
    dynamic_slice x1, local copies, waits for them, and re-layouts, on_device(): lax.dynamic_index_in_dim(by, c, 2, keepdims=False)  4.38 us
  transfers between devices with their start and end apart: 18, of which 6 were waited for; matrix products, arithmetic and copies ran while one was open for 13% of the time, Pallas kernels for 14%

profile of v4, /device:TPU:0, one launch (start us, length us, event | category | flops | bytes accessed | tf_op | source)
XLA Modules:
  0.0 155.4 jit_solution(5385437874459470104)
XLA Ops:
  0.6 4.1 %collective-permute-start.1 = (bf16[384,768]{1,0:T(8,128)(2,1)}, bf16[384,768]{1,0:T(8,128)(2,1)S(1)}, u32[]{:S(2)}, u32[]{:S(2)}) collective-permute-start(bf16[384,768]{1,0:T(8,128)(2,1)} %rest_0_.1), channel_id=1, source_target_pairs={{0,16},{4,20},{8,24},{12,28},{16,0},{20,4},{24,8},{28,12},{1,17},{... | collective-permute-start | bytes 1769480 | tf_op jit(solution)/shard_map/ppermute | solution.py:205
  4.7 1.6 %collective-permute-start = (bf16[384,768]{1,0:T(8,128)(2,1)}, bf16[384,768]{1,0:T(8,128)(2,1)S(1)}, u32[]{:S(2)}, u32[]{:S(2)}) collective-permute-start(bf16[384,768]{1,0:T(8,128)(2,1)} %rest_0_.1), channel_id=1, source_target_pairs={{0,8},{4,12},{8,0},{12,4},{16,24},{20,28},{24,16},{28,20},{1,9},{5... | collective-permute-start | bytes 1769480 | tf_op jit(solution)/shard_map/ppermute | solution.py:205
  6.3 1.5 collective-permute-start.3
  7.8 1.0 dynamic-slice_dynamic-update-slice_fusion.1
  8.8 1.0 fusion.3
  9.8 0.1 fusion.6
  9.9 1.1 slice.72
  11.1 0.1 fusion.5
  11.1 19.9 %collective-permute-done.1.rest_2_ = bf16[384,768]{1,0:T(8,128)(2,1)S(1)} collective-permute-done((bf16[384,768]{1,0:T(8,128)(2,1)}, bf16[384,768]{1,0:T(8,128)(2,1)S(1)}, u32[]{:S(2)}, u32[]{:S(2)}) %collective-permute-start.1) | collective-permute-done | bytes 589856 | tf_op jit(solution)/shard_map/ppermute | solution.py:205
  31.0 0.7 collective-permute-start.2
  31.7 1.1 fusion.2
  32.8 3.3 %collective-permute-start.8 = (bf16[704,512]{1,0:T(8,128)(2,1)S(1)}, bf16[704,512]{1,0:T(8,128)(2,1)S(1)}, u32[]{:S(2)}, u32[]{:S(2)}) collective-permute-start(bf16[704,512]{1,0:T(8,128)(2,1)S(1)} %maximum_dynamic-update-slice_fusion), channel_id=1, source_target_pairs={{0,16},{4,20},{8,24},{12,28},{16,0},{20,4},{24,8},{28,12},{1,17},{... | collective-permute-start | bytes 2162696 | tf_op jit(solution)/shard_map/ppermute | solution.py:205
  36.2 0.1 fusion.4
  36.2 1.6 %collective-permute-start.5 = (bf16[384,768]{1,0:T(8,128)(2,1)S(1)}, bf16[384,768]{1,0:T(8,128)(2,1)}, u32[]{:S(2)}, u32[]{:S(2)}) collective-permute-start(bf16[384,768]{1,0:T(8,128)(2,1)S(1)} %collective-permute-done.1.rest_2_), channel_id=1, source_target_pairs={{0,4},{4,0},{8,12},{12,8},{16,20},{20,16},{24,28},{28,24},{1,5},{5... | collective-permute-start | bytes 1769480 | tf_op jit(solution)/shard_map/ppermute | solution.py:205
  37.8 0.0 collective-permute-done.rest_1_
  37.8 0.5 collective-permute-start.4
  38.3 18.5 %collective-permute-done.2.rest_3_ = bf16[384,768]{1,0:T(8,128)(2,1)} collective-permute-done((bf16[384,768]{1,0:T(8,128)(2,1)S(1)}, bf16[384,768]{1,0:T(8,128)(2,1)}, u32[]{:S(2)}, u32[]{:S(2)}) %collective-permute-start.2) | collective-permute-done | bytes 589856 | tf_op jit(solution)/shard_map/ppermute | solution.py:205
  56.9 1.3 collective-permute-start.6
  58.1 0.0 copy-start.8
  58.1 0.9 maximum_maximum_fusion
  59.0 8.7 %collective-permute-done.8.refs_1_.refs_5_ = bf16[704,512]{1,0:T(8,128)(2,1)S(1)} collective-permute-done((bf16[704,512]{1,0:T(8,128)(2,1)S(1)}, bf16[704,512]{1,0:T(8,128)(2,1)S(1)}, u32[]{:S(2)}, u32[]{:S(2)}) %collective-permute-start.8) | collective-permute-done | bytes 720928 | tf_op jit(solution)/shard_map/ppermute | solution.py:205
  67.7 0.0 collective-permute-start.7
  67.7 0.9 slice.110
  68.6 0.0 collective-permute-done.3.rest_4_
  68.6 2.1 %collective-permute-start.9 = (bf16[608,512]{1,0:T(8,128)(2,1)}, bf16[608,512]{1,0:T(8,128)(2,1)}, u32[]{:S(2)}, u32[]{:S(2)}) collective-permute-start(bf16[608,512]{1,0:T(8,128)(2,1)} %slice.110), channel_id=1, source_target_pairs={{0,8},{4,12},{8,0},{12,4},{16,24},{20,28},{24,16},{28,20},{1,9},{5... | collective-permute-start | bytes 1867784 | tf_op jit(solution)/shard_map/ppermute | solution.py:205
  70.7 0.1 pad_add_fusion.where_ref
  70.7 0.0 collective-permute-done.5.rest_6_
  70.7 0.0 collective-permute-done.4.rest_5_
  70.7 5.6 %collective-permute-done.6.rest_7_ = bf16[384,768]{1,0:T(8,128)(2,1)} collective-permute-done((bf16[384,768]{1,0:T(8,128)(2,1)}, bf16[384,768]{1,0:T(8,128)(2,1)}, u32[]{:S(2)}, u32[]{:S(2)}) %collective-permute-start.6) | collective-permute-done | bytes 589856 | tf_op jit(solution)/shard_map/ppermute | solution.py:205
  76.4 1.1 copy-done
  77.5 1.1 copy-done.1
  78.6 1.1 copy-done.2
  79.7 1.1 copy-done.4
  80.8 1.1 copy-done.6
  81.8 9.8 %forward_and_input.1 = (bf16[4,128,768]{2,1,0:T(8,128)(2,1)}, f32[128,3072]{1,0:T(8,128)S(1)}) custom-call(s32[4]{0:T(128)S(1)} %pad_add_fusion.where_ref, s32[4,12,12]{2,1,0:T(8,128)S(1)} %copy.10.mask_ref, bf16[128,3072]{1,0:T(8,128)(2,1)S(1)} %copy-done.1, bf16[4,128,768]{2,1,0:T(8,128)(2,1)S(1)} %copy-done, bf16[384,768]{1,0:T(8,128)(2,1)S(1)} %copy-done.2, ...), custom_call_target="tpu_custom_call" | custom-call | flops 1811939328 | bytes 9437184 | tf_op jit(solution)/shard_map/forward_and_input/pallas_call | solution.py:168
  91.6 2.5 %reshape.29 = f32[128,2,2,768]{3,2,1,0:T(2,128)} reshape(f32[128,3072]{1,0:T(8,128)S(1)} %get-tuple-element.14) | data formatting | bytes 3145728 | tf_op jit(solution)/shard_map/reshape | solution.py:259
  94.1 4.4 %constant_dynamic-slice_fusion.1 = (f32[128,2,1,768]{3,2,1,0:T(1,128)}, f32[128,2,1,768]{3,2,1,0:T(1,128)S(1)}) fusion(f32[128,2,2,768]{3,2,1,0:T(2,128)} %reshape.29, s32[]{:T(128)S(6)} %select_n.69, s32[]{:T(128)S(6)} %select_n.70), kind=kLoop, calls=%fused_computation.27 | loop fusion | bytes 3145736 | tf_op jit(solution)/shard_map/jit(dynamic_index_in_dim)/dynamic_slice | solution.py:260
  98.5 0.9 copy.57
  99.4 1.0 slice.95
  100.4 0.4 collective-permute-start.13
  100.8 0.0 collective-permute-done.7.refs_0_.refs_4_
  100.8 0.0 collective-permute-done.9.refs_2_.refs_6_
  100.8 0.9 slice.111
  101.7 0.3 collective-permute-start.10
  102.0 0.4 collective-permute-start.12
  102.5 13.3 %collective-permute-done.13.refs_5_ = bf16[512,256]{1,0:T(8,128)(2,1)} collective-permute-done((bf16[512,256]{1,0:T(8,128)(2,1)S(1)}, bf16[512,256]{1,0:T(8,128)(2,1)}, u32[]{:S(2)}, u32[]{:S(2)}) %collective-permute-start.13) | collective-permute-done | bytes 262176 | tf_op jit(solution)/shard_map/ppermute | solution.py:205
  115.7 0.0 collective-permute-start.14
  115.7 0.9 constant_dynamic-slice_fusion.2.own_ref
  116.7 0.0 collective-permute-done.10.swap_ref
  116.7 7.4 %weight_grad_part.2 = (f32[384,512]{1,0:T(8,128)S(1)}, f32[384,512]{1,0:T(8,128)}) custom-call(s32[4]{0:T(128)S(1)} %pad_add_fusion.where_ref, s32[4,12,12]{2,1,0:T(8,128)S(1)} %copy.10.mask_ref, bf16[128,768]{1,0:T(8,128)(2,1)S(1)} %constant_dynamic-slice_fusion.2.own_ref, bf16[288,512]{1,0:T(8,128)(2,1)S(1)} %collective-permute-done.10.swap_ref, ...), custom_call_target="tpu_custom_call" | custom-call | flops 1610612736 | bytes 1572864 | tf_op jit(solution)/shard_map/weight_grad_part/pallas_call | solution.py:107
  124.1 1.6 %collective-permute-start.11 = (f32[384,512]{1,0:T(8,128)}, f32[384,512]{1,0:T(8,128)}, u32[]{:S(2)}, u32[]{:S(2)}) collective-permute-start(f32[384,512]{1,0:T(8,128)} %get-tuple-element.11), channel_id=1, source_target_pairs={{0,4},{4,0},{8,12},{12,8},{16,20},{20,16},{24,28},{28,24},{1,5},{5... | collective-permute-start | bytes 2359304 | tf_op jit(solution)/shard_map/ppermute | solution.py:205
  125.7 0.0 collective-permute-done.14.refs_6_
  125.7 4.8 %weight_grad_part.3 = (f32[384,256]{1,0:T(8,128)S(1)}, f32[384,256]{1,0:T(8,128)}) custom-call(s32[4]{0:T(128)S(1)} %pad_add_fusion.where_ref, s32[4,12,12]{2,1,0:T(8,128)S(1)} %copy.10.mask_ref, bf16[128,768]{1,0:T(8,128)(2,1)S(1)} %constant_dynamic-slice_fusion.2.own_ref, bf16[288,512]{1,0:T(8,128)(2,1)S(1)} %collective-permute-done.10.swap_ref, ...), custom_call_target="tpu_custom_call" | custom-call | flops 805306368 | bytes 786432 | tf_op jit(solution)/shard_map/weight_grad_part/pallas_call | solution.py:107
  130.5 0.4 collective-permute-start.15
  131.0 0.0 collective-permute-done.16
  131.0 1.2 fusion
  132.3 1.6 %collective-permute-start.17 = (f32[128,768]{1,0:T(8,128)S(1)}, f32[128,768]{1,0:T(8,128)S(1)}, u32[]{:S(2)}, u32[]{:S(2)}) collective-permute-start(f32[128,768]{1,0:T(8,128)S(1)} %dynamic-slice_bitcast_fusion), channel_id=1, source_target_pairs={{0,2},{1,3},{2,0},{3,1},{4,6},{5,7},{6,4},{7,5},{8,10},{9,11},{10,... | collective-permute-start | bytes 1179656 | tf_op jit(solution)/shard_map/ppermute | solution.py:214
  133.8 18.4 %collective-permute-done.15 = f32[384,256]{1,0:T(8,128)S(1)} collective-permute-done((f32[384,256]{1,0:T(8,128)}, f32[384,256]{1,0:T(8,128)S(1)}, u32[]{:S(2)}, u32[]{:S(2)}) %collective-permute-start.15) | collective-permute-done | bytes 393248 | tf_op jit(solution)/shard_map/ppermute | solution.py:205
  152.2 0.1 add.68
  152.3 0.0 collective-permute-done.11
  152.3 1.3 add.67
  153.6 1.1 pad_maximum_fusion
  154.7 0.0 collective-permute-done.17
  154.7 0.7 fusion.1
  (31 shorter events, 0.2 us)
Async XLA Ops:
  0.6 30.4 %collective-permute-start.1 = (bf16[384,768]{1,0:T(8,128)(2,1)}, bf16[384,768]{1,0:T(8,128)(2,1)S(1)}, u32[]{:S(2)}, u32[]{:S(2)}) collective-permute-start(bf16[384,768]{1,0:T(8,128)(2,1)} %rest_0_.1), channel_id=1, source_target_pairs={{0,16},{4,20},{8,24},{12,28},{16,0},{20,4},{24,8},{28,12},{1,17},{... | collective-permute-start | bytes 1769480 | tf_op jit(solution)/shard_map/ppermute | solution.py:205
  4.7 33.1 %collective-permute-start = (bf16[384,768]{1,0:T(8,128)(2,1)}, bf16[384,768]{1,0:T(8,128)(2,1)S(1)}, u32[]{:S(2)}, u32[]{:S(2)}) collective-permute-start(bf16[384,768]{1,0:T(8,128)(2,1)} %rest_0_.1), channel_id=1, source_target_pairs={{0,8},{4,12},{8,0},{12,4},{16,24},{20,28},{24,16},{28,20},{1,9},{5... | collective-permute-start | bytes 1769480 | tf_op jit(solution)/shard_map/ppermute | solution.py:205
  6.3 62.3 %collective-permute-start.3 = (bf16[384,768]{1,0:T(8,128)(2,1)}, bf16[384,768]{1,0:T(8,128)(2,1)}, u32[]{:S(2)}, u32[]{:S(2)}) collective-permute-start(bf16[384,768]{1,0:T(8,128)(2,1)} %rest_0_.1), channel_id=1, source_target_pairs={{0,4},{4,0},{8,12},{12,8},{16,20},{20,16},{24,28},{28,24},{1,5},{5... | collective-permute-start | bytes 1769480 | tf_op jit(solution)/shard_map/ppermute | solution.py:205
  31.0 37.5 %copy-start.3 = (bf16[384,768]{1,0:T(8,128)(2,1)}, bf16[384,768]{1,0:T(8,128)(2,1)S(1)}, u32[]{:S(2)}) copy-start(bf16[384,768]{1,0:T(8,128)(2,1)S(1)} %collective-permute-done.1.rest_2_) | copy-start | bytes 1769476
  31.0 25.8 %collective-permute-start.2 = (bf16[384,768]{1,0:T(8,128)(2,1)S(1)}, bf16[384,768]{1,0:T(8,128)(2,1)}, u32[]{:S(2)}, u32[]{:S(2)}) collective-permute-start(bf16[384,768]{1,0:T(8,128)(2,1)S(1)} %collective-permute-done.1.rest_2_), channel_id=1, source_target_pairs={{0,8},{4,12},{8,0},{12,4},{16,24},{20,28},{24,16},{28,20},{1,9},{5... | collective-permute-start | bytes 1769480 | tf_op jit(solution)/shard_map/ppermute | solution.py:205
  32.8 34.9 %collective-permute-start.8 = (bf16[704,512]{1,0:T(8,128)(2,1)S(1)}, bf16[704,512]{1,0:T(8,128)(2,1)S(1)}, u32[]{:S(2)}, u32[]{:S(2)}) collective-permute-start(bf16[704,512]{1,0:T(8,128)(2,1)S(1)} %maximum_dynamic-update-slice_fusion), channel_id=1, source_target_pairs={{0,16},{4,20},{8,24},{12,28},{16,0},{20,4},{24,8},{28,12},{1,17},{... | collective-permute-start | bytes 2162696 | tf_op jit(solution)/shard_map/ppermute | solution.py:205
  36.2 34.5 %collective-permute-start.5 = (bf16[384,768]{1,0:T(8,128)(2,1)S(1)}, bf16[384,768]{1,0:T(8,128)(2,1)}, u32[]{:S(2)}, u32[]{:S(2)}) collective-permute-start(bf16[384,768]{1,0:T(8,128)(2,1)S(1)} %collective-permute-done.1.rest_2_), channel_id=1, source_target_pairs={{0,4},{4,0},{8,12},{12,8},{16,20},{20,16},{24,28},{28,24},{1,5},{5... | collective-permute-start | bytes 1769480 | tf_op jit(solution)/shard_map/ppermute | solution.py:205
  37.8 30.8 %copy-start.5 = (bf16[384,768]{1,0:T(8,128)(2,1)}, bf16[384,768]{1,0:T(8,128)(2,1)S(1)}, u32[]{:S(2)}) copy-start(bf16[384,768]{1,0:T(8,128)(2,1)S(1)} %collective-permute-done.rest_1_) | copy-start | bytes 1769476
  37.8 32.9 %collective-permute-start.4 = (bf16[384,768]{1,0:T(8,128)(2,1)S(1)}, bf16[384,768]{1,0:T(8,128)(2,1)}, u32[]{:S(2)}, u32[]{:S(2)}) collective-permute-start(bf16[384,768]{1,0:T(8,128)(2,1)S(1)} %collective-permute-done.rest_1_), channel_id=1, source_target_pairs={{0,4},{4,0},{8,12},{12,8},{16,20},{20,16},{24,28},{28,24},{1,5},{5... | collective-permute-start | bytes 1769480 | tf_op jit(solution)/shard_map/ppermute | solution.py:205
  56.9 19.5 %collective-permute-start.6 = (bf16[384,768]{1,0:T(8,128)(2,1)}, bf16[384,768]{1,0:T(8,128)(2,1)}, u32[]{:S(2)}, u32[]{:S(2)}) collective-permute-start(bf16[384,768]{1,0:T(8,128)(2,1)} %collective-permute-done.2.rest_3_), channel_id=1, source_target_pairs={{0,4},{4,0},{8,12},{12,8},{16,20},{20,16},{24,28},{28,24},{1,5},{5... | collective-permute-start | bytes 1769480 | tf_op jit(solution)/shard_map/ppermute | solution.py:205
  58.1 12.5 %copy-start.8 = (s32[4,12,12]{2,0,1:T(4,128)S(1)}, s32[4,12,12]{2,0,1:T(4,128)}, u32[]{:S(2)}) copy-start(s32[4,12,12]{2,0,1:T(4,128)} %param.6) | copy-start | bytes 6916
  67.7 33.1 %collective-permute-start.7 = (bf16[608,512]{1,0:T(8,128)(2,1)}, bf16[608,512]{1,0:T(8,128)(2,1)S(1)}, u32[]{:S(2)}, u32[]{:S(2)}) collective-permute-start(bf16[608,512]{1,0:T(8,128)(2,1)} %maximum_maximum_fusion), channel_id=1, source_target_pairs={{0,8},{4,12},{8,0},{12,4},{16,24},{20,28},{24,16},{28,20},{1,9},{5... | collective-permute-start | bytes 1867784 | tf_op jit(solution)/shard_map/ppermute | solution.py:205
  68.6 32.2 %collective-permute-start.9 = (bf16[608,512]{1,0:T(8,128)(2,1)}, bf16[608,512]{1,0:T(8,128)(2,1)}, u32[]{:S(2)}, u32[]{:S(2)}) collective-permute-start(bf16[608,512]{1,0:T(8,128)(2,1)} %slice.110), channel_id=1, source_target_pairs={{0,8},{4,12},{8,0},{12,4},{16,24},{20,28},{24,16},{28,20},{1,9},{5... | collective-permute-start | bytes 1867784 | tf_op jit(solution)/shard_map/ppermute | solution.py:205
  76.4 1.1 copy-start
  77.5 1.1 copy-start.1
  78.6 1.1 copy-start.2
  79.7 1.1 copy-start.4
  80.8 1.1 copy-start.6
  99.4 31.6 %collective-permute-start.16 = (f32[128,2,768]{2,0,1:T(8,128)}, f32[128,2,768]{2,0,1:T(8,128)}, u32[]{:S(2)}, u32[]{:S(2)}) collective-permute-start(f32[128,2,768]{2,0,1:T(8,128)} %bitcast.42), channel_id=1, source_target_pairs={{0,1},{1,0},{2,3},{3,2},{4,5},{5,4},{6,7},{7,6},{8,9},{9,8},{10,11... | collective-permute-start | bytes 2359304 | tf_op jit(solution)/shard_map/ppermute | solution.py:214
  100.4 15.3 %collective-permute-start.13 = (bf16[512,256]{1,0:T(8,128)(2,1)S(1)}, bf16[512,256]{1,0:T(8,128)(2,1)}, u32[]{:S(2)}, u32[]{:S(2)}) collective-permute-start(bf16[512,256]{1,0:T(8,128)(2,1)S(1)} %bitcast.46), channel_id=1, source_target_pairs={{0,16},{4,20},{8,24},{12,28},{16,0},{20,4},{24,8},{28,12},{1,17},{... | collective-permute-start | bytes 786440 | tf_op jit(solution)/shard_map/ppermute | solution.py:205
  101.7 14.9 %collective-permute-start.10 = (bf16[288,512]{1,0:T(8,128)(2,1)S(1)}, bf16[288,512]{1,0:T(8,128)(2,1)S(1)}, u32[]{:S(2)}, u32[]{:S(2)}) collective-permute-start(bf16[288,512]{1,0:T(8,128)(2,1)S(1)} %pad_maximum_fusion.1), channel_id=1, source_target_pairs={{0,1},{1,0},{2,3},{3,2},{4,5},{5,4},{6,7},{7,6},{8,9},{9,8},{10,11... | collective-permute-start | bytes 884744 | tf_op jit(solution)/shard_map/ppermute | solution.py:214
  102.0 23.7 %collective-permute-start.12 = (bf16[512,256]{1,0:T(8,128)(2,1)S(1)}, bf16[512,256]{1,0:T(8,128)(2,1)}, u32[]{:S(2)}, u32[]{:S(2)}) collective-permute-start(bf16[512,256]{1,0:T(8,128)(2,1)S(1)} %bitcast.47), channel_id=1, source_target_pairs={{0,8},{4,12},{8,0},{12,4},{16,24},{20,28},{24,16},{28,20},{1,9},{5... | collective-permute-start | bytes 786440 | tf_op jit(solution)/shard_map/ppermute | solution.py:205
  115.7 10.0 %collective-permute-start.14 = (bf16[512,256]{1,0:T(8,128)(2,1)}, bf16[512,256]{1,0:T(8,128)(2,1)}, u32[]{:S(2)}, u32[]{:S(2)}) collective-permute-start(bf16[512,256]{1,0:T(8,128)(2,1)} %collective-permute-done.13.refs_5_), channel_id=1, source_target_pairs={{0,8},{4,12},{8,0},{12,4},{16,24},{20,28},{24,16},{28,20},{1,9},{5... | collective-permute-start | bytes 786440 | tf_op jit(solution)/shard_map/ppermute | solution.py:205
  124.1 28.2 %collective-permute-start.11 = (f32[384,512]{1,0:T(8,128)}, f32[384,512]{1,0:T(8,128)}, u32[]{:S(2)}, u32[]{:S(2)}) collective-permute-start(f32[384,512]{1,0:T(8,128)} %get-tuple-element.11), channel_id=1, source_target_pairs={{0,4},{4,0},{8,12},{12,8},{16,20},{20,16},{24,28},{28,24},{1,5},{5... | collective-permute-start | bytes 2359304 | tf_op jit(solution)/shard_map/ppermute | solution.py:205
  125.7 5.3 %copy-start.7 = (f32[128,2,1,768]{3,2,1,0:T(1,128)S(1)}, f32[128,2,1,768]{3,2,1,0:T(1,128)}, u32[]{:S(2)}) copy-start(f32[128,2,1,768]{3,2,1,0:T(1,128)} %get-tuple-element.15) | copy-start | bytes 2359300
  130.5 21.7 %collective-permute-start.15 = (f32[384,256]{1,0:T(8,128)}, f32[384,256]{1,0:T(8,128)S(1)}, u32[]{:S(2)}, u32[]{:S(2)}) collective-permute-start(f32[384,256]{1,0:T(8,128)} %get-tuple-element.13), channel_id=1, source_target_pairs={{0,4},{4,0},{8,12},{12,8},{16,20},{20,16},{24,28},{28,24},{1,5},{5... | collective-permute-start | bytes 1179656 | tf_op jit(solution)/shard_map/ppermute | solution.py:205
  132.3 22.4 %collective-permute-start.17 = (f32[128,768]{1,0:T(8,128)S(1)}, f32[128,768]{1,0:T(8,128)S(1)}, u32[]{:S(2)}, u32[]{:S(2)}) collective-permute-start(f32[128,768]{1,0:T(8,128)S(1)} %dynamic-slice_bitcast_fusion), channel_id=1, source_target_pairs={{0,2},{1,3},{2,0},{3,1},{4,6},{5,7},{6,4},{7,5},{8,10},{9,11},{10,... | collective-permute-start | bytes 1179656 | tf_op jit(solution)/shard_map/ppermute | solution.py:214

commit v5 on v4

--- a/solution.py
+++ b/solution.py
@@ -56,28 +56,37 @@
     )
 
 
-def weight_grad_part(acts_own, acts_got, acts_swap, og, og_first, block_mask, where, rows, first):
+def weight_grad_part(acts_in, og, og_first, block_mask, where, rows, first, acts_first):
     nsub = block_mask.shape[0]
-    tokens = acts_own.shape[0]
+    fresh = acts_first is not None
+    tokens = acts_in[0].shape[0] if fresh else acts_in[0].shape[2]
     half = tokens // 2
     packed = half + half // 2
     cw = og[0].shape[-1]
     ng = len(og)
 
-    def kernel(where_ref, mask_ref, own_ref, swap_ref, *refs):
-        got_refs, og_refs = refs[: ng - 1], refs[ng - 1 : 2 * ng - 1]
-        keep_ref, send_ref = refs[2 * ng - 1 :]
+    def kernel(where_ref, mask_ref, *refs):
+        acts_refs, og_refs = refs[: len(acts_in)], refs[len(acts_in) : len(acts_in) + ng]
+        outs = refs[len(acts_in) + ng :]
+        keep_ref, send_ref = outs[:2]
         z, x, core = where_ref[0], where_ref[1], where_ref[3]
         for g in range(2 * rows // LANES):
             side, inside = divmod(g * LANES, rows)
             block = (z * 2 * rows + g * LANES) // BS
-            tiles = [own_ref[:, g * LANES : (g + 1) * LANES].T]
-            for k, r in enumerate(got_refs):
-                mine = unpack_acts(r, acts_first[k], half, g)
-                other = unpack_acts(swap_ref, k * packed, half, g)
-                low = jnp.where(core == 0, mine, other)
-                high = jnp.where(core == 0, other, mine)
-                tiles.append(jnp.concatenate([low, high]).T)
+            at = slice(g * LANES, (g + 1) * LANES)
+            if fresh:
+                own_ref, swap_ref, *got_refs = acts_refs
+                tiles = [own_ref[:, at].T]
+                for k, r in enumerate(got_refs):
+                    mine = unpack_acts(r, acts_first[k], half, g)
+                    other = unpack_acts(swap_ref, k * packed, half, g)
+                    low = jnp.where(core == 0, mine, other)
+                    high = jnp.where(core == 0, other, mine)
+                    tiles.append(jnp.concatenate([low, high]).T)
+                for k, t in enumerate(tiles):
+                    outs[2][k, at, :] = t
+            else:
+                tiles = [acts_refs[0][k, at, :] for k in range(ng)]
             for b in range(cw // BS):
                 col = where_ref[2] + first // BS + b
                 lanes = slice(b * BS, (b + 1) * BS)
@@ -100,15 +109,16 @@
                 def _():
                     send_ref[inside : inside + LANES, lanes] = total
 
-    acts_first = [nsub * tokens, 0, nsub * tokens]
     smem = pl.BlockSpec(memory_space=pltpu.SMEM)
     vmem = pl.BlockSpec(memory_space=pltpu.VMEM)
-    shape = jax.ShapeDtypeStruct((rows, cw), F32)
+    shapes = [jax.ShapeDtypeStruct((rows, cw), F32)] * 2
+    if fresh:
+        shapes.append(jax.ShapeDtypeStruct((ng, 2 * rows, tokens), BF16))
     return pl.pallas_call(
         kernel,
-        out_shape=(shape, shape),
-        in_specs=[smem, smem] + [vmem] * (2 * ng + 1),
-        out_specs=(vmem, vmem),
+        out_shape=tuple(shapes),
+        in_specs=[smem, smem] + [vmem] * (len(acts_in) + ng),
+        out_specs=(vmem,) * len(shapes),
         compiler_params=pltpu.CompilerParams(vmem_limit_bytes=VMEM_BYTES),
         cost_estimate=pl.CostEstimate(
             flops=4 * ng * rows * cw * nsub * tokens,
@@ -116,7 +126,7 @@
             transcendentals=0,
         ),
         name="weight_grad_part",
-    )(where, block_mask, acts_own, acts_swap, *acts_got, *og)
+    )(where, block_mask, *acts_in, *og)
 
 
 def forward_and_input(acts, w_mine, w_peer, og, block_mask, where):
@@ -125,6 +135,7 @@
     nz = len(w_mine)
     rows = w_mine[0].shape[0]
     per = rows // LANES
+    two = BS // LANES
 
     def kernel(where_ref, mask_ref, acts_ref, og_ref, *rest):
         w_refs, (out_ref, gx_ref, acc, hilo) = rest[: 2 * nz], rest[2 * nz :]
@@ -145,43 +156,47 @@
             hilo[b, :tokens] = hi
             hilo[b, tokens:] = (total - hi.astype(F32)).astype(BF16)
 
-        for i, w_ref in enumerate(w_refs):
-            xs = x if i < nz else 1 - x
-            owner = z ^ (i % nz)
-            for g in range(per):
-                start = (owner * 2 + xs) * rows + g * LANES
-                block = start // BS
-                at = pl.ds(pl.multiple_of(start, LANES), LANES)
-                w = w_ref[g * LANES : (g + 1) * LANES, :]
-                prod = jnp.dot(acts_ref[:, at], w, preferred_element_type=F32)
+        for k in range(nz):
+            owner = z ^ k
+            tiles = []
+            for side in range(2):
+                for g in range(per):
+                    at = slice(g * LANES, (g + 1) * LANES)
+                    tiles.append(jnp.where(x == side, w_refs[k][at, :], w_refs[nz + k][at, :]))
+            for b in range(2 * per // two):
+                block = owner * (2 * per // two) + b
+                w = jnp.concatenate(tiles[b * two : (b + 1) * two])
+                cols = pl.ds(pl.multiple_of(block * BS, BS), BS)
+                prod = jnp.dot(acts_ref[:, cols], w, preferred_element_type=F32)
                 for s in range(nsub):
                     acc[s] += mask_ref[s, block, col].astype(F32) * prod
-                two = lax.dot_general(
+                both = lax.dot_general(
                     hilo[block], w, (((1,), (1,)), ((), ())), preferred_element_type=F32
                 )
-                gx_ref[:, at] += two[:tokens] + two[tokens:]
+                gx_ref[owner, :, b * BS : (b + 1) * BS] += both[:tokens] + both[tokens:]
         out_ref[...] = acc[...].astype(BF16)
 
     smem = pl.BlockSpec(memory_space=pltpu.SMEM)
     by_col = pl.BlockSpec((nsub, tokens, BS), lambda j: (0, 0, j))
     whole = pl.BlockSpec((tokens, depth), lambda j: (0, 0))
+    by_owner = (nz, tokens, depth // nz)
     return pl.pallas_call(
         kernel,
         grid=(width // BS,),
         out_shape=(
             jax.ShapeDtypeStruct((nsub, tokens, width), BF16),
-            jax.ShapeDtypeStruct((tokens, depth), F32),
+            jax.ShapeDtypeStruct(by_owner, F32),
         ),
         in_specs=[smem, smem, whole, by_col]
         + [pl.BlockSpec((rows, BS), lambda j: (0, j))] * (2 * nz),
-        out_specs=(by_col, whole),
+        out_specs=(by_col, pl.BlockSpec(by_owner, lambda j: (0, 0, 0))),
         scratch_shapes=[
             pltpu.VMEM((nsub, tokens, BS), F32),
             pltpu.VMEM((depth // BS, 2 * tokens, BS), BF16),
         ],
         compiler_params=pltpu.CompilerParams(vmem_limit_bytes=VMEM_BYTES),
         cost_estimate=pl.CostEstimate(
-            flops=6 * tokens * depth * width, bytes_accessed=4 * depth * width, transcendentals=0
+            flops=36 * tokens * depth * width, bytes_accessed=4 * depth * width, transcendentals=0
         ),
         name="forward_and_input",
     )(where, block_mask, acts, og, *w_mine, *w_peer)
@@ -213,13 +228,8 @@
     def swap_f(a, bit):
         return lax.ppermute(a, "fsdp", [(d, d ^ bit) for d in range(fsdp)])
 
-    def gather_z(a):
-        two = swap_z(a, 2)
-        one = swap_z(a, 1)
-        return [a, one, two, swap_z(two, 1)]
-
-    w_mine = gather_z(weight)
-    w_peer = [swap_x(w) for w in w_mine]
+    def after(a, *others):
+        return lax.optimization_barrier((a, *others))[0]
 
     def acts_of(k):
         return lax.dynamic_slice_in_dim(acts, (z ^ k) * nx * rows, nx * rows, 1)
@@ -229,6 +239,9 @@
     flat = nsub * tokens
     packed = half + half // 2
     wide = 2 * BS
+
+    w_two = swap_z(weight, 2)
+    w_one = swap_z(weight, 1)
     a1, a2, a3 = [
         pack_acts(lax.dynamic_slice_in_dim(acts_of(k), c * half, half, 0), wide) for k in (1, 2, 3)
     ]
@@ -236,32 +249,45 @@
     og_b = out_grad[:, :, wide:].reshape(flat, width - wide)
     two_a = swap_z(jnp.concatenate([a2, og_a, a3]), 2)
     one_a = swap_z(jnp.concatenate([og_a, a1]), 1)
+    x_own = swap_x(weight)
+    w_three = swap_z(after(w_two, one_a, x_own), 1)
+    w_mine = [weight, w_one, w_two, w_three]
+    w_peer = [x_own] + [swap_x(w) for w in w_mine[1:]]
+
     three_a = swap_z(two_a[packed:], 1)
-    b_own, b_one, b_two, b_three = gather_z(og_b)
+    b_two = swap_z(og_b, 2)
+    b_one = swap_z(og_b, 1)
+    b_three = swap_z(b_two, 1)
     acts_swap = swap_f(
         jnp.concatenate([one_a[flat:], two_a[:packed], three_a[flat:]]), 1
     )
-    acts_own = acts_of(0)
-    acts_got = [one_a, two_a, three_a]
-    grads = []
-    for first, og, og_first in (
-        (0, [og_a, one_a, two_a, three_a], [0, 0, packed, 0]),
-        (wide, [b_own, b_one, b_two, b_three], [0, 0, 0, 0]),
-    ):
-        keep, send = weight_grad_part(
-            acts_own, acts_got, acts_swap, og, og_first, block_mask, where, rows, first
-        )
-        grads.append(keep + swap_x(send))
-    grad_w = jnp.concatenate(grads, axis=1)
-
-    outputs, gx = forward_and_input(acts, w_mine, w_peer, out_grad, block_mask, where)
-
-    by = gx.reshape(tokens, 2, 2, depth // 4)
-    half = lax.dynamic_index_in_dim(by, c, 2, keepdims=False) + swap_f(
-        lax.dynamic_index_in_dim(by, 1 - c, 2, keepdims=False), 1
-    )
-    grad_x = lax.dynamic_index_in_dim(half, y, 1, keepdims=False) + swap_f(
-        lax.dynamic_index_in_dim(half, 1 - y, 1, keepdims=False), 2
+    keep_a, send_a, acts_t = weight_grad_part(
+        [acts_of(0), acts_swap, one_a, two_a, three_a],
+        [og_a, one_a, two_a, three_a],
+        [0, 0, packed, 0],
+        block_mask,
+        where,
+        rows,
+        0,
+        [flat, 0, flat],
+    )
+    got_a = swap_x(send_a)
+
+    outputs, gx = forward_and_input(
+        acts, w_mine, w_peer, after(out_grad, keep_a, b_two, b_one), block_mask, where
+    )
+
+    keep_b, send_b = weight_grad_part(
+        [acts_t], [og_b, b_one, b_two, b_three], [0, 0, 0, 0], block_mask, where, rows, wide, None
+    )
+    grad_w = jnp.concatenate([keep_a + got_a, keep_b + swap_x(send_b)], axis=1)
+
+    by = gx.reshape(2, 2, tokens, depth // 4)
+    both = lax.dynamic_index_in_dim(by, c, 1, keepdims=False) + swap_f(
+        lax.dynamic_index_in_dim(by, 1 - c, 1, keepdims=False), 1
+    )
+    grad_x = lax.dynamic_index_in_dim(both, y, 0, keepdims=False) + swap_f(
+        lax.dynamic_index_in_dim(both, 1 - y, 0, keepdims=False), 2
     )
     return (outputs, grad_w, grad_x.astype(BF16))
 

time: 156 us -> 169 us (1.083)
  waiting for transfers between devices: 84.4 us -> 103 us
  Pallas kernels: 22 us -> 18.6 us
  local copies, waits for them, and re-layouts: 21.4 us -> 18.2 us
    ppermute x15, waiting for transfers between devices: 84.4 us -> 103 us  [swap_dp(): return lax.ppermute(a, 'dp', [(d, d ^ bits) for d in range(dp)])]
    unnamed x22 -> x41, local copies, waits for them, and re-layouts: 7.45 us -> 12.2 us
    dynamic_slice x1 -> x0, local copies, waits for them, and re-layouts: 4.38 us -> none  [on_device(): lax.dynamic_index_in_dim(by, c, 2, keepdims=False)]
    reshape x1 -> x0, local copies, waits for them, and re-layouts: 2.52 us -> none  [on_device(): by = gx.reshape(tokens, 2, 2, depth // 4)]
    pallas_call x1, Pallas kernels: 9.75 us -> 7.85 us  [forward_and_input(): pl.pallas_call(kernel, grid=(width // BS,), out_shape=(jax.ShapeDtypeStru...]
  transfers between devices with their start and end apart: 18 -> 18, of which waited for: 6 -> 7; matrix products, arithmetic and copies ran while one was open for 13% -> 3% of each run, Pallas kernels for 14% -> 6%
where the time goes in v5:
time: 169 us; the launch traced here: 168 us
  waiting for transfers between devices  103 us (61%)
  starting transfers between devices  21.7 us (13%)
  Pallas kernels  18.6 us (11%)
  local copies, waits for them, and re-layouts  18.2 us (11%)
  other arithmetic  5.74 us (3%)
    ppermute x15, waiting for transfers between devices, swap_dp(): return lax.ppermute(a, 'dp', [(d, d ^ bits) for d in range(dp)])  103 us
    ppermute x15, starting transfers between devices, swap_dp(): return lax.ppermute(a, 'dp', [(d, d ^ bits) for d in range(dp)])  20 us
    unnamed x41, local copies, waits for them, and re-layouts  12.2 us
    pallas_call x2, Pallas kernels, weight_grad_part(): pl.pallas_call(kernel, out_shape=tuple(shapes), in_specs=[smem, smem] + [...  10.8 us
    pallas_call x1, Pallas kernels, forward_and_input(): pl.pallas_call(kernel, grid=(width // BS,), out_shape=(jax.ShapeDtypeStru...  7.85 us
  transfers between devices with their start and end apart: 18, of which 7 were waited for; matrix products, arithmetic and copies ran while one was open for 3% of the time, Pallas kernels for 6%

profile of v5, /device:TPU:0, one launch (start us, length us, event | category | flops | bytes accessed | tf_op | source)
XLA Modules:
  0.0 168.2 jit_solution(550674425528619741)
XLA Ops:
  0.7 1.6 dynamic-slice_dynamic-update-slice_fusion.1
  2.3 0.9 fusion.2
  3.3 0.1 fusion.5
  3.3 1.1 slice.72
  4.5 0.6 maximum_dynamic-update-slice_fusion.1
  5.1 0.8 constant_dynamic-update-slice_fusion
  5.9 1.7 %fusion.1 = (bf16[64,512]{1,0:T(8,128)(2,1)S(1)}, bf16[704,512]{1,0:T(8,128)(2,1)}) fusion(bf16[128,3072]{1,0:T(8,128)(2,1)} %acts_ref.1, s32[]{:T(128)S(6)} %select_n.62, s32[]{:T(128)S(6)} %select_n.64, bf16[704,512]{1,0:T(8,128)(2,1)} %constant_dynamic-update-slice_fusion, s32[]{:T(128)S(6)} %select_n.68), kind=kLoop, calls=%fused_computation.27 | loop fusion | bytes 262156 | tf_op jit(solution)/shard_map/slice | solution.py:43
  7.7 0.1 fusion.4
  7.7 0.6 maximum_dynamic-update-slice_fusion
  8.4 4.1 %collective-permute-start.1 = (bf16[704,512]{1,0:T(8,128)(2,1)}, bf16[704,512]{1,0:T(8,128)(2,1)S(1)}, u32[]{:S(2)}, u32[]{:S(2)}) collective-permute-start(bf16[704,512]{1,0:T(8,128)(2,1)} %maximum_dynamic-update-slice_fusion), channel_id=1, source_target_pairs={{0,16},{4,20},{8,24},{12,28},{16,0},{20,4},{24,8},{28,12},{1,17},{... | collective-permute-start | bytes 2162696 | tf_op jit(solution)/shard_map/ppermute | solution.py:220
  12.4 0.1 fusion.3
  12.6 0.0 copy-start
  12.6 0.0 copy-start.18
  12.6 1.6 collective-permute-start
  14.3 0.3 collective-permute-start.7
  14.6 1.5 collective-permute-start.8
  16.1 41.6 %collective-permute-done.1.refs_3_.refs_7_ = bf16[704,512]{1,0:T(8,128)(2,1)S(1)} collective-permute-done((bf16[704,512]{1,0:T(8,128)(2,1)}, bf16[704,512]{1,0:T(8,128)(2,1)S(1)}, u32[]{:S(2)}, u32[]{:S(2)}) %collective-permute-start.1) | collective-permute-done | bytes 720928 | tf_op jit(solution)/shard_map/ppermute | solution.py:220
  57.7 0.1 collective-permute-start.2
  57.9 2.0 %collective-permute-start.6 = (bf16[384,768]{1,0:T(8,128)(2,1)S(1)}, bf16[384,768]{1,0:T(8,128)(2,1)}, u32[]{:S(2)}, u32[]{:S(2)}) collective-permute-start(bf16[384,768]{1,0:T(8,128)(2,1)S(1)} %copy-done.6), channel_id=1, source_target_pairs={{0,8},{4,12},{8,0},{12,4},{16,24},{20,28},{24,16},{28,20},{1,9},{5... | collective-permute-start | bytes 1769480 | tf_op jit(solution)/shard_map/ppermute | solution.py:220
  59.8 9.8 %collective-permute-done.7.rest_2_ = bf16[384,768]{1,0:T(8,128)(2,1)} collective-permute-done((bf16[384,768]{1,0:T(8,128)(2,1)S(1)}, bf16[384,768]{1,0:T(8,128)(2,1)}, u32[]{:S(2)}, u32[]{:S(2)}) %collective-permute-start.7) | collective-permute-done | bytes 589856 | tf_op jit(solution)/shard_map/ppermute | solution.py:220
  69.7 0.0 collective-permute-done.8.rest_4_
  69.7 0.8 copy-done.8
  70.5 0.0 collective-permute-done.refs_2_.refs_6_
  70.5 0.6 collective-permute-start.9
  71.1 1.5 collective-permute-start.11
  72.6 23.1 %collective-permute-done.6.rest_1_ = bf16[384,768]{1,0:T(8,128)(2,1)} collective-permute-done((bf16[384,768]{1,0:T(8,128)(2,1)S(1)}, bf16[384,768]{1,0:T(8,128)(2,1)}, u32[]{:S(2)}, u32[]{:S(2)}) %collective-permute-start.6) | collective-permute-done | bytes 589856 | tf_op jit(solution)/shard_map/ppermute | solution.py:220
  95.7 1.5 collective-permute-start.10
  97.2 11.0 %collective-permute-done.9.rest_3_ = bf16[384,768]{1,0:T(8,128)(2,1)} collective-permute-done((bf16[384,768]{1,0:T(8,128)(2,1)}, bf16[384,768]{1,0:T(8,128)(2,1)}, u32[]{:S(2)}, u32[]{:S(2)}) %collective-permute-start.9) | collective-permute-done | bytes 589856 | tf_op jit(solution)/shard_map/ppermute | solution.py:220
  108.2 1.5 collective-permute-start.12
  109.7 0.0 copy-start.4
  109.8 0.8 copy-done.4
  110.6 0.1 collective-permute-start.3
  110.7 1.7 collective-permute-start.4
  112.4 0.9 constant_dynamic-slice_fusion.refs_0_
  113.3 2.5 %collective-permute-start.5 = (bf16[512,256]{1,0:T(8,128)(2,1)S(1)}, bf16[512,256]{1,0:T(8,128)(2,1)S(1)}, u32[]{:S(2)}, u32[]{:S(2)}) collective-permute-start(bf16[512,256]{1,0:T(8,128)(2,1)S(1)} %bitcast.47), channel_id=1, source_target_pairs={{0,8},{4,12},{8,0},{12,4},{16,24},{20,28},{24,16},{28,20},{1,9},{5... | collective-permute-start | bytes 786440 | tf_op jit(solution)/shard_map/ppermute | solution.py:220
  115.9 0.1 pad_add_fusion.where_ref
  116.0 1.1 copy-done.3
  117.0 1.1 copy-done.5
  118.1 7.2 %weight_grad_part.2 = (f32[384,512]{1,0:T(8,128)S(1)}, f32[384,512]{1,0:T(8,128)}, bf16[4,768,128]{2,1,0:T(8,128)(2,1)S(1)}) custom-call(s32[4]{0:T(128)S(1)} %pad_add_fusion.where_ref, s32[4,12,12]{2,1,0:T(8,128)S(1)} %copy.23.mask_ref, bf16[128,768]{1,0:T(8,128)(2,1)S(1)} %constant_dynamic-slice_fusion.refs_0_, ...), custom_call_target="tpu_custom_call" | custom-call | flops 1610612736 | bytes 1572864 | tf_op jit(solution)/shard_map/weight_grad_part/pallas_call | solution.py:117
  125.3 0.9 copy-done.14
  126.2 0.0 collective-permute-done.4.refs_3_
  126.2 1.0 collective-permute-done.5.refs_2_
  127.2 0.0 collective-permute-done.11.rest_6_
  127.2 0.0 collective-permute-done.10.rest_5_
  127.3 7.8 %forward_and_input.1 = (bf16[4,128,768]{2,1,0:T(8,128)(2,1)}, f32[4,128,768]{2,1,0:T(8,128)S(1)}) custom-call(s32[4]{0:T(128)S(1)} %pad_add_fusion.where_ref, s32[4,12,12]{2,1,0:T(8,128)S(1)} %copy.23.mask_ref, bf16[128,3072]{1,0:T(8,128)(2,1)S(1)} %copy-done.1, bf16[4,128,768]{2,1,0:T(8,128)(2,1)S(1)} %copy-done, bf16[384,768]{1,0:T(8,128)(2,1)S(1)} %copy-done.7, ...), custom_call_target="tpu_custom_call" | custom-call | flops 10871635968 | bytes 9437184 | tf_op jit(solution)/shard_map/forward_and_input/pallas_call | solution.py:183
  135.1 1.0 dynamic-slice_bitcast_fusion
  136.1 0.5 collective-permute-start.13
  136.6 8.4 %collective-permute-done.14.refs_4_ = bf16[512,256]{1,0:T(8,128)(2,1)S(1)} collective-permute-done((bf16[512,256]{1,0:T(8,128)(2,1)}, bf16[512,256]{1,0:T(8,128)(2,1)S(1)}, u32[]{:S(2)}, u32[]{:S(2)}) %collective-permute-start.14) | collective-permute-done | bytes 262176 | tf_op jit(solution)/shard_map/ppermute | solution.py:220
  145.0 0.7 copy-done.12
  145.7 0.9 copy-done.11
  146.7 0.9 copy-done.13
  147.6 1.1 copy-done.15
  148.7 3.6 %weight_grad_part.3 = (f32[384,256]{1,0:T(8,128)S(1)}, f32[384,256]{1,0:T(8,128)S(1)}) custom-call(s32[4]{0:T(128)S(1)} %pad_add_fusion.where_ref, s32[4,12,12]{2,1,0:T(8,128)S(1)} %copy.23.mask_ref, bf16[4,768,128]{2,1,0:T(8,128)(2,1)S(1)} %copy-done.15, bf16[512,256]{1,0:T(8,128)(2,1)S(1)} %bitcast.48, bf16[512,256]{1,0:T(8,128)(2,1)S(1)} %copy-done.11, ...), custom_call_target="tpu_custom_call" | custom-call | flops 805306368 | bytes 786432 | tf_op jit(solution)/shard_map/weight_grad_part/pallas_call | solution.py:117
  152.4 0.6 collective-permute-start.15
  152.9 0.0 collective-permute-done.16
  152.9 1.2 bitcast_add_fusion
  154.2 0.9 copy-done.16
  155.1 1.6 collective-permute-start.17
  156.7 8.0 %collective-permute-done.15 = f32[384,256]{1,0:T(8,128)S(1)} collective-permute-done((f32[384,256]{1,0:T(8,128)S(1)}, f32[384,256]{1,0:T(8,128)S(1)}, u32[]{:S(2)}, u32[]{:S(2)}) %collective-permute-start.15) | collective-permute-done | bytes 393248 | tf_op jit(solution)/shard_map/ppermute | solution.py:220
  164.7 0.1 add.68
  164.7 1.3 add.67
  166.0 1.1 pad_maximum_fusion
  167.1 0.4 copy-done.17
  167.5 0.7 fusion
  (49 shorter events, 0.3 us)
Async XLA Ops:
  5.9 8.3 %copy-start.6 = (bf16[384,768]{1,0:T(8,128)(2,1)S(1)}, bf16[384,768]{1,0:T(8,128)(2,1)}, u32[]{:S(2)}) copy-start(bf16[384,768]{1,0:T(8,128)(2,1)} %rest_0_.1) | copy-start | bytes 1769476
  8.4 49.3 %collective-permute-start.1 = (bf16[704,512]{1,0:T(8,128)(2,1)}, bf16[704,512]{1,0:T(8,128)(2,1)S(1)}, u32[]{:S(2)}, u32[]{:S(2)}) collective-permute-start(bf16[704,512]{1,0:T(8,128)(2,1)} %maximum_dynamic-update-slice_fusion), channel_id=1, source_target_pairs={{0,16},{4,20},{8,24},{12,28},{16,0},{20,4},{24,8},{28,12},{1,17},{... | collective-permute-start | bytes 2162696 | tf_op jit(solution)/shard_map/ppermute | solution.py:220
  12.6 98.1 %copy-start = (bf16[4,128,768]{2,1,0:T(8,128)(2,1)S(1)}, bf16[4,128,768]{2,1,0:T(8,128)(2,1)}, u32[]{:S(2)}) copy-start(bf16[4,128,768]{2,1,0:T(8,128)(2,1)} %og_ref) | copy-start | bytes 2359300
  12.6 99.8 %copy-start.18 = (s32[4,12,12]{2,0,1:T(4,128)S(1)}, s32[4,12,12]{2,0,1:T(4,128)}, u32[]{:S(2)}) copy-start(s32[4,12,12]{2,0,1:T(4,128)} %param.6) | copy-start | bytes 6916
  12.6 57.9 %collective-permute-start = (bf16[608,512]{1,0:T(8,128)(2,1)S(1)}, bf16[608,512]{1,0:T(8,128)(2,1)S(1)}, u32[]{:S(2)}, u32[]{:S(2)}) collective-permute-start(bf16[608,512]{1,0:T(8,128)(2,1)S(1)} %maximum_maximum_fusion), channel_id=1, source_target_pairs={{0,8},{4,12},{8,0},{12,4},{16,24},{20,28},{24,16},{28,20},{1,9},{5... | collective-permute-start | bytes 1867784 | tf_op jit(solution)/shard_map/ppermute | solution.py:220
  14.3 55.4 %collective-permute-start.7 = (bf16[384,768]{1,0:T(8,128)(2,1)S(1)}, bf16[384,768]{1,0:T(8,128)(2,1)}, u32[]{:S(2)}, u32[]{:S(2)}) collective-permute-start(bf16[384,768]{1,0:T(8,128)(2,1)S(1)} %copy-done.6), channel_id=1, source_target_pairs={{0,16},{4,20},{8,24},{12,28},{16,0},{20,4},{24,8},{28,12},{1,17},{... | collective-permute-start | bytes 1769480 | tf_op jit(solution)/shard_map/ppermute | solution.py:220
  14.6 55.1 %collective-permute-start.8 = (bf16[384,768]{1,0:T(8,128)(2,1)S(1)}, bf16[384,768]{1,0:T(8,128)(2,1)S(1)}, u32[]{:S(2)}, u32[]{:S(2)}) collective-permute-start(bf16[384,768]{1,0:T(8,128)(2,1)S(1)} %copy-done.6), channel_id=1, source_target_pairs={{0,4},{4,0},{8,12},{12,8},{16,20},{20,16},{24,28},{28,24},{1,5},{5... | collective-permute-start | bytes 1769480 | tf_op jit(solution)/shard_map/ppermute | solution.py:220
  57.7 52.0 %collective-permute-start.2 = (bf16[608,512]{1,0:T(8,128)(2,1)S(1)}, bf16[608,512]{1,0:T(8,128)(2,1)S(1)}, u32[]{:S(2)}, u32[]{:S(2)}) collective-permute-start(bf16[608,512]{1,0:T(8,128)(2,1)S(1)} %slice.110), channel_id=1, source_target_pairs={{0,8},{4,12},{8,0},{12,4},{16,24},{20,28},{24,16},{28,20},{1,9},{5... | collective-permute-start | bytes 1867784 | tf_op jit(solution)/shard_map/ppermute | solution.py:220
  57.9 37.8 %collective-permute-start.6 = (bf16[384,768]{1,0:T(8,128)(2,1)S(1)}, bf16[384,768]{1,0:T(8,128)(2,1)}, u32[]{:S(2)}, u32[]{:S(2)}) collective-permute-start(bf16[384,768]{1,0:T(8,128)(2,1)S(1)} %copy-done.6), channel_id=1, source_target_pairs={{0,8},{4,12},{8,0},{12,4},{16,24},{20,28},{24,16},{28,20},{1,9},{5... | collective-permute-start | bytes 1769480 | tf_op jit(solution)/shard_map/ppermute | solution.py:220
  69.7 0.8 copy-start.8
  70.5 40.2 %copy-start.2 = (bf16[608,512]{1,0:T(8,128)(2,1)}, bf16[608,512]{1,0:T(8,128)(2,1)S(1)}, u32[]{:S(2)}) copy-start(bf16[608,512]{1,0:T(8,128)(2,1)S(1)} %collective-permute-done.refs_2_.refs_6_) | copy-start | bytes 1867780
  70.5 37.7 %collective-permute-start.9 = (bf16[384,768]{1,0:T(8,128)(2,1)}, bf16[384,768]{1,0:T(8,128)(2,1)}, u32[]{:S(2)}, u32[]{:S(2)}) collective-permute-start(bf16[384,768]{1,0:T(8,128)(2,1)} %collective-permute-done.7.rest_2_), channel_id=1, source_target_pairs={{0,8},{4,12},{8,0},{12,4},{16,24},{20,28},{24,16},{28,20},{1,9},{5... | collective-permute-start | bytes 1769480 | tf_op jit(solution)/shard_map/ppermute | solution.py:220
  71.1 56.1 %collective-permute-start.11 = (bf16[384,768]{1,0:T(8,128)(2,1)}, bf16[384,768]{1,0:T(8,128)(2,1)}, u32[]{:S(2)}, u32[]{:S(2)}) collective-permute-start(bf16[384,768]{1,0:T(8,128)(2,1)} %collective-permute-done.7.rest_2_), channel_id=1, source_target_pairs={{0,4},{4,0},{8,12},{12,8},{16,20},{20,16},{24,28},{28,24},{1,5},{5... | collective-permute-start | bytes 1769480 | tf_op jit(solution)/shard_map/ppermute | solution.py:220
  95.7 31.6 %collective-permute-start.10 = (bf16[384,768]{1,0:T(8,128)(2,1)}, bf16[384,768]{1,0:T(8,128)(2,1)}, u32[]{:S(2)}, u32[]{:S(2)}) collective-permute-start(bf16[384,768]{1,0:T(8,128)(2,1)} %collective-permute-done.6.rest_1_), channel_id=1, source_target_pairs={{0,4},{4,0},{8,12},{12,8},{16,20},{20,16},{24,28},{28,24},{1,5},{5... | collective-permute-start | bytes 1769480 | tf_op jit(solution)/shard_map/ppermute | solution.py:220
  108.2 19.0 %collective-permute-start.12 = (bf16[384,768]{1,0:T(8,128)(2,1)}, bf16[384,768]{1,0:T(8,128)(2,1)}, u32[]{:S(2)}, u32[]{:S(2)}) collective-permute-start(bf16[384,768]{1,0:T(8,128)(2,1)} %collective-permute-done.9.rest_3_), channel_id=1, source_target_pairs={{0,4},{4,0},{8,12},{12,8},{16,20},{20,16},{24,28},{28,24},{1,5},{5... | collective-permute-start | bytes 1769480 | tf_op jit(solution)/shard_map/ppermute | solution.py:220
  109.7 0.8 copy-start.4
  110.6 2.7 %collective-permute-start.3 = (bf16[288,512]{1,0:T(8,128)(2,1)S(1)}, bf16[288,512]{1,0:T(8,128)(2,1)S(1)}, u32[]{:S(2)}, u32[]{:S(2)}) collective-permute-start(bf16[288,512]{1,0:T(8,128)(2,1)S(1)} %pad_maximum_fusion.1), channel_id=1, source_target_pairs={{0,1},{1,0},{2,3},{3,2},{4,5},{5,4},{6,7},{7,6},{8,9},{9,8},{10,11... | collective-permute-start | bytes 884744 | tf_op jit(solution)/shard_map/ppermute | solution.py:229
  110.7 15.5 %collective-permute-start.4 = (bf16[512,256]{1,0:T(8,128)(2,1)S(1)}, bf16[512,256]{1,0:T(8,128)(2,1)}, u32[]{:S(2)}, u32[]{:S(2)}) collective-permute-start(bf16[512,256]{1,0:T(8,128)(2,1)S(1)} %bitcast.46), channel_id=1, source_target_pairs={{0,16},{4,20},{8,24},{12,28},{16,0},{20,4},{24,8},{28,12},{1,17},{... | collective-permute-start | bytes 786440 | tf_op jit(solution)/shard_map/ppermute | solution.py:220
  113.3 13.9 %collective-permute-start.5 = (bf16[512,256]{1,0:T(8,128)(2,1)S(1)}, bf16[512,256]{1,0:T(8,128)(2,1)S(1)}, u32[]{:S(2)}, u32[]{:S(2)}) collective-permute-start(bf16[512,256]{1,0:T(8,128)(2,1)S(1)} %bitcast.47), channel_id=1, source_target_pairs={{0,8},{4,12},{8,0},{12,4},{16,24},{20,28},{24,16},{28,20},{1,9},{5... | collective-permute-start | bytes 786440 | tf_op jit(solution)/shard_map/ppermute | solution.py:220
  116.0 1.1 copy-start.3
  117.0 1.1 copy-start.5
  118.1 9.1 %copy-start.1 = (bf16[128,3072]{1,0:T(8,128)(2,1)S(1)}, bf16[128,3072]{1,0:T(8,128)(2,1)}, u32[]{:S(2)}) copy-start(bf16[128,3072]{1,0:T(8,128)(2,1)} %acts_ref.1) | copy-start | bytes 2359300
  118.1 9.1 %copy-start.7 = (bf16[384,768]{1,0:T(8,128)(2,1)S(1)}, bf16[384,768]{1,0:T(8,128)(2,1)}, u32[]{:S(2)}) copy-start(bf16[384,768]{1,0:T(8,128)(2,1)} %rest_0_.1) | copy-start | bytes 1769476
  118.1 9.1 %copy-start.9 = (bf16[384,768]{1,0:T(8,128)(2,1)S(1)}, bf16[384,768]{1,0:T(8,128)(2,1)}, u32[]{:S(2)}) copy-start(bf16[384,768]{1,0:T(8,128)(2,1)} %copy-done.8) | copy-start | bytes 1769476
  125.3 0.9 copy-start.14
  127.2 7.9 %copy-start.10 = (bf16[512,256]{1,0:T(8,128)(2,1)}, bf16[512,256]{1,0:T(8,128)(2,1)S(1)}, u32[]{:S(2)}) copy-start(bf16[512,256]{1,0:T(8,128)(2,1)S(1)} %collective-permute-done.5.refs_2_) | copy-start | bytes 786436
  136.1 16.9 %collective-permute-start.16 = (f32[2,128,768]{2,1,0:T(8,128)}, f32[2,128,768]{2,1,0:T(8,128)}, u32[]{:S(2)}, u32[]{:S(2)}) collective-permute-start(f32[2,128,768]{2,1,0:T(8,128)} %dynamic-slice_bitcast_fusion), channel_id=1, source_target_pairs={{0,1},{1,0},{2,3},{3,2},{4,5},{5,4},{6,7},{7,6},{8,9},{9,8},{10,11... | collective-permute-start | bytes 2359304 | tf_op jit(solution)/shard_map/ppermute | solution.py:229
  136.1 8.9 %collective-permute-start.14 = (bf16[512,256]{1,0:T(8,128)(2,1)}, bf16[512,256]{1,0:T(8,128)(2,1)S(1)}, u32[]{:S(2)}, u32[]{:S(2)}) collective-permute-start(bf16[512,256]{1,0:T(8,128)(2,1)} %collective-permute-done.4.refs_3_), channel_id=1, source_target_pairs={{0,8},{4,12},{8,0},{12,4},{16,24},{20,28},{24,16},{28,20},{1,9},{5... | collective-permute-start | bytes 786440 | tf_op jit(solution)/shard_map/ppermute | solution.py:220
  136.1 28.6 %collective-permute-start.13 = (f32[384,512]{1,0:T(8,128)}, f32[384,512]{1,0:T(8,128)}, u32[]{:S(2)}, u32[]{:S(2)}) collective-permute-start(f32[384,512]{1,0:T(8,128)} %get-tuple-element.16), channel_id=1, source_target_pairs={{0,4},{4,0},{8,12},{12,8},{16,20},{20,16},{24,28},{28,24},{1,5},{5... | collective-permute-start | bytes 2359304 | tf_op jit(solution)/shard_map/ppermute | solution.py:220
  145.0 0.7 copy-start.12
  145.7 0.9 copy-start.11
  146.7 0.9 copy-start.13
  147.6 1.1 copy-start.15
  152.4 12.3 %collective-permute-start.15 = (f32[384,256]{1,0:T(8,128)S(1)}, f32[384,256]{1,0:T(8,128)S(1)}, u32[]{:S(2)}, u32[]{:S(2)}) collective-permute-start(f32[384,256]{1,0:T(8,128)S(1)} %get-tuple-element.19), channel_id=1, source_target_pairs={{0,4},{4,0},{8,12},{12,8},{16,20},{20,16},{24,28},{28,24},{1,5},{5... | collective-permute-start | bytes 1179656 | tf_op jit(solution)/shard_map/ppermute | solution.py:220
  154.1 0.9 copy-start.16
  155.1 12.0 %collective-permute-start.17 = (f32[128,768]{1,0:T(8,128)S(1)}, f32[128,768]{1,0:T(8,128)S(1)}, u32[]{:S(2)}, u32[]{:S(2)}) collective-permute-start(f32[128,768]{1,0:T(8,128)S(1)} %dynamic-slice_bitcast_fusion.1), channel_id=1, source_target_pairs={{0,2},{1,3},{2,0},{3,1},{4,6},{5,7},{6,4},{7,5},{8,10},{9,11},{10,... | collective-permute-start | bytes 1179656 | tf_op jit(solution)/shard_map/ppermute | solution.py:229
  166.0 1.5 copy-start.17

commit v6 on v3

v6 whole, which is shorter than its diff:
```python
import jax
import jax.numpy as jnp
from jax import lax
from jax.experimental import pallas as pl
from jax.experimental.pallas import tpu as pltpu
from jax.sharding import PartitionSpec as P

BS = 256
TOK_G = 128
LANES = 128
F32 = jnp.float32
BF16 = jnp.bfloat16
VMEM_BYTES = 40 * 1024 * 1024


def plain(acts, weight, block_mask, out_grad):
    width = weight.shape[1]
    kblocks = block_mask.shape[1]
    oblocks = block_mask.shape[2]
    first_col = lax.axis_index("fsdp") * width
    col_ids = (first_col + jnp.arange(width, dtype=jnp.int32)) // BS
    col_select = (col_ids[None, :] == jnp.arange(oblocks, dtype=jnp.int32)[:, None]).astype(F32)
    col_mask = jnp.einsum("skb,bc->skc", block_mask.astype(F32), col_select)
    full = lax.all_gather(weight, "dp", axis=0, tiled=True)
    row_ids = jnp.arange(full.shape[0], dtype=jnp.int32) // BS
    row_select = (row_ids[:, None] == jnp.arange(kblocks, dtype=jnp.int32)[None, :]).astype(F32)
    mask = jnp.einsum("nk,skc->snc", row_select, col_mask)
    masked = mask.astype(BF16) * full[None]
    forward = jnp.einsum("tn,snc->stc", acts, masked, preferred_element_type=F32)
    input_part = jnp.einsum("stc,snc->tn", out_grad, masked, preferred_element_type=F32)
    products = jnp.einsum("tn,stc->snc", acts, out_grad, preferred_element_type=F32)
    grad_w = lax.psum_scatter(
        jnp.sum(mask * products, axis=0) * (1.0 / TOK_G), "dp", scatter_dimension=0, tiled=True
    )
    grad_x = lax.psum_scatter(input_part, "fsdp", scatter_dimension=1, tiled=True).astype(BF16)
    return (forward.astype(BF16), grad_w, grad_x)


def weight_grad_part(acts_in, og, block_mask, where, rows, chunk):
    nsub = block_mask.shape[0]
    fresh = acts_in.ndim == 2
    tokens = acts_in.shape[0] if fresh else acts_in.shape[2]
    flat = nsub * tokens
    ng = len(og)
    per = rows // LANES

    def kernel(where_ref, mask_ref, acts_ref, *refs):
        og_refs, outs = refs[:ng], refs[ng:]
        z, x = where_ref[0], where_ref[1]
        for r in range(2):
            zz = z ^ (2 * r)
            for g in range(per):
                start = (zz * 2 + x) * rows + g * LANES
                block = start // BS
                at = slice(g * LANES, (g + 1) * LANES)
                dst = slice((r * per + g) * LANES, (r * per + g + 1) * LANES)
                if fresh:
                    here = pl.ds(pl.multiple_of(start, LANES), LANES)
                    there = pl.ds(pl.multiple_of(x * rows + g * LANES, LANES), LANES)
                    own_ref, one_ref, side_ref, both_ref = og_refs
                    tiles = [
                        acts_ref[:, here].T,
                        one_ref[flat + r * tokens : flat + (r + 1) * tokens, there].T,
                        side_ref[flat : flat + tokens, dst].T,
                        both_ref[flat : flat + tokens, dst].T,
                    ]
                    for k, t in enumerate(tiles):
                        outs[2][k, dst, :] = t
                else:
                    tiles = [acts_ref[k, dst, :] for k in range(ng)]
                col = where_ref[2] + chunk
                keep = [mask_ref[s, block, col].astype(F32) for s in range(nsub)]
                keep = [jnp.full((LANES, tokens), k).astype(BF16) for k in keep]
                total = None
                for t, o_ref in zip(tiles, og_refs):
                    lhs = jnp.concatenate([t * k for k in keep], axis=1)
                    rhs = o_ref[:flat, chunk * BS : (chunk + 1) * BS]
                    term = jnp.dot(lhs, rhs, preferred_element_type=F32)
                    total = term if total is None else total + term
                outs[r][at, :] = total * (1.0 / TOK_G)

    smem = pl.BlockSpec(memory_space=pltpu.SMEM)
    vmem = pl.BlockSpec(memory_space=pltpu.VMEM)
    shapes = [jax.ShapeDtypeStruct((rows, BS), F32)] * 2
    if fresh:
        shapes.append(jax.ShapeDtypeStruct((ng, 2 * rows, tokens), BF16))
    return pl.pallas_call(
        kernel,
        out_shape=tuple(shapes),
        in_specs=[smem, smem] + [vmem] * (1 + ng),
        out_specs=(vmem,) * len(shapes),
        compiler_params=pltpu.CompilerParams(vmem_limit_bytes=VMEM_BYTES),
        cost_estimate=pl.CostEstimate(
            flops=4 * ng * rows * BS * flat, bytes_accessed=8 * rows * BS, transcendentals=0
        ),
        name="weight_grad_part",
    )(where, block_mask, acts_in, *og)


def forward_and_input(acts, w_mine, w_peer, og, block_mask, where):
    nsub, tokens, width = og.shape
    depth = acts.shape[1]
    nz = len(w_mine)
    rows = w_mine[0].shape[0]
    per = rows // LANES
    two = BS // LANES

    def kernel(where_ref, mask_ref, acts_ref, og_ref, *rest):
        w_refs, (out_ref, gx_ref, acc, hilo) = rest[: 2 * nz], rest[2 * nz :]
        z, x = where_ref[0], where_ref[1]
        step = pl.program_id(0)
        col = where_ref[2] + step

        @pl.when(step == 0)
        def _():
            gx_ref[...] = jnp.zeros_like(gx_ref)

        acc[...] = jnp.zeros_like(acc)
        for b in range(depth // BS):
            total = jnp.zeros((tokens, BS), F32)
            for s in range(nsub):
                total = total + mask_ref[s, b, col].astype(F32) * og_ref[s].astype(F32)
            hi = total.astype(BF16)
            hilo[b, :tokens] = hi
            hilo[b, tokens:] = (total - hi.astype(F32)).astype(BF16)

        for k in range(nz):
            owner = z ^ k
            tiles = []
            for side in range(2):
                for g in range(per):
                    at = slice(g * LANES, (g + 1) * LANES)
                    tiles.append(jnp.where(x == side, w_refs[k][at, :], w_refs[nz + k][at, :]))
            for b in range(2 * per // two):
                block = owner * (2 * per // two) + b
                w = jnp.concatenate(tiles[b * two : (b + 1) * two])
                cols = pl.ds(pl.multiple_of(block * BS, BS), BS)
                prod = jnp.dot(acts_ref[:, cols], w, preferred_element_type=F32)
                for s in range(nsub):
                    acc[s] += mask_ref[s, block, col].astype(F32) * prod
                both = lax.dot_general(
                    hilo[block], w, (((1,), (1,)), ((), ())), preferred_element_type=F32
                )
                gx_ref[owner, :, b * BS : (b + 1) * BS] += both[:tokens] + both[tokens:]
        out_ref[...] = acc[...].astype(BF16)

    smem = pl.BlockSpec(memory_space=pltpu.SMEM)
    by_col = pl.BlockSpec((nsub, tokens, BS), lambda j: (0, 0, j))
    whole = pl.BlockSpec((tokens, depth), lambda j: (0, 0))
    by_owner = (nz, tokens, depth // nz)
    return pl.pallas_call(
        kernel,
        grid=(width // BS,),
        out_shape=(
            jax.ShapeDtypeStruct((nsub, tokens, width), BF16),
            jax.ShapeDtypeStruct(by_owner, F32),
        ),
        in_specs=[smem, smem, whole, by_col]
        + [pl.BlockSpec((rows, BS), lambda j: (0, j))] * (2 * nz),
        out_specs=(by_col, pl.BlockSpec(by_owner, lambda j: (0, 0, 0))),
        scratch_shapes=[
            pltpu.VMEM((nsub, tokens, BS), F32),
            pltpu.VMEM((depth // BS, 2 * tokens, BS), BF16),
        ],
        compiler_params=pltpu.CompilerParams(vmem_limit_bytes=VMEM_BYTES),
        cost_estimate=pl.CostEstimate(
            flops=36 * tokens * depth * width, bytes_accessed=4 * depth * width, transcendentals=0
        ),
        name="forward_and_input",
    )(where, block_mask, acts, og, *w_mine, *w_peer)


def on_device(acts, weight, block_mask, out_grad):
    rows, width = weight.shape
    tokens, depth = acts.shape
    dp = lax.axis_size("dp")
    fsdp = lax.axis_size("fsdp")
    if rows != 3 * LANES or width != 3 * BS or dp != 8 or fsdp != 4 or tokens != LANES:
        return plain(acts, weight, block_mask, out_grad)
    nx = 2
    me = lax.axis_index("dp")
    z, x = me // nx, me % nx
    f = lax.axis_index("fsdp")
    y, c = f // 2, f % 2
    where = jnp.stack([z, x, f * (width // BS), c]).astype(jnp.int32)

    def swap_dp(a, bits):
        return lax.ppermute(a, "dp", [(d, d ^ bits) for d in range(dp)])

    def swap_x(a):
        return swap_dp(a, 1)

    def swap_z(a, k):
        return swap_dp(a, k * nx)

    def swap_f(a, bit):
        return lax.ppermute(a, "fsdp", [(d, d ^ bit) for d in range(fsdp)])

    def after(a, *others):
        return lax.optimization_barrier((a, *others))[0]

    nsub = out_grad.shape[0]
    flat = nsub * tokens
    own = out_grad.reshape(flat, width)
    by_z = acts.reshape(tokens, dp // nx, nx * rows)

    def acts_of(k):
        return lax.dynamic_index_in_dim(by_z, z ^ k, 1, keepdims=False)

    def of_x(a, side):
        return lax.dynamic_slice_in_dim(a, side * rows, rows, 1)

    one = swap_z(jnp.concatenate([own, acts_of(1), acts_of(3)]), 1)
    side = swap_x(
        jnp.concatenate(
            [own, jnp.concatenate([of_x(acts_of(0), 1 - x), of_x(acts_of(2), 1 - x)], axis=1)]
        )
    )
    one = after(one, side)
    passed = [
        of_x(one[flat + r * tokens : flat + (r + 1) * tokens], 1 - x) for r in range(2)
    ]
    both = swap_x(jnp.concatenate([one[:flat], jnp.concatenate(passed, axis=1)]))

    w_two = swap_z(weight, 2)
    w_one = swap_z(weight, 1)
    w_three = swap_z(w_two, 1)
    w_mine = [weight, w_one, w_two, w_three]
    w_peer = [swap_x(after(weight, both))]

    og = [own, one, side, both]
    acts_in = acts
    grads = []
    for j in range(width // BS):
        ready = ((w_two,), (w_peer[0],), (w_peer[0], *[got for _, got in grads[:1]]))[j]
        keep, send, *made = weight_grad_part(
            acts_in, og, block_mask, after(where, *ready), rows, j
        )
        if made:
            acts_in = made[0]
        grads.append((keep, swap_z(send, 2)))
        w_peer.append(swap_x(after(w_mine[j + 1], keep)))
    grad_w = jnp.concatenate([keep + got for keep, got in grads], axis=1)

    outputs, gx = forward_and_input(
        acts, w_mine, w_peer, after(out_grad, grads[1][1], grads[2][1]), block_mask, where
    )

    by = gx.reshape(2, 2, tokens, depth // 4)
    pair = lax.dynamic_index_in_dim(by, c, 1, keepdims=False) + swap_f(
        lax.dynamic_index_in_dim(by, 1 - c, 1, keepdims=False), 1
    )
    grad_x = lax.dynamic_index_in_dim(pair, y, 0, keepdims=False) + swap_f(
        lax.dynamic_index_in_dim(pair, 1 - y, 0, keepdims=False), 2
    )
    return (outputs, grad_w, grad_x.astype(BF16))


def solution(mesh):
    in_specs = (P("dp", None), P("dp", "fsdp"), P(), P(None, "dp", "fsdp"))
    out_specs = (P(None, "dp", "fsdp"), P("dp", "fsdp"), P("dp", "fsdp"))
    return jax.shard_map(
        on_device, mesh=mesh, in_specs=in_specs, out_specs=out_specs, check_vma=False
    )
```

time: 171 us -> 160 us (0.936)
  starting transfers between devices: 42.7 us -> 22.8 us
  waiting for transfers between devices: 86.3 us -> 103 us
  other arithmetic: 7.24 us -> 3.37 us
  local copies, waits for them, and re-layouts: 16.5 us -> 14.4 us
    ppermute x22 -> x13, starting transfers between devices: 41.2 us -> 21.3 us  [swap_dp(): return lax.ppermute(a, 'dp', [(d, d ^ bits) for d in range(dp)])]
    ppermute x2, waiting for transfers between devices: 1.32 us -> 11 us  [swap_f(): return lax.ppermute(a, 'fsdp', [(d, d ^ bit) for d in range(fsdp)])]
    ppermute x22 -> x13, waiting for transfers between devices: 85 us -> 91.9 us  [swap_dp(): return lax.ppermute(a, 'dp', [(d, d ^ bits) for d in range(dp)])]
    add x4, other arithmetic: 4.36 us -> 0.24 us  [the longest x3 0.15 us: on_device(): grad_w = jnp.concatenate([keep + got for keep, got in grads], axis=1)]
    dynamic_slice x2 -> x5, local copies, waits for them, and re-layouts: 4.35 us -> 1.68 us  [the longest x4 0.87 us: of_x(): return lax.dynamic_slice_in_dim(a, side * rows, rows, 1)]
    pallas_call x1, Pallas kernels: 9.75 us -> 7.78 us  [forward_and_input(): pl.pallas_call(kernel, grid=(width // BS,), out_shape=(jax.ShapeDtypeStru...]
    unnamed x36 -> x41, local copies, waits for them, and re-layouts: 9.14 us -> 8.94 us
  transfers between devices with their start and end apart: 24 -> 15, of which waited for: 12 -> 9; matrix products, arithmetic and copies ran while one was open for 8% -> 1% of each run, Pallas kernels for 10% -> 5%
where the time goes in v6:
time: 160 us
  waiting for transfers between devices  103 us (64%)
  starting transfers between devices  22.8 us (14%)
  Pallas kernels  15.5 us (10%)
  local copies, waits for them, and re-layouts  14.4 us (9%)
  other arithmetic  3.37 us (2%)
    ppermute x13, waiting for transfers between devices, swap_dp(): return lax.ppermute(a, 'dp', [(d, d ^ bits) for d in range(dp)])  91.9 us
    ppermute x13, starting transfers between devices, swap_dp(): return lax.ppermute(a, 'dp', [(d, d ^ bits) for d in range(dp)])  21.3 us
    ppermute x2, waiting for transfers between devices, swap_f(): return lax.ppermute(a, 'fsdp', [(d, d ^ bit) for d in range(fsdp)])  11 us
    unnamed x41, local copies, waits for them, and re-layouts  8.94 us
    pallas_call x1, Pallas kernels, forward_and_input(): pl.pallas_call(kernel, grid=(width // BS,), out_shape=(jax.ShapeDtypeStru...  7.78 us
    pallas_call x3, Pallas kernels, weight_grad_part(): pl.pallas_call(kernel, out_shape=tuple(shapes), in_specs=[smem, smem] + [...  7.74 us
  transfers between devices with their start and end apart: 15, of which 9 were waited for; matrix products, arithmetic and copies ran while one was open for 1% of the time, Pallas kernels for 5%

profile of v6, /device:TPU:0, one launch (start us, length us, event | category | flops | bytes accessed | tf_op | source)
XLA Modules:
  0.0 160.0 jit_solution(5335541028268129778)
XLA Ops:
  0.7 2.0 %reshape.18 = bf16[128,4,768]{2,1,0:T(4,128)(2,1)S(1)} reshape(bf16[128,3072]{1,0:T(8,128)(2,1)} %acts_ref.3) | data formatting | bytes 1572864 | tf_op jit(solution)/shard_map/reshape | solution.py:205
  2.6 0.0 copy-start
  2.7 0.8 constant_dynamic-slice_fusion.5
  3.5 0.2 copy-done
  3.8 1.1 pad_maximum_fusion
  4.9 3.0 %collective-permute-start = (bf16[768,768]{1,0:T(8,128)(2,1)}, bf16[768,768]{1,0:T(8,128)(2,1)S(1)}, u32[]{:S(2)}, u32[]{:S(2)}) collective-permute-start(bf16[768,768]{1,0:T(8,128)(2,1)} %pad_maximum_fusion), channel_id=1, source_target_pairs={{0,8},{4,12},{8,0},{12,4},{16,24},{20,28},{24,16},{28,20},{1,9},{5... | collective-permute-start | bytes 3538952 | tf_op jit(solution)/shard_map/ppermute | solution.py:188
  7.9 0.8 constant_dynamic-slice_fusion.3
  8.7 0.1 maximum_maximum_fusion
  8.8 1.5 collective-permute-start.1
  10.4 21.7 %collective-permute-done.1.refs_2_ = bf16[640,768]{1,0:T(8,128)(2,1)S(1)} collective-permute-done((bf16[640,768]{1,0:T(8,128)(2,1)S(1)}, bf16[640,768]{1,0:T(8,128)(2,1)S(1)}, u32[]{:S(2)}, u32[]{:S(2)}) %collective-permute-start.1) | collective-permute-done | bytes 983072 | tf_op jit(solution)/shard_map/ppermute | solution.py:188
  32.1 2.0 %collective-permute-done.refs_1_ = bf16[768,768]{1,0:T(8,128)(2,1)S(1)} collective-permute-done((bf16[768,768]{1,0:T(8,128)(2,1)}, bf16[768,768]{1,0:T(8,128)(2,1)S(1)}, u32[]{:S(2)}, u32[]{:S(2)}) %collective-permute-start) | collective-permute-done | bytes 1179680 | tf_op jit(solution)/shard_map/ppermute | solution.py:188
  34.1 0.1 slice.9
  34.2 0.0 copy-start.19
  34.2 0.1 maximum_maximum_fusion.1
  34.3 1.7 %collective-permute-start.2 = (bf16[640,768]{1,0:T(8,128)(2,1)S(1)}, bf16[640,768]{1,0:T(8,128)(2,1)S(1)}, u32[]{:S(2)}, u32[]{:S(2)}) collective-permute-start(bf16[640,768]{1,0:T(8,128)(2,1)S(1)} %maximum_maximum_fusion.1), channel_id=1, source_target_pairs={{0,4},{4,0},{8,12},{12,8},{16,20},{20,16},{24,28},{28,24},{1,5},{5... | collective-permute-start | bytes 2949128 | tf_op jit(solution)/shard_map/ppermute | solution.py:188
  36.0 2.6 %collective-permute-start.4 = (bf16[384,768]{1,0:T(8,128)(2,1)}, bf16[384,768]{1,0:T(8,128)(2,1)}, u32[]{:S(2)}, u32[]{:S(2)}) collective-permute-start(bf16[384,768]{1,0:T(8,128)(2,1)} %rest_0_.1), channel_id=1, source_target_pairs={{0,16},{4,20},{8,24},{12,28},{16,0},{20,4},{24,8},{28,12},{1,17},{... | collective-permute-start | bytes 1769480 | tf_op jit(solution)/shard_map/ppermute | solution.py:188
  38.6 1.6 collective-permute-start.8
  40.2 17.1 %collective-permute-done.2.refs_3_ = bf16[640,768]{1,0:T(8,128)(2,1)S(1)} collective-permute-done((bf16[640,768]{1,0:T(8,128)(2,1)S(1)}, bf16[640,768]{1,0:T(8,128)(2,1)S(1)}, u32[]{:S(2)}, u32[]{:S(2)}) %collective-permute-start.2) | collective-permute-done | bytes 983072 | tf_op jit(solution)/shard_map/ppermute | solution.py:188
  57.3 0.9 copy-done.1
  58.3 1.3 collective-permute-start.3
  59.6 4.3 %collective-permute-done.4.rest_2_ = bf16[384,768]{1,0:T(8,128)(2,1)} collective-permute-done((bf16[384,768]{1,0:T(8,128)(2,1)}, bf16[384,768]{1,0:T(8,128)(2,1)}, u32[]{:S(2)}, u32[]{:S(2)}) %collective-permute-start.4) | collective-permute-done | bytes 589856 | tf_op jit(solution)/shard_map/ppermute | solution.py:188
  63.9 0.6 collective-permute-start.9
  64.5 0.1 pad_add_fusion.where_ref
  64.6 0.0 copy-start.2
  64.6 1.2 copy-done.2
  65.8 1.1 copy-done.3
  66.9 2.1 %weight_grad_part.3 = (f32[384,256]{1,0:T(8,128)S(1)}, f32[384,256]{1,0:T(8,128)S(1)}, bf16[4,768,128]{2,1,0:T(8,128)(2,1)S(1)}) custom-call(s32[4]{0:T(128)S(1)} %pad_add_fusion.where_ref, s32[4,12,12]{2,1,0:T(8,128)S(1)} %copy.14.mask_ref, bf16[128,3072]{1,0:T(8,128)(2,1)S(1)} %copy-done.3, bf16[512,768]{1,0:T(8,128)(2,1)S(1)} %bitcast.26, ...), custom_call_target="tpu_custom_call" | custom-call | flops 805306368 | bytes 786432 | tf_op jit(solution)/shard_map/weight_grad_part/pallas_call | solution.py:87
  69.0 3.4 %collective-permute-start.6 = (f32[384,256]{1,0:T(8,128)S(1)}, f32[384,256]{1,0:T(8,128)S(1)}, u32[]{:S(2)}, u32[]{:S(2)}) collective-permute-start(f32[384,256]{1,0:T(8,128)S(1)} %get-tuple-element.27), channel_id=1, source_target_pairs={{0,16},{4,20},{8,24},{12,28},{16,0},{20,4},{24,8},{28,12},{1,17},{... | collective-permute-start | bytes 1179656 | tf_op jit(solution)/shard_map/ppermute | solution.py:188
  72.5 0.0 collective-permute-done.8.rest_1_
  72.5 0.5 collective-permute-start.10
  73.0 0.0 collective-permute-done.3.rest_4_
  73.0 16.9 %collective-permute-done.6 = f32[384,256]{1,0:T(8,128)S(1)} collective-permute-done((f32[384,256]{1,0:T(8,128)S(1)}, f32[384,256]{1,0:T(8,128)S(1)}, u32[]{:S(2)}, u32[]{:S(2)}) %collective-permute-start.6) | collective-permute-done | bytes 393248 | tf_op jit(solution)/shard_map/ppermute | solution.py:188
  90.0 2.8 %weight_grad_part.5 = (f32[384,256]{1,0:T(8,128)S(1)}, f32[384,256]{1,0:T(8,128)}) custom-call(s32[4]{0:T(128)S(1)} %pad_add_fusion.where_ref, s32[4,12,12]{2,1,0:T(8,128)S(1)} %copy.14.mask_ref, bf16[4,768,128]{2,1,0:T(8,128)(2,1)S(1)} %get-tuple-element.25.acts_ref, bf16[512,768]{1,0:T(8,128)(2,1)S(1)} %bitcast.27, ...), custom_call_target="tpu_custom_call" | custom-call | flops 805306368 | bytes 786432 | tf_op jit(solution)/shard_map/weight_grad_part/pallas_call | solution.py:87
  92.8 0.0 collective-permute-done.9.rest_3_
  92.8 2.8 %weight_grad_part.4 = (f32[384,256]{1,0:T(8,128)S(1)}, f32[384,256]{1,0:T(8,128)}) custom-call(s32[4]{0:T(128)S(1)} %pad_add_fusion.where_ref, s32[4,12,12]{2,1,0:T(8,128)S(1)} %copy.14.mask_ref, bf16[4,768,128]{2,1,0:T(8,128)(2,1)S(1)} %get-tuple-element.25.acts_ref, bf16[512,768]{1,0:T(8,128)(2,1)S(1)} %bitcast.28, ...), custom_call_target="tpu_custom_call" | custom-call | flops 805306368 | bytes 786432 | tf_op jit(solution)/shard_map/weight_grad_part/pallas_call | solution.py:87
  95.6 0.7 copy-done.7
  96.3 0.5 collective-permute-start.11
  96.9 1.5 collective-permute-start.12
  98.4 0.0 collective-permute-start.7
  98.4 2.9 %collective-permute-start.5 = (f32[384,256]{1,0:T(8,128)}, f32[384,256]{1,0:T(8,128)S(1)}, u32[]{:S(2)}, u32[]{:S(2)}) collective-permute-start(f32[384,256]{1,0:T(8,128)} %get-tuple-element.26), channel_id=1, source_target_pairs={{0,16},{4,20},{8,24},{12,28},{16,0},{20,4},{24,8},{28,12},{1,17},{... | collective-permute-start | bytes 1179656 | tf_op jit(solution)/shard_map/ppermute | solution.py:188
  101.3 24.7 %collective-permute-done.7 = f32[384,256]{1,0:T(8,128)S(1)} collective-permute-done((f32[384,256]{1,0:T(8,128)}, f32[384,256]{1,0:T(8,128)S(1)}, u32[]{:S(2)}, u32[]{:S(2)}) %collective-permute-start.7) | collective-permute-done | bytes 393248 | tf_op jit(solution)/shard_map/ppermute | solution.py:188
  126.0 5.1 %collective-permute-done.5 = f32[384,256]{1,0:T(8,128)S(1)} collective-permute-done((f32[384,256]{1,0:T(8,128)}, f32[384,256]{1,0:T(8,128)S(1)}, u32[]{:S(2)}, u32[]{:S(2)}) %collective-permute-start.5) | collective-permute-done | bytes 393248 | tf_op jit(solution)/shard_map/ppermute | solution.py:188
  131.1 0.0 collective-permute-done.10.rest_5_
  131.1 0.0 collective-permute-done.11.rest_6_
  131.1 0.7 copy-done.17
  131.8 0.0 collective-permute-done.12.rest_7_
  131.9 0.8 copy-done.9
  132.7 1.1 copy-done.4
  133.8 1.1 copy-done.10
  134.9 7.8 %forward_and_input.1 = (bf16[4,128,768]{2,1,0:T(8,128)(2,1)}, f32[4,128,768]{2,1,0:T(8,128)S(1)}) custom-call(s32[4]{0:T(128)S(1)} %pad_add_fusion.where_ref, s32[4,12,12]{2,1,0:T(8,128)S(1)} %copy.14.mask_ref, bf16[128,3072]{1,0:T(8,128)(2,1)S(1)} %copy-done.4, bf16[4,128,768]{2,1,0:T(8,128)(2,1)S(1)} %copy-done, bf16[384,768]{1,0:T(8,128)(2,1)} %rest_0_.1, ...), custom_call_target="tpu_custom_call" | custom-call | flops 10871635968 | bytes 9437184 | tf_op jit(solution)/shard_map/forward_and_input/pallas_call | solution.py:151
  142.6 0.9 dynamic-slice_bitcast_fusion
  143.6 0.0 collective-permute-start.13
  143.6 2.5 %collective-permute-done.13 = f32[2,128,768]{2,1,0:T(8,128)S(1)} collective-permute-done((f32[2,128,768]{2,1,0:T(8,128)}, f32[2,128,768]{2,1,0:T(8,128)S(1)}, u32[]{:S(2)}, u32[]{:S(2)}) %collective-permute-start.13) | collective-permute-done | bytes 786464 | tf_op jit(solution)/shard_map/ppermute | solution.py:197
  146.1 0.1 bitcast_add_fusion
  146.2 0.0 copy-start.11
  146.2 0.9 copy-done.11
  147.1 0.8 dynamic-slice_bitcast_fusion.1
  147.9 1.5 collective-permute-start.14
  149.4 0.1 add.72
  149.5 0.1 add.74
  149.5 0.1 add.73
  149.6 1.1 pad_maximum_fusion.1
  150.7 8.5 %collective-permute-done.14 = f32[128,768]{1,0:T(8,128)S(1)} collective-permute-done((f32[128,768]{1,0:T(8,128)}, f32[128,768]{1,0:T(8,128)S(1)}, u32[]{:S(2)}, u32[]{:S(2)}) %collective-permute-start.14) | collective-permute-done | bytes 393248 | tf_op jit(solution)/shard_map/ppermute | solution.py:197
  159.2 0.7 fusion
  (32 shorter events, 0.2 us)
Async XLA Ops:
  2.6 1.1 copy-start
  4.9 29.2 %collective-permute-start = (bf16[768,768]{1,0:T(8,128)(2,1)}, bf16[768,768]{1,0:T(8,128)(2,1)S(1)}, u32[]{:S(2)}, u32[]{:S(2)}) collective-permute-start(bf16[768,768]{1,0:T(8,128)(2,1)} %pad_maximum_fusion), channel_id=1, source_target_pairs={{0,8},{4,12},{8,0},{12,4},{16,24},{20,28},{24,16},{28,20},{1,9},{5... | collective-permute-start | bytes 3538952 | tf_op jit(solution)/shard_map/ppermute | solution.py:188
  8.8 23.3 %collective-permute-start.1 = (bf16[640,768]{1,0:T(8,128)(2,1)S(1)}, bf16[640,768]{1,0:T(8,128)(2,1)S(1)}, u32[]{:S(2)}, u32[]{:S(2)}) collective-permute-start(bf16[640,768]{1,0:T(8,128)(2,1)S(1)} %maximum_maximum_fusion), channel_id=1, source_target_pairs={{0,4},{4,0},{8,12},{12,8},{16,20},{20,16},{24,28},{28,24},{1,5},{5... | collective-permute-start | bytes 2949128 | tf_op jit(solution)/shard_map/ppermute | solution.py:188
  34.2 30.4 %copy-start.19 = (s32[4,12,12]{2,0,1:T(4,128)S(1)}, s32[4,12,12]{2,0,1:T(4,128)}, u32[]{:S(2)}) copy-start(s32[4,12,12]{2,0,1:T(4,128)} %param.6) | copy-start | bytes 6916
  34.3 23.0 %collective-permute-start.2 = (bf16[640,768]{1,0:T(8,128)(2,1)S(1)}, bf16[640,768]{1,0:T(8,128)(2,1)S(1)}, u32[]{:S(2)}, u32[]{:S(2)}) collective-permute-start(bf16[640,768]{1,0:T(8,128)(2,1)S(1)} %maximum_maximum_fusion.1), channel_id=1, source_target_pairs={{0,4},{4,0},{8,12},{12,8},{16,20},{20,16},{24,28},{28,24},{1,5},{5... | collective-permute-start | bytes 2949128 | tf_op jit(solution)/shard_map/ppermute | solution.py:188
  36.0 27.9 %collective-permute-start.4 = (bf16[384,768]{1,0:T(8,128)(2,1)}, bf16[384,768]{1,0:T(8,128)(2,1)}, u32[]{:S(2)}, u32[]{:S(2)}) collective-permute-start(bf16[384,768]{1,0:T(8,128)(2,1)} %rest_0_.1), channel_id=1, source_target_pairs={{0,16},{4,20},{8,24},{12,28},{16,0},{20,4},{24,8},{28,12},{1,17},{... | collective-permute-start | bytes 1769480 | tf_op jit(solution)/shard_map/ppermute | solution.py:188
  38.6 33.9 %collective-permute-start.8 = (bf16[384,768]{1,0:T(8,128)(2,1)}, bf16[384,768]{1,0:T(8,128)(2,1)}, u32[]{:S(2)}, u32[]{:S(2)}) collective-permute-start(bf16[384,768]{1,0:T(8,128)(2,1)} %rest_0_.1), channel_id=1, source_target_pairs={{0,8},{4,12},{8,0},{12,4},{16,24},{20,28},{24,16},{28,20},{1,9},{5... | collective-permute-start | bytes 1769480 | tf_op jit(solution)/shard_map/ppermute | solution.py:188
  57.3 0.9 copy-start.1
  58.3 14.8 %collective-permute-start.3 = (bf16[384,768]{1,0:T(8,128)(2,1)}, bf16[384,768]{1,0:T(8,128)(2,1)}, u32[]{:S(2)}, u32[]{:S(2)}) collective-permute-start(bf16[384,768]{1,0:T(8,128)(2,1)} %rest_0_.1), channel_id=1, source_target_pairs={{0,4},{4,0},{8,12},{12,8},{16,20},{20,16},{24,28},{28,24},{1,5},{5... | collective-permute-start | bytes 1769480 | tf_op jit(solution)/shard_map/ppermute | solution.py:188
  63.9 28.9 %collective-permute-start.9 = (bf16[384,768]{1,0:T(8,128)(2,1)}, bf16[384,768]{1,0:T(8,128)(2,1)}, u32[]{:S(2)}, u32[]{:S(2)}) collective-permute-start(bf16[384,768]{1,0:T(8,128)(2,1)} %collective-permute-done.4.rest_2_), channel_id=1, source_target_pairs={{0,8},{4,12},{8,0},{12,4},{16,24},{20,28},{24,16},{28,20},{1,9},{5... | collective-permute-start | bytes 1769480 | tf_op jit(solution)/shard_map/ppermute | solution.py:188
  64.6 1.2 copy-start.2
  65.8 1.1 copy-start.3
  69.0 20.9 %collective-permute-start.6 = (f32[384,256]{1,0:T(8,128)S(1)}, f32[384,256]{1,0:T(8,128)S(1)}, u32[]{:S(2)}, u32[]{:S(2)}) collective-permute-start(f32[384,256]{1,0:T(8,128)S(1)} %get-tuple-element.27), channel_id=1, source_target_pairs={{0,16},{4,20},{8,24},{12,28},{16,0},{20,4},{24,8},{28,12},{1,17},{... | collective-permute-start | bytes 1179656 | tf_op jit(solution)/shard_map/ppermute | solution.py:188
  72.5 58.6 %collective-permute-start.10 = (bf16[384,768]{1,0:T(8,128)(2,1)}, bf16[384,768]{1,0:T(8,128)(2,1)}, u32[]{:S(2)}, u32[]{:S(2)}) collective-permute-start(bf16[384,768]{1,0:T(8,128)(2,1)} %collective-permute-done.8.rest_1_), channel_id=1, source_target_pairs={{0,4},{4,0},{8,12},{12,8},{16,20},{20,16},{24,28},{28,24},{1,5},{5... | collective-permute-start | bytes 1769480 | tf_op jit(solution)/shard_map/ppermute | solution.py:188
  90.0 2.8 %copy-start.13 = (f32[384,256]{1,0:T(8,128)}, f32[384,256]{1,0:T(8,128)S(1)}, u32[]{:S(2)}) copy-start(f32[384,256]{1,0:T(8,128)S(1)} %collective-permute-done.6) | copy-start | bytes 1179652
  92.8 2.8 %copy-start.5 = (f32[384,256]{1,0:T(8,128)}, f32[384,256]{1,0:T(8,128)S(1)}, u32[]{:S(2)}) copy-start(f32[384,256]{1,0:T(8,128)S(1)} %get-tuple-element.35) | copy-start | bytes 1179652
  95.6 0.7 copy-start.7
  96.3 34.8 %collective-permute-start.11 = (bf16[384,768]{1,0:T(8,128)(2,1)}, bf16[384,768]{1,0:T(8,128)(2,1)S(1)}, u32[]{:S(2)}, u32[]{:S(2)}) collective-permute-start(bf16[384,768]{1,0:T(8,128)(2,1)} %collective-permute-done.4.rest_2_), channel_id=1, source_target_pairs={{0,4},{4,0},{8,12},{12,8},{16,20},{20,16},{24,28},{28,24},{1,5},{5... | collective-permute-start | bytes 1769480 | tf_op jit(solution)/shard_map/ppermute | solution.py:188
  96.9 35.0 %collective-permute-start.12 = (bf16[384,768]{1,0:T(8,128)(2,1)}, bf16[384,768]{1,0:T(8,128)(2,1)S(1)}, u32[]{:S(2)}, u32[]{:S(2)}) collective-permute-start(bf16[384,768]{1,0:T(8,128)(2,1)} %collective-permute-done.9.rest_3_), channel_id=1, source_target_pairs={{0,4},{4,0},{8,12},{12,8},{16,20},{20,16},{24,28},{28,24},{1,5},{5... | collective-permute-start | bytes 1769480 | tf_op jit(solution)/shard_map/ppermute | solution.py:188
  98.4 27.6 %collective-permute-start.7 = (f32[384,256]{1,0:T(8,128)}, f32[384,256]{1,0:T(8,128)S(1)}, u32[]{:S(2)}, u32[]{:S(2)}) collective-permute-start(f32[384,256]{1,0:T(8,128)} %get-tuple-element.29), channel_id=1, source_target_pairs={{0,16},{4,20},{8,24},{12,28},{16,0},{20,4},{24,8},{28,12},{1,17},{... | collective-permute-start | bytes 1179656 | tf_op jit(solution)/shard_map/ppermute | solution.py:188
  98.4 32.7 %collective-permute-start.5 = (f32[384,256]{1,0:T(8,128)}, f32[384,256]{1,0:T(8,128)S(1)}, u32[]{:S(2)}, u32[]{:S(2)}) collective-permute-start(f32[384,256]{1,0:T(8,128)} %get-tuple-element.26), channel_id=1, source_target_pairs={{0,16},{4,20},{8,24},{12,28},{16,0},{20,4},{24,8},{28,12},{1,17},{... | collective-permute-start | bytes 1179656 | tf_op jit(solution)/shard_map/ppermute | solution.py:188
  126.0 5.1 %copy-start.15 = (f32[384,256]{1,0:T(8,128)}, f32[384,256]{1,0:T(8,128)S(1)}, u32[]{:S(2)}) copy-start(f32[384,256]{1,0:T(8,128)S(1)} %collective-permute-done.7) | copy-start | bytes 1179652
  131.1 0.8 copy-start.17
  131.8 0.8 copy-start.9
  132.7 1.1 copy-start.4
  133.8 1.1 copy-start.10
  143.6 2.5 %collective-permute-start.13 = (f32[2,128,768]{2,1,0:T(8,128)}, f32[2,128,768]{2,1,0:T(8,128)S(1)}, u32[]{:S(2)}, u32[]{:S(2)}) collective-permute-start(f32[2,128,768]{2,1,0:T(8,128)} %dynamic-slice_bitcast_fusion), channel_id=1, source_target_pairs={{0,1},{1,0},{2,3},{3,2},{4,5},{5,4},{6,7},{7,6},{8,9},{9,8},{10,11... | collective-permute-start | bytes 2359304 | tf_op jit(solution)/shard_map/ppermute | solution.py:197
  143.6 5.8 %copy-start.14 = (f32[384,256]{1,0:T(8,128)S(1)}, f32[384,256]{1,0:T(8,128)}, u32[]{:S(2)}) copy-start(f32[384,256]{1,0:T(8,128)} %copy-done.13) | copy-start | bytes 1179652
  146.2 0.9 copy-start.11
  147.1 2.4 %copy-start.6 = (f32[384,256]{1,0:T(8,128)S(1)}, f32[384,256]{1,0:T(8,128)}, u32[]{:S(2)}) copy-start(f32[384,256]{1,0:T(8,128)} %copy-done.5) | copy-start | bytes 1179652
  147.1 2.4 %copy-start.16 = (f32[384,256]{1,0:T(8,128)S(1)}, f32[384,256]{1,0:T(8,128)}, u32[]{:S(2)}) copy-start(f32[384,256]{1,0:T(8,128)} %copy-done.15) | copy-start | bytes 1179652
  147.1 2.4 %copy-start.8 = (f32[384,256]{1,0:T(8,128)S(1)}, f32[384,256]{1,0:T(8,128)}, u32[]{:S(2)}) copy-start(f32[384,256]{1,0:T(8,128)} %copy-done.7) | copy-start | bytes 1179652
  147.1 2.5 %copy-start.18 = (f32[384,256]{1,0:T(8,128)S(1)}, f32[384,256]{1,0:T(8,128)}, u32[]{:S(2)}) copy-start(f32[384,256]{1,0:T(8,128)} %copy-done.17) | copy-start | bytes 1179652
  147.9 11.4 %collective-permute-start.14 = (f32[128,768]{1,0:T(8,128)}, f32[128,768]{1,0:T(8,128)S(1)}, u32[]{:S(2)}, u32[]{:S(2)}) collective-permute-start(f32[128,768]{1,0:T(8,128)} %dynamic-slice_bitcast_fusion.1), channel_id=1, source_target_pairs={{0,2},{1,3},{2,0},{3,1},{4,6},{5,7},{6,4},{7,5},{8,10},{9,11},{10,... | collective-permute-start | bytes 1179656 | tf_op jit(solution)/shard_map/ppermute | solution.py:197
  149.5 9.7 %copy-start.12 = (f32[2,128,768]{2,1,0:T(8,128)S(1)}, f32[2,128,768]{2,1,0:T(8,128)}, u32[]{:S(2)}) copy-start(f32[2,128,768]{2,1,0:T(8,128)} %copy-done.11) | copy-start | bytes 2359300

commit v7 on v6

v7 whole, which is shorter than its diff:
```python
import jax
import jax.numpy as jnp
from jax import lax
from jax.experimental import pallas as pl
from jax.experimental.pallas import tpu as pltpu
from jax.sharding import PartitionSpec as P

BS = 256
TOK_G = 128
LANES = 128
F32 = jnp.float32
BF16 = jnp.bfloat16
VMEM_BYTES = 40 * 1024 * 1024


def plain(acts, weight, block_mask, out_grad):
    width = weight.shape[1]
    kblocks = block_mask.shape[1]
    oblocks = block_mask.shape[2]
    first_col = lax.axis_index("fsdp") * width
    col_ids = (first_col + jnp.arange(width, dtype=jnp.int32)) // BS
    col_select = (col_ids[None, :] == jnp.arange(oblocks, dtype=jnp.int32)[:, None]).astype(F32)
    col_mask = jnp.einsum("skb,bc->skc", block_mask.astype(F32), col_select)
    full = lax.all_gather(weight, "dp", axis=0, tiled=True)
    row_ids = jnp.arange(full.shape[0], dtype=jnp.int32) // BS
    row_select = (row_ids[:, None] == jnp.arange(kblocks, dtype=jnp.int32)[None, :]).astype(F32)
    mask = jnp.einsum("nk,skc->snc", row_select, col_mask)
    masked = mask.astype(BF16) * full[None]
    forward = jnp.einsum("tn,snc->stc", acts, masked, preferred_element_type=F32)
    input_part = jnp.einsum("stc,snc->tn", out_grad, masked, preferred_element_type=F32)
    products = jnp.einsum("tn,stc->snc", acts, out_grad, preferred_element_type=F32)
    grad_w = lax.psum_scatter(
        jnp.sum(mask * products, axis=0) * (1.0 / TOK_G), "dp", scatter_dimension=0, tiled=True
    )
    grad_x = lax.psum_scatter(input_part, "fsdp", scatter_dimension=1, tiled=True).astype(BF16)
    return (forward.astype(BF16), grad_w, grad_x)


def weight_grad_part(acts, og, block_mask, where, rows, chunk, chunks):
    nsub = block_mask.shape[0]
    tokens = acts.shape[0]
    flat = nsub * tokens
    ng = len(og)
    per = rows // LANES
    width = og[0].shape[1]
    made = chunks * BS

    def kernel(where_ref, mask_ref, acts_ref, *refs):
        extra, og_refs, outs, tiles = refs[:3], refs[3 : 3 + ng], refs[3 + ng : -1], refs[-1]
        z, x = where_ref[0], where_ref[1]
        step = pl.program_id(0)
        col = where_ref[2] + chunk + step

        @pl.when(step == 0)
        def _():
            one_ref, side_ref, both_ref = extra
            for r in range(2):
                for g in range(per):
                    start = ((z ^ (2 * r)) * 2 + x) * rows + g * LANES
                    here = pl.ds(pl.multiple_of(start, LANES), LANES)
                    there = pl.ds(pl.multiple_of(x * rows + g * LANES, LANES), LANES)
                    dst = slice((r * per + g) * LANES, (r * per + g + 1) * LANES)
                    tiles[0, dst, :] = acts_ref[:, here].T
                    tiles[1, dst, :] = one_ref[r * tokens : (r + 1) * tokens, there].T
                    tiles[2, dst, :] = side_ref[:, dst].T
                    tiles[3, dst, :] = both_ref[:, dst].T

        for r in range(2):
            for g in range(per):
                block = (((z ^ (2 * r)) * 2 + x) * rows + g * LANES) // BS
                dst = slice((r * per + g) * LANES, (r * per + g + 1) * LANES)
                keep = [mask_ref[s, block, col].astype(F32) for s in range(nsub)]
                keep = [jnp.full((LANES, tokens), k).astype(BF16) for k in keep]
                total = None
                for k in range(ng):
                    t = tiles[k, dst, :]
                    lhs = jnp.concatenate([t * m for m in keep], axis=1)
                    term = jnp.dot(lhs, og_refs[k][...], preferred_element_type=F32)
                    total = term if total is None else total + term
                outs[r][g * LANES : (g + 1) * LANES, :] = total * (1.0 / TOK_G)

    smem = pl.BlockSpec(memory_space=pltpu.SMEM)
    out = pl.BlockSpec((rows, BS), lambda j: (0, j))
    return pl.pallas_call(
        kernel,
        grid=(chunks,),
        out_shape=(jax.ShapeDtypeStruct((rows, made), F32),) * 2,
        in_specs=[smem, smem, pl.BlockSpec(acts.shape, lambda j: (0, 0))]
        + [
            pl.BlockSpec((2 * tokens, width), lambda j: (flat // (2 * tokens), 0)),
            pl.BlockSpec((tokens, width), lambda j: (flat // tokens, 0)),
            pl.BlockSpec((tokens, width), lambda j: (flat // tokens, 0)),
        ]
        + [pl.BlockSpec((flat, BS), lambda j: (0, chunk + j))] * ng,
        out_specs=(out, out),
        scratch_shapes=[pltpu.VMEM((ng, 2 * rows, tokens), BF16)],
        compiler_params=pltpu.CompilerParams(vmem_limit_bytes=VMEM_BYTES),
        cost_estimate=pl.CostEstimate(
            flops=4 * ng * rows * made * flat, bytes_accessed=8 * rows * made, transcendentals=0
        ),
        name="weight_grad_part",
    )(where, block_mask, acts, *og[1:], *og)


def forward_and_input(acts, side, og, weights, block_mask, where):
    nsub, tokens, width = og.shape
    flat = nsub * tokens
    nz = len(weights)
    rows = weights[0].shape[0]
    per = rows // LANES

    def kernel(where_ref, mask_ref, acts_ref, sacts_ref, og_ref, sog_ref, *rest):
        w_refs, (keep_ref, send_ref, gx_ref, acc, hilo) = rest[:nz], rest[nz:]
        z, x = where_ref[0], where_ref[1]
        step = pl.program_id(0)
        col = where_ref[2] + step
        first = step == 0
        near = (1 - x).astype(F32)
        far = x.astype(F32)

        def keep_of(block):
            return [mask_ref[s, block, col].astype(F32) for s in range(nsub)]

        for k in range(nz):
            start = ((z ^ k) * 2 + x) * rows
            blocks = [start // BS, (start + rows - LANES) // BS]
            keeps = [keep_of(block) for block in blocks]
            for i in range(2):
                for t, ref in enumerate((og_ref, sog_ref)):
                    total = jnp.zeros((tokens, BS), F32)
                    for s in range(nsub):
                        if t == 0:
                            piece = ref[s]
                        else:
                            piece = ref[s * tokens : (s + 1) * tokens, :]
                        total = total + keeps[i][s] * piece.astype(F32)
                    hi = total.astype(BF16)
                    hilo[k, i, t * tokens : (t + 1) * tokens] = hi
                    hilo[k, i, (t + 2) * tokens : (t + 3) * tokens] = (
                        total - hi.astype(F32)
                    ).astype(BF16)
            prods = []
            for g in range(per):
                here = pl.ds(pl.multiple_of(start + g * LANES, LANES), LANES)
                there = slice((k // 2) * rows + g * LANES, (k // 2) * rows + (g + 1) * LANES)
                both = jnp.concatenate(
                    [acts_ref[:, here], sacts_ref[(k % 2) * tokens : (k % 2 + 1) * tokens, there]]
                )
                at = slice(g * LANES, (g + 1) * LANES)
                w = w_refs[k][at, :]
                prods.append(jnp.dot(both, w, preferred_element_type=F32))
                i = (0, x, 1)[g]
                four = lax.dot_general(
                    hilo[k, i], w, (((1,), (1,)), ((), ())), preferred_element_type=F32
                )
                term = four[: 2 * tokens] + four[2 * tokens :]
                gx_ref[z ^ k, :, at] = jnp.where(first, term, gx_ref[z ^ k, :, at] + term)
            low = prods[0] + near * prods[1]
            high = prods[2] + far * prods[1]
            for s in range(nsub):
                term = keeps[0][s] * low + keeps[1][s] * high
                acc[s] = term if k == 0 else acc[s] + term
        for s in range(nsub):
            keep_ref[s] = acc[s, :tokens]
            send_ref[0, s] = acc[s, tokens:]

    smem = pl.BlockSpec(memory_space=pltpu.SMEM)
    by_col = pl.BlockSpec((nsub, tokens, BS), lambda j: (0, 0, j))
    gx_shape = (nz, 2 * tokens, rows)
    assert per == 3
    return pl.pallas_call(
        kernel,
        grid=(width // BS,),
        out_shape=(
            jax.ShapeDtypeStruct((nsub, tokens, width), F32),
            jax.ShapeDtypeStruct((width // BS, nsub, tokens, BS), F32),
            jax.ShapeDtypeStruct(gx_shape, F32),
        ),
        in_specs=[
            smem,
            smem,
            pl.BlockSpec(acts.shape, lambda j: (0, 0)),
            pl.BlockSpec((2 * tokens, width), lambda j: (flat // (2 * tokens), 0)),
            by_col,
            pl.BlockSpec((flat, BS), lambda j: (0, j)),
        ]
        + [pl.BlockSpec((rows, BS), lambda j: (0, j))] * nz,
        out_specs=(
            by_col,
            pl.BlockSpec((1, nsub, tokens, BS), lambda j: (j, 0, 0, 0)),
            pl.BlockSpec(gx_shape, lambda j: (0, 0, 0)),
        ),
        scratch_shapes=[
            pltpu.VMEM((nsub, 2 * tokens, BS), F32),
            pltpu.VMEM((nz, 2, 4 * tokens, BS), BF16),
        ],
        compiler_params=pltpu.CompilerParams(vmem_limit_bytes=VMEM_BYTES),
        cost_estimate=pl.CostEstimate(
            flops=36 * tokens * nz * 2 * rows * width,
            bytes_accessed=4 * nz * 2 * rows * width,
            transcendentals=0,
        ),
        name="forward_and_input",
    )(where, block_mask, acts, side, og, side, *weights)


def on_device(acts, weight, block_mask, out_grad):
    rows, width = weight.shape
    tokens, depth = acts.shape
    dp = lax.axis_size("dp")
    fsdp = lax.axis_size("fsdp")
    if rows != 3 * LANES or width != 3 * BS or dp != 8 or fsdp != 4 or tokens != LANES:
        return plain(acts, weight, block_mask, out_grad)
    nx = 2
    me = lax.axis_index("dp")
    z, x = me // nx, me % nx
    f = lax.axis_index("fsdp")
    y, c = f // 2, f % 2
    where = jnp.stack([z, x, f * (width // BS), c]).astype(jnp.int32)

    def swap_dp(a, bits):
        return lax.ppermute(a, "dp", [(d, d ^ bits) for d in range(dp)])

    def swap_x(a):
        return swap_dp(a, 1)

    def swap_z(a, k):
        return swap_dp(a, k * nx)

    def swap_f(a, bit):
        return lax.ppermute(a, "fsdp", [(d, d ^ bit) for d in range(fsdp)])

    def after(a, *others):
        return lax.optimization_barrier((a, *others))[0]

    nsub = out_grad.shape[0]
    flat = nsub * tokens
    own = out_grad.reshape(flat, width)
    by_z = acts.reshape(tokens, dp // nx, nx * rows)

    def acts_of(k):
        return lax.dynamic_index_in_dim(by_z, z ^ k, 1, keepdims=False)

    def of_x(a, side):
        return lax.dynamic_slice_in_dim(a, side * rows, rows, 1)

    def for_other(k):
        return of_x(acts_of(k), 1 - x)

    one = swap_z(jnp.concatenate([own, acts_of(1), acts_of(3)]), 1)
    side = swap_x(
        jnp.concatenate(
            [own]
            + [jnp.concatenate([for_other(k), for_other(k + 2)], axis=1) for k in range(2)]
        )
    )
    one = after(one, side)
    passed = [
        of_x(one[flat + r * tokens : flat + (r + 1) * tokens], 1 - x) for r in range(2)
    ]
    both = swap_x(jnp.concatenate([one[:flat], jnp.concatenate(passed, axis=1)]))

    w_two = swap_z(weight, 2)
    w_one = swap_z(weight, 1)
    w_three = swap_z(w_two, 1)

    og = [own, one, side, both]
    keep_0, send = weight_grad_part(acts, og, block_mask, where, rows, 0, 1)
    got_0 = swap_z(send, 2)
    keep_1, send = weight_grad_part(acts, og, block_mask, where, rows, 1, width // BS - 1)
    got_1 = swap_z(send, 2)
    grad_w = jnp.concatenate([keep_0 + got_0, keep_1 + got_1], axis=1)

    mine, theirs, gx = forward_and_input(
        acts, side, after(out_grad, got_0, keep_1), [weight, w_one, w_two, w_three], block_mask, where
    )
    got = jnp.concatenate([swap_x(t) for t in theirs], axis=2)
    outputs = (mine + got).astype(BF16)

    by = gx.reshape(2, 2, 2 * tokens, rows)
    pair = lax.dynamic_index_in_dim(by, c, 1, keepdims=False) + swap_f(
        lax.dynamic_index_in_dim(by, 1 - c, 1, keepdims=False), 1
    )
    done = lax.dynamic_index_in_dim(pair, y, 0, keepdims=False) + swap_f(
        lax.dynamic_index_in_dim(pair, 1 - y, 0, keepdims=False), 2
    )
    done = done.astype(BF16)
    mine, got = done[:tokens], swap_x(done[tokens:])
    low, high = jnp.where(x == 0, mine, got), jnp.where(x == 0, got, mine)
    return (outputs, grad_w, jnp.concatenate([low, high], axis=1))


def solution(mesh):
    in_specs = (P("dp", None), P("dp", "fsdp"), P(), P(None, "dp", "fsdp"))
    out_specs = (P(None, "dp", "fsdp"), P("dp", "fsdp"), P("dp", "fsdp"))
    return jax.shard_map(
        on_device, mesh=mesh, in_specs=in_specs, out_specs=out_specs, check_vma=False
    )
```

time: 160 us -> 152 us (0.950)
  waiting for transfers between devices: 103 us -> 91.5 us
  starting transfers between devices: 22.8 us -> 16.8 us
  other arithmetic: 3.37 us -> 8.63 us
  local copies, waits for them, and re-layouts: 14.4 us -> 17.9 us
    ppermute x2, waiting for transfers between devices: 11 us -> 2.02 us  [swap_f(): return lax.ppermute(a, 'fsdp', [(d, d ^ bit) for d in range(fsdp)])]
    ppermute x13 -> x12, starting transfers between devices: 21.3 us -> 15.3 us  [swap_dp(): return lax.ppermute(a, 'dp', [(d, d ^ bits) for d in range(dp)])]
    convert_element_type x1 -> x2, other arithmetic: 0.73 us -> 3.17 us  [the longest x1 2.14 us: on_device(): outputs = (mine + got).astype(BF16)]
    ppermute x13 -> x12, waiting for transfers between devices: 91.9 us -> 89.5 us  [swap_dp(): return lax.ppermute(a, 'dp', [(d, d ^ bits) for d in range(dp)])]
    add x3 -> x2, other arithmetic: 0.15 us -> 2.32 us  [on_device(): grad_w = jnp.concatenate([keep_0 + got_0, keep_1 + got_1], axis=1)]
    unnamed x41 -> x37, local copies, waits for them, and re-layouts: 8.94 us -> 10.2 us
    pallas_call x3 -> x2, Pallas kernels: 7.74 us -> 6.52 us  [weight_grad_part(): pl.pallas_call(kernel, grid=(chunks,), out_shape=(jax.ShapeDtypeStruct((r...]
  transfers between devices with their start and end apart: 15 -> 14, of which waited for: 9 -> 8; matrix products, arithmetic and copies ran while one was open for 1% -> 6% of each run, Pallas kernels for 5% -> 4%
where the time goes in v7:
time: 152 us; the launch traced here: 151 us
  waiting for transfers between devices  91.5 us (60%)
  local copies, waits for them, and re-layouts  17.9 us (12%)
  starting transfers between devices  16.8 us (11%)
  Pallas kernels  15.3 us (10%)
  other arithmetic  8.63 us (6%)
    ppermute x12, waiting for transfers between devices, swap_dp(): return lax.ppermute(a, 'dp', [(d, d ^ bits) for d in range(dp)])  89.5 us
    ppermute x12, starting transfers between devices, swap_dp(): return lax.ppermute(a, 'dp', [(d, d ^ bits) for d in range(dp)])  15.3 us
    unnamed x37, local copies, waits for them, and re-layouts  10.2 us
    pallas_call x1, Pallas kernels, forward_and_input(): pl.pallas_call(kernel, grid=(width // BS,), out_shape=(jax.ShapeDtypeStru...  8.77 us
    pallas_call x2, Pallas kernels, weight_grad_part(): pl.pallas_call(kernel, grid=(chunks,), out_shape=(jax.ShapeDtypeStruct((r...  6.52 us
  transfers between devices with their start and end apart: 14, of which 8 were waited for; matrix products, arithmetic and copies ran while one was open for 6% of the time, Pallas kernels for 4%

profile of v7, /device:TPU:0, one launch (start us, length us, event | category | flops | bytes accessed | tf_op | source)
XLA Modules:
  0.0 151.0 jit_solution(7746824660196364113)
XLA Ops:
  0.7 2.0 %reshape.20 = bf16[128,4,768]{2,1,0:T(4,128)(2,1)S(1)} reshape(bf16[128,3072]{1,0:T(8,128)(2,1)} %acts_ref.5) | data formatting | bytes 1572864 | tf_op jit(solution)/shard_map/reshape | solution.py:239
  2.7 0.8 constant_dynamic-slice_fusion.3
  3.6 0.0 copy-start.2
  3.6 1.6 %constant_dynamic-slice_fusion.7 = (bf16[128,1,384]{2,1,0:T(2,128)(2,1)S(1)}, bf16[128,1,384]{2,1,0:T(2,128)(2,1)S(1)}, bf16[128,1,384]{2,1,0:T(2,128)(2,1)S(1)}, bf16[128,1,384]{2,1,0:T(2,128)(2,1)S(1)}) fusion(bf16[128,4,768]{2,1,0:T(4,128)(2,1)S(1)} %reshape.20, s32[]{:T(128)S(6)} %select_n.81, s32[]{:T(128)S(6)} %select_n.83, s32[]{:T(128)S(6)} %select_n.89, ...), kind=kLoop, calls=%fused_computation.32 | loop fusion | bytes 786452 | tf_op jit(solution)/shard_map/dynamic_slice | solution.py:245
  5.2 0.2 fusion.2
  5.4 3.1 %collective-permute-start.1 = (bf16[768,768]{1,0:T(8,128)(2,1)S(1)}, bf16[768,768]{1,0:T(8,128)(2,1)S(1)}, u32[]{:S(2)}, u32[]{:S(2)}) collective-permute-start(bf16[768,768]{1,0:T(8,128)(2,1)S(1)} %get-tuple-element.26), channel_id=1, source_target_pairs={{0,8},{4,12},{8,0},{12,4},{16,24},{20,28},{24,16},{28,20},{1,9},{5... | collective-permute-start | bytes 3538952 | tf_op jit(solution)/shard_map/ppermute | solution.py:222
  8.5 1.5 collective-permute-start
  10.0 24.5 %collective-permute-done.1.refs_0_.refs_4_ = bf16[768,768]{1,0:T(8,128)(2,1)S(1)} collective-permute-done((bf16[768,768]{1,0:T(8,128)(2,1)S(1)}, bf16[768,768]{1,0:T(8,128)(2,1)S(1)}, u32[]{:S(2)}, u32[]{:S(2)}) %collective-permute-start.1) | collective-permute-done | bytes 1179680 | tf_op jit(solution)/shard_map/ppermute | solution.py:222
  34.5 1.5 collective-permute-done.refs_1_.refs_5_.sacts_ref.sog_ref
  35.9 0.1 slice.15
  36.0 0.0 copy-start.17
  36.1 1.0 maximum_maximum_fusion
  37.1 1.5 collective-permute-start.2
  38.6 2.6 %collective-permute-start.5 = (bf16[384,768]{1,0:T(8,128)(2,1)}, bf16[384,768]{1,0:T(8,128)(2,1)}, u32[]{:S(2)}, u32[]{:S(2)}) collective-permute-start(bf16[384,768]{1,0:T(8,128)(2,1)} %rest_0_.1), channel_id=1, source_target_pairs={{0,16},{4,20},{8,24},{12,28},{16,0},{20,4},{24,8},{28,12},{1,17},{... | collective-permute-start | bytes 1769480 | tf_op jit(solution)/shard_map/ppermute | solution.py:222
  41.1 0.4 collective-permute-start.4
  41.6 24.5 %collective-permute-done.5.rest_2_ = bf16[384,768]{1,0:T(8,128)(2,1)} collective-permute-done((bf16[384,768]{1,0:T(8,128)(2,1)}, bf16[384,768]{1,0:T(8,128)(2,1)}, u32[]{:S(2)}, u32[]{:S(2)}) %collective-permute-start.5) | collective-permute-done | bytes 589856 | tf_op jit(solution)/shard_map/ppermute | solution.py:222
  66.1 0.0 collective-permute-start.6
  66.1 0.1 pad_add_fusion.where_ref
  66.2 0.0 collective-permute-done.2.refs_2_.refs_6_
  66.2 1.1 copy-done
  67.4 1.1 copy-done.3
  68.5 2.9 %weight_grad_part.2 = (f32[384,256]{1,0:T(8,128)S(1)}, f32[384,256]{1,0:T(8,128)}) custom-call(s32[4]{0:T(128)S(1)} %pad_add_fusion.where_ref, s32[4,12,12]{2,1,0:T(8,128)S(1)} %copy.15.mask_ref, bf16[128,3072]{1,0:T(8,128)(2,1)S(1)} %copy-done, bf16[768,768]{1,0:T(8,128)(2,1)S(1)} %collective-permute-done.1.refs_0_.refs_4_, ...), custom_call_target="tpu_custom_call" | custom-call | flops 805306368 | bytes 786432 | tf_op jit(solution)/shard_map/weight_grad_part/pallas_call | solution.py:84
  71.4 0.7 copy-done.11
  72.2 3.1 %collective-permute-start.3 = (f32[384,256]{1,0:T(8,128)}, f32[384,256]{1,0:T(8,128)}, u32[]{:S(2)}, u32[]{:S(2)}) collective-permute-start(f32[384,256]{1,0:T(8,128)} %get-tuple-element.13), channel_id=1, source_target_pairs={{0,16},{4,20},{8,24},{12,28},{16,0},{20,4},{24,8},{28,12},{1,17},{... | collective-permute-start | bytes 1179656 | tf_op jit(solution)/shard_map/ppermute | solution.py:222
  75.2 1.1 copy-done.1
  76.4 1.1 copy-done.4
  77.5 3.6 %weight_grad_part.3 = (f32[384,512]{1,0:T(8,128)S(1)}, f32[384,512]{1,0:T(8,128)S(1)}) custom-call(s32[4]{0:T(128)S(1)} %pad_add_fusion.where_ref, s32[4,12,12]{2,1,0:T(8,128)S(1)} %copy.15.mask_ref, bf16[128,3072]{1,0:T(8,128)(2,1)S(1)} %copy-done.1, bf16[768,768]{1,0:T(8,128)(2,1)S(1)} %collective-permute-done.1.refs_0_.refs_4_, ...), custom_call_target="tpu_custom_call" | custom-call | flops 1610612736 | bytes 1572864 | tf_op jit(solution)/shard_map/weight_grad_part/pallas_call | solution.py:84
  81.1 0.0 copy-start.9
  81.1 0.9 copy-done.9
  82.0 0.9 copy-done.13
  82.9 9.9 %collective-permute-done.3 = f32[384,256]{1,0:T(8,128)} collective-permute-done((f32[384,256]{1,0:T(8,128)}, f32[384,256]{1,0:T(8,128)}, u32[]{:S(2)}, u32[]{:S(2)}) %collective-permute-start.3) | collective-permute-done | bytes 393248 | tf_op jit(solution)/shard_map/ppermute | solution.py:222
  92.8 0.0 collective-permute-done.4.rest_1_
  92.8 0.0 collective-permute-done.6.rest_3_
  92.8 8.8 %forward_and_input.1 = (f32[4,128,768]{2,1,0:T(8,128)S(1)}, f32[3,4,128,256]{3,2,1,0:T(8,128)S(1)}, f32[4,256,384]{2,1,0:T(8,128)S(1)}) custom-call(s32[4]{0:T(128)S(1)} %pad_add_fusion.where_ref, s32[4,12,12]{2,1,0:T(8,128)S(1)} %copy.15.mask_ref, bf16[128,3072]{1,0:T(8,128)(2,1)S(1)} %copy-done.1, ...), custom_call_target="tpu_custom_call" | custom-call | flops 10871635968 | bytes 9437184 | tf_op jit(solution)/shard_map/forward_and_input/pallas_call | solution.py:171
  101.6 1.2 copy-done.5
  102.7 1.2 copy-done.7
  103.9 0.9 dynamic-slice_bitcast_fusion
  104.9 0.0 collective-permute-start.11
  104.9 0.5 copy-done.14
  105.3 0.0 collective-permute-start.10
  105.3 2.0 %collective-permute-done.11 = f32[2,256,384]{2,1,0:T(8,128)S(1)} collective-permute-done((f32[2,256,384]{2,1,0:T(8,128)}, f32[2,256,384]{2,1,0:T(8,128)S(1)}, u32[]{:S(2)}, u32[]{:S(2)}) %collective-permute-start.11) | collective-permute-done | bytes 786464 | tf_op jit(solution)/shard_map/ppermute | solution.py:231
  107.3 0.1 bitcast_add_fusion
  107.4 0.0 copy-start.15
  107.4 0.9 dynamic-slice_bitcast_fusion.1
  108.3 1.5 %collective-permute-start.12 = (f32[256,384]{1,0:T(8,128)}, f32[256,384]{1,0:T(8,128)}, u32[]{:S(2)}, u32[]{:S(2)}) collective-permute-start(f32[256,384]{1,0:T(8,128)} %dynamic-slice_bitcast_fusion.1), channel_id=1, source_target_pairs={{0,2},{1,3},{2,0},{3,1},{4,6},{5,7},{6,4},{7,5},{8,10},{9,11},{10,... | collective-permute-start | bytes 1179656 | tf_op jit(solution)/shard_map/ppermute | solution.py:231
  109.8 1.3 slice_bitcast_fusion.2
  111.1 0.5 collective-permute-start.7
  111.7 1.5 collective-permute-start.9
  113.1 0.5 collective-permute-start.8
  113.7 1.0 add.83
  114.7 27.0 %collective-permute-done.10 = f32[384,512]{1,0:T(8,128)} collective-permute-done((f32[384,512]{1,0:T(8,128)S(1)}, f32[384,512]{1,0:T(8,128)}, u32[]{:S(2)}, u32[]{:S(2)}) %collective-permute-start.10) | collective-permute-done | bytes 786464 | tf_op jit(solution)/shard_map/ppermute | solution.py:222
  141.7 1.3 add.84
  143.0 0.0 copy-start.16
  143.0 1.1 pad_maximum_fusion.2
  144.1 0.0 collective-permute-done.12
  144.1 0.3 copy-done.16
  144.5 1.0 fusion.3
  145.5 0.6 collective-permute-start.13
  146.1 0.0 collective-permute-done.7
  146.1 0.0 collective-permute-done.9
  146.1 1.5 collective-permute-done.8
  147.6 2.1 %fusion = bf16[4,128,768]{2,1,0:T(8,128)(2,1)} fusion(f32[4,128,768]{2,1,0:T(8,128)S(1)} %copy-done.8, f32[4,128,256]{2,1,0:T(8,128)S(1)} %collective-permute-done.9, f32[4,128,256]{2,1,0:T(8,128)} %collective-permute-done.8, f32[4,128,256]{2,1,0:T(8,128)S(1)} %collective-permute-done.7), kind=kLoop, calls=%fused_computation.1 | loop fusion | flops 1572864 | bytes 3932160 | tf_op jit(solution)/shard_map/convert_element_type | solution.py:278
  149.7 0.6 collective-permute-done.13
  150.3 0.7 pad_maximum_fusion.3
  (29 shorter events, 0.2 us)
Async XLA Ops:
  3.6 1.7 %copy-start.2 = (bf16[4,128,768]{2,1,0:T(8,128)(2,1)S(1)}, bf16[4,128,768]{2,1,0:T(8,128)(2,1)}, u32[]{:S(2)}) copy-start(bf16[4,128,768]{2,1,0:T(8,128)(2,1)} %og_ref) | copy-start | bytes 2359300
  5.4 29.1 %collective-permute-start.1 = (bf16[768,768]{1,0:T(8,128)(2,1)S(1)}, bf16[768,768]{1,0:T(8,128)(2,1)S(1)}, u32[]{:S(2)}, u32[]{:S(2)}) collective-permute-start(bf16[768,768]{1,0:T(8,128)(2,1)S(1)} %get-tuple-element.26), channel_id=1, source_target_pairs={{0,8},{4,12},{8,0},{12,4},{16,24},{20,28},{24,16},{28,20},{1,9},{5... | collective-permute-start | bytes 3538952 | tf_op jit(solution)/shard_map/ppermute | solution.py:222
  8.5 27.4 %collective-permute-start = (bf16[768,768]{1,0:T(8,128)(2,1)S(1)}, bf16[768,768]{1,0:T(8,128)(2,1)S(1)}, u32[]{:S(2)}, u32[]{:S(2)}) collective-permute-start(bf16[768,768]{1,0:T(8,128)(2,1)S(1)} %get-tuple-element.27), channel_id=1, source_target_pairs={{0,4},{4,0},{8,12},{12,8},{16,20},{20,16},{24,28},{28,24},{1,5},{5... | collective-permute-start | bytes 3538952 | tf_op jit(solution)/shard_map/ppermute | solution.py:222
  36.0 30.1 %copy-start.17 = (s32[4,12,12]{2,0,1:T(4,128)S(1)}, s32[4,12,12]{2,0,1:T(4,128)}, u32[]{:S(2)}) copy-start(s32[4,12,12]{2,0,1:T(4,128)} %param.6) | copy-start | bytes 6916
  37.1 29.1 %collective-permute-start.2 = (bf16[640,768]{1,0:T(8,128)(2,1)}, bf16[640,768]{1,0:T(8,128)(2,1)S(1)}, u32[]{:S(2)}, u32[]{:S(2)}) collective-permute-start(bf16[640,768]{1,0:T(8,128)(2,1)} %maximum_maximum_fusion), channel_id=1, source_target_pairs={{0,4},{4,0},{8,12},{12,8},{16,20},{20,16},{24,28},{28,24},{1,5},{5... | collective-permute-start | bytes 2949128 | tf_op jit(solution)/shard_map/ppermute | solution.py:222
  38.6 27.6 %collective-permute-start.5 = (bf16[384,768]{1,0:T(8,128)(2,1)}, bf16[384,768]{1,0:T(8,128)(2,1)}, u32[]{:S(2)}, u32[]{:S(2)}) collective-permute-start(bf16[384,768]{1,0:T(8,128)(2,1)} %rest_0_.1), channel_id=1, source_target_pairs={{0,16},{4,20},{8,24},{12,28},{16,0},{20,4},{24,8},{28,12},{1,17},{... | collective-permute-start | bytes 1769480 | tf_op jit(solution)/shard_map/ppermute | solution.py:222
  41.1 51.6 %collective-permute-start.4 = (bf16[384,768]{1,0:T(8,128)(2,1)}, bf16[384,768]{1,0:T(8,128)(2,1)}, u32[]{:S(2)}, u32[]{:S(2)}) collective-permute-start(bf16[384,768]{1,0:T(8,128)(2,1)} %rest_0_.1), channel_id=1, source_target_pairs={{0,8},{4,12},{8,0},{12,4},{16,24},{20,28},{24,16},{28,20},{1,9},{5... | collective-permute-start | bytes 1769480 | tf_op jit(solution)/shard_map/ppermute | solution.py:222
  66.1 26.7 %collective-permute-start.6 = (bf16[384,768]{1,0:T(8,128)(2,1)}, bf16[384,768]{1,0:T(8,128)(2,1)}, u32[]{:S(2)}, u32[]{:S(2)}) collective-permute-start(bf16[384,768]{1,0:T(8,128)(2,1)} %collective-permute-done.5.rest_2_), channel_id=1, source_target_pairs={{0,8},{4,12},{8,0},{12,4},{16,24},{20,28},{24,16},{28,20},{1,9},{5... | collective-permute-start | bytes 1769480 | tf_op jit(solution)/shard_map/ppermute | solution.py:222
  66.2 1.1 copy-start
  67.4 1.1 copy-start.3
  71.4 0.7 copy-start.11
  72.2 20.6 %collective-permute-start.3 = (f32[384,256]{1,0:T(8,128)}, f32[384,256]{1,0:T(8,128)}, u32[]{:S(2)}, u32[]{:S(2)}) collective-permute-start(f32[384,256]{1,0:T(8,128)} %get-tuple-element.13), channel_id=1, source_target_pairs={{0,16},{4,20},{8,24},{12,28},{16,0},{20,4},{24,8},{28,12},{1,17},{... | collective-permute-start | bytes 1179656 | tf_op jit(solution)/shard_map/ppermute | solution.py:222
  75.2 1.1 copy-start.1
  76.4 1.1 copy-start.4
  81.1 0.9 copy-start.9
  82.0 0.9 copy-start.13
  101.6 1.2 copy-start.5
  102.7 1.2 copy-start.7
  103.9 1.4 copy-start.14
  104.9 2.5 %collective-permute-start.11 = (f32[2,256,384]{2,1,0:T(8,128)}, f32[2,256,384]{2,1,0:T(8,128)S(1)}, u32[]{:S(2)}, u32[]{:S(2)}) collective-permute-start(f32[2,256,384]{2,1,0:T(8,128)} %dynamic-slice_bitcast_fusion), channel_id=1, source_target_pairs={{0,1},{1,0},{2,3},{3,2},{4,5},{5,4},{6,7},{7,6},{8,9},{9,8},{10,11... | collective-permute-start | bytes 2359304 | tf_op jit(solution)/shard_map/ppermute | solution.py:231
  105.3 4.5 %copy-start.6 = (f32[3,4,128,256]{3,2,1,0:T(8,128)S(1)}, f32[3,4,128,256]{3,2,1,0:T(8,128)}, u32[]{:S(2)}) copy-start(f32[3,4,128,256]{3,2,1,0:T(8,128)} %copy-done.5) | copy-start | bytes 4718596
  105.3 36.4 %collective-permute-start.10 = (f32[384,512]{1,0:T(8,128)S(1)}, f32[384,512]{1,0:T(8,128)}, u32[]{:S(2)}, u32[]{:S(2)}) collective-permute-start(f32[384,512]{1,0:T(8,128)S(1)} %copy-done.14), channel_id=1, source_target_pairs={{0,16},{4,20},{8,24},{12,28},{16,0},{20,4},{24,8},{28,12},{1,17},{... | collective-permute-start | bytes 2359304 | tf_op jit(solution)/shard_map/ppermute | solution.py:222
  107.4 2.4 %copy-start.15 = (f32[2,256,384]{2,1,0:T(8,128)}, f32[2,256,384]{2,1,0:T(8,128)S(1)}, u32[]{:S(2)}) copy-start(f32[2,256,384]{2,1,0:T(8,128)S(1)} %bitcast_add_fusion) | copy-start | bytes 2359300
  108.3 35.8 %collective-permute-start.12 = (f32[256,384]{1,0:T(8,128)}, f32[256,384]{1,0:T(8,128)}, u32[]{:S(2)}, u32[]{:S(2)}) collective-permute-start(f32[256,384]{1,0:T(8,128)} %dynamic-slice_bitcast_fusion.1), channel_id=1, source_target_pairs={{0,2},{1,3},{2,0},{3,1},{4,6},{5,7},{6,4},{7,5},{8,10},{9,11},{10,... | collective-permute-start | bytes 1179656 | tf_op jit(solution)/shard_map/ppermute | solution.py:231
  109.8 3.9 %copy-start.12 = (f32[384,256]{1,0:T(8,128)S(1)}, f32[384,256]{1,0:T(8,128)}, u32[]{:S(2)}) copy-start(f32[384,256]{1,0:T(8,128)} %copy-done.11) | copy-start | bytes 1179652
  109.8 31.9 %copy-start.10 = (f32[384,512]{1,0:T(8,128)S(1)}, f32[384,512]{1,0:T(8,128)}, u32[]{:S(2)}) copy-start(f32[384,512]{1,0:T(8,128)} %copy-done.9) | copy-start | bytes 2359300
  111.1 35.0 %collective-permute-start.7 = (f32[4,128,256]{2,1,0:T(8,128)}, f32[4,128,256]{2,1,0:T(8,128)S(1)}, u32[]{:S(2)}, u32[]{:S(2)}) collective-permute-start(f32[4,128,256]{2,1,0:T(8,128)} %get-tuple-element.21), channel_id=1, source_target_pairs={{0,4},{4,0},{8,12},{12,8},{16,20},{20,16},{24,28},{28,24},{1,5},{5... | collective-permute-start | bytes 1572872 | tf_op jit(solution)/shard_map/ppermute | solution.py:222
  111.7 34.5 %collective-permute-start.9 = (f32[4,128,256]{2,1,0:T(8,128)}, f32[4,128,256]{2,1,0:T(8,128)S(1)}, u32[]{:S(2)}, u32[]{:S(2)}) collective-permute-start(f32[4,128,256]{2,1,0:T(8,128)} %get-tuple-element.22), channel_id=1, source_target_pairs={{0,4},{4,0},{8,12},{12,8},{16,20},{20,16},{24,28},{28,24},{1,5},{5... | collective-permute-start | bytes 1572872 | tf_op jit(solution)/shard_map/ppermute | solution.py:222
  113.1 34.4 %collective-permute-start.8 = (f32[4,128,256]{2,1,0:T(8,128)}, f32[4,128,256]{2,1,0:T(8,128)}, u32[]{:S(2)}, u32[]{:S(2)}) collective-permute-start(f32[4,128,256]{2,1,0:T(8,128)} %get-tuple-element.23), channel_id=1, source_target_pairs={{0,4},{4,0},{8,12},{12,8},{16,20},{20,16},{24,28},{28,24},{1,5},{5... | collective-permute-start | bytes 1572872 | tf_op jit(solution)/shard_map/ppermute | solution.py:222
  143.0 1.4 copy-start.16
  143.0 4.6 %copy-start.8 = (f32[4,128,768]{2,1,0:T(8,128)S(1)}, f32[4,128,768]{2,1,0:T(8,128)}, u32[]{:S(2)}) copy-start(f32[4,128,768]{2,1,0:T(8,128)} %copy-done.7) | copy-start | bytes 4718596
  145.5 4.8 %collective-permute-start.13 = (bf16[128,384]{1,0:T(8,128)(2,1)S(1)}, bf16[128,384]{1,0:T(8,128)(2,1)S(1)}, u32[]{:S(2)}, u32[]{:S(2)}) collective-permute-start(bf16[128,384]{1,0:T(8,128)(2,1)S(1)} %slice.21), channel_id=1, source_target_pairs={{0,4},{4,0},{8,12},{12,8},{16,20},{20,16},{24,28},{28,24},{1,5},{5... | collective-permute-start | bytes 294920 | tf_op jit(solution)/shard_map/ppermute | solution.py:222

commit v8 on v7

--- a/solution.py
+++ b/solution.py
@@ -10,7 +10,8 @@
 LANES = 128
 F32 = jnp.float32
 BF16 = jnp.bfloat16
-VMEM_BYTES = 40 * 1024 * 1024
+PART_VMEM = 16 * 1024 * 1024
+FORWARD_VMEM = 28 * 1024 * 1024
 
 
 def plain(acts, weight, block_mask, out_grad):
@@ -94,7 +95,7 @@
         + [pl.BlockSpec((flat, BS), lambda j: (0, chunk + j))] * ng,
         out_specs=(out, out),
         scratch_shapes=[pltpu.VMEM((ng, 2 * rows, tokens), BF16)],
-        compiler_params=pltpu.CompilerParams(vmem_limit_bytes=VMEM_BYTES),
+        compiler_params=pltpu.CompilerParams(vmem_limit_bytes=PART_VMEM),
         cost_estimate=pl.CostEstimate(
             flops=4 * ng * rows * made * flat, bytes_accessed=8 * rows * made, transcendentals=0
         ),
@@ -110,7 +111,7 @@
     per = rows // LANES
 
     def kernel(where_ref, mask_ref, acts_ref, sacts_ref, og_ref, sog_ref, *rest):
-        w_refs, (keep_ref, send_ref, gx_ref, acc, hilo) = rest[:nz], rest[nz:]
+        w_refs, (keep_ref, send_ref, rest_ref, gx_ref, acc, hilo) = rest[:nz], rest[nz:]
         z, x = where_ref[0], where_ref[1]
         step = pl.program_id(0)
         col = where_ref[2] + step
@@ -162,7 +163,16 @@
                 acc[s] = term if k == 0 else acc[s] + term
         for s in range(nsub):
             keep_ref[s] = acc[s, :tokens]
-            send_ref[0, s] = acc[s, tokens:]
+
+        @pl.when(first)
+        def _():
+            for s in range(nsub):
+                send_ref[s] = acc[s, tokens:]
+
+        @pl.when(step > 0)
+        def _():
+            for s in range(nsub):
+                rest_ref[0, s] = acc[s, tokens:]
 
     smem = pl.BlockSpec(memory_space=pltpu.SMEM)
     by_col = pl.BlockSpec((nsub, tokens, BS), lambda j: (0, 0, j))
@@ -173,7 +183,8 @@
         grid=(width // BS,),
         out_shape=(
             jax.ShapeDtypeStruct((nsub, tokens, width), F32),
-            jax.ShapeDtypeStruct((width // BS, nsub, tokens, BS), F32),
+            jax.ShapeDtypeStruct((nsub, tokens, BS), F32),
+            jax.ShapeDtypeStruct((width // BS - 1, nsub, tokens, BS), F32),
             jax.ShapeDtypeStruct(gx_shape, F32),
         ),
         in_specs=[
@@ -187,14 +198,15 @@
         + [pl.BlockSpec((rows, BS), lambda j: (0, j))] * nz,
         out_specs=(
             by_col,
-            pl.BlockSpec((1, nsub, tokens, BS), lambda j: (j, 0, 0, 0)),
+            pl.BlockSpec((nsub, tokens, BS), lambda j: (0, 0, 0)),
+            pl.BlockSpec((1, nsub, tokens, BS), lambda j: (jnp.maximum(j - 1, 0), 0, 0, 0)),
             pl.BlockSpec(gx_shape, lambda j: (0, 0, 0)),
         ),
         scratch_shapes=[
             pltpu.VMEM((nsub, 2 * tokens, BS), F32),
             pltpu.VMEM((nz, 2, 4 * tokens, BS), BF16),
         ],
-        compiler_params=pltpu.CompilerParams(vmem_limit_bytes=VMEM_BYTES),
+        compiler_params=pltpu.CompilerParams(vmem_limit_bytes=FORWARD_VMEM),
         cost_estimate=pl.CostEstimate(
             flops=36 * tokens * nz * 2 * rows * width,
             bytes_accessed=4 * nz * 2 * rows * width,
@@ -262,31 +274,38 @@
 
     w_two = swap_z(weight, 2)
     w_one = swap_z(weight, 1)
-    w_three = swap_z(w_two, 1)
 
     og = [own, one, side, both]
-    keep_0, send = weight_grad_part(acts, og, block_mask, where, rows, 0, 1)
-    got_0 = swap_z(send, 2)
-    keep_1, send = weight_grad_part(acts, og, block_mask, where, rows, 1, width // BS - 1)
-    got_1 = swap_z(send, 2)
-    grad_w = jnp.concatenate([keep_0 + got_0, keep_1 + got_1], axis=1)
-
-    mine, theirs, gx = forward_and_input(
-        acts, side, after(out_grad, got_0, keep_1), [weight, w_one, w_two, w_three], block_mask, where
-    )
-    got = jnp.concatenate([swap_x(t) for t in theirs], axis=2)
-    outputs = (mine + got).astype(BF16)
-
-    by = gx.reshape(2, 2, 2 * tokens, rows)
-    pair = lax.dynamic_index_in_dim(by, c, 1, keepdims=False) + swap_f(
-        lax.dynamic_index_in_dim(by, 1 - c, 1, keepdims=False), 1
-    )
+    keeps, gots = [], []
+    for j in range(width // BS):
+        keep, send = weight_grad_part(acts, og, block_mask, where, rows, j, 1)
+        keeps.append(keep)
+        gots.append(swap_z(send, 2))
+    grad_w = jnp.concatenate([k + g for k, g in zip(keeps, gots)], axis=1)
+    w_three = swap_z(after(w_two, keeps[0]), 1)
+
+    mine_out, first, rest, gx = forward_and_input(
+        acts,
+        side,
+        after(out_grad, gots[0], *keeps[1:]),
+        [weight, w_one, w_two, w_three],
+        block_mask,
+        where,
+    )
+
+    by = after(gx, gots[1]).reshape(2, 2, 2 * tokens, rows)
+    pair = swap_f(lax.dynamic_index_in_dim(by, 1 - c, 1, keepdims=False), 1)
+    first = swap_x(first)
+    rest = swap_x(after(rest, pair))
+    pair = after(pair, first) + lax.dynamic_index_in_dim(by, c, 1, keepdims=False)
     done = lax.dynamic_index_in_dim(pair, y, 0, keepdims=False) + swap_f(
         lax.dynamic_index_in_dim(pair, 1 - y, 0, keepdims=False), 2
     )
     done = done.astype(BF16)
     mine, got = done[:tokens], swap_x(done[tokens:])
     low, high = jnp.where(x == 0, mine, got), jnp.where(x == 0, got, mine)
+    got = jnp.concatenate([first] + [rest[j] for j in range(rest.shape[0])], axis=2)
+    outputs = (mine_out + got).astype(BF16)
     return (outputs, grad_w, jnp.concatenate([low, high], axis=1))
 
 

time: 152 us -> 153 us (level)
  local copies, waits for them, and re-layouts: 17.9 us -> 15 us
  Pallas kernels: 15.3 us -> 17.9 us
  waiting for transfers between devices: 91.5 us -> 93.6 us
    unnamed x37 -> x35, local copies, waits for them, and re-layouts: 10.2 us -> 8.11 us
    ppermute x12, waiting for transfers between devices: 89.5 us -> 91.2 us  [swap_dp(): return lax.ppermute(a, 'dp', [(d, d ^ bits) for d in range(dp)])]
    pallas_call x2 -> x3, Pallas kernels: 6.52 us -> 8.05 us  [weight_grad_part(): pl.pallas_call(kernel, grid=(chunks,), out_shape=(jax.ShapeDtypeStruct((r...]
    add x3 -> x4, other arithmetic: 2.4 us -> 3.22 us  [the longest x3 3.14 us: on_device(): grad_w = jnp.concatenate([k + g for k, g in zip(keeps, gots)], axis=1)]
  transfers between devices with their start and end apart: 14 -> 14, of which waited for: 8 -> 10; matrix products, arithmetic and copies ran while one was open for 6% -> 3% of each run, Pallas kernels for 4% -> 12%
where the time goes in v8:
time: 153 us; the launch traced here: 152 us
  waiting for transfers between devices  93.6 us (61%)
  Pallas kernels  17.9 us (12%)
  starting transfers between devices  16.6 us (11%)
  local copies, waits for them, and re-layouts  15 us (10%)
  other arithmetic  8.4 us (5%)
    ppermute x12, waiting for transfers between devices, swap_dp(): return lax.ppermute(a, 'dp', [(d, d ^ bits) for d in range(dp)])  91.2 us
    ppermute x12, starting transfers between devices, swap_dp(): return lax.ppermute(a, 'dp', [(d, d ^ bits) for d in range(dp)])  15 us
    pallas_call x1, Pallas kernels, forward_and_input(): pl.pallas_call(kernel, grid=(width // BS,), out_shape=(jax.ShapeDtypeStru...  9.82 us
    unnamed x35, local copies, waits for them, and re-layouts  8.11 us
    pallas_call x3, Pallas kernels, weight_grad_part(): pl.pallas_call(kernel, grid=(chunks,), out_shape=(jax.ShapeDtypeStruct((r...  8.05 us
    add x3, other arithmetic, on_device(): grad_w = jnp.concatenate([k + g for k, g in zip(keeps, gots)], axis=1)  3.14 us
  transfers between devices with their start and end apart: 14, of which 10 were waited for; matrix products, arithmetic and copies ran while one was open for 3% of the time, Pallas kernels for 12%

profile of v8, /device:TPU:0, one launch (start us, length us, event | category | flops | bytes accessed | tf_op | source)
XLA Modules:
  0.0 152.4 jit_solution(11092352528926917095)
XLA Ops:
  0.7 2.0 %reshape.20 = bf16[128,4,768]{2,1,0:T(4,128)(2,1)S(1)} reshape(bf16[128,3072]{1,0:T(8,128)(2,1)} %acts_ref.7) | data formatting | bytes 1572864 | tf_op jit(solution)/shard_map/reshape | solution.py:251
  2.7 0.8 constant_dynamic-slice_fusion.3
  3.6 0.0 copy-start.3
  3.6 1.6 %constant_dynamic-slice_fusion.7 = (bf16[128,1,384]{2,1,0:T(2,128)(2,1)S(1)}, bf16[128,1,384]{2,1,0:T(2,128)(2,1)S(1)}, bf16[128,1,384]{2,1,0:T(2,128)(2,1)S(1)}, bf16[128,1,384]{2,1,0:T(2,128)(2,1)S(1)}) fusion(bf16[128,4,768]{2,1,0:T(4,128)(2,1)S(1)} %reshape.20, s32[]{:T(128)S(6)} %select_n.81, s32[]{:T(128)S(6)} %select_n.83, s32[]{:T(128)S(6)} %select_n.89, ...), kind=kLoop, calls=%fused_computation.31 | loop fusion | bytes 786452 | tf_op jit(solution)/shard_map/dynamic_slice | solution.py:257
  5.2 0.2 fusion.2
  5.4 3.1 %collective-permute-start.1 = (bf16[768,768]{1,0:T(8,128)(2,1)S(1)}, bf16[768,768]{1,0:T(8,128)(2,1)S(1)}, u32[]{:S(2)}, u32[]{:S(2)}) collective-permute-start(bf16[768,768]{1,0:T(8,128)(2,1)S(1)} %get-tuple-element.39), channel_id=1, source_target_pairs={{0,8},{4,12},{8,0},{12,4},{16,24},{20,28},{24,16},{28,20},{1,9},{5... | collective-permute-start | bytes 3538952 | tf_op jit(solution)/shard_map/ppermute | solution.py:234
  8.5 1.5 collective-permute-start
  10.0 24.5 %collective-permute-done.1.refs_0_.refs_4_ = bf16[768,768]{1,0:T(8,128)(2,1)S(1)} collective-permute-done((bf16[768,768]{1,0:T(8,128)(2,1)S(1)}, bf16[768,768]{1,0:T(8,128)(2,1)S(1)}, u32[]{:S(2)}, u32[]{:S(2)}) %collective-permute-start.1) | collective-permute-done | bytes 1179680 | tf_op jit(solution)/shard_map/ppermute | solution.py:234
  34.5 1.5 collective-permute-done.refs_1_.refs_5_.sacts_ref.sog_ref
  35.9 0.1 slice.21
  36.0 0.0 copy-start.16
  36.1 1.0 maximum_maximum_fusion
  37.1 1.5 collective-permute-start.2
  38.6 2.6 %collective-permute-start.5 = (bf16[384,768]{1,0:T(8,128)(2,1)}, bf16[384,768]{1,0:T(8,128)(2,1)}, u32[]{:S(2)}, u32[]{:S(2)}) collective-permute-start(bf16[384,768]{1,0:T(8,128)(2,1)} %rest_0_.1), channel_id=1, source_target_pairs={{0,16},{4,20},{8,24},{12,28},{16,0},{20,4},{24,8},{28,12},{1,17},{... | collective-permute-start | bytes 1769480 | tf_op jit(solution)/shard_map/ppermute | solution.py:234
  41.1 0.4 collective-permute-start.4
  41.6 0.1 pad_add_fusion.where_ref
  41.7 17.9 %collective-permute-done.2.refs_2_.refs_6_ = bf16[640,768]{1,0:T(8,128)(2,1)S(1)} collective-permute-done((bf16[640,768]{1,0:T(8,128)(2,1)}, bf16[640,768]{1,0:T(8,128)(2,1)S(1)}, u32[]{:S(2)}, u32[]{:S(2)}) %collective-permute-start.2) | collective-permute-done | bytes 983072 | tf_op jit(solution)/shard_map/ppermute | solution.py:234
  59.6 1.1 copy-done
  60.7 1.1 copy-done.4
  61.9 2.9 %weight_grad_part.3 = (f32[384,256]{1,0:T(8,128)S(1)}, f32[384,256]{1,0:T(8,128)}) custom-call(s32[4]{0:T(128)S(1)} %pad_add_fusion.where_ref, s32[4,12,12]{2,1,0:T(8,128)S(1)} %copy.16.mask_ref, bf16[128,3072]{1,0:T(8,128)(2,1)S(1)} %copy-done, bf16[768,768]{1,0:T(8,128)(2,1)S(1)} %collective-permute-done.1.refs_0_.refs_4_, ...), custom_call_target="tpu_custom_call" | custom-call | flops 805306368 | bytes 786432 | tf_op jit(solution)/shard_map/weight_grad_part/pallas_call | solution.py:85
  64.8 0.8 copy-done.9
  65.6 0.6 collective-permute-done.5.rest_2_
  66.1 0.1 collective-permute-start.6
  66.2 3.0 %collective-permute-start.3 = (f32[384,256]{1,0:T(8,128)}, f32[384,256]{1,0:T(8,128)}, u32[]{:S(2)}, u32[]{:S(2)}) collective-permute-start(f32[384,256]{1,0:T(8,128)} %get-tuple-element.20), channel_id=1, source_target_pairs={{0,16},{4,20},{8,24},{12,28},{16,0},{20,4},{24,8},{28,12},{1,17},{... | collective-permute-start | bytes 1179656 | tf_op jit(solution)/shard_map/ppermute | solution.py:234
  69.2 1.1 copy-done.1
  70.3 1.1 copy-done.5
  71.5 2.2 %weight_grad_part.4 = (f32[384,256]{1,0:T(8,128)S(1)}, f32[384,256]{1,0:T(8,128)S(1)}) custom-call(s32[4]{0:T(128)S(1)} %pad_add_fusion.where_ref, s32[4,12,12]{2,1,0:T(8,128)S(1)} %copy.16.mask_ref, bf16[128,3072]{1,0:T(8,128)(2,1)S(1)} %copy-done.1, bf16[768,768]{1,0:T(8,128)(2,1)S(1)} %collective-permute-done.1.refs_0_.refs_4_, ...), custom_call_target="tpu_custom_call" | custom-call | flops 805306368 | bytes 786432 | tf_op jit(solution)/shard_map/weight_grad_part/pallas_call | solution.py:85
  73.7 0.7 copy-done.13
  74.4 0.0 collective-permute-start.8
  74.4 2.9 %weight_grad_part.5 = (f32[384,256]{1,0:T(8,128)S(1)}, f32[384,256]{1,0:T(8,128)}) custom-call(s32[4]{0:T(128)S(1)} %pad_add_fusion.where_ref, s32[4,12,12]{2,1,0:T(8,128)S(1)} %copy.16.mask_ref, bf16[128,3072]{1,0:T(8,128)(2,1)S(1)} %copy-done.1, bf16[768,768]{1,0:T(8,128)(2,1)S(1)} %collective-permute-done.1.refs_0_.refs_4_, ...), custom_call_target="tpu_custom_call" | custom-call | flops 805306368 | bytes 786432 | tf_op jit(solution)/shard_map/weight_grad_part/pallas_call | solution.py:85
  77.3 0.8 copy-done.11
  78.1 10.6 %collective-permute-done.3 = f32[384,256]{1,0:T(8,128)} collective-permute-done((f32[384,256]{1,0:T(8,128)}, f32[384,256]{1,0:T(8,128)}, u32[]{:S(2)}, u32[]{:S(2)}) %collective-permute-start.3) | collective-permute-done | bytes 393248 | tf_op jit(solution)/shard_map/ppermute | solution.py:234
  88.7 0.0 collective-permute-done.4.rest_1_
  88.7 4.6 %collective-permute-done.6.rest_3_ = bf16[384,768]{1,0:T(8,128)(2,1)} collective-permute-done((bf16[384,768]{1,0:T(8,128)(2,1)}, bf16[384,768]{1,0:T(8,128)(2,1)}, u32[]{:S(2)}, u32[]{:S(2)}) %collective-permute-start.6) | collective-permute-done | bytes 589856 | tf_op jit(solution)/shard_map/ppermute | solution.py:234
  93.3 0.0 copy-done.2
  93.3 9.8 %forward_and_input.1 = (f32[4,128,768]{2,1,0:T(8,128)S(1)}, f32[4,128,256]{2,1,0:T(8,128)S(1)}, f32[2,4,128,256]{3,2,1,0:T(8,128)}, f32[4,256,384]{2,1,0:T(8,128)S(1)}) custom-call(s32[4]{0:T(128)S(1)} %pad_add_fusion.where_ref, s32[4,12,12]{2,1,0:T(8,128)S(1)} %copy.16.mask_ref, bf16[128,3072]{1,0:T(8,128)(2,1)S(1)} %copy-done.2, ...), custom_call_target="tpu_custom_call" | custom-call | flops 10871635968 | bytes 9437184 | tf_op jit(solution)/shard_map/forward_and_input/pallas_call | solution.py:181
  103.2 1.2 copy-done.7
  104.3 0.0 collective-permute-done.8
  104.3 1.0 dynamic-slice_bitcast_fusion
  105.3 0.0 collective-permute-start.9
  105.3 0.1 copy-done.15
  105.4 0.9 collective-permute-start.7
  106.3 0.0 collective-permute-start.11
  106.3 13.4 %collective-permute-done.7 = f32[4,128,256]{2,1,0:T(8,128)} collective-permute-done((f32[4,128,256]{2,1,0:T(8,128)S(1)}, f32[4,128,256]{2,1,0:T(8,128)}, u32[]{:S(2)}, u32[]{:S(2)}) %collective-permute-start.7) | collective-permute-done | bytes 524320 | tf_op jit(solution)/shard_map/ppermute | solution.py:234
  119.8 0.0 collective-permute-done.9
  119.8 0.1 bitcast_add_fusion
  119.9 0.0 copy-start.10
  119.9 0.0 copy-start.12
  119.9 1.6 %collective-permute-start.12 = (f32[256,384]{1,0:T(8,128)S(1)}, f32[256,384]{1,0:T(8,128)S(1)}, u32[]{:S(2)}, u32[]{:S(2)}) collective-permute-start(f32[256,384]{1,0:T(8,128)S(1)} %dynamic-slice_bitcast_fusion.1), channel_id=1, source_target_pairs={{0,2},{1,3},{2,0},{3,1},{4,6},{5,7},{6,4},{7,5},{8,10},{9,11},{10,... | collective-permute-start | bytes 1179656 | tf_op jit(solution)/shard_map/ppermute | solution.py:243
  121.5 0.9 collective-permute-start.10
  122.4 0.0 copy-done.14
  122.4 1.0 add.88
  123.5 1.0 add.87
  124.5 2.6 %collective-permute-done.11 = f32[384,256]{1,0:T(8,128)} collective-permute-done((f32[384,256]{1,0:T(8,128)}, f32[384,256]{1,0:T(8,128)}, u32[]{:S(2)}, u32[]{:S(2)}) %collective-permute-start.11) | collective-permute-done | bytes 393248 | tf_op jit(solution)/shard_map/ppermute | solution.py:234
  127.1 0.0 copy-done.12
  127.1 1.0 add.89
  128.2 2.5 %collective-permute-done.12 = f32[256,384]{1,0:T(8,128)S(1)} collective-permute-done((f32[256,384]{1,0:T(8,128)S(1)}, f32[256,384]{1,0:T(8,128)S(1)}, u32[]{:S(2)}, u32[]{:S(2)}) %collective-permute-start.12) | collective-permute-done | bytes 393248 | tf_op jit(solution)/shard_map/ppermute | solution.py:243
  130.7 1.0 collective-permute-start.13
  131.7 1.1 pad_maximum_fusion.2
  132.8 15.5 %collective-permute-done.13 = bf16[128,384]{1,0:T(8,128)(2,1)S(1)} collective-permute-done((bf16[128,384]{1,0:T(8,128)(2,1)S(1)}, bf16[128,384]{1,0:T(8,128)(2,1)S(1)}, u32[]{:S(2)}, u32[]{:S(2)}) %collective-permute-start.13) | collective-permute-done | bytes 98336 | tf_op jit(solution)/shard_map/ppermute | solution.py:234
  148.3 0.7 pad_maximum_fusion.3
  149.0 0.0 collective-permute-done.10
  149.0 1.3 slice_bitcast_fusion.1
  150.3 2.1 %fusion = bf16[4,128,768]{2,1,0:T(8,128)(2,1)} fusion(f32[4,128,768]{2,1,0:T(8,128)S(1)} %copy-done.8, f32[4,128,256]{2,1,0:T(8,128)S(1)} %get-tuple-element.38, f32[4,128,256]{2,1,0:T(8,128)S(1)} %get-tuple-element.37, f32[4,128,256]{2,1,0:T(8,128)} %collective-permute-done.7), kind=kLoop, calls=%fused_computation.1 | loop fusion | flops 1572864 | bytes 3932160 | tf_op jit(solution)/shard_map/convert_element_type | solution.py:308
  (29 shorter events, 0.3 us)
Async XLA Ops:
  3.6 1.7 %copy-start.3 = (bf16[4,128,768]{2,1,0:T(8,128)(2,1)S(1)}, bf16[4,128,768]{2,1,0:T(8,128)(2,1)}, u32[]{:S(2)}) copy-start(bf16[4,128,768]{2,1,0:T(8,128)(2,1)} %og_ref) | copy-start | bytes 2359300
  5.4 29.1 %collective-permute-start.1 = (bf16[768,768]{1,0:T(8,128)(2,1)S(1)}, bf16[768,768]{1,0:T(8,128)(2,1)S(1)}, u32[]{:S(2)}, u32[]{:S(2)}) collective-permute-start(bf16[768,768]{1,0:T(8,128)(2,1)S(1)} %get-tuple-element.39), channel_id=1, source_target_pairs={{0,8},{4,12},{8,0},{12,4},{16,24},{20,28},{24,16},{28,20},{1,9},{5... | collective-permute-start | bytes 3538952 | tf_op jit(solution)/shard_map/ppermute | solution.py:234
  8.5 27.4 %collective-permute-start = (bf16[768,768]{1,0:T(8,128)(2,1)S(1)}, bf16[768,768]{1,0:T(8,128)(2,1)S(1)}, u32[]{:S(2)}, u32[]{:S(2)}) collective-permute-start(bf16[768,768]{1,0:T(8,128)(2,1)S(1)} %get-tuple-element.40), channel_id=1, source_target_pairs={{0,4},{4,0},{8,12},{12,8},{16,20},{20,16},{24,28},{28,24},{1,5},{5... | collective-permute-start | bytes 3538952 | tf_op jit(solution)/shard_map/ppermute | solution.py:234
  36.0 5.6 %copy-start.16 = (s32[4,12,12]{2,0,1:T(4,128)S(1)}, s32[4,12,12]{2,0,1:T(4,128)}, u32[]{:S(2)}) copy-start(s32[4,12,12]{2,0,1:T(4,128)} %param.6) | copy-start | bytes 6916
  37.1 22.5 %collective-permute-start.2 = (bf16[640,768]{1,0:T(8,128)(2,1)}, bf16[640,768]{1,0:T(8,128)(2,1)S(1)}, u32[]{:S(2)}, u32[]{:S(2)}) collective-permute-start(bf16[640,768]{1,0:T(8,128)(2,1)} %maximum_maximum_fusion), channel_id=1, source_target_pairs={{0,4},{4,0},{8,12},{12,8},{16,20},{20,16},{24,28},{28,24},{1,5},{5... | collective-permute-start | bytes 2949128 | tf_op jit(solution)/shard_map/ppermute | solution.py:234
  38.6 27.6 %collective-permute-start.5 = (bf16[384,768]{1,0:T(8,128)(2,1)}, bf16[384,768]{1,0:T(8,128)(2,1)}, u32[]{:S(2)}, u32[]{:S(2)}) collective-permute-start(bf16[384,768]{1,0:T(8,128)(2,1)} %rest_0_.1), channel_id=1, source_target_pairs={{0,16},{4,20},{8,24},{12,28},{16,0},{20,4},{24,8},{28,12},{1,17},{... | collective-permute-start | bytes 1769480 | tf_op jit(solution)/shard_map/ppermute | solution.py:234
  41.1 47.6 %collective-permute-start.4 = (bf16[384,768]{1,0:T(8,128)(2,1)}, bf16[384,768]{1,0:T(8,128)(2,1)}, u32[]{:S(2)}, u32[]{:S(2)}) collective-permute-start(bf16[384,768]{1,0:T(8,128)(2,1)} %rest_0_.1), channel_id=1, source_target_pairs={{0,8},{4,12},{8,0},{12,4},{16,24},{20,28},{24,16},{28,20},{1,9},{5... | collective-permute-start | bytes 1769480 | tf_op jit(solution)/shard_map/ppermute | solution.py:234
  59.6 1.1 copy-start
  60.7 1.1 copy-start.4
  64.8 0.8 copy-start.9
  66.1 27.2 %collective-permute-start.6 = (bf16[384,768]{1,0:T(8,128)(2,1)}, bf16[384,768]{1,0:T(8,128)(2,1)}, u32[]{:S(2)}, u32[]{:S(2)}) collective-permute-start(bf16[384,768]{1,0:T(8,128)(2,1)} %collective-permute-done.5.rest_2_), channel_id=1, source_target_pairs={{0,8},{4,12},{8,0},{12,4},{16,24},{20,28},{24,16},{28,20},{1,9},{5... | collective-permute-start | bytes 1769480 | tf_op jit(solution)/shard_map/ppermute | solution.py:234
  66.2 22.5 %collective-permute-start.3 = (f32[384,256]{1,0:T(8,128)}, f32[384,256]{1,0:T(8,128)}, u32[]{:S(2)}, u32[]{:S(2)}) collective-permute-start(f32[384,256]{1,0:T(8,128)} %get-tuple-element.20), channel_id=1, source_target_pairs={{0,16},{4,20},{8,24},{12,28},{16,0},{20,4},{24,8},{28,12},{1,17},{... | collective-permute-start | bytes 1179656 | tf_op jit(solution)/shard_map/ppermute | solution.py:234
  69.2 1.1 copy-start.1
  70.3 1.1 copy-start.5
  73.7 0.7 copy-start.13
  74.4 18.9 %copy-start.2 = (bf16[128,3072]{1,0:T(8,128)(2,1)S(1)}, bf16[128,3072]{1,0:T(8,128)(2,1)}, u32[]{:S(2)}) copy-start(bf16[128,3072]{1,0:T(8,128)(2,1)} %acts_ref.7) | copy-start | bytes 2359300
  74.4 18.9 %copy-start.6 = (bf16[4,128,768]{2,1,0:T(8,128)(2,1)S(1)}, bf16[4,128,768]{2,1,0:T(8,128)(2,1)}, u32[]{:S(2)}) copy-start(bf16[4,128,768]{2,1,0:T(8,128)(2,1)} %og_ref) | copy-start | bytes 2359300
  74.4 29.9 %collective-permute-start.8 = (f32[384,256]{1,0:T(8,128)S(1)}, f32[384,256]{1,0:T(8,128)S(1)}, u32[]{:S(2)}, u32[]{:S(2)}) collective-permute-start(f32[384,256]{1,0:T(8,128)S(1)} %get-tuple-element.30), channel_id=1, source_target_pairs={{0,16},{4,20},{8,24},{12,28},{16,0},{20,4},{24,8},{28,12},{1,17},{... | collective-permute-start | bytes 1179656 | tf_op jit(solution)/shard_map/ppermute | solution.py:234
  77.3 0.8 copy-start.11
  103.2 1.2 copy-start.7
  104.3 1.1 copy-start.15
  105.3 14.5 %collective-permute-start.9 = (f32[2,256,384]{2,1,0:T(8,128)}, f32[2,256,384]{2,1,0:T(8,128)S(1)}, u32[]{:S(2)}, u32[]{:S(2)}) collective-permute-start(f32[2,256,384]{2,1,0:T(8,128)} %dynamic-slice_bitcast_fusion), channel_id=1, source_target_pairs={{0,1},{1,0},{2,3},{3,2},{4,5},{5,4},{6,7},{7,6},{8,9},{9,8},{10,11... | collective-permute-start | bytes 2359304 | tf_op jit(solution)/shard_map/ppermute | solution.py:243
  105.4 14.4 %collective-permute-start.7 = (f32[4,128,256]{2,1,0:T(8,128)S(1)}, f32[4,128,256]{2,1,0:T(8,128)}, u32[]{:S(2)}, u32[]{:S(2)}) collective-permute-start(f32[4,128,256]{2,1,0:T(8,128)S(1)} %get-tuple-element.27), channel_id=1, source_target_pairs={{0,4},{4,0},{8,12},{12,8},{16,20},{20,16},{24,28},{28,24},{1,5},{5... | collective-permute-start | bytes 1572872 | tf_op jit(solution)/shard_map/ppermute | solution.py:234
  106.3 16.1 %copy-start.14 = (f32[384,256]{1,0:T(8,128)S(1)}, f32[384,256]{1,0:T(8,128)}, u32[]{:S(2)}) copy-start(f32[384,256]{1,0:T(8,128)} %copy-done.13) | copy-start | bytes 1179652
  106.3 20.8 %collective-permute-start.11 = (f32[384,256]{1,0:T(8,128)}, f32[384,256]{1,0:T(8,128)}, u32[]{:S(2)}, u32[]{:S(2)}) collective-permute-start(f32[384,256]{1,0:T(8,128)} %get-tuple-element.33), channel_id=1, source_target_pairs={{0,16},{4,20},{8,24},{12,28},{16,0},{20,4},{24,8},{28,12},{1,17},{... | collective-permute-start | bytes 1179656 | tf_op jit(solution)/shard_map/ppermute | solution.py:234
  119.9 3.6 %copy-start.10 = (f32[384,256]{1,0:T(8,128)S(1)}, f32[384,256]{1,0:T(8,128)}, u32[]{:S(2)}) copy-start(f32[384,256]{1,0:T(8,128)} %copy-done.9) | copy-start | bytes 1179652
  119.9 7.3 %copy-start.12 = (f32[384,256]{1,0:T(8,128)S(1)}, f32[384,256]{1,0:T(8,128)}, u32[]{:S(2)}) copy-start(f32[384,256]{1,0:T(8,128)} %copy-done.11) | copy-start | bytes 1179652
  119.9 10.7 %collective-permute-start.12 = (f32[256,384]{1,0:T(8,128)S(1)}, f32[256,384]{1,0:T(8,128)S(1)}, u32[]{:S(2)}, u32[]{:S(2)}) collective-permute-start(f32[256,384]{1,0:T(8,128)S(1)} %dynamic-slice_bitcast_fusion.1), channel_id=1, source_target_pairs={{0,2},{1,3},{2,0},{3,1},{4,6},{5,7},{6,4},{7,5},{8,10},{9,11},{10,... | collective-permute-start | bytes 1179656 | tf_op jit(solution)/shard_map/ppermute | solution.py:243
  121.5 27.5 %collective-permute-start.10 = (f32[2,4,128,256]{3,2,1,0:T(8,128)}, f32[2,4,128,256]{3,2,1,0:T(8,128)}, u32[]{:S(2)}, u32[]{:S(2)}) collective-permute-start(f32[2,4,128,256]{3,2,1,0:T(8,128)} %get-tuple-element.32), channel_id=1, source_target_pairs={{0,4},{4,0},{8,12},{12,8},{16,20},{20,16},{24,28},{28,24},{1,5},{5... | collective-permute-start | bytes 3145736 | tf_op jit(solution)/shard_map/ppermute | solution.py:234
  130.7 17.6 %collective-permute-start.13 = (bf16[128,384]{1,0:T(8,128)(2,1)S(1)}, bf16[128,384]{1,0:T(8,128)(2,1)S(1)}, u32[]{:S(2)}, u32[]{:S(2)}) collective-permute-start(bf16[128,384]{1,0:T(8,128)(2,1)S(1)} %slice.31), channel_id=1, source_target_pairs={{0,4},{4,0},{8,12},{12,8},{16,20},{20,16},{24,28},{28,24},{1,5},{5... | collective-permute-start | bytes 294920 | tf_op jit(solution)/shard_map/ppermute | solution.py:234
  132.8 17.5 %copy-start.8 = (f32[4,128,768]{2,1,0:T(8,128)S(1)}, f32[4,128,768]{2,1,0:T(8,128)}, u32[]{:S(2)}) copy-start(f32[4,128,768]{2,1,0:T(8,128)} %copy-done.7) | copy-start | bytes 4718596

commit v9 on v6

--- a/solution.py
+++ b/solution.py
@@ -10,7 +10,8 @@
 LANES = 128
 F32 = jnp.float32
 BF16 = jnp.bfloat16
-VMEM_BYTES = 40 * 1024 * 1024
+PART_VMEM = 16 * 1024 * 1024
+FORWARD_VMEM = 28 * 1024 * 1024
 
 
 def plain(acts, weight, block_mask, out_grad):
@@ -36,65 +37,70 @@
     return (forward.astype(BF16), grad_w, grad_x)
 
 
-def weight_grad_part(acts_in, og, block_mask, where, rows, chunk):
+def weight_grad_part(acts, og, block_mask, where, rows, chunk, chunks):
     nsub = block_mask.shape[0]
-    fresh = acts_in.ndim == 2
-    tokens = acts_in.shape[0] if fresh else acts_in.shape[2]
+    tokens = acts.shape[0]
     flat = nsub * tokens
     ng = len(og)
     per = rows // LANES
+    width = og[0].shape[1]
+    made = chunks * BS
 
     def kernel(where_ref, mask_ref, acts_ref, *refs):
-        og_refs, outs = refs[:ng], refs[ng:]
+        extra, og_refs, outs, tiles = refs[:3], refs[3 : 3 + ng], refs[3 + ng : -1], refs[-1]
         z, x = where_ref[0], where_ref[1]
-        for r in range(2):
-            zz = z ^ (2 * r)
-            for g in range(per):
-                start = (zz * 2 + x) * rows + g * LANES
-                block = start // BS
-                at = slice(g * LANES, (g + 1) * LANES)
-                dst = slice((r * per + g) * LANES, (r * per + g + 1) * LANES)
-                if fresh:
+        step = pl.program_id(0)
+        col = where_ref[2] + chunk + step
+
+        @pl.when(step == 0)
+        def _():
+            one_ref, side_ref, both_ref = extra
+            for r in range(2):
+                for g in range(per):
+                    start = ((z ^ (2 * r)) * 2 + x) * rows + g * LANES
                     here = pl.ds(pl.multiple_of(start, LANES), LANES)
                     there = pl.ds(pl.multiple_of(x * rows + g * LANES, LANES), LANES)
-                    own_ref, one_ref, side_ref, both_ref = og_refs
-                    tiles = [
-                        acts_ref[:, here].T,
-                        one_ref[flat + r * tokens : flat + (r + 1) * tokens, there].T,
-                        side_ref[flat : flat + tokens, dst].T,
-                        both_ref[flat : flat + tokens, dst].T,
-                    ]
-                    for k, t in enumerate(tiles):
-                        outs[2][k, dst, :] = t
-                else:
-                    tiles = [acts_ref[k, dst, :] for k in range(ng)]
-                col = where_ref[2] + chunk
+                    dst = slice((r * per + g) * LANES, (r * per + g + 1) * LANES)
+                    tiles[0, dst, :] = acts_ref[:, here].T
+                    tiles[1, dst, :] = one_ref[r * tokens : (r + 1) * tokens, there].T
+                    tiles[2, dst, :] = side_ref[:, dst].T
+                    tiles[3, dst, :] = both_ref[:, dst].T
+
+        for r in range(2):
+            for g in range(per):
+                block = (((z ^ (2 * r)) * 2 + x) * rows + g * LANES) // BS
+                dst = slice((r * per + g) * LANES, (r * per + g + 1) * LANES)
                 keep = [mask_ref[s, block, col].astype(F32) for s in range(nsub)]
                 keep = [jnp.full((LANES, tokens), k).astype(BF16) for k in keep]
                 total = None
-                for t, o_ref in zip(tiles, og_refs):
-                    lhs = jnp.concatenate([t * k for k in keep], axis=1)
-                    rhs = o_ref[:flat, chunk * BS : (chunk + 1) * BS]
-                    term = jnp.dot(lhs, rhs, preferred_element_type=F32)
+                for k in range(ng):
+                    t = tiles[k, dst, :]
+                    lhs = jnp.concatenate([t * m for m in keep], axis=1)
+                    term = jnp.dot(lhs, og_refs[k][...], preferred_element_type=F32)
                     total = term if total is None else total + term
-                outs[r][at, :] = total * (1.0 / TOK_G)
+                outs[r][g * LANES : (g + 1) * LANES, :] = total * (1.0 / TOK_G)
 
     smem = pl.BlockSpec(memory_space=pltpu.SMEM)
-    vmem = pl.BlockSpec(memory_space=pltpu.VMEM)
-    shapes = [jax.ShapeDtypeStruct((rows, BS), F32)] * 2
-    if fresh:
-        shapes.append(jax.ShapeDtypeStruct((ng, 2 * rows, tokens), BF16))
+    out = pl.BlockSpec((rows, BS), lambda j: (0, j))
     return pl.pallas_call(
         kernel,
-        out_shape=tuple(shapes),
-        in_specs=[smem, smem] + [vmem] * (1 + ng),
-        out_specs=(vmem,) * len(shapes),
-        compiler_params=pltpu.CompilerParams(vmem_limit_bytes=VMEM_BYTES),
+        grid=(chunks,),
+        out_shape=(jax.ShapeDtypeStruct((rows, made), F32),) * 2,
+        in_specs=[smem, smem, pl.BlockSpec(acts.shape, lambda j: (0, 0))]
+        + [
+            pl.BlockSpec((2 * tokens, width), lambda j: (flat // (2 * tokens), 0)),
+            pl.BlockSpec((tokens, width), lambda j: (flat // tokens, 0)),
+            pl.BlockSpec((tokens, width), lambda j: (flat // tokens, 0)),
+        ]
+        + [pl.BlockSpec((flat, BS), lambda j: (0, chunk + j))] * ng,
+        out_specs=(out, out),
+        scratch_shapes=[pltpu.VMEM((ng, 2 * rows, tokens), BF16)],
+        compiler_params=pltpu.CompilerParams(vmem_limit_bytes=PART_VMEM),
         cost_estimate=pl.CostEstimate(
-            flops=4 * ng * rows * BS * flat, bytes_accessed=8 * rows * BS, transcendentals=0
+            flops=4 * ng * rows * made * flat, bytes_accessed=8 * rows * made, transcendentals=0
         ),
         name="weight_grad_part",
-    )(where, block_mask, acts_in, *og)
+    )(where, block_mask, acts, *og[1:], *og)
 
 
 def forward_and_input(acts, w_mine, w_peer, og, block_mask, where):
@@ -162,7 +168,7 @@
             pltpu.VMEM((nsub, tokens, BS), F32),
             pltpu.VMEM((depth // BS, 2 * tokens, BS), BF16),
         ],
-        compiler_params=pltpu.CompilerParams(vmem_limit_bytes=VMEM_BYTES),
+        compiler_params=pltpu.CompilerParams(vmem_limit_bytes=FORWARD_VMEM),
         cost_estimate=pl.CostEstimate(
             flops=36 * tokens * depth * width, bytes_accessed=4 * depth * width, transcendentals=0
         ),
@@ -216,7 +222,8 @@
             [own, jnp.concatenate([of_x(acts_of(0), 1 - x), of_x(acts_of(2), 1 - x)], axis=1)]
         )
     )
-    one = after(one, side)
+    w_peer = [swap_x(weight)]
+    one = after(one, side, w_peer[0])
     passed = [
         of_x(one[flat + r * tokens : flat + (r + 1) * tokens], 1 - x) for r in range(2)
     ]
@@ -224,26 +231,20 @@
 
     w_two = swap_z(weight, 2)
     w_one = swap_z(weight, 1)
-    w_three = swap_z(w_two, 1)
+    w_peer += [swap_x(w_one), swap_x(w_two)]
+    og = [own, one, side, both]
+    keeps, gots = [], []
+    for j in range(width // BS):
+        keep, send = weight_grad_part(acts, og, block_mask, where, rows, j, 1)
+        keeps.append(keep)
+        gots.append(swap_z(send, 2))
+    w_three = swap_z(after(w_two, keeps[0]), 1)
     w_mine = [weight, w_one, w_two, w_three]
-    w_peer = [swap_x(after(weight, both))]
-
-    og = [own, one, side, both]
-    acts_in = acts
-    grads = []
-    for j in range(width // BS):
-        ready = ((w_two,), (w_peer[0],), (w_peer[0], *[got for _, got in grads[:1]]))[j]
-        keep, send, *made = weight_grad_part(
-            acts_in, og, block_mask, after(where, *ready), rows, j
-        )
-        if made:
-            acts_in = made[0]
-        grads.append((keep, swap_z(send, 2)))
-        w_peer.append(swap_x(after(w_mine[j + 1], keep)))
-    grad_w = jnp.concatenate([keep + got for keep, got in grads], axis=1)
+    w_peer.append(swap_x(after(w_three, *w_peer[1:], gots[0], keeps[1])))
+    grad_w = jnp.concatenate([k + g for k, g in zip(keeps, gots)], axis=1)
 
     outputs, gx = forward_and_input(
-        acts, w_mine, w_peer, after(out_grad, grads[1][1], grads[2][1]), block_mask, where
+        acts, w_mine, w_peer, after(out_grad, gots[1], keeps[2]), block_mask, where
     )
 
     by = gx.reshape(2, 2, tokens, depth // 4)

time: 160 us -> 152 us (0.950)
  waiting for transfers between devices: 103 us -> 92.5 us
  other arithmetic: 3.37 us -> 7.42 us
  starting transfers between devices: 22.8 us -> 20.1 us
    ppermute x2, waiting for transfers between devices: 11 us -> 1.54 us  [swap_f(): return lax.ppermute(a, 'fsdp', [(d, d ^ bit) for d in range(fsdp)])]
    ppermute x13, starting transfers between devices: 21.3 us -> 18.5 us  [swap_dp(): return lax.ppermute(a, 'dp', [(d, d ^ bits) for d in range(dp)])]
    unnamed x41 -> x49, local copies, waits for them, and re-layouts: 8.94 us -> 11.1 us
    add x3, other arithmetic: 0.15 us -> 2.14 us  [on_device(): grad_w = jnp.concatenate([k + g for k, g in zip(keeps, gots)], axis=1)]
  transfers between devices with their start and end apart: 15 -> 15, of which waited for: 9 -> 8; matrix products, arithmetic and copies ran while one was open for 1% -> 4% of each run, Pallas kernels for 5% -> 5%
where the time goes in v9:
time: 152 us
  waiting for transfers between devices  92.5 us (61%)
  starting transfers between devices  20.1 us (13%)
  local copies, waits for them, and re-layouts  15.7 us (10%)
  Pallas kernels  15.1 us (10%)
  other arithmetic  7.42 us (5%)
    ppermute x13, waiting for transfers between devices, swap_dp(): return lax.ppermute(a, 'dp', [(d, d ^ bits) for d in range(dp)])  91 us
    ppermute x13, starting transfers between devices, swap_dp(): return lax.ppermute(a, 'dp', [(d, d ^ bits) for d in range(dp)])  18.5 us
    unnamed x49, local copies, waits for them, and re-layouts  11.1 us
    pallas_call x1, Pallas kernels, forward_and_input(): pl.pallas_call(kernel, grid=(width // BS,), out_shape=(jax.ShapeDtypeStru...  7.81 us
    pallas_call x3, Pallas kernels, weight_grad_part(): pl.pallas_call(kernel, grid=(chunks,), out_shape=(jax.ShapeDtypeStruct((r...  7.3 us
  transfers between devices with their start and end apart: 15, of which 8 were waited for; matrix products, arithmetic and copies ran while one was open for 4% of the time, Pallas kernels for 5%

profile of v9, /device:TPU:0, one launch (start us, length us, event | category | flops | bytes accessed | tf_op | source)
XLA Modules:
  0.0 151.8 jit_solution(947601541099074013)
XLA Ops:
  0.7 2.0 %reshape.18 = bf16[128,4,768]{2,1,0:T(4,128)(2,1)S(1)} reshape(bf16[128,3072]{1,0:T(8,128)(2,1)} %acts_ref.7) | data formatting | bytes 1572864 | tf_op jit(solution)/shard_map/reshape | solution.py:211
  2.6 0.0 copy-start
  2.7 0.8 constant_dynamic-slice_fusion.5
  3.5 0.2 copy-done
  3.8 1.1 pad_maximum_fusion
  4.9 3.0 %collective-permute-start = (bf16[768,768]{1,0:T(8,128)(2,1)}, bf16[768,768]{1,0:T(8,128)(2,1)S(1)}, u32[]{:S(2)}, u32[]{:S(2)}) collective-permute-start(bf16[768,768]{1,0:T(8,128)(2,1)} %pad_maximum_fusion), channel_id=1, source_target_pairs={{0,8},{4,12},{8,0},{12,4},{16,24},{20,28},{24,16},{28,20},{1,9},{5... | collective-permute-start | bytes 3538952 | tf_op jit(solution)/shard_map/ppermute | solution.py:194
  7.9 0.8 constant_dynamic-slice_fusion.3
  8.7 0.1 maximum_maximum_fusion
  8.8 1.5 %collective-permute-start.1 = (bf16[640,768]{1,0:T(8,128)(2,1)S(1)}, bf16[640,768]{1,0:T(8,128)(2,1)S(1)}, u32[]{:S(2)}, u32[]{:S(2)}) collective-permute-start(bf16[640,768]{1,0:T(8,128)(2,1)S(1)} %maximum_maximum_fusion), channel_id=1, source_target_pairs={{0,4},{4,0},{8,12},{12,8},{16,20},{20,16},{24,28},{28,24},{1,5},{5... | collective-permute-start | bytes 2949128 | tf_op jit(solution)/shard_map/ppermute | solution.py:194
  10.4 0.5 collective-permute-start.2
  10.9 33.8 %collective-permute-done.2.rest_4_ = bf16[384,768]{1,0:T(8,128)(2,1)S(1)} collective-permute-done((bf16[384,768]{1,0:T(8,128)(2,1)}, bf16[384,768]{1,0:T(8,128)(2,1)S(1)}, u32[]{:S(2)}, u32[]{:S(2)}) %collective-permute-start.2) | collective-permute-done | bytes 589856 | tf_op jit(solution)/shard_map/ppermute | solution.py:194
  44.7 0.8 copy-done.13
  45.6 0.0 collective-permute-done.1.refs_1_.refs_5_
  45.6 0.0 collective-permute-done.refs_0_.refs_4_
  45.6 0.1 slice.9
  45.6 0.0 copy-start.23
  45.7 1.0 maximum_maximum_fusion.1
  46.7 1.5 collective-permute-start.3
  48.2 0.4 collective-permute-start.5
  48.7 2.6 %collective-permute-start.6 = (bf16[384,768]{1,0:T(8,128)(2,1)}, bf16[384,768]{1,0:T(8,128)(2,1)}, u32[]{:S(2)}, u32[]{:S(2)}) collective-permute-start(bf16[384,768]{1,0:T(8,128)(2,1)} %rest_0_.1), channel_id=1, source_target_pairs={{0,16},{4,20},{8,24},{12,28},{16,0},{20,4},{24,8},{28,12},{1,17},{... | collective-permute-start | bytes 1769480 | tf_op jit(solution)/shard_map/ppermute | solution.py:194
  51.3 0.1 pad_add_fusion.where_ref
  51.3 23.4 %collective-permute-done.5.rest_1_ = bf16[384,768]{1,0:T(8,128)(2,1)} collective-permute-done((bf16[384,768]{1,0:T(8,128)(2,1)}, bf16[384,768]{1,0:T(8,128)(2,1)}, u32[]{:S(2)}, u32[]{:S(2)}) %collective-permute-start.5) | collective-permute-done | bytes 589856 | tf_op jit(solution)/shard_map/ppermute | solution.py:194
  74.8 0.5 collective-permute-start.8
  75.3 0.0 collective-permute-done.6.rest_2_
  75.3 1.5 collective-permute-start.9
  76.8 0.0 collective-permute-done.3.refs_2_.refs_6_
  76.8 1.1 copy-done.1
  77.9 1.1 copy-done.4
  79.1 2.2 %weight_grad_part.5 = (f32[384,256]{1,0:T(8,128)S(1)}, f32[384,256]{1,0:T(8,128)S(1)}) custom-call(s32[4]{0:T(128)S(1)} %pad_add_fusion.where_ref, s32[4,12,12]{2,1,0:T(8,128)S(1)} %copy.14.mask_ref, bf16[128,3072]{1,0:T(8,128)(2,1)S(1)} %copy-done.4, bf16[768,768]{1,0:T(8,128)(2,1)S(1)} %collective-permute-done.refs_0_.refs_4_, ...), custom_call_target="tpu_custom_call" | custom-call | flops 805306368 | bytes 786432 | tf_op jit(solution)/shard_map/weight_grad_part/pallas_call | solution.py:85
  81.3 1.2 collective-permute-start.7
  82.4 2.7 %collective-permute-start.10 = (f32[384,256]{1,0:T(8,128)S(1)}, f32[384,256]{1,0:T(8,128)S(1)}, u32[]{:S(2)}, u32[]{:S(2)}) collective-permute-start(f32[384,256]{1,0:T(8,128)S(1)} %get-tuple-element.21), channel_id=1, source_target_pairs={{0,16},{4,20},{8,24},{12,28},{16,0},{20,4},{24,8},{28,12},{1,17},{... | collective-permute-start | bytes 1179656 | tf_op jit(solution)/shard_map/ppermute | solution.py:194
  85.1 2.9 %weight_grad_part.3 = (f32[384,256]{1,0:T(8,128)S(1)}, f32[384,256]{1,0:T(8,128)}) custom-call(s32[4]{0:T(128)S(1)} %pad_add_fusion.where_ref, s32[4,12,12]{2,1,0:T(8,128)S(1)} %copy.14.mask_ref, bf16[128,3072]{1,0:T(8,128)(2,1)S(1)} %copy-done.4, bf16[768,768]{1,0:T(8,128)(2,1)S(1)} %collective-permute-done.refs_0_.refs_4_, ...), custom_call_target="tpu_custom_call" | custom-call | flops 805306368 | bytes 786432 | tf_op jit(solution)/shard_map/weight_grad_part/pallas_call | solution.py:85
  88.1 0.8 copy-done.9
  88.8 2.4 %collective-permute-done.8.rest_5_ = bf16[384,768]{1,0:T(8,128)(2,1)S(1)} collective-permute-done((bf16[384,768]{1,0:T(8,128)(2,1)}, bf16[384,768]{1,0:T(8,128)(2,1)S(1)}, u32[]{:S(2)}, u32[]{:S(2)}) %collective-permute-start.8) | collective-permute-done | bytes 589856 | tf_op jit(solution)/shard_map/ppermute | solution.py:194
  91.2 0.8 copy-done.15
  92.1 9.7 %collective-permute-done.9.rest_6_ = bf16[384,768]{1,0:T(8,128)(2,1)S(1)} collective-permute-done((bf16[384,768]{1,0:T(8,128)(2,1)}, bf16[384,768]{1,0:T(8,128)(2,1)S(1)}, u32[]{:S(2)}, u32[]{:S(2)}) %collective-permute-start.9) | collective-permute-done | bytes 589856 | tf_op jit(solution)/shard_map/ppermute | solution.py:194
  101.7 0.8 copy-done.17
  102.5 0.7 copy-done.21
  103.3 0.3 collective-permute-done.7.rest_3_
  103.6 0.4 collective-permute-start.11
  104.0 2.6 %collective-permute-start.4 = (f32[384,256]{1,0:T(8,128)}, f32[384,256]{1,0:T(8,128)}, u32[]{:S(2)}, u32[]{:S(2)}) collective-permute-start(f32[384,256]{1,0:T(8,128)} %get-tuple-element.16), channel_id=1, source_target_pairs={{0,16},{4,20},{8,24},{12,28},{16,0},{20,4},{24,8},{28,12},{1,17},{... | collective-permute-start | bytes 1179656 | tf_op jit(solution)/shard_map/ppermute | solution.py:194
  106.6 1.1 copy-done.2
  107.7 1.1 copy-done.5
  108.9 2.2 %weight_grad_part.4 = (f32[384,256]{1,0:T(8,128)S(1)}, f32[384,256]{1,0:T(8,128)S(1)}) custom-call(s32[4]{0:T(128)S(1)} %pad_add_fusion.where_ref, s32[4,12,12]{2,1,0:T(8,128)S(1)} %copy.14.mask_ref, bf16[128,3072]{1,0:T(8,128)(2,1)S(1)} %copy-done.5, bf16[768,768]{1,0:T(8,128)(2,1)S(1)} %collective-permute-done.refs_0_.refs_4_, ...), custom_call_target="tpu_custom_call" | custom-call | flops 805306368 | bytes 786432 | tf_op jit(solution)/shard_map/weight_grad_part/pallas_call | solution.py:85
  111.1 0.7 copy-done.11
  111.8 0.8 copy-done.19
  112.6 9.8 %collective-permute-done.4 = f32[384,256]{1,0:T(8,128)} collective-permute-done((f32[384,256]{1,0:T(8,128)}, f32[384,256]{1,0:T(8,128)}, u32[]{:S(2)}, u32[]{:S(2)}) %collective-permute-start.4) | collective-permute-done | bytes 393248 | tf_op jit(solution)/shard_map/ppermute | solution.py:194
  122.4 0.0 collective-permute-done.11.rest_7_
  122.5 7.8 %forward_and_input.1 = (bf16[4,128,768]{2,1,0:T(8,128)(2,1)}, f32[4,128,768]{2,1,0:T(8,128)S(1)}) custom-call(s32[4]{0:T(128)S(1)} %pad_add_fusion.where_ref, s32[4,12,12]{2,1,0:T(8,128)S(1)} %copy.14.mask_ref, bf16[128,3072]{1,0:T(8,128)(2,1)S(1)} %copy-done.6, bf16[4,128,768]{2,1,0:T(8,128)(2,1)S(1)} %copy-done.3, bf16[384,768]{1,0:T(8,128)(2,1)} %rest_0_.1, ...), custom_call_target="tpu_custom_call" | custom-call | flops 10871635968 | bytes 9437184 | tf_op jit(solution)/shard_map/forward_and_input/pallas_call | solution.py:157
  130.3 0.1 dynamic-slice_bitcast_fusion
  130.3 0.1 collective-permute-start.13
  130.5 0.8 copy-done.20
  131.3 0.0 collective-permute-start.12
  131.3 1.5 %collective-permute-done.13 = f32[2,128,768]{2,1,0:T(8,128)} collective-permute-done((f32[2,128,768]{2,1,0:T(8,128)S(1)}, f32[2,128,768]{2,1,0:T(8,128)}, u32[]{:S(2)}, u32[]{:S(2)}) %collective-permute-start.13) | collective-permute-done | bytes 786464 | tf_op jit(solution)/shard_map/ppermute | solution.py:203
  132.8 1.2 bitcast_add_fusion
  134.1 0.8 dynamic-slice_bitcast_fusion.1
  134.9 1.5 collective-permute-start.14
  136.4 1.0 add.73
  137.4 0.1 add.72
  137.5 11.5 %collective-permute-done.12 = f32[384,256]{1,0:T(8,128)} collective-permute-done((f32[384,256]{1,0:T(8,128)S(1)}, f32[384,256]{1,0:T(8,128)}, u32[]{:S(2)}, u32[]{:S(2)}) %collective-permute-start.12) | collective-permute-done | bytes 393248 | tf_op jit(solution)/shard_map/ppermute | solution.py:194
  149.0 1.0 add.74
  150.0 1.1 pad_maximum_fusion.1
  151.1 0.0 collective-permute-done.14
  151.1 0.7 fusion
  (40 shorter events, 0.2 us)
Async XLA Ops:
  2.6 1.1 copy-start
  4.9 40.7 %collective-permute-start = (bf16[768,768]{1,0:T(8,128)(2,1)}, bf16[768,768]{1,0:T(8,128)(2,1)S(1)}, u32[]{:S(2)}, u32[]{:S(2)}) collective-permute-start(bf16[768,768]{1,0:T(8,128)(2,1)} %pad_maximum_fusion), channel_id=1, source_target_pairs={{0,8},{4,12},{8,0},{12,4},{16,24},{20,28},{24,16},{28,20},{1,9},{5... | collective-permute-start | bytes 3538952 | tf_op jit(solution)/shard_map/ppermute | solution.py:194
  8.8 36.7 %collective-permute-start.1 = (bf16[640,768]{1,0:T(8,128)(2,1)S(1)}, bf16[640,768]{1,0:T(8,128)(2,1)S(1)}, u32[]{:S(2)}, u32[]{:S(2)}) collective-permute-start(bf16[640,768]{1,0:T(8,128)(2,1)S(1)} %maximum_maximum_fusion), channel_id=1, source_target_pairs={{0,4},{4,0},{8,12},{12,8},{16,20},{20,16},{24,28},{28,24},{1,5},{5... | collective-permute-start | bytes 2949128 | tf_op jit(solution)/shard_map/ppermute | solution.py:194
  10.4 34.4 %collective-permute-start.2 = (bf16[384,768]{1,0:T(8,128)(2,1)}, bf16[384,768]{1,0:T(8,128)(2,1)S(1)}, u32[]{:S(2)}, u32[]{:S(2)}) collective-permute-start(bf16[384,768]{1,0:T(8,128)(2,1)} %rest_0_.1), channel_id=1, source_target_pairs={{0,4},{4,0},{8,12},{12,8},{16,20},{20,16},{24,28},{28,24},{1,5},{5... | collective-permute-start | bytes 1769480 | tf_op jit(solution)/shard_map/ppermute | solution.py:194
  44.7 0.8 copy-start.13
  45.6 5.6 %copy-start.23 = (s32[4,12,12]{2,0,1:T(4,128)S(1)}, s32[4,12,12]{2,0,1:T(4,128)}, u32[]{:S(2)}) copy-start(s32[4,12,12]{2,0,1:T(4,128)} %param.6) | copy-start | bytes 6916
  46.7 30.1 %collective-permute-start.3 = (bf16[640,768]{1,0:T(8,128)(2,1)}, bf16[640,768]{1,0:T(8,128)(2,1)S(1)}, u32[]{:S(2)}, u32[]{:S(2)}) collective-permute-start(bf16[640,768]{1,0:T(8,128)(2,1)} %maximum_maximum_fusion.1), channel_id=1, source_target_pairs={{0,4},{4,0},{8,12},{12,8},{16,20},{20,16},{24,28},{28,24},{1,5},{5... | collective-permute-start | bytes 2949128 | tf_op jit(solution)/shard_map/ppermute | solution.py:194
  48.2 26.6 %collective-permute-start.5 = (bf16[384,768]{1,0:T(8,128)(2,1)}, bf16[384,768]{1,0:T(8,128)(2,1)}, u32[]{:S(2)}, u32[]{:S(2)}) collective-permute-start(bf16[384,768]{1,0:T(8,128)(2,1)} %rest_0_.1), channel_id=1, source_target_pairs={{0,8},{4,12},{8,0},{12,4},{16,24},{20,28},{24,16},{28,20},{1,9},{5... | collective-permute-start | bytes 1769480 | tf_op jit(solution)/shard_map/ppermute | solution.py:194
  48.7 26.6 %collective-permute-start.6 = (bf16[384,768]{1,0:T(8,128)(2,1)}, bf16[384,768]{1,0:T(8,128)(2,1)}, u32[]{:S(2)}, u32[]{:S(2)}) collective-permute-start(bf16[384,768]{1,0:T(8,128)(2,1)} %rest_0_.1), channel_id=1, source_target_pairs={{0,16},{4,20},{8,24},{12,28},{16,0},{20,4},{24,8},{28,12},{1,17},{... | collective-permute-start | bytes 1769480 | tf_op jit(solution)/shard_map/ppermute | solution.py:194
  74.8 16.5 %collective-permute-start.8 = (bf16[384,768]{1,0:T(8,128)(2,1)}, bf16[384,768]{1,0:T(8,128)(2,1)S(1)}, u32[]{:S(2)}, u32[]{:S(2)}) collective-permute-start(bf16[384,768]{1,0:T(8,128)(2,1)} %collective-permute-done.5.rest_1_), channel_id=1, source_target_pairs={{0,4},{4,0},{8,12},{12,8},{16,20},{20,16},{24,28},{28,24},{1,5},{5... | collective-permute-start | bytes 1769480 | tf_op jit(solution)/shard_map/ppermute | solution.py:194
  75.3 26.4 %collective-permute-start.9 = (bf16[384,768]{1,0:T(8,128)(2,1)}, bf16[384,768]{1,0:T(8,128)(2,1)S(1)}, u32[]{:S(2)}, u32[]{:S(2)}) collective-permute-start(bf16[384,768]{1,0:T(8,128)(2,1)} %collective-permute-done.6.rest_2_), channel_id=1, source_target_pairs={{0,4},{4,0},{8,12},{12,8},{16,20},{20,16},{24,28},{28,24},{1,5},{5... | collective-permute-start | bytes 1769480 | tf_op jit(solution)/shard_map/ppermute | solution.py:194
  76.8 1.1 copy-start.1
  77.9 1.1 copy-start.4
  81.3 6.8 %copy-start.7 = (f32[384,256]{1,0:T(8,128)}, f32[384,256]{1,0:T(8,128)S(1)}, u32[]{:S(2)}) copy-start(f32[384,256]{1,0:T(8,128)S(1)} %get-tuple-element.19) | copy-start | bytes 1179652
  81.3 22.3 %collective-permute-start.7 = (bf16[384,768]{1,0:T(8,128)(2,1)}, bf16[384,768]{1,0:T(8,128)(2,1)}, u32[]{:S(2)}, u32[]{:S(2)}) collective-permute-start(bf16[384,768]{1,0:T(8,128)(2,1)} %collective-permute-done.6.rest_2_), channel_id=1, source_target_pairs={{0,8},{4,12},{8,0},{12,4},{16,24},{20,28},{24,16},{28,20},{1,9},{5... | collective-permute-start | bytes 1769480 | tf_op jit(solution)/shard_map/ppermute | solution.py:194
  82.4 20.1 %collective-permute-start.10 = (f32[384,256]{1,0:T(8,128)S(1)}, f32[384,256]{1,0:T(8,128)S(1)}, u32[]{:S(2)}, u32[]{:S(2)}) collective-permute-start(f32[384,256]{1,0:T(8,128)S(1)} %get-tuple-element.21), channel_id=1, source_target_pairs={{0,16},{4,20},{8,24},{12,28},{16,0},{20,4},{24,8},{28,12},{1,17},{... | collective-permute-start | bytes 1179656 | tf_op jit(solution)/shard_map/ppermute | solution.py:194
  88.1 0.8 copy-start.9
  91.2 0.8 copy-start.15
  101.7 0.8 copy-start.17
  102.5 0.7 copy-start.21
  103.6 18.8 %collective-permute-start.11 = (bf16[384,768]{1,0:T(8,128)(2,1)}, bf16[384,768]{1,0:T(8,128)(2,1)}, u32[]{:S(2)}, u32[]{:S(2)}) collective-permute-start(bf16[384,768]{1,0:T(8,128)(2,1)} %collective-permute-done.7.rest_3_), channel_id=1, source_target_pairs={{0,4},{4,0},{8,12},{12,8},{16,20},{20,16},{24,28},{28,24},{1,5},{5... | collective-permute-start | bytes 1769480 | tf_op jit(solution)/shard_map/ppermute | solution.py:194
  104.0 18.4 %collective-permute-start.4 = (f32[384,256]{1,0:T(8,128)}, f32[384,256]{1,0:T(8,128)}, u32[]{:S(2)}, u32[]{:S(2)}) collective-permute-start(f32[384,256]{1,0:T(8,128)} %get-tuple-element.16), channel_id=1, source_target_pairs={{0,16},{4,20},{8,24},{12,28},{16,0},{20,4},{24,8},{28,12},{1,17},{... | collective-permute-start | bytes 1179656 | tf_op jit(solution)/shard_map/ppermute | solution.py:194
  106.6 1.1 copy-start.2
  107.7 1.1 copy-start.5
  108.9 13.6 %copy-start.3 = (bf16[4,128,768]{2,1,0:T(8,128)(2,1)S(1)}, bf16[4,128,768]{2,1,0:T(8,128)(2,1)}, u32[]{:S(2)}) copy-start(bf16[4,128,768]{2,1,0:T(8,128)(2,1)} %og_ref) | copy-start | bytes 2359300
  108.9 13.6 %copy-start.6 = (bf16[128,3072]{1,0:T(8,128)(2,1)S(1)}, bf16[128,3072]{1,0:T(8,128)(2,1)}, u32[]{:S(2)}) copy-start(bf16[128,3072]{1,0:T(8,128)(2,1)} %acts_ref.7) | copy-start | bytes 2359300
  108.9 13.6 %copy-start.14 = (bf16[384,768]{1,0:T(8,128)(2,1)S(1)}, bf16[384,768]{1,0:T(8,128)(2,1)}, u32[]{:S(2)}) copy-start(bf16[384,768]{1,0:T(8,128)(2,1)} %copy-done.13) | copy-start | bytes 1769476
  108.9 13.6 %copy-start.16 = (bf16[384,768]{1,0:T(8,128)(2,1)S(1)}, bf16[384,768]{1,0:T(8,128)(2,1)}, u32[]{:S(2)}) copy-start(bf16[384,768]{1,0:T(8,128)(2,1)} %copy-done.15) | copy-start | bytes 1769476
  108.9 13.6 %copy-start.18 = (bf16[384,768]{1,0:T(8,128)(2,1)S(1)}, bf16[384,768]{1,0:T(8,128)(2,1)}, u32[]{:S(2)}) copy-start(bf16[384,768]{1,0:T(8,128)(2,1)} %copy-done.17) | copy-start | bytes 1769476
  111.1 0.8 copy-start.11
  111.8 0.8 copy-start.19
  130.3 1.0 copy-start.20
  130.3 2.5 %collective-permute-start.13 = (f32[2,128,768]{2,1,0:T(8,128)S(1)}, f32[2,128,768]{2,1,0:T(8,128)}, u32[]{:S(2)}, u32[]{:S(2)}) collective-permute-start(f32[2,128,768]{2,1,0:T(8,128)S(1)} %dynamic-slice_bitcast_fusion), channel_id=1, source_target_pairs={{0,1},{1,0},{2,3},{3,2},{4,5},{5,4},{6,7},{7,6},{8,9},{9,8},{10,11... | collective-permute-start | bytes 2359304 | tf_op jit(solution)/shard_map/ppermute | solution.py:203
  131.3 5.1 %copy-start.10 = (f32[384,256]{1,0:T(8,128)S(1)}, f32[384,256]{1,0:T(8,128)}, u32[]{:S(2)}) copy-start(f32[384,256]{1,0:T(8,128)} %copy-done.9) | copy-start | bytes 1179652
  131.3 17.7 %collective-permute-start.12 = (f32[384,256]{1,0:T(8,128)S(1)}, f32[384,256]{1,0:T(8,128)}, u32[]{:S(2)}, u32[]{:S(2)}) collective-permute-start(f32[384,256]{1,0:T(8,128)S(1)} %copy-done.20), channel_id=1, source_target_pairs={{0,16},{4,20},{8,24},{12,28},{16,0},{20,4},{24,8},{28,12},{1,17},{... | collective-permute-start | bytes 1179656 | tf_op jit(solution)/shard_map/ppermute | solution.py:194
  134.0 3.4 %copy-start.8 = (f32[384,256]{1,0:T(8,128)S(1)}, f32[384,256]{1,0:T(8,128)}, u32[]{:S(2)}) copy-start(f32[384,256]{1,0:T(8,128)} %copy-done.7) | copy-start | bytes 1179652
  134.1 3.4 %copy-start.22 = (f32[384,256]{1,0:T(8,128)S(1)}, f32[384,256]{1,0:T(8,128)}, u32[]{:S(2)}) copy-start(f32[384,256]{1,0:T(8,128)} %copy-done.21) | copy-start | bytes 1179652
  134.1 14.9 %copy-start.12 = (f32[384,256]{1,0:T(8,128)S(1)}, f32[384,256]{1,0:T(8,128)}, u32[]{:S(2)}) copy-start(f32[384,256]{1,0:T(8,128)} %copy-done.11) | copy-start | bytes 1179652
  134.9 16.3 %collective-permute-start.14 = (f32[128,768]{1,0:T(8,128)}, f32[128,768]{1,0:T(8,128)S(1)}, u32[]{:S(2)}, u32[]{:S(2)}) collective-permute-start(f32[128,768]{1,0:T(8,128)} %dynamic-slice_bitcast_fusion.1), channel_id=1, source_target_pairs={{0,2},{1,3},{2,0},{3,1},{4,6},{5,7},{6,4},{7,5},{8,10},{9,11},{10,... | collective-permute-start | bytes 1179656 | tf_op jit(solution)/shard_map/ppermute | solution.py:203

commit v10 on v9

--- a/solution.py
+++ b/solution.py
@@ -223,31 +223,30 @@
         )
     )
     w_peer = [swap_x(weight)]
-    one = after(one, side, w_peer[0])
+    one = after(one, side)
     passed = [
         of_x(one[flat + r * tokens : flat + (r + 1) * tokens], 1 - x) for r in range(2)
     ]
     both = swap_x(jnp.concatenate([one[:flat], jnp.concatenate(passed, axis=1)]))
 
-    w_two = swap_z(weight, 2)
-    w_one = swap_z(weight, 1)
-    w_peer += [swap_x(w_one), swap_x(w_two)]
+    w_two = swap_z(after(weight, w_peer[0]), 2)
+    w_one = swap_z(after(weight, w_peer[0]), 1)
     og = [own, one, side, both]
-    keeps, gots = [], []
-    for j in range(width // BS):
-        keep, send = weight_grad_part(acts, og, block_mask, where, rows, j, 1)
-        keeps.append(keep)
-        gots.append(swap_z(send, 2))
-    w_three = swap_z(after(w_two, keeps[0]), 1)
+    keep_0, send_0 = weight_grad_part(acts, og, block_mask, where, rows, 0, 2)
+    got_0 = swap_z(send_0, 2)
+    keep_1, send_1 = weight_grad_part(acts, og, block_mask, where, rows, 2, width // BS - 2)
+    got_1 = swap_z(send_1, 2)
+    grad_w = jnp.concatenate([keep_0 + got_0, keep_1 + got_1], axis=1)
+    w_three = swap_z(after(w_two, keep_0), 1)
     w_mine = [weight, w_one, w_two, w_three]
-    w_peer.append(swap_x(after(w_three, *w_peer[1:], gots[0], keeps[1])))
-    grad_w = jnp.concatenate([k + g for k, g in zip(keeps, gots)], axis=1)
+    w_peer += [swap_x(after(w_one, keep_0)), swap_x(after(w_two, keep_0))]
+    w_peer.append(swap_x(after(w_three, *w_peer[1:], got_0, keep_1)))
 
     outputs, gx = forward_and_input(
-        acts, w_mine, w_peer, after(out_grad, gots[1], keeps[2]), block_mask, where
-    )
-
-    by = gx.reshape(2, 2, tokens, depth // 4)
+        acts, w_mine, w_peer, out_grad, block_mask, where
+    )
+
+    by = after(gx, got_1).reshape(2, 2, tokens, depth // 4)
     pair = lax.dynamic_index_in_dim(by, c, 1, keepdims=False) + swap_f(
         lax.dynamic_index_in_dim(by, 1 - c, 1, keepdims=False), 1
     )

time: 152 us -> 182 us (1.20)
  waiting for transfers between devices: 92.5 us -> 129 us
  starting transfers between devices: 20.1 us -> 14.7 us
    ppermute x13 -> x12, waiting for transfers between devices: 91 us -> 119 us  [swap_dp(): return lax.ppermute(a, 'dp', [(d, d ^ bits) for d in range(dp)])]
    ppermute x2, waiting for transfers between devices: 1.54 us -> 9.13 us  [swap_f(): return lax.ppermute(a, 'fsdp', [(d, d ^ bit) for d in range(fsdp)])]
    ppermute x13 -> x12, starting transfers between devices: 18.5 us -> 13.6 us  [swap_dp(): return lax.ppermute(a, 'dp', [(d, d ^ bits) for d in range(dp)])]
    unnamed x49 -> x37, local copies, waits for them, and re-layouts: 11.1 us -> 12.7 us
    pallas_call x3 -> x2, Pallas kernels: 7.3 us -> 5.76 us  [weight_grad_part(): pl.pallas_call(kernel, grid=(chunks,), out_shape=(jax.ShapeDtypeStruct((r...]
  transfers between devices with their start and end apart: 15 -> 14, of which waited for: 8 -> 9; matrix products, arithmetic and copies ran while one was open for 4% -> 2% of each run, Pallas kernels for 5% -> 7%
where the time goes in v10:
time: 182 us; the launch traced here: 181 us
  waiting for transfers between devices  129 us (71%)
  local copies, waits for them, and re-layouts  17.3 us (10%)
  starting transfers between devices  14.7 us (8%)
  Pallas kernels  13.4 us (7%)
  other arithmetic  6.47 us (4%)
    ppermute x12, waiting for transfers between devices, swap_dp(): return lax.ppermute(a, 'dp', [(d, d ^ bits) for d in range(dp)])  119 us
    ppermute x12, starting transfers between devices, swap_dp(): return lax.ppermute(a, 'dp', [(d, d ^ bits) for d in range(dp)])  13.6 us
    unnamed x37, local copies, waits for them, and re-layouts  12.7 us
    ppermute x2, waiting for transfers between devices, swap_f(): return lax.ppermute(a, 'fsdp', [(d, d ^ bit) for d in range(fsdp)])  9.13 us
    pallas_call x1, Pallas kernels, forward_and_input(): pl.pallas_call(kernel, grid=(width // BS,), out_shape=(jax.ShapeDtypeStru...  7.68 us
    pallas_call x2, Pallas kernels, weight_grad_part(): pl.pallas_call(kernel, grid=(chunks,), out_shape=(jax.ShapeDtypeStruct((r...  5.76 us
  transfers between devices with their start and end apart: 14, of which 9 were waited for; matrix products, arithmetic and copies ran while one was open for 2% of the time, Pallas kernels for 7%

profile of v10, /device:TPU:0, one launch (start us, length us, event | category | flops | bytes accessed | tf_op | source)
XLA Modules:
  0.0 181.4 jit_solution(4184316606344046249)
XLA Ops:
  0.7 2.0 %reshape.18 = bf16[128,4,768]{2,1,0:T(4,128)(2,1)S(1)} reshape(bf16[128,3072]{1,0:T(8,128)(2,1)} %acts_ref.5) | data formatting | bytes 1572864 | tf_op jit(solution)/shard_map/reshape | solution.py:211
  2.6 0.0 copy-start
  2.7 0.8 constant_dynamic-slice_fusion.5
  3.5 0.2 copy-done
  3.8 1.1 pad_maximum_fusion
  4.9 3.0 %collective-permute-start.3 = (bf16[768,768]{1,0:T(8,128)(2,1)}, bf16[768,768]{1,0:T(8,128)(2,1)S(1)}, u32[]{:S(2)}, u32[]{:S(2)}) collective-permute-start(bf16[768,768]{1,0:T(8,128)(2,1)} %pad_maximum_fusion), channel_id=1, source_target_pairs={{0,8},{4,12},{8,0},{12,4},{16,24},{20,28},{24,16},{28,20},{1,9},{5... | collective-permute-start | bytes 3538952 | tf_op jit(solution)/shard_map/ppermute | solution.py:194
  7.9 0.8 constant_dynamic-slice_fusion.3
  8.7 0.1 maximum_maximum_fusion
  8.8 1.5 collective-permute-start.4
  10.4 21.7 %collective-permute-done.4.refs_1_.refs_5_ = bf16[640,768]{1,0:T(8,128)(2,1)S(1)} collective-permute-done((bf16[640,768]{1,0:T(8,128)(2,1)S(1)}, bf16[640,768]{1,0:T(8,128)(2,1)S(1)}, u32[]{:S(2)}, u32[]{:S(2)}) %collective-permute-start.4) | collective-permute-done | bytes 983072 | tf_op jit(solution)/shard_map/ppermute | solution.py:194
  32.1 2.0 %collective-permute-done.3.refs_0_.refs_4_ = bf16[768,768]{1,0:T(8,128)(2,1)S(1)} collective-permute-done((bf16[768,768]{1,0:T(8,128)(2,1)}, bf16[768,768]{1,0:T(8,128)(2,1)S(1)}, u32[]{:S(2)}, u32[]{:S(2)}) %collective-permute-start.3) | collective-permute-done | bytes 1179680 | tf_op jit(solution)/shard_map/ppermute | solution.py:194
  34.1 0.1 slice.9
  34.2 0.0 copy-start.17
  34.2 1.0 maximum_maximum_fusion.1
  35.2 1.7 collective-permute-start.5
  36.9 0.4 collective-permute-start
  37.3 33.8 %collective-permute-done.rest_4_ = bf16[384,768]{1,0:T(8,128)(2,1)S(1)} collective-permute-done((bf16[384,768]{1,0:T(8,128)(2,1)}, bf16[384,768]{1,0:T(8,128)(2,1)S(1)}, u32[]{:S(2)}, u32[]{:S(2)}) %collective-permute-start) | collective-permute-done | bytes 589856 | tf_op jit(solution)/shard_map/ppermute | solution.py:194
  71.0 0.8 copy-done.10
  71.9 2.4 %collective-permute-start.2 = (bf16[384,768]{1,0:T(8,128)(2,1)}, bf16[384,768]{1,0:T(8,128)(2,1)}, u32[]{:S(2)}, u32[]{:S(2)}) collective-permute-start(bf16[384,768]{1,0:T(8,128)(2,1)} %rest_0_.1), channel_id=1, source_target_pairs={{0,16},{4,20},{8,24},{12,28},{16,0},{20,4},{24,8},{28,12},{1,17},{... | collective-permute-start | bytes 1769480 | tf_op jit(solution)/shard_map/ppermute | solution.py:194
  74.3 1.6 collective-permute-start.1
  75.9 0.1 pad_add_fusion.where_ref
  76.0 0.0 collective-permute-done.5.refs_2_.refs_6_
  76.0 1.1 copy-done.1
  77.1 1.1 copy-done.3
  78.2 3.6 %weight_grad_part.2 = (f32[384,512]{1,0:T(8,128)S(1)}, f32[384,512]{1,0:T(8,128)S(1)}) custom-call(s32[4]{0:T(128)S(1)} %pad_add_fusion.where_ref, s32[4,12,12]{2,1,0:T(8,128)S(1)} %copy.13.mask_ref, bf16[128,3072]{1,0:T(8,128)(2,1)S(1)} %copy-done.3, bf16[768,768]{1,0:T(8,128)(2,1)S(1)} %collective-permute-done.3.refs_0_.refs_4_, ...), custom_call_target="tpu_custom_call" | custom-call | flops 1610612736 | bytes 1572864 | tf_op jit(solution)/shard_map/weight_grad_part/pallas_call | solution.py:85
  81.8 0.0 copy-start.5
  81.9 0.4 collective-permute-start.9
  82.3 31.8 %collective-permute-done.2.rest_2_ = bf16[384,768]{1,0:T(8,128)(2,1)} collective-permute-done((bf16[384,768]{1,0:T(8,128)(2,1)}, bf16[384,768]{1,0:T(8,128)(2,1)}, u32[]{:S(2)}, u32[]{:S(2)}) %collective-permute-start.2) | collective-permute-done | bytes 589856 | tf_op jit(solution)/shard_map/ppermute | solution.py:194
  114.1 1.5 collective-permute-start.8
  115.6 0.0 collective-permute-start.6
  115.6 0.0 collective-permute-done.1.rest_1_
  115.6 0.5 collective-permute-start.7
  116.1 0.8 copy-done.8
  116.9 2.2 %weight_grad_part.3 = (f32[384,256]{1,0:T(8,128)S(1)}, f32[384,256]{1,0:T(8,128)S(1)}) custom-call(s32[4]{0:T(128)S(1)} %pad_add_fusion.where_ref, s32[4,12,12]{2,1,0:T(8,128)S(1)} %copy-done.8, bf16[128,3072]{1,0:T(8,128)(2,1)S(1)} %copy-done.3, bf16[768,768]{1,0:T(8,128)(2,1)S(1)} %collective-permute-done.3.refs_0_.refs_4_, ...), custom_call_target="tpu_custom_call" | custom-call | flops 805306368 | bytes 786432 | tf_op jit(solution)/shard_map/weight_grad_part/pallas_call | solution.py:85
  119.1 0.7 copy-done.16
  119.8 4.3 %collective-permute-done.8.rest_6_ = bf16[384,768]{1,0:T(8,128)(2,1)S(1)} collective-permute-done((bf16[384,768]{1,0:T(8,128)(2,1)}, bf16[384,768]{1,0:T(8,128)(2,1)S(1)}, u32[]{:S(2)}, u32[]{:S(2)}) %collective-permute-start.8) | collective-permute-done | bytes 589856 | tf_op jit(solution)/shard_map/ppermute | solution.py:194
  124.2 0.8 copy-done.12
  125.0 16.2 %collective-permute-done.6.rest_3_ = bf16[384,768]{1,0:T(8,128)(2,1)} collective-permute-done((bf16[384,768]{1,0:T(8,128)(2,1)}, bf16[384,768]{1,0:T(8,128)(2,1)}, u32[]{:S(2)}, u32[]{:S(2)}) %collective-permute-start.6) | collective-permute-done | bytes 589856 | tf_op jit(solution)/shard_map/ppermute | solution.py:194
  141.2 0.0 collective-permute-done.7.rest_5_
  141.2 0.8 copy-done.14
  142.0 0.0 collective-permute-done.9
  142.0 0.5 collective-permute-start.10
  142.6 0.0 collective-permute-start.11
  142.6 9.5 %collective-permute-done.10.rest_7_ = bf16[384,768]{1,0:T(8,128)(2,1)S(1)} collective-permute-done((bf16[384,768]{1,0:T(8,128)(2,1)}, bf16[384,768]{1,0:T(8,128)(2,1)S(1)}, u32[]{:S(2)}, u32[]{:S(2)}) %collective-permute-start.10) | collective-permute-done | bytes 589856 | tf_op jit(solution)/shard_map/ppermute | solution.py:194
  152.1 1.1 copy-done.2
  153.2 1.1 copy-done.4
  154.4 0.8 copy-done.9
  155.1 1.1 copy-done.11
  156.2 1.1 copy-done.13
  157.3 1.1 copy-done.15
  158.3 7.7 %forward_and_input.1 = (bf16[4,128,768]{2,1,0:T(8,128)(2,1)}, f32[4,128,768]{2,1,0:T(8,128)S(1)}) custom-call(s32[4]{0:T(128)S(1)} %pad_add_fusion.where_ref, s32[4,12,12]{2,1,0:T(8,128)S(1)} %copy-done.9, bf16[128,3072]{1,0:T(8,128)(2,1)S(1)} %copy-done.4, bf16[4,128,768]{2,1,0:T(8,128)(2,1)S(1)} %copy-done.2, bf16[384,768]{1,0:T(8,128)(2,1)} %rest_0_.1, ...), custom_call_target="tpu_custom_call" | custom-call | flops 10871635968 | bytes 9437184 | tf_op jit(solution)/shard_map/forward_and_input/pallas_call | solution.py:157
  166.0 0.0 collective-permute-done.11
  166.0 0.1 dynamic-slice_bitcast_fusion
  166.1 0.1 collective-permute-start.12
  166.2 2.2 %collective-permute-done.12 = f32[2,128,768]{2,1,0:T(8,128)S(1)} collective-permute-done((f32[2,128,768]{2,1,0:T(8,128)S(1)}, f32[2,128,768]{2,1,0:T(8,128)S(1)}, u32[]{:S(2)}, u32[]{:S(2)}) %collective-permute-start.12) | collective-permute-done | bytes 786464 | tf_op jit(solution)/shard_map/ppermute | solution.py:203
  168.4 0.1 bitcast_add_fusion
  168.5 0.0 copy-start.6
  168.5 0.8 dynamic-slice_bitcast_fusion.1
  169.3 1.0 collective-permute-start.13
  170.4 1.0 add.70
  171.4 1.3 add.69
  172.7 1.1 pad_maximum_fusion.1
  173.8 6.9 %collective-permute-done.13 = f32[128,768]{1,0:T(8,128)S(1)} collective-permute-done((f32[128,768]{1,0:T(8,128)}, f32[128,768]{1,0:T(8,128)S(1)}, u32[]{:S(2)}, u32[]{:S(2)}) %collective-permute-start.13) | collective-permute-done | bytes 393248 | tf_op jit(solution)/shard_map/ppermute | solution.py:203
  180.7 0.7 fusion
  (24 shorter events, 0.2 us)
Async XLA Ops:
  2.6 1.1 copy-start
  4.9 29.2 %collective-permute-start.3 = (bf16[768,768]{1,0:T(8,128)(2,1)}, bf16[768,768]{1,0:T(8,128)(2,1)S(1)}, u32[]{:S(2)}, u32[]{:S(2)}) collective-permute-start(bf16[768,768]{1,0:T(8,128)(2,1)} %pad_maximum_fusion), channel_id=1, source_target_pairs={{0,8},{4,12},{8,0},{12,4},{16,24},{20,28},{24,16},{28,20},{1,9},{5... | collective-permute-start | bytes 3538952 | tf_op jit(solution)/shard_map/ppermute | solution.py:194
  8.8 23.3 %collective-permute-start.4 = (bf16[640,768]{1,0:T(8,128)(2,1)S(1)}, bf16[640,768]{1,0:T(8,128)(2,1)S(1)}, u32[]{:S(2)}, u32[]{:S(2)}) collective-permute-start(bf16[640,768]{1,0:T(8,128)(2,1)S(1)} %maximum_maximum_fusion), channel_id=1, source_target_pairs={{0,4},{4,0},{8,12},{12,8},{16,20},{20,16},{24,28},{28,24},{1,5},{5... | collective-permute-start | bytes 2949128 | tf_op jit(solution)/shard_map/ppermute | solution.py:194
  34.2 41.7 %copy-start.17 = (s32[4,12,12]{2,0,1:T(4,128)S(1)}, s32[4,12,12]{2,0,1:T(4,128)}, u32[]{:S(2)}) copy-start(s32[4,12,12]{2,0,1:T(4,128)} %param.6) | copy-start | bytes 6916
  35.2 40.7 %collective-permute-start.5 = (bf16[640,768]{1,0:T(8,128)(2,1)}, bf16[640,768]{1,0:T(8,128)(2,1)S(1)}, u32[]{:S(2)}, u32[]{:S(2)}) collective-permute-start(bf16[640,768]{1,0:T(8,128)(2,1)} %maximum_maximum_fusion.1), channel_id=1, source_target_pairs={{0,4},{4,0},{8,12},{12,8},{16,20},{20,16},{24,28},{28,24},{1,5},{5... | collective-permute-start | bytes 2949128 | tf_op jit(solution)/shard_map/ppermute | solution.py:194
  36.9 34.1 %collective-permute-start = (bf16[384,768]{1,0:T(8,128)(2,1)}, bf16[384,768]{1,0:T(8,128)(2,1)S(1)}, u32[]{:S(2)}, u32[]{:S(2)}) collective-permute-start(bf16[384,768]{1,0:T(8,128)(2,1)} %rest_0_.1), channel_id=1, source_target_pairs={{0,4},{4,0},{8,12},{12,8},{16,20},{20,16},{24,28},{28,24},{1,5},{5... | collective-permute-start | bytes 1769480 | tf_op jit(solution)/shard_map/ppermute | solution.py:194
  71.0 0.8 copy-start.10
  71.9 42.2 %collective-permute-start.2 = (bf16[384,768]{1,0:T(8,128)(2,1)}, bf16[384,768]{1,0:T(8,128)(2,1)}, u32[]{:S(2)}, u32[]{:S(2)}) collective-permute-start(bf16[384,768]{1,0:T(8,128)(2,1)} %rest_0_.1), channel_id=1, source_target_pairs={{0,16},{4,20},{8,24},{12,28},{16,0},{20,4},{24,8},{28,12},{1,17},{... | collective-permute-start | bytes 1769480 | tf_op jit(solution)/shard_map/ppermute | solution.py:194
  74.3 41.3 %collective-permute-start.1 = (bf16[384,768]{1,0:T(8,128)(2,1)}, bf16[384,768]{1,0:T(8,128)(2,1)}, u32[]{:S(2)}, u32[]{:S(2)}) collective-permute-start(bf16[384,768]{1,0:T(8,128)(2,1)} %rest_0_.1), channel_id=1, source_target_pairs={{0,8},{4,12},{8,0},{12,4},{16,24},{20,28},{24,16},{28,20},{1,9},{5... | collective-permute-start | bytes 1769480 | tf_op jit(solution)/shard_map/ppermute | solution.py:194
  75.9 6.0 %copy-start.7 = (s32[4,12,12]{2,1,0:T(8,128)}, s32[4,12,12]{2,1,0:T(8,128)S(1)}, u32[]{:S(2)}) copy-start(s32[4,12,12]{2,1,0:T(8,128)S(1)} %copy.13.mask_ref) | copy-start | bytes 6916
  76.0 1.1 copy-start.1
  77.1 1.1 copy-start.3
  81.8 37.2 %copy-start.5 = (f32[384,512]{1,0:T(8,128)}, f32[384,512]{1,0:T(8,128)S(1)}, u32[]{:S(2)}) copy-start(f32[384,512]{1,0:T(8,128)S(1)} %get-tuple-element.17) | copy-start | bytes 2359300
  81.9 60.2 %collective-permute-start.9 = (f32[384,512]{1,0:T(8,128)S(1)}, f32[384,512]{1,0:T(8,128)}, u32[]{:S(2)}, u32[]{:S(2)}) collective-permute-start(f32[384,512]{1,0:T(8,128)S(1)} %get-tuple-element.20), channel_id=1, source_target_pairs={{0,16},{4,20},{8,24},{12,28},{16,0},{20,4},{24,8},{28,12},{1,17},{... | collective-permute-start | bytes 2359304 | tf_op jit(solution)/shard_map/ppermute | solution.py:194
  114.1 10.1 %collective-permute-start.8 = (bf16[384,768]{1,0:T(8,128)(2,1)}, bf16[384,768]{1,0:T(8,128)(2,1)S(1)}, u32[]{:S(2)}, u32[]{:S(2)}) collective-permute-start(bf16[384,768]{1,0:T(8,128)(2,1)} %collective-permute-done.2.rest_2_), channel_id=1, source_target_pairs={{0,4},{4,0},{8,12},{12,8},{16,20},{20,16},{24,28},{28,24},{1,5},{5... | collective-permute-start | bytes 1769480 | tf_op jit(solution)/shard_map/ppermute | solution.py:194
  115.6 25.6 %collective-permute-start.6 = (bf16[384,768]{1,0:T(8,128)(2,1)}, bf16[384,768]{1,0:T(8,128)(2,1)}, u32[]{:S(2)}, u32[]{:S(2)}) collective-permute-start(bf16[384,768]{1,0:T(8,128)(2,1)} %collective-permute-done.2.rest_2_), channel_id=1, source_target_pairs={{0,8},{4,12},{8,0},{12,4},{16,24},{20,28},{24,16},{28,20},{1,9},{5... | collective-permute-start | bytes 1769480 | tf_op jit(solution)/shard_map/ppermute | solution.py:194
  115.6 25.6 %collective-permute-start.7 = (bf16[384,768]{1,0:T(8,128)(2,1)}, bf16[384,768]{1,0:T(8,128)(2,1)S(1)}, u32[]{:S(2)}, u32[]{:S(2)}) collective-permute-start(bf16[384,768]{1,0:T(8,128)(2,1)} %collective-permute-done.1.rest_1_), channel_id=1, source_target_pairs={{0,4},{4,0},{8,12},{12,8},{16,20},{20,16},{24,28},{28,24},{1,5},{5... | collective-permute-start | bytes 1769480 | tf_op jit(solution)/shard_map/ppermute | solution.py:194
  116.1 0.8 copy-start.8
  119.1 0.8 copy-start.16
  124.2 0.8 copy-start.12
  141.2 0.8 copy-start.14
  142.0 10.1 %collective-permute-start.10 = (bf16[384,768]{1,0:T(8,128)(2,1)}, bf16[384,768]{1,0:T(8,128)(2,1)S(1)}, u32[]{:S(2)}, u32[]{:S(2)}) collective-permute-start(bf16[384,768]{1,0:T(8,128)(2,1)} %collective-permute-done.6.rest_3_), channel_id=1, source_target_pairs={{0,4},{4,0},{8,12},{12,8},{16,20},{20,16},{24,28},{28,24},{1,5},{5... | collective-permute-start | bytes 1769480 | tf_op jit(solution)/shard_map/ppermute | solution.py:194
  142.6 23.5 %collective-permute-start.11 = (f32[384,256]{1,0:T(8,128)}, f32[384,256]{1,0:T(8,128)}, u32[]{:S(2)}, u32[]{:S(2)}) collective-permute-start(f32[384,256]{1,0:T(8,128)} %copy-done.16), channel_id=1, source_target_pairs={{0,16},{4,20},{8,24},{12,28},{16,0},{20,4},{24,8},{28,12},{1,17},{... | collective-permute-start | bytes 1179656 | tf_op jit(solution)/shard_map/ppermute | solution.py:194
  152.1 1.1 copy-start.2
  153.2 1.1 copy-start.4
  154.4 0.8 copy-start.9
  155.1 1.1 copy-start.11
  156.2 1.1 copy-start.13
  157.3 1.1 copy-start.15
  166.1 2.4 %collective-permute-start.12 = (f32[2,128,768]{2,1,0:T(8,128)S(1)}, f32[2,128,768]{2,1,0:T(8,128)S(1)}, u32[]{:S(2)}, u32[]{:S(2)}) collective-permute-start(f32[2,128,768]{2,1,0:T(8,128)S(1)} %dynamic-slice_bitcast_fusion), channel_id=1, source_target_pairs={{0,1},{1,0},{2,3},{3,2},{4,5},{5,4},{6,7},{7,6},{8,9},{9,8},{10,11... | collective-permute-start | bytes 2359304 | tf_op jit(solution)/shard_map/ppermute | solution.py:203
  168.5 2.9 %copy-start.6 = (f32[384,512]{1,0:T(8,128)S(1)}, f32[384,512]{1,0:T(8,128)}, u32[]{:S(2)}) copy-start(f32[384,512]{1,0:T(8,128)} %copy-done.5) | copy-start | bytes 2359300
  169.3 11.4 %collective-permute-start.13 = (f32[128,768]{1,0:T(8,128)}, f32[128,768]{1,0:T(8,128)S(1)}, u32[]{:S(2)}, u32[]{:S(2)}) collective-permute-start(f32[128,768]{1,0:T(8,128)} %dynamic-slice_bitcast_fusion.1), channel_id=1, source_target_pairs={{0,2},{1,3},{2,0},{3,1},{4,6},{5,7},{6,4},{7,5},{8,10},{9,11},{10,... | collective-permute-start | bytes 1179656 | tf_op jit(solution)/shard_map/ppermute | solution.py:203

commit v11 on v10

--- a/solution.py
+++ b/solution.py
@@ -38,23 +38,21 @@
 
 
 def weight_grad_part(acts, og, block_mask, where, rows, chunk, chunks):
-    nsub = block_mask.shape[0]
-    tokens = acts.shape[0]
+    nsub, tokens, width = og[0].shape
     flat = nsub * tokens
     ng = len(og)
     per = rows // LANES
-    width = og[0].shape[1]
     made = chunks * BS
 
-    def kernel(where_ref, mask_ref, acts_ref, *refs):
-        extra, og_refs, outs, tiles = refs[:3], refs[3 : 3 + ng], refs[3 + ng : -1], refs[-1]
+    def kernel(where_ref, mask_ref, *refs):
+        og_refs, outs, tiles = refs[ng : 2 * ng], refs[2 * ng : -1], refs[-1]
         z, x = where_ref[0], where_ref[1]
         step = pl.program_id(0)
         col = where_ref[2] + chunk + step
 
         @pl.when(step == 0)
         def _():
-            one_ref, side_ref, both_ref = extra
+            acts_ref, one_ref, side_ref, both_ref = refs[:ng]
             for r in range(2):
                 for g in range(per):
                     start = ((z ^ (2 * r)) * 2 + x) * rows + g * LANES
@@ -62,10 +60,11 @@
                     there = pl.ds(pl.multiple_of(x * rows + g * LANES, LANES), LANES)
                     dst = slice((r * per + g) * LANES, (r * per + g + 1) * LANES)
                     tiles[0, dst, :] = acts_ref[:, here].T
-                    tiles[1, dst, :] = one_ref[r * tokens : (r + 1) * tokens, there].T
+                    tiles[1, dst, :] = one_ref[r, :, there].T
                     tiles[2, dst, :] = side_ref[:, dst].T
                     tiles[3, dst, :] = both_ref[:, dst].T
 
+        rhs = [ref[...].reshape(flat, BS) for ref in og_refs]
         for r in range(2):
             for g in range(per):
                 block = (((z ^ (2 * r)) * 2 + x) * rows + g * LANES) // BS
@@ -76,7 +75,7 @@
                 for k in range(ng):
                     t = tiles[k, dst, :]
                     lhs = jnp.concatenate([t * m for m in keep], axis=1)
-                    term = jnp.dot(lhs, og_refs[k][...], preferred_element_type=F32)
+                    term = jnp.dot(lhs, rhs[k], preferred_element_type=F32)
                     total = term if total is None else total + term
                 outs[r][g * LANES : (g + 1) * LANES, :] = total * (1.0 / TOK_G)
 
@@ -86,13 +85,9 @@
         kernel,
         grid=(chunks,),
         out_shape=(jax.ShapeDtypeStruct((rows, made), F32),) * 2,
-        in_specs=[smem, smem, pl.BlockSpec(acts.shape, lambda j: (0, 0))]
-        + [
-            pl.BlockSpec((2 * tokens, width), lambda j: (flat // (2 * tokens), 0)),
-            pl.BlockSpec((tokens, width), lambda j: (flat // tokens, 0)),
-            pl.BlockSpec((tokens, width), lambda j: (flat // tokens, 0)),
-        ]
-        + [pl.BlockSpec((flat, BS), lambda j: (0, chunk + j))] * ng,
+        in_specs=[smem, smem]
+        + [pl.BlockSpec(a.shape, lambda j, n=a.ndim: (0,) * n) for a in acts]
+        + [pl.BlockSpec((nsub, tokens, BS), lambda j: (0, 0, chunk + j))] * ng,
         out_specs=(out, out),
         scratch_shapes=[pltpu.VMEM((ng, 2 * rows, tokens), BF16)],
         compiler_params=pltpu.CompilerParams(vmem_limit_bytes=PART_VMEM),
@@ -100,7 +95,7 @@
             flops=4 * ng * rows * made * flat, bytes_accessed=8 * rows * made, transcendentals=0
         ),
         name="weight_grad_part",
-    )(where, block_mask, acts, *og[1:], *og)
+    )(where, block_mask, *acts, *og)
 
 
 def forward_and_input(acts, w_mine, w_peer, og, block_mask, where):
@@ -205,42 +200,33 @@
     def after(a, *others):
         return lax.optimization_barrier((a, *others))[0]
 
-    nsub = out_grad.shape[0]
-    flat = nsub * tokens
-    own = out_grad.reshape(flat, width)
-    by_z = acts.reshape(tokens, dp // nx, nx * rows)
-
-    def acts_of(k):
-        return lax.dynamic_index_in_dim(by_z, z ^ k, 1, keepdims=False)
-
-    def of_x(a, side):
-        return lax.dynamic_slice_in_dim(a, side * rows, rows, 1)
-
-    one = swap_z(jnp.concatenate([own, acts_of(1), acts_of(3)]), 1)
-    side = swap_x(
-        jnp.concatenate(
-            [own, jnp.concatenate([of_x(acts_of(0), 1 - x), of_x(acts_of(2), 1 - x)], axis=1)]
-        )
-    )
-    w_peer = [swap_x(weight)]
-    one = after(one, side)
-    passed = [
-        of_x(one[flat + r * tokens : flat + (r + 1) * tokens], 1 - x) for r in range(2)
-    ]
-    both = swap_x(jnp.concatenate([one[:flat], jnp.concatenate(passed, axis=1)]))
-
-    w_two = swap_z(after(weight, w_peer[0]), 2)
-    w_one = swap_z(after(weight, w_peer[0]), 1)
-    og = [own, one, side, both]
-    keep_0, send_0 = weight_grad_part(acts, og, block_mask, where, rows, 0, 2)
+    og_one = swap_z(out_grad, 1)
+    og_side = swap_x(out_grad)
+    og_both = swap_x(after(og_one, og_side))
+
+    def acts_of(a, first, count):
+        return lax.dynamic_slice_in_dim(a, first * rows, count * rows, 1)
+
+    acts_one = swap_z(jnp.stack([acts_of(acts, (z ^ k) * nx, nx) for k in (1, 3)]), 1)
+    acts_side = swap_x(
+        jnp.concatenate([acts_of(acts, (z ^ k) * nx + 1 - x, 1) for k in (0, 2)], axis=1)
+    )
+    passed = after(acts_one, acts_side)
+    acts_both = swap_x(jnp.concatenate([acts_of(passed[r], 1 - x, 1) for r in range(2)], axis=1))
+
+    w_two = swap_z(weight, 2)
+    w_one = swap_z(weight, 1)
+    og = [out_grad, og_one, og_side, og_both]
+    acts_all = [acts, acts_one, acts_side, acts_both]
+    keep_0, send_0 = weight_grad_part(acts_all, og, block_mask, where, rows, 0, 1)
     got_0 = swap_z(send_0, 2)
-    keep_1, send_1 = weight_grad_part(acts, og, block_mask, where, rows, 2, width // BS - 2)
+    keep_1, send_1 = weight_grad_part(acts_all, og, block_mask, where, rows, 1, width // BS - 1)
     got_1 = swap_z(send_1, 2)
     grad_w = jnp.concatenate([keep_0 + got_0, keep_1 + got_1], axis=1)
     w_three = swap_z(after(w_two, keep_0), 1)
     w_mine = [weight, w_one, w_two, w_three]
-    w_peer += [swap_x(after(w_one, keep_0)), swap_x(after(w_two, keep_0))]
-    w_peer.append(swap_x(after(w_three, *w_peer[1:], got_0, keep_1)))
+    w_peer = [swap_x(after(w, keep_0)) for w in w_mine[:3]]
+    w_peer.append(swap_x(after(w_three, got_0, keep_1)))
 
     outputs, gx = forward_and_input(
         acts, w_mine, w_peer, out_grad, block_mask, where

time: 182 us -> 133 us (0.73)
  waiting for transfers between devices: 129 us -> 82.3 us
  local copies, waits for them, and re-layouts: 17.3 us -> 8.28 us
  starting transfers between devices: 14.7 us -> 22.8 us
  other arithmetic: 6.47 us -> 4.36 us
    ppermute x12 -> x15, waiting for transfers between devices: 119 us -> 73.8 us  [swap_dp(): return lax.ppermute(a, 'dp', [(d, d ^ bits) for d in range(dp)])]
    ppermute x12 -> x15, starting transfers between devices: 13.6 us -> 21.1 us  [swap_dp(): return lax.ppermute(a, 'dp', [(d, d ^ bits) for d in range(dp)])]
    unnamed x37 -> x21, local copies, waits for them, and re-layouts: 12.7 us -> 6.3 us
    concatenate x3 -> x2, other arithmetic: 2.17 us -> 0.04 us  [the longest x1 0.02 us: on_device(): jnp.concatenate([acts_of(acts, (z ^ k) * nx + 1 - x, 1) for k in (0, 2)],...]
    reshape x1 -> x0, local copies, waits for them, and re-layouts: 1.99 us -> none  [on_device(): by_z = acts.reshape(tokens, dp // nx, nx * rows)]
  transfers between devices with their start and end apart: 14 -> 17, of which waited for: 9 -> 13; matrix products, arithmetic and copies ran while one was open for 2% -> 4% of each run, Pallas kernels for 7% -> 10%
where the time goes in v11:
time: 133 us; the launch traced here: 132 us
  waiting for transfers between devices  82.3 us (62%)
  starting transfers between devices  22.8 us (17%)
  Pallas kernels  13.6 us (10%)
  local copies, waits for them, and re-layouts  8.28 us (6%)
  other arithmetic  4.36 us (3%)
    ppermute x15, waiting for transfers between devices, swap_dp(): return lax.ppermute(a, 'dp', [(d, d ^ bits) for d in range(dp)])  73.8 us
    ppermute x15, starting transfers between devices, swap_dp(): return lax.ppermute(a, 'dp', [(d, d ^ bits) for d in range(dp)])  21.1 us
    ppermute x2, waiting for transfers between devices, swap_f(): return lax.ppermute(a, 'fsdp', [(d, d ^ bit) for d in range(fsdp)])  8.54 us
    pallas_call x1, Pallas kernels, forward_and_input(): pl.pallas_call(kernel, grid=(width // BS,), out_shape=(jax.ShapeDtypeStru...  7.85 us
    unnamed x21, local copies, waits for them, and re-layouts  6.3 us
    pallas_call x2, Pallas kernels, weight_grad_part(): pl.pallas_call(kernel, grid=(chunks,), out_shape=(jax.ShapeDtypeStruct((r...  5.76 us
  transfers between devices with their start and end apart: 17, of which 13 were waited for; matrix products, arithmetic and copies ran while one was open for 4% of the time, Pallas kernels for 10%

profile of v11, /device:TPU:0, one launch (start us, length us, event | category | flops | bytes accessed | tf_op | source)
XLA Modules:
  0.0 132.1 jit_solution(6160885924274575608)
XLA Ops:
  0.6 0.0 copy-start
  0.6 3.0 %collective-permute-start.6 = (bf16[4,128,768]{2,1,0:T(8,128)(2,1)}, bf16[4,128,768]{2,1,0:T(8,128)(2,1)S(1)}, u32[]{:S(2)}, u32[]{:S(2)}) collective-permute-start(bf16[4,128,768]{2,1,0:T(8,128)(2,1)} %og_ref.1), channel_id=1, source_target_pairs={{0,4},{4,0},{8,12},{12,8},{16,20},{20,16},{24,28},{28,24},{1,5},{5... | collective-permute-start | bytes 2359304 | tf_op jit(solution)/shard_map/ppermute | solution.py:189
  3.6 1.6 %collective-permute-start.5 = (bf16[4,128,768]{2,1,0:T(8,128)(2,1)}, bf16[4,128,768]{2,1,0:T(8,128)(2,1)}, u32[]{:S(2)}, u32[]{:S(2)}) collective-permute-start(bf16[4,128,768]{2,1,0:T(8,128)(2,1)} %og_ref.1), channel_id=1, source_target_pairs={{0,8},{4,12},{8,0},{12,4},{16,24},{20,28},{24,16},{28,20},{1,9},{5... | collective-permute-start | bytes 2359304 | tf_op jit(solution)/shard_map/ppermute | solution.py:189
  5.2 1.0 dynamic-slice_bitcast_fusion.3
  6.3 0.5 collective-permute-start.2
  6.8 0.0 copy-done
  6.8 0.0 copy-start.1
  6.9 0.2 collective-permute-start.3
  7.1 15.1 %collective-permute-done.6.refs_6_ = bf16[4,128,768]{2,1,0:T(8,128)(2,1)S(1)} collective-permute-done((bf16[4,128,768]{2,1,0:T(8,128)(2,1)}, bf16[4,128,768]{2,1,0:T(8,128)(2,1)S(1)}, u32[]{:S(2)}, u32[]{:S(2)}) %collective-permute-start.6) | collective-permute-done | bytes 786464 | tf_op jit(solution)/shard_map/ppermute | solution.py:189
  22.2 2.2 %collective-permute-done.5.refs_5_ = bf16[4,128,768]{2,1,0:T(8,128)(2,1)} collective-permute-done((bf16[4,128,768]{2,1,0:T(8,128)(2,1)}, bf16[4,128,768]{2,1,0:T(8,128)(2,1)}, u32[]{:S(2)}, u32[]{:S(2)}) %collective-permute-start.5) | collective-permute-done | bytes 786464 | tf_op jit(solution)/shard_map/ppermute | solution.py:189
  24.4 0.1 collective-permute-start.7
  24.5 3.0 %collective-permute-start.1 = (bf16[384,768]{1,0:T(8,128)(2,1)}, bf16[384,768]{1,0:T(8,128)(2,1)}, u32[]{:S(2)}, u32[]{:S(2)}) collective-permute-start(bf16[384,768]{1,0:T(8,128)(2,1)} %rest_0_.1), channel_id=1, source_target_pairs={{0,16},{4,20},{8,24},{12,28},{16,0},{20,4},{24,8},{28,12},{1,17},{... | collective-permute-start | bytes 1769480 | tf_op jit(solution)/shard_map/ppermute | solution.py:189
  27.6 0.0 collective-permute-done.3.refs_2_
  27.6 11.3 %collective-permute-done.2.refs_1_ = bf16[2,128,768]{2,1,0:T(8,128)(2,1)S(1)} collective-permute-done((bf16[2,128,768]{2,1,0:T(8,128)(2,1)S(1)}, bf16[2,128,768]{2,1,0:T(8,128)(2,1)S(1)}, u32[]{:S(2)}, u32[]{:S(2)}) %collective-permute-start.2) | collective-permute-done | bytes 393248 | tf_op jit(solution)/shard_map/ppermute | solution.py:189
  38.9 0.0 copy-start.9
  39.0 0.1 collective-permute-start.4
  39.1 0.1 collective-permute-start
  39.2 0.5 copy-done.9
  39.6 0.6 copy.9.mask_ref
  40.3 0.1 pad_add_fusion.where_ref
  40.3 6.3 %collective-permute-done.4.refs_3_ = bf16[128,768]{1,0:T(8,128)(2,1)S(1)} collective-permute-done((bf16[128,768]{1,0:T(8,128)(2,1)S(1)}, bf16[128,768]{1,0:T(8,128)(2,1)S(1)}, u32[]{:S(2)}, u32[]{:S(2)}) %collective-permute-start.4) | collective-permute-done | bytes 196640 | tf_op jit(solution)/shard_map/ppermute | solution.py:189
  46.7 0.0 collective-permute-done.7.refs_7_
  46.7 0.0 copy-done.1
  46.7 0.0 copy-start.4
  46.7 0.8 copy-done.4
  47.4 2.2 %weight_grad_part.2 = (f32[384,256]{1,0:T(8,128)S(1)}, f32[384,256]{1,0:T(8,128)S(1)}) custom-call(s32[4]{0:T(128)S(1)} %pad_add_fusion.where_ref, s32[4,12,12]{2,1,0:T(8,128)S(1)} %copy-done.4, bf16[128,3072]{1,0:T(8,128)(2,1)S(1)} %copy-done, bf16[2,128,768]{2,1,0:T(8,128)(2,1)S(1)} %collective-permute-done.2.refs_1_, ...), custom_call_target="tpu_custom_call" | custom-call | flops 805306368 | bytes 786432 | tf_op jit(solution)/shard_map/weight_grad_part/pallas_call | solution.py:84
  49.6 1.6 %collective-permute-done.1.rest_2_ = bf16[384,768]{1,0:T(8,128)(2,1)} collective-permute-done((bf16[384,768]{1,0:T(8,128)(2,1)}, bf16[384,768]{1,0:T(8,128)(2,1)}, u32[]{:S(2)}, u32[]{:S(2)}) %collective-permute-start.1) | collective-permute-done | bytes 589856 | tf_op jit(solution)/shard_map/ppermute | solution.py:189
  51.3 0.6 collective-permute-start.8
  51.9 3.4 %collective-permute-start.12 = (f32[384,256]{1,0:T(8,128)S(1)}, f32[384,256]{1,0:T(8,128)}, u32[]{:S(2)}, u32[]{:S(2)}) collective-permute-start(f32[384,256]{1,0:T(8,128)S(1)} %get-tuple-element.22), channel_id=1, source_target_pairs={{0,16},{4,20},{8,24},{12,28},{16,0},{20,4},{24,8},{28,12},{1,17},{... | collective-permute-start | bytes 1179656 | tf_op jit(solution)/shard_map/ppermute | solution.py:189
  55.3 1.4 %collective-permute-start.11 = (bf16[384,768]{1,0:T(8,128)(2,1)}, bf16[384,768]{1,0:T(8,128)(2,1)}, u32[]{:S(2)}, u32[]{:S(2)}) collective-permute-start(bf16[384,768]{1,0:T(8,128)(2,1)} %collective-permute-done.1.rest_2_), channel_id=1, source_target_pairs={{0,4},{4,0},{8,12},{12,8},{16,20},{20,16},{24,28},{28,24},{1,5},{5... | collective-permute-start | bytes 1769480 | tf_op jit(solution)/shard_map/ppermute | solution.py:189
  56.8 12.4 %collective-permute-done.rest_1_ = bf16[384,768]{1,0:T(8,128)(2,1)} collective-permute-done((bf16[384,768]{1,0:T(8,128)(2,1)}, bf16[384,768]{1,0:T(8,128)(2,1)}, u32[]{:S(2)}, u32[]{:S(2)}) %collective-permute-start) | collective-permute-done | bytes 589856 | tf_op jit(solution)/shard_map/ppermute | solution.py:189
  69.2 2.7 %collective-permute-start.9 = (bf16[384,768]{1,0:T(8,128)(2,1)}, bf16[384,768]{1,0:T(8,128)(2,1)}, u32[]{:S(2)}, u32[]{:S(2)}) collective-permute-start(bf16[384,768]{1,0:T(8,128)(2,1)} %rest_0_.1), channel_id=1, source_target_pairs={{0,4},{4,0},{8,12},{12,8},{16,20},{20,16},{24,28},{28,24},{1,5},{5... | collective-permute-start | bytes 1769480 | tf_op jit(solution)/shard_map/ppermute | solution.py:189
  71.9 0.0 collective-permute-start.10
  71.9 3.6 %weight_grad_part.3 = (f32[384,512]{1,0:T(8,128)S(1)}, f32[384,512]{1,0:T(8,128)S(1)}) custom-call(s32[4]{0:T(128)S(1)} %pad_add_fusion.where_ref, s32[4,12,12]{2,1,0:T(8,128)S(1)} %copy-done.4, bf16[128,3072]{1,0:T(8,128)(2,1)S(1)} %copy-done, bf16[2,128,768]{2,1,0:T(8,128)(2,1)S(1)} %collective-permute-done.2.refs_1_, ...), custom_call_target="tpu_custom_call" | custom-call | flops 1610612736 | bytes 1572864 | tf_op jit(solution)/shard_map/weight_grad_part/pallas_call | solution.py:84
  75.5 0.0 copy-start.2
  75.5 0.9 copy-done.2
  76.4 0.0 copy-start.6
  76.4 0.9 copy-done.6
  77.3 0.0 collective-permute-done.12
  77.3 2.2 %collective-permute-done.8.rest_3_ = bf16[384,768]{1,0:T(8,128)(2,1)} collective-permute-done((bf16[384,768]{1,0:T(8,128)(2,1)}, bf16[384,768]{1,0:T(8,128)(2,1)}, u32[]{:S(2)}, u32[]{:S(2)}) %collective-permute-start.8) | collective-permute-done | bytes 589856 | tf_op jit(solution)/shard_map/ppermute | solution.py:189
  79.5 2.4 %collective-permute-start.13 = (bf16[384,768]{1,0:T(8,128)(2,1)}, bf16[384,768]{1,0:T(8,128)(2,1)S(1)}, u32[]{:S(2)}, u32[]{:S(2)}) collective-permute-start(bf16[384,768]{1,0:T(8,128)(2,1)} %collective-permute-done.8.rest_3_), channel_id=1, source_target_pairs={{0,4},{4,0},{8,12},{12,8},{16,20},{20,16},{24,28},{28,24},{1,5},{5... | collective-permute-start | bytes 1769480 | tf_op jit(solution)/shard_map/ppermute | solution.py:189
  82.0 1.8 %collective-permute-start.14 = (f32[384,512]{1,0:T(8,128)}, f32[384,512]{1,0:T(8,128)}, u32[]{:S(2)}, u32[]{:S(2)}) collective-permute-start(f32[384,512]{1,0:T(8,128)} %copy-done.6), channel_id=1, source_target_pairs={{0,16},{4,20},{8,24},{12,28},{16,0},{20,4},{24,8},{28,12},{1,17},{... | collective-permute-start | bytes 2359304 | tf_op jit(solution)/shard_map/ppermute | solution.py:189
  83.8 0.0 collective-permute-done.11.rest_6_
  83.8 2.7 %collective-permute-done.9.rest_4_ = bf16[384,768]{1,0:T(8,128)(2,1)} collective-permute-done((bf16[384,768]{1,0:T(8,128)(2,1)}, bf16[384,768]{1,0:T(8,128)(2,1)}, u32[]{:S(2)}, u32[]{:S(2)}) %collective-permute-start.9) | collective-permute-done | bytes 589856 | tf_op jit(solution)/shard_map/ppermute | solution.py:189
  86.5 12.6 %collective-permute-done.10.rest_5_ = bf16[384,768]{1,0:T(8,128)(2,1)} collective-permute-done((bf16[384,768]{1,0:T(8,128)(2,1)}, bf16[384,768]{1,0:T(8,128)(2,1)}, u32[]{:S(2)}, u32[]{:S(2)}) %collective-permute-start.10) | collective-permute-done | bytes 589856 | tf_op jit(solution)/shard_map/ppermute | solution.py:189
  99.1 6.8 %collective-permute-done.13.rest_7_ = bf16[384,768]{1,0:T(8,128)(2,1)S(1)} collective-permute-done((bf16[384,768]{1,0:T(8,128)(2,1)}, bf16[384,768]{1,0:T(8,128)(2,1)S(1)}, u32[]{:S(2)}, u32[]{:S(2)}) %collective-permute-start.13) | collective-permute-done | bytes 589856 | tf_op jit(solution)/shard_map/ppermute | solution.py:189
  105.9 0.8 copy-done.7
  106.7 0.8 copy-done.5
  107.4 1.1 copy-done.8
  108.5 7.8 %forward_and_input.1 = (bf16[4,128,768]{2,1,0:T(8,128)(2,1)}, f32[4,128,768]{2,1,0:T(8,128)S(1)}) custom-call(s32[4]{0:T(128)S(1)} %pad_add_fusion.where_ref, s32[4,12,12]{2,1,0:T(8,128)S(1)} %copy-done.5, bf16[128,3072]{1,0:T(8,128)(2,1)S(1)} %copy-done, bf16[4,128,768]{2,1,0:T(8,128)(2,1)S(1)} %copy-done.1, bf16[384,768]{1,0:T(8,128)(2,1)} %rest_0_.1, ...), custom_call_target="tpu_custom_call" | custom-call | flops 10871635968 | bytes 9437184 | tf_op jit(solution)/shard_map/forward_and_input/pallas_call | solution.py:152
  116.3 0.4 collective-permute-done.14
  116.8 0.1 dynamic-slice_bitcast_fusion
  116.8 0.1 collective-permute-start.15
  116.9 2.2 %collective-permute-done.15 = f32[2,128,768]{2,1,0:T(8,128)S(1)} collective-permute-done((f32[2,128,768]{2,1,0:T(8,128)S(1)}, f32[2,128,768]{2,1,0:T(8,128)S(1)}, u32[]{:S(2)}, u32[]{:S(2)}) %collective-permute-start.15) | collective-permute-done | bytes 786464 | tf_op jit(solution)/shard_map/ppermute | solution.py:198
  119.2 0.1 bitcast_add_fusion
  119.3 0.0 copy-start.3
  119.3 0.8 dynamic-slice_bitcast_fusion.1
  120.1 1.6 %collective-permute-start.16 = (f32[128,768]{1,0:T(8,128)}, f32[128,768]{1,0:T(8,128)S(1)}, u32[]{:S(2)}, u32[]{:S(2)}) collective-permute-start(f32[128,768]{1,0:T(8,128)} %dynamic-slice_bitcast_fusion.1), channel_id=1, source_target_pairs={{0,2},{1,3},{2,0},{3,1},{4,6},{5,7},{6,4},{7,5},{8,10},{9,11},{10,... | collective-permute-start | bytes 1179656 | tf_op jit(solution)/shard_map/ppermute | solution.py:198
  121.7 1.0 add.68
  122.8 0.0 copy-done.3
  122.8 1.3 add.69
  124.0 1.1 pad_maximum_fusion
  125.1 6.3 %collective-permute-done.16 = f32[128,768]{1,0:T(8,128)S(1)} collective-permute-done((f32[128,768]{1,0:T(8,128)}, f32[128,768]{1,0:T(8,128)S(1)}, u32[]{:S(2)}, u32[]{:S(2)}) %collective-permute-start.16) | collective-permute-done | bytes 393248 | tf_op jit(solution)/shard_map/ppermute | solution.py:198
  131.4 0.7 fusion
  (9 shorter events, 0.2 us)
Async XLA Ops:
  0.6 6.2 %copy-start = (bf16[128,3072]{1,0:T(8,128)(2,1)S(1)}, bf16[128,3072]{1,0:T(8,128)(2,1)}, u32[]{:S(2)}) copy-start(bf16[128,3072]{1,0:T(8,128)(2,1)} %acts_ref.1) | copy-start | bytes 2359300
  0.6 21.6 %collective-permute-start.6 = (bf16[4,128,768]{2,1,0:T(8,128)(2,1)}, bf16[4,128,768]{2,1,0:T(8,128)(2,1)S(1)}, u32[]{:S(2)}, u32[]{:S(2)}) collective-permute-start(bf16[4,128,768]{2,1,0:T(8,128)(2,1)} %og_ref.1), channel_id=1, source_target_pairs={{0,4},{4,0},{8,12},{12,8},{16,20},{20,16},{24,28},{28,24},{1,5},{5... | collective-permute-start | bytes 2359304 | tf_op jit(solution)/shard_map/ppermute | solution.py:189
  3.6 20.8 %collective-permute-start.5 = (bf16[4,128,768]{2,1,0:T(8,128)(2,1)}, bf16[4,128,768]{2,1,0:T(8,128)(2,1)}, u32[]{:S(2)}, u32[]{:S(2)}) collective-permute-start(bf16[4,128,768]{2,1,0:T(8,128)(2,1)} %og_ref.1), channel_id=1, source_target_pairs={{0,8},{4,12},{8,0},{12,4},{16,24},{20,28},{24,16},{28,20},{1,9},{5... | collective-permute-start | bytes 2359304 | tf_op jit(solution)/shard_map/ppermute | solution.py:189
  6.3 32.6 %collective-permute-start.2 = (bf16[2,128,768]{2,1,0:T(8,128)(2,1)S(1)}, bf16[2,128,768]{2,1,0:T(8,128)(2,1)S(1)}, u32[]{:S(2)}, u32[]{:S(2)}) collective-permute-start(bf16[2,128,768]{2,1,0:T(8,128)(2,1)S(1)} %pad_maximum_fusion.1), channel_id=1, source_target_pairs={{0,8},{4,12},{8,0},{12,4},{16,24},{20,28},{24,16},{28,20},{1,9},{5... | collective-permute-start | bytes 1179656 | tf_op jit(solution)/shard_map/ppermute | solution.py:189
  6.8 39.8 %copy-start.1 = (bf16[4,128,768]{2,1,0:T(8,128)(2,1)S(1)}, bf16[4,128,768]{2,1,0:T(8,128)(2,1)}, u32[]{:S(2)}) copy-start(bf16[4,128,768]{2,1,0:T(8,128)(2,1)} %og_ref.1) | copy-start | bytes 2359300
  6.9 20.7 %collective-permute-start.3 = (bf16[128,768]{1,0:T(8,128)(2,1)S(1)}, bf16[128,768]{1,0:T(8,128)(2,1)S(1)}, u32[]{:S(2)}, u32[]{:S(2)}) collective-permute-start(bf16[128,768]{1,0:T(8,128)(2,1)S(1)} %pad_maximum_fusion.2), channel_id=1, source_target_pairs={{0,4},{4,0},{8,12},{12,8},{16,20},{20,16},{24,28},{28,24},{1,5},{5... | collective-permute-start | bytes 589832 | tf_op jit(solution)/shard_map/ppermute | solution.py:189
  24.4 22.3 %collective-permute-start.7 = (bf16[4,128,768]{2,1,0:T(8,128)(2,1)}, bf16[4,128,768]{2,1,0:T(8,128)(2,1)}, u32[]{:S(2)}, u32[]{:S(2)}) collective-permute-start(bf16[4,128,768]{2,1,0:T(8,128)(2,1)} %collective-permute-done.5.refs_5_), channel_id=1, source_target_pairs={{0,4},{4,0},{8,12},{12,8},{16,20},{20,16},{24,28},{28,24},{1,5},{5... | collective-permute-start | bytes 2359304 | tf_op jit(solution)/shard_map/ppermute | solution.py:189
  24.5 26.8 %collective-permute-start.1 = (bf16[384,768]{1,0:T(8,128)(2,1)}, bf16[384,768]{1,0:T(8,128)(2,1)}, u32[]{:S(2)}, u32[]{:S(2)}) collective-permute-start(bf16[384,768]{1,0:T(8,128)(2,1)} %rest_0_.1), channel_id=1, source_target_pairs={{0,16},{4,20},{8,24},{12,28},{16,0},{20,4},{24,8},{28,12},{1,17},{... | collective-permute-start | bytes 1769480 | tf_op jit(solution)/shard_map/ppermute | solution.py:189
  38.9 0.7 copy-start.9
  39.0 7.7 %collective-permute-start.4 = (bf16[128,768]{1,0:T(8,128)(2,1)S(1)}, bf16[128,768]{1,0:T(8,128)(2,1)S(1)}, u32[]{:S(2)}, u32[]{:S(2)}) collective-permute-start(bf16[128,768]{1,0:T(8,128)(2,1)S(1)} %pad_maximum_fusion.3), channel_id=1, source_target_pairs={{0,4},{4,0},{8,12},{12,8},{16,20},{20,16},{24,28},{28,24},{1,5},{5... | collective-permute-start | bytes 589832 | tf_op jit(solution)/shard_map/ppermute | solution.py:189
  39.1 30.1 %collective-permute-start = (bf16[384,768]{1,0:T(8,128)(2,1)}, bf16[384,768]{1,0:T(8,128)(2,1)}, u32[]{:S(2)}, u32[]{:S(2)}) collective-permute-start(bf16[384,768]{1,0:T(8,128)(2,1)} %rest_0_.1), channel_id=1, source_target_pairs={{0,8},{4,12},{8,0},{12,4},{16,24},{20,28},{24,16},{28,20},{1,9},{5... | collective-permute-start | bytes 1769480 | tf_op jit(solution)/shard_map/ppermute | solution.py:189
  46.7 0.8 copy-start.4
  51.3 28.2 %collective-permute-start.8 = (bf16[384,768]{1,0:T(8,128)(2,1)}, bf16[384,768]{1,0:T(8,128)(2,1)}, u32[]{:S(2)}, u32[]{:S(2)}) collective-permute-start(bf16[384,768]{1,0:T(8,128)(2,1)} %collective-permute-done.1.rest_2_), channel_id=1, source_target_pairs={{0,8},{4,12},{8,0},{12,4},{16,24},{20,28},{24,16},{28,20},{1,9},{5... | collective-permute-start | bytes 1769480 | tf_op jit(solution)/shard_map/ppermute | solution.py:189
  51.9 25.4 %collective-permute-start.12 = (f32[384,256]{1,0:T(8,128)S(1)}, f32[384,256]{1,0:T(8,128)}, u32[]{:S(2)}, u32[]{:S(2)}) collective-permute-start(f32[384,256]{1,0:T(8,128)S(1)} %get-tuple-element.22), channel_id=1, source_target_pairs={{0,16},{4,20},{8,24},{12,28},{16,0},{20,4},{24,8},{28,12},{1,17},{... | collective-permute-start | bytes 1179656 | tf_op jit(solution)/shard_map/ppermute | solution.py:189
  55.3 28.5 %collective-permute-start.11 = (bf16[384,768]{1,0:T(8,128)(2,1)}, bf16[384,768]{1,0:T(8,128)(2,1)}, u32[]{:S(2)}, u32[]{:S(2)}) collective-permute-start(bf16[384,768]{1,0:T(8,128)(2,1)} %collective-permute-done.1.rest_2_), channel_id=1, source_target_pairs={{0,4},{4,0},{8,12},{12,8},{16,20},{20,16},{24,28},{28,24},{1,5},{5... | collective-permute-start | bytes 1769480 | tf_op jit(solution)/shard_map/ppermute | solution.py:189
  69.2 17.3 %collective-permute-start.9 = (bf16[384,768]{1,0:T(8,128)(2,1)}, bf16[384,768]{1,0:T(8,128)(2,1)}, u32[]{:S(2)}, u32[]{:S(2)}) collective-permute-start(bf16[384,768]{1,0:T(8,128)(2,1)} %rest_0_.1), channel_id=1, source_target_pairs={{0,4},{4,0},{8,12},{12,8},{16,20},{20,16},{24,28},{28,24},{1,5},{5... | collective-permute-start | bytes 1769480 | tf_op jit(solution)/shard_map/ppermute | solution.py:189
  71.9 27.2 %collective-permute-start.10 = (bf16[384,768]{1,0:T(8,128)(2,1)}, bf16[384,768]{1,0:T(8,128)(2,1)}, u32[]{:S(2)}, u32[]{:S(2)}) collective-permute-start(bf16[384,768]{1,0:T(8,128)(2,1)} %collective-permute-done.rest_1_), channel_id=1, source_target_pairs={{0,4},{4,0},{8,12},{12,8},{16,20},{20,16},{24,28},{28,24},{1,5},{5... | collective-permute-start | bytes 1769480 | tf_op jit(solution)/shard_map/ppermute | solution.py:189
  75.5 0.9 copy-start.2
  76.4 0.9 copy-start.6
  79.5 26.3 %collective-permute-start.13 = (bf16[384,768]{1,0:T(8,128)(2,1)}, bf16[384,768]{1,0:T(8,128)(2,1)S(1)}, u32[]{:S(2)}, u32[]{:S(2)}) collective-permute-start(bf16[384,768]{1,0:T(8,128)(2,1)} %collective-permute-done.8.rest_3_), channel_id=1, source_target_pairs={{0,4},{4,0},{8,12},{12,8},{16,20},{20,16},{24,28},{28,24},{1,5},{5... | collective-permute-start | bytes 1769480 | tf_op jit(solution)/shard_map/ppermute | solution.py:189
  82.0 34.8 %collective-permute-start.14 = (f32[384,512]{1,0:T(8,128)}, f32[384,512]{1,0:T(8,128)}, u32[]{:S(2)}, u32[]{:S(2)}) collective-permute-start(f32[384,512]{1,0:T(8,128)} %copy-done.6), channel_id=1, source_target_pairs={{0,16},{4,20},{8,24},{12,28},{16,0},{20,4},{24,8},{28,12},{1,17},{... | collective-permute-start | bytes 2359304 | tf_op jit(solution)/shard_map/ppermute | solution.py:189
  105.9 0.8 copy-start.7
  106.7 0.8 copy-start.5
  107.4 1.1 copy-start.8
  116.8 2.4 %collective-permute-start.15 = (f32[2,128,768]{2,1,0:T(8,128)S(1)}, f32[2,128,768]{2,1,0:T(8,128)S(1)}, u32[]{:S(2)}, u32[]{:S(2)}) collective-permute-start(f32[2,128,768]{2,1,0:T(8,128)S(1)} %dynamic-slice_bitcast_fusion), channel_id=1, source_target_pairs={{0,1},{1,0},{2,3},{3,2},{4,5},{5,4},{6,7},{7,6},{8,9},{9,8},{10,11... | collective-permute-start | bytes 2359304 | tf_op jit(solution)/shard_map/ppermute | solution.py:198
  119.3 3.5 %copy-start.3 = (f32[384,512]{1,0:T(8,128)S(1)}, f32[384,512]{1,0:T(8,128)}, u32[]{:S(2)}) copy-start(f32[384,512]{1,0:T(8,128)} %copy-done.2) | copy-start | bytes 2359300
  120.1 11.4 %collective-permute-start.16 = (f32[128,768]{1,0:T(8,128)}, f32[128,768]{1,0:T(8,128)S(1)}, u32[]{:S(2)}, u32[]{:S(2)}) collective-permute-start(f32[128,768]{1,0:T(8,128)} %dynamic-slice_bitcast_fusion.1), channel_id=1, source_target_pairs={{0,2},{1,3},{2,0},{3,1},{4,6},{5,7},{6,4},{7,5},{8,10},{9,11},{10,... | collective-permute-start | bytes 1179656 | tf_op jit(solution)/shard_map/ppermute | solution.py:198

commit v12 on v11

--- a/solution.py
+++ b/solution.py
@@ -98,35 +98,29 @@
     )(where, block_mask, *acts, *og)
 
 
-def forward_and_input(acts, w_mine, w_peer, og, block_mask, where):
+def forward_and_input(acts, w_mine, w_peer, og, block_mask, where, first, before):
     nsub, tokens, width = og.shape
     depth = acts.shape[1]
     nz = len(w_mine)
+    owners = depth // (2 * w_mine[0].shape[0])
     rows = w_mine[0].shape[0]
     per = rows // LANES
     two = BS // LANES
 
     def kernel(where_ref, mask_ref, acts_ref, og_ref, *rest):
-        w_refs, (out_ref, gx_ref, acc, hilo) = rest[: 2 * nz], rest[2 * nz :]
+        w_refs, rest = rest[: 2 * nz], rest[2 * nz :]
+        out_ref, gx_ref, acc, hilo = rest[-4:]
         z, x = where_ref[0], where_ref[1]
         step = pl.program_id(0)
         col = where_ref[2] + step
 
         @pl.when(step == 0)
         def _():
-            gx_ref[...] = jnp.zeros_like(gx_ref)
-
-        acc[...] = jnp.zeros_like(acc)
-        for b in range(depth // BS):
-            total = jnp.zeros((tokens, BS), F32)
-            for s in range(nsub):
-                total = total + mask_ref[s, b, col].astype(F32) * og_ref[s].astype(F32)
-            hi = total.astype(BF16)
-            hilo[b, :tokens] = hi
-            hilo[b, tokens:] = (total - hi.astype(F32)).astype(BF16)
-
+            gx_ref[...] = rest[1][...] if before else jnp.zeros_like(gx_ref)
+
+        acc[...] = rest[0][...] if before else jnp.zeros_like(acc)
         for k in range(nz):
-            owner = z ^ k
+            owner = z ^ (first + k)
             tiles = []
             for side in range(2):
                 for g in range(per):
@@ -136,39 +130,49 @@
                 block = owner * (2 * per // two) + b
                 w = jnp.concatenate(tiles[b * two : (b + 1) * two])
                 cols = pl.ds(pl.multiple_of(block * BS, BS), BS)
+                total = jnp.zeros((tokens, BS), F32)
+                for s in range(nsub):
+                    total = total + mask_ref[s, block, col].astype(F32) * og_ref[s].astype(F32)
+                hi = total.astype(BF16)
+                hilo[:tokens] = hi
+                hilo[tokens:] = (total - hi.astype(F32)).astype(BF16)
                 prod = jnp.dot(acts_ref[:, cols], w, preferred_element_type=F32)
                 for s in range(nsub):
                     acc[s] += mask_ref[s, block, col].astype(F32) * prod
                 both = lax.dot_general(
-                    hilo[block], w, (((1,), (1,)), ((), ())), preferred_element_type=F32
+                    hilo[...], w, (((1,), (1,)), ((), ())), preferred_element_type=F32
                 )
                 gx_ref[owner, :, b * BS : (b + 1) * BS] += both[:tokens] + both[tokens:]
-        out_ref[...] = acc[...].astype(BF16)
+        out_ref[...] = acc[...].astype(out_ref.dtype)
 
     smem = pl.BlockSpec(memory_space=pltpu.SMEM)
     by_col = pl.BlockSpec((nsub, tokens, BS), lambda j: (0, 0, j))
     whole = pl.BlockSpec((tokens, depth), lambda j: (0, 0))
-    by_owner = (nz, tokens, depth // nz)
+    by_owner = (owners, tokens, depth // owners)
+    gx_spec = pl.BlockSpec(by_owner, lambda j: (0, 0, 0))
     return pl.pallas_call(
         kernel,
         grid=(width // BS,),
         out_shape=(
-            jax.ShapeDtypeStruct((nsub, tokens, width), BF16),
+            jax.ShapeDtypeStruct((nsub, tokens, width), BF16 if before else F32),
             jax.ShapeDtypeStruct(by_owner, F32),
         ),
         in_specs=[smem, smem, whole, by_col]
-        + [pl.BlockSpec((rows, BS), lambda j: (0, j))] * (2 * nz),
-        out_specs=(by_col, pl.BlockSpec(by_owner, lambda j: (0, 0, 0))),
+        + [pl.BlockSpec((rows, BS), lambda j: (0, j))] * (2 * nz)
+        + ([by_col, gx_spec] if before else []),
+        out_specs=(by_col, gx_spec),
         scratch_shapes=[
             pltpu.VMEM((nsub, tokens, BS), F32),
-            pltpu.VMEM((depth // BS, 2 * tokens, BS), BF16),
+            pltpu.VMEM((2 * tokens, BS), BF16),
         ],
         compiler_params=pltpu.CompilerParams(vmem_limit_bytes=FORWARD_VMEM),
         cost_estimate=pl.CostEstimate(
-            flops=36 * tokens * depth * width, bytes_accessed=4 * depth * width, transcendentals=0
+            flops=72 * tokens * nz * rows * width,
+            bytes_accessed=8 * nz * rows * width,
+            transcendentals=0,
         ),
         name="forward_and_input",
-    )(where, block_mask, acts, og, *w_mine, *w_peer)
+    )(where, block_mask, acts, og, *w_mine, *w_peer, *(before or ()))
 
 
 def on_device(acts, weight, block_mask, out_grad):
@@ -220,16 +224,22 @@
     acts_all = [acts, acts_one, acts_side, acts_both]
     keep_0, send_0 = weight_grad_part(acts_all, og, block_mask, where, rows, 0, 1)
     got_0 = swap_z(send_0, 2)
-    keep_1, send_1 = weight_grad_part(acts_all, og, block_mask, where, rows, 1, width // BS - 1)
+    w_peer = [swap_x(after(weight, acts_side))]
+    keep_1, send_1 = weight_grad_part(
+        acts_all, og, block_mask, after(where, w_peer[0]), rows, 1, width // BS - 1
+    )
     got_1 = swap_z(send_1, 2)
     grad_w = jnp.concatenate([keep_0 + got_0, keep_1 + got_1], axis=1)
     w_three = swap_z(after(w_two, keep_0), 1)
     w_mine = [weight, w_one, w_two, w_three]
-    w_peer = [swap_x(after(w, keep_0)) for w in w_mine[:3]]
-    w_peer.append(swap_x(after(w_three, got_0, keep_1)))
-
+    w_peer += [swap_x(after(w_one, got_0)), swap_x(after(w_two, keep_0))]
+    w_peer.append(swap_x(after(w_three, keep_1)))
+
+    sums = forward_and_input(
+        acts, w_mine[:3], w_peer[:3], out_grad, block_mask, where, 0, None
+    )
     outputs, gx = forward_and_input(
-        acts, w_mine, w_peer, out_grad, block_mask, where
+        acts, w_mine[3:], w_peer[3:], out_grad, block_mask, where, 3, sums
     )
 
     by = after(gx, got_1).reshape(2, 2, tokens, depth // 4)

time: 133 us -> 135 us (1.015)
  waiting for transfers between devices: 82.3 us -> 89 us
  local copies, waits for them, and re-layouts: 8.28 us -> 5.01 us
  starting transfers between devices: 22.8 us -> 20.2 us
  Pallas kernels: 13.6 us -> 15.1 us
    ppermute x15, waiting for transfers between devices: 73.8 us -> 80.4 us  [swap_dp(): return lax.ppermute(a, 'dp', [(d, d ^ bits) for d in range(dp)])]
    unnamed x21 -> x17, local copies, waits for them, and re-layouts: 6.3 us -> 3.03 us
    ppermute x15, starting transfers between devices: 21.1 us -> 18.7 us  [swap_dp(): return lax.ppermute(a, 'dp', [(d, d ^ bits) for d in range(dp)])]
    pallas_call x1 -> x2, Pallas kernels: 7.85 us -> 9.33 us  [forward_and_input(): pl.pallas_call(kernel, grid=(width // BS,), out_shape=(jax.ShapeDtypeStru...]
  transfers between devices with their start and end apart: 17 -> 17, of which waited for: 13 -> 13; matrix products, arithmetic and copies ran while one was open for 4% -> 4% of each run, Pallas kernels for 10% -> 11%
where the time goes in v12:
time: 135 us
  waiting for transfers between devices  89 us (66%)
  starting transfers between devices  20.2 us (15%)
  Pallas kernels  15.1 us (11%)
  local copies, waits for them, and re-layouts  5.01 us (4%)
  other arithmetic  4.36 us (3%)
    ppermute x15, waiting for transfers between devices, swap_dp(): return lax.ppermute(a, 'dp', [(d, d ^ bits) for d in range(dp)])  80.4 us
    ppermute x15, starting transfers between devices, swap_dp(): return lax.ppermute(a, 'dp', [(d, d ^ bits) for d in range(dp)])  18.7 us
    pallas_call x2, Pallas kernels, forward_and_input(): pl.pallas_call(kernel, grid=(width // BS,), out_shape=(jax.ShapeDtypeStru...  9.33 us
    ppermute x2, waiting for transfers between devices, swap_f(): return lax.ppermute(a, 'fsdp', [(d, d ^ bit) for d in range(fsdp)])  8.67 us
    pallas_call x2, Pallas kernels, weight_grad_part(): pl.pallas_call(kernel, grid=(chunks,), out_shape=(jax.ShapeDtypeStruct((r...  5.76 us
    unnamed x17, local copies, waits for them, and re-layouts  3.03 us
  transfers between devices with their start and end apart: 17, of which 13 were waited for; matrix products, arithmetic and copies ran while one was open for 4% of the time, Pallas kernels for 11%

profile of v12, /device:TPU:0, one launch (start us, length us, event | category | flops | bytes accessed | tf_op | source)
XLA Modules:
  0.0 134.5 jit_solution(729626066427756768)
XLA Ops:
  0.6 0.0 copy-start
  0.6 3.0 %collective-permute-start.5 = (bf16[4,128,768]{2,1,0:T(8,128)(2,1)}, bf16[4,128,768]{2,1,0:T(8,128)(2,1)S(1)}, u32[]{:S(2)}, u32[]{:S(2)}) collective-permute-start(bf16[4,128,768]{2,1,0:T(8,128)(2,1)} %og_ref.3), channel_id=1, source_target_pairs={{0,4},{4,0},{8,12},{12,8},{16,20},{20,16},{24,28},{28,24},{1,5},{5... | collective-permute-start | bytes 2359304 | tf_op jit(solution)/shard_map/ppermute | solution.py:193
  3.6 1.6 %collective-permute-start.4 = (bf16[4,128,768]{2,1,0:T(8,128)(2,1)}, bf16[4,128,768]{2,1,0:T(8,128)(2,1)}, u32[]{:S(2)}, u32[]{:S(2)}) collective-permute-start(bf16[4,128,768]{2,1,0:T(8,128)(2,1)} %og_ref.3), channel_id=1, source_target_pairs={{0,8},{4,12},{8,0},{12,4},{16,24},{20,28},{24,16},{28,20},{1,9},{5... | collective-permute-start | bytes 2359304 | tf_op jit(solution)/shard_map/ppermute | solution.py:193
  5.2 1.0 dynamic-slice_bitcast_fusion.3
  6.3 0.0 copy-start.1
  6.3 0.5 collective-permute-start.1
  6.8 0.0 copy-done
  6.9 0.2 collective-permute-start.2
  7.1 15.1 %collective-permute-done.5.refs_6_ = bf16[4,128,768]{2,1,0:T(8,128)(2,1)S(1)} collective-permute-done((bf16[4,128,768]{2,1,0:T(8,128)(2,1)}, bf16[4,128,768]{2,1,0:T(8,128)(2,1)S(1)}, u32[]{:S(2)}, u32[]{:S(2)}) %collective-permute-start.5) | collective-permute-done | bytes 786464 | tf_op jit(solution)/shard_map/ppermute | solution.py:193
  22.2 2.2 %collective-permute-done.4.refs_5_ = bf16[4,128,768]{2,1,0:T(8,128)(2,1)} collective-permute-done((bf16[4,128,768]{2,1,0:T(8,128)(2,1)}, bf16[4,128,768]{2,1,0:T(8,128)(2,1)}, u32[]{:S(2)}, u32[]{:S(2)}) %collective-permute-start.4) | collective-permute-done | bytes 786464 | tf_op jit(solution)/shard_map/ppermute | solution.py:193
  24.4 0.1 collective-permute-start.6
  24.5 1.9 %collective-permute-done.2.refs_2_ = bf16[128,768]{1,0:T(8,128)(2,1)S(1)} collective-permute-done((bf16[128,768]{1,0:T(8,128)(2,1)S(1)}, bf16[128,768]{1,0:T(8,128)(2,1)S(1)}, u32[]{:S(2)}, u32[]{:S(2)}) %collective-permute-start.2) | collective-permute-done | bytes 196640 | tf_op jit(solution)/shard_map/ppermute | solution.py:193
  26.4 4.8 %collective-permute-done.1.refs_1_ = bf16[2,128,768]{2,1,0:T(8,128)(2,1)S(1)} collective-permute-done((bf16[2,128,768]{2,1,0:T(8,128)(2,1)S(1)}, bf16[2,128,768]{2,1,0:T(8,128)(2,1)S(1)}, u32[]{:S(2)}, u32[]{:S(2)}) %collective-permute-start.1) | collective-permute-done | bytes 393248 | tf_op jit(solution)/shard_map/ppermute | solution.py:193
  31.3 0.0 copy-start.7
  31.4 0.5 collective-permute-start.3
  31.8 2.7 %collective-permute-start = (bf16[384,768]{1,0:T(8,128)(2,1)}, bf16[384,768]{1,0:T(8,128)(2,1)}, u32[]{:S(2)}, u32[]{:S(2)}) collective-permute-start(bf16[384,768]{1,0:T(8,128)(2,1)} %rest_0_.1), channel_id=1, source_target_pairs={{0,16},{4,20},{8,24},{12,28},{16,0},{20,4},{24,8},{28,12},{1,17},{... | collective-permute-start | bytes 1769480 | tf_op jit(solution)/shard_map/ppermute | solution.py:193
  34.6 1.6 %collective-permute-start.10 = (bf16[384,768]{1,0:T(8,128)(2,1)}, bf16[384,768]{1,0:T(8,128)(2,1)}, u32[]{:S(2)}, u32[]{:S(2)}) collective-permute-start(bf16[384,768]{1,0:T(8,128)(2,1)} %rest_0_.1), channel_id=1, source_target_pairs={{0,8},{4,12},{8,0},{12,4},{16,24},{20,28},{24,16},{28,20},{1,9},{5... | collective-permute-start | bytes 1769480 | tf_op jit(solution)/shard_map/ppermute | solution.py:193
  36.1 0.0 copy-done.7
  36.2 0.6 copy.10.mask_ref
  36.8 0.1 pad_add_fusion.where_ref
  36.8 9.8 %collective-permute-done.3.refs_3_ = bf16[128,768]{1,0:T(8,128)(2,1)S(1)} collective-permute-done((bf16[128,768]{1,0:T(8,128)(2,1)S(1)}, bf16[128,768]{1,0:T(8,128)(2,1)S(1)}, u32[]{:S(2)}, u32[]{:S(2)}) %collective-permute-start.3) | collective-permute-done | bytes 196640 | tf_op jit(solution)/shard_map/ppermute | solution.py:193
  46.7 0.0 collective-permute-done.6.refs_7_
  46.7 0.0 copy-done.1
  46.7 0.0 copy-start.4
  46.7 0.8 copy-done.4
  47.4 2.2 %weight_grad_part.2 = (f32[384,256]{1,0:T(8,128)S(1)}, f32[384,256]{1,0:T(8,128)S(1)}) custom-call(s32[4]{0:T(128)S(1)} %pad_add_fusion.where_ref, s32[4,12,12]{2,1,0:T(8,128)S(1)} %copy-done.4, bf16[128,3072]{1,0:T(8,128)(2,1)S(1)} %copy-done, bf16[2,128,768]{2,1,0:T(8,128)(2,1)S(1)} %collective-permute-done.1.refs_1_, ...), custom_call_target="tpu_custom_call" | custom-call | flops 805306368 | bytes 786432 | tf_op jit(solution)/shard_map/weight_grad_part/pallas_call | solution.py:84
  49.6 2.9 %collective-permute-start.11 = (f32[384,256]{1,0:T(8,128)S(1)}, f32[384,256]{1,0:T(8,128)}, u32[]{:S(2)}, u32[]{:S(2)}) collective-permute-start(f32[384,256]{1,0:T(8,128)S(1)} %get-tuple-element.27), channel_id=1, source_target_pairs={{0,16},{4,20},{8,24},{12,28},{16,0},{20,4},{24,8},{28,12},{1,17},{... | collective-permute-start | bytes 1179656 | tf_op jit(solution)/shard_map/ppermute | solution.py:193
  52.5 1.5 %collective-permute-start.8 = (bf16[384,768]{1,0:T(8,128)(2,1)}, bf16[384,768]{1,0:T(8,128)(2,1)}, u32[]{:S(2)}, u32[]{:S(2)}) collective-permute-start(bf16[384,768]{1,0:T(8,128)(2,1)} %rest_0_.1), channel_id=1, source_target_pairs={{0,4},{4,0},{8,12},{12,8},{16,20},{20,16},{24,28},{28,24},{1,5},{5... | collective-permute-start | bytes 1769480 | tf_op jit(solution)/shard_map/ppermute | solution.py:193
  54.0 12.8 %collective-permute-done.rest_2_ = bf16[384,768]{1,0:T(8,128)(2,1)} collective-permute-done((bf16[384,768]{1,0:T(8,128)(2,1)}, bf16[384,768]{1,0:T(8,128)(2,1)}, u32[]{:S(2)}, u32[]{:S(2)}) %collective-permute-start) | collective-permute-done | bytes 589856 | tf_op jit(solution)/shard_map/ppermute | solution.py:193
  66.9 0.0 collective-permute-start.7
  66.9 1.5 %collective-permute-start.13 = (bf16[384,768]{1,0:T(8,128)(2,1)}, bf16[384,768]{1,0:T(8,128)(2,1)}, u32[]{:S(2)}, u32[]{:S(2)}) collective-permute-start(bf16[384,768]{1,0:T(8,128)(2,1)} %collective-permute-done.rest_2_), channel_id=1, source_target_pairs={{0,4},{4,0},{8,12},{12,8},{16,20},{20,16},{24,28},{28,24},{1,5},{5... | collective-permute-start | bytes 1769480 | tf_op jit(solution)/shard_map/ppermute | solution.py:193
  68.4 0.0 collective-permute-done.10.rest_1_
  68.4 8.3 %collective-permute-done.11 = f32[384,256]{1,0:T(8,128)} collective-permute-done((f32[384,256]{1,0:T(8,128)S(1)}, f32[384,256]{1,0:T(8,128)}, u32[]{:S(2)}, u32[]{:S(2)}) %collective-permute-start.11) | collective-permute-done | bytes 393248 | tf_op jit(solution)/shard_map/ppermute | solution.py:193
  76.7 1.3 collective-permute-start.12
  78.0 0.0 collective-permute-done.8.rest_3_
  78.0 0.0 copy-start.5
  78.0 0.8 copy-done.5
  78.8 0.0 copy-start.6
  78.8 3.6 %weight_grad_part.3 = (f32[384,512]{1,0:T(8,128)S(1)}, f32[384,512]{1,0:T(8,128)S(1)}) custom-call(s32[4]{0:T(128)S(1)} %pad_add_fusion.where_ref, s32[4,12,12]{2,1,0:T(8,128)S(1)} %copy-done.5, bf16[128,3072]{1,0:T(8,128)(2,1)S(1)} %copy-done, bf16[2,128,768]{2,1,0:T(8,128)(2,1)S(1)} %collective-permute-done.1.refs_1_, ...), custom_call_target="tpu_custom_call" | custom-call | flops 1610612736 | bytes 1572864 | tf_op jit(solution)/shard_map/weight_grad_part/pallas_call | solution.py:84
  82.4 0.0 copy-start.2
  82.4 0.9 copy-done.2
  83.3 0.0 collective-permute-start.14
  83.3 0.2 collective-permute-done.7.rest_0_
  83.4 1.3 collective-permute-start.9
  84.7 0.0 collective-permute-done.13.rest_5_
  84.7 8.6 %collective-permute-done.12.rest_4_ = bf16[384,768]{1,0:T(8,128)(2,1)} collective-permute-done((bf16[384,768]{1,0:T(8,128)(2,1)}, bf16[384,768]{1,0:T(8,128)(2,1)}, u32[]{:S(2)}, u32[]{:S(2)}) %collective-permute-start.12) | collective-permute-done | bytes 589856 | tf_op jit(solution)/shard_map/ppermute | solution.py:193
  93.3 0.0 copy-done.6
  93.3 5.5 %forward_and_input.2 = (f32[4,128,768]{2,1,0:T(8,128)S(1)}, f32[4,128,768]{2,1,0:T(8,128)S(1)}) custom-call(s32[4]{0:T(128)S(1)} %pad_add_fusion.where_ref, s32[4,12,12]{2,1,0:T(8,128)S(1)} %copy-done.6, bf16[128,3072]{1,0:T(8,128)(2,1)S(1)} %copy-done, bf16[4,128,768]{2,1,0:T(8,128)(2,1)S(1)} %copy-done.1, bf16[384,768]{1,0:T(8,128)(2,1)} %rest_0_.1, ...), custom_call_target="tpu_custom_call" | custom-call | flops 8153726976 | bytes 7077888 | tf_op jit(solution)/shard_map/forward_and_input/pallas_call | solution.py:153
  98.8 5.4 %collective-permute-done.9.rest_1_ = bf16[384,768]{1,0:T(8,128)(2,1)S(1)} collective-permute-done((bf16[384,768]{1,0:T(8,128)(2,1)}, bf16[384,768]{1,0:T(8,128)(2,1)S(1)}, u32[]{:S(2)}, u32[]{:S(2)}) %collective-permute-start.9) | collective-permute-done | bytes 589856 | tf_op jit(solution)/shard_map/ppermute | solution.py:193
  104.1 3.9 %forward_and_input.3 = (bf16[4,128,768]{2,1,0:T(8,128)(2,1)}, f32[4,128,768]{2,1,0:T(8,128)S(1)}) custom-call(s32[4]{0:T(128)S(1)} %pad_add_fusion.where_ref, s32[4,12,12]{2,1,0:T(8,128)S(1)} %copy-done.6, bf16[128,3072]{1,0:T(8,128)(2,1)S(1)} %copy-done, bf16[4,128,768]{2,1,0:T(8,128)(2,1)S(1)} %copy-done.1, ...), custom_call_target="tpu_custom_call" | custom-call | flops 2717908992 | bytes 2359296 | tf_op jit(solution)/shard_map/forward_and_input/pallas_call | solution.py:153
  108.0 11.1 %collective-permute-done.14 = f32[384,512]{1,0:T(8,128)} collective-permute-done((f32[384,512]{1,0:T(8,128)S(1)}, f32[384,512]{1,0:T(8,128)}, u32[]{:S(2)}, u32[]{:S(2)}) %collective-permute-start.14) | collective-permute-done | bytes 786464 | tf_op jit(solution)/shard_map/ppermute | solution.py:193
  119.2 0.1 dynamic-slice_bitcast_fusion
  119.2 0.1 collective-permute-start.15
  119.3 2.2 %collective-permute-done.15 = f32[2,128,768]{2,1,0:T(8,128)S(1)} collective-permute-done((f32[2,128,768]{2,1,0:T(8,128)S(1)}, f32[2,128,768]{2,1,0:T(8,128)S(1)}, u32[]{:S(2)}, u32[]{:S(2)}) %collective-permute-start.15) | collective-permute-done | bytes 786464 | tf_op jit(solution)/shard_map/ppermute | solution.py:202
  121.6 0.1 bitcast_add_fusion
  121.7 0.0 copy-start.3
  121.7 0.8 dynamic-slice_bitcast_fusion.1
  122.5 1.5 %collective-permute-start.16 = (f32[128,768]{1,0:T(8,128)}, f32[128,768]{1,0:T(8,128)S(1)}, u32[]{:S(2)}, u32[]{:S(2)}) collective-permute-start(f32[128,768]{1,0:T(8,128)} %dynamic-slice_bitcast_fusion.1), channel_id=1, source_target_pairs={{0,2},{1,3},{2,0},{3,1},{4,6},{5,7},{6,4},{7,5},{8,10},{9,11},{10,... | collective-permute-start | bytes 1179656 | tf_op jit(solution)/shard_map/ppermute | solution.py:202
  124.0 1.0 add.68
  125.0 0.0 copy-done.3
  125.0 1.3 add.69
  126.3 1.1 pad_maximum_fusion
  127.4 6.4 %collective-permute-done.16 = f32[128,768]{1,0:T(8,128)S(1)} collective-permute-done((f32[128,768]{1,0:T(8,128)}, f32[128,768]{1,0:T(8,128)S(1)}, u32[]{:S(2)}, u32[]{:S(2)}) %collective-permute-start.16) | collective-permute-done | bytes 393248 | tf_op jit(solution)/shard_map/ppermute | solution.py:202
  133.8 0.7 fusion
  (6 shorter events, 0.2 us)
Async XLA Ops:
  0.6 6.2 %copy-start = (bf16[128,3072]{1,0:T(8,128)(2,1)S(1)}, bf16[128,3072]{1,0:T(8,128)(2,1)}, u32[]{:S(2)}) copy-start(bf16[128,3072]{1,0:T(8,128)(2,1)} %acts_ref.3) | copy-start | bytes 2359300
  0.6 21.6 %collective-permute-start.5 = (bf16[4,128,768]{2,1,0:T(8,128)(2,1)}, bf16[4,128,768]{2,1,0:T(8,128)(2,1)S(1)}, u32[]{:S(2)}, u32[]{:S(2)}) collective-permute-start(bf16[4,128,768]{2,1,0:T(8,128)(2,1)} %og_ref.3), channel_id=1, source_target_pairs={{0,4},{4,0},{8,12},{12,8},{16,20},{20,16},{24,28},{28,24},{1,5},{5... | collective-permute-start | bytes 2359304 | tf_op jit(solution)/shard_map/ppermute | solution.py:193
  3.6 20.8 %collective-permute-start.4 = (bf16[4,128,768]{2,1,0:T(8,128)(2,1)}, bf16[4,128,768]{2,1,0:T(8,128)(2,1)}, u32[]{:S(2)}, u32[]{:S(2)}) collective-permute-start(bf16[4,128,768]{2,1,0:T(8,128)(2,1)} %og_ref.3), channel_id=1, source_target_pairs={{0,8},{4,12},{8,0},{12,4},{16,24},{20,28},{24,16},{28,20},{1,9},{5... | collective-permute-start | bytes 2359304 | tf_op jit(solution)/shard_map/ppermute | solution.py:193
  6.3 40.4 %copy-start.1 = (bf16[4,128,768]{2,1,0:T(8,128)(2,1)S(1)}, bf16[4,128,768]{2,1,0:T(8,128)(2,1)}, u32[]{:S(2)}) copy-start(bf16[4,128,768]{2,1,0:T(8,128)(2,1)} %og_ref.3) | copy-start | bytes 2359300
  6.3 25.0 %collective-permute-start.1 = (bf16[2,128,768]{2,1,0:T(8,128)(2,1)S(1)}, bf16[2,128,768]{2,1,0:T(8,128)(2,1)S(1)}, u32[]{:S(2)}, u32[]{:S(2)}) collective-permute-start(bf16[2,128,768]{2,1,0:T(8,128)(2,1)S(1)} %pad_maximum_fusion.1), channel_id=1, source_target_pairs={{0,8},{4,12},{8,0},{12,4},{16,24},{20,28},{24,16},{28,20},{1,9},{5... | collective-permute-start | bytes 1179656 | tf_op jit(solution)/shard_map/ppermute | solution.py:193
  6.9 19.5 %collective-permute-start.2 = (bf16[128,768]{1,0:T(8,128)(2,1)S(1)}, bf16[128,768]{1,0:T(8,128)(2,1)S(1)}, u32[]{:S(2)}, u32[]{:S(2)}) collective-permute-start(bf16[128,768]{1,0:T(8,128)(2,1)S(1)} %pad_maximum_fusion.2), channel_id=1, source_target_pairs={{0,4},{4,0},{8,12},{12,8},{16,20},{20,16},{24,28},{28,24},{1,5},{5... | collective-permute-start | bytes 589832 | tf_op jit(solution)/shard_map/ppermute | solution.py:193
  24.4 22.3 %collective-permute-start.6 = (bf16[4,128,768]{2,1,0:T(8,128)(2,1)}, bf16[4,128,768]{2,1,0:T(8,128)(2,1)}, u32[]{:S(2)}, u32[]{:S(2)}) collective-permute-start(bf16[4,128,768]{2,1,0:T(8,128)(2,1)} %collective-permute-done.4.refs_5_), channel_id=1, source_target_pairs={{0,4},{4,0},{8,12},{12,8},{16,20},{20,16},{24,28},{28,24},{1,5},{5... | collective-permute-start | bytes 2359304 | tf_op jit(solution)/shard_map/ppermute | solution.py:193
  31.3 4.9 %copy-start.7 = (s32[4,12,12]{2,0,1:T(4,128)S(1)}, s32[4,12,12]{2,0,1:T(4,128)}, u32[]{:S(2)}) copy-start(s32[4,12,12]{2,0,1:T(4,128)} %param.6) | copy-start | bytes 6916
  31.4 15.3 %collective-permute-start.3 = (bf16[128,768]{1,0:T(8,128)(2,1)S(1)}, bf16[128,768]{1,0:T(8,128)(2,1)S(1)}, u32[]{:S(2)}, u32[]{:S(2)}) collective-permute-start(bf16[128,768]{1,0:T(8,128)(2,1)S(1)} %pad_maximum_fusion.3), channel_id=1, source_target_pairs={{0,4},{4,0},{8,12},{12,8},{16,20},{20,16},{24,28},{28,24},{1,5},{5... | collective-permute-start | bytes 589832 | tf_op jit(solution)/shard_map/ppermute | solution.py:193
  31.8 35.0 %collective-permute-start = (bf16[384,768]{1,0:T(8,128)(2,1)}, bf16[384,768]{1,0:T(8,128)(2,1)}, u32[]{:S(2)}, u32[]{:S(2)}) collective-permute-start(bf16[384,768]{1,0:T(8,128)(2,1)} %rest_0_.1), channel_id=1, source_target_pairs={{0,16},{4,20},{8,24},{12,28},{16,0},{20,4},{24,8},{28,12},{1,17},{... | collective-permute-start | bytes 1769480 | tf_op jit(solution)/shard_map/ppermute | solution.py:193
  34.6 33.8 %collective-permute-start.10 = (bf16[384,768]{1,0:T(8,128)(2,1)}, bf16[384,768]{1,0:T(8,128)(2,1)}, u32[]{:S(2)}, u32[]{:S(2)}) collective-permute-start(bf16[384,768]{1,0:T(8,128)(2,1)} %rest_0_.1), channel_id=1, source_target_pairs={{0,8},{4,12},{8,0},{12,4},{16,24},{20,28},{24,16},{28,20},{1,9},{5... | collective-permute-start | bytes 1769480 | tf_op jit(solution)/shard_map/ppermute | solution.py:193
  46.7 0.8 copy-start.4
  49.6 27.1 %collective-permute-start.11 = (f32[384,256]{1,0:T(8,128)S(1)}, f32[384,256]{1,0:T(8,128)}, u32[]{:S(2)}, u32[]{:S(2)}) collective-permute-start(f32[384,256]{1,0:T(8,128)S(1)} %get-tuple-element.27), channel_id=1, source_target_pairs={{0,16},{4,20},{8,24},{12,28},{16,0},{20,4},{24,8},{28,12},{1,17},{... | collective-permute-start | bytes 1179656 | tf_op jit(solution)/shard_map/ppermute | solution.py:193
  52.5 25.5 %collective-permute-start.8 = (bf16[384,768]{1,0:T(8,128)(2,1)}, bf16[384,768]{1,0:T(8,128)(2,1)}, u32[]{:S(2)}, u32[]{:S(2)}) collective-permute-start(bf16[384,768]{1,0:T(8,128)(2,1)} %rest_0_.1), channel_id=1, source_target_pairs={{0,4},{4,0},{8,12},{12,8},{16,20},{20,16},{24,28},{28,24},{1,5},{5... | collective-permute-start | bytes 1769480 | tf_op jit(solution)/shard_map/ppermute | solution.py:193
  66.9 16.5 %collective-permute-start.7 = (bf16[384,768]{1,0:T(8,128)(2,1)}, bf16[384,768]{1,0:T(8,128)(2,1)}, u32[]{:S(2)}, u32[]{:S(2)}) collective-permute-start(bf16[384,768]{1,0:T(8,128)(2,1)} %collective-permute-done.rest_2_), channel_id=1, source_target_pairs={{0,8},{4,12},{8,0},{12,4},{16,24},{20,28},{24,16},{28,20},{1,9},{5... | collective-permute-start | bytes 1769480 | tf_op jit(solution)/shard_map/ppermute | solution.py:193
  66.9 17.8 %collective-permute-start.13 = (bf16[384,768]{1,0:T(8,128)(2,1)}, bf16[384,768]{1,0:T(8,128)(2,1)}, u32[]{:S(2)}, u32[]{:S(2)}) collective-permute-start(bf16[384,768]{1,0:T(8,128)(2,1)} %collective-permute-done.rest_2_), channel_id=1, source_target_pairs={{0,4},{4,0},{8,12},{12,8},{16,20},{20,16},{24,28},{28,24},{1,5},{5... | collective-permute-start | bytes 1769480 | tf_op jit(solution)/shard_map/ppermute | solution.py:193
  76.7 16.6 %collective-permute-start.12 = (bf16[384,768]{1,0:T(8,128)(2,1)}, bf16[384,768]{1,0:T(8,128)(2,1)}, u32[]{:S(2)}, u32[]{:S(2)}) collective-permute-start(bf16[384,768]{1,0:T(8,128)(2,1)} %collective-permute-done.10.rest_1_), channel_id=1, source_target_pairs={{0,4},{4,0},{8,12},{12,8},{16,20},{20,16},{24,28},{28,24},{1,5},{5... | collective-permute-start | bytes 1769480 | tf_op jit(solution)/shard_map/ppermute | solution.py:193
  78.0 0.8 copy-start.5
  78.8 14.5 %copy-start.6 = (s32[4,12,12]{2,1,0:T(8,128)S(1)}, s32[4,12,12]{2,1,0:T(8,128)}, u32[]{:S(2)}) copy-start(s32[4,12,12]{2,1,0:T(8,128)} %copy.10.mask_ref) | copy-start | bytes 6916
  82.4 0.9 copy-start.2
  83.3 35.9 %collective-permute-start.14 = (f32[384,512]{1,0:T(8,128)S(1)}, f32[384,512]{1,0:T(8,128)}, u32[]{:S(2)}, u32[]{:S(2)}) collective-permute-start(f32[384,512]{1,0:T(8,128)S(1)} %get-tuple-element.32), channel_id=1, source_target_pairs={{0,16},{4,20},{8,24},{12,28},{16,0},{20,4},{24,8},{28,12},{1,17},{... | collective-permute-start | bytes 2359304 | tf_op jit(solution)/shard_map/ppermute | solution.py:193
  83.4 20.7 %collective-permute-start.9 = (bf16[384,768]{1,0:T(8,128)(2,1)}, bf16[384,768]{1,0:T(8,128)(2,1)S(1)}, u32[]{:S(2)}, u32[]{:S(2)}) collective-permute-start(bf16[384,768]{1,0:T(8,128)(2,1)} %collective-permute-done.7.rest_0_), channel_id=1, source_target_pairs={{0,4},{4,0},{8,12},{12,8},{16,20},{20,16},{24,28},{28,24},{1,5},{5... | collective-permute-start | bytes 1769480 | tf_op jit(solution)/shard_map/ppermute | solution.py:193
  119.2 2.4 %collective-permute-start.15 = (f32[2,128,768]{2,1,0:T(8,128)S(1)}, f32[2,128,768]{2,1,0:T(8,128)S(1)}, u32[]{:S(2)}, u32[]{:S(2)}) collective-permute-start(f32[2,128,768]{2,1,0:T(8,128)S(1)} %dynamic-slice_bitcast_fusion), channel_id=1, source_target_pairs={{0,1},{1,0},{2,3},{3,2},{4,5},{5,4},{6,7},{7,6},{8,9},{9,8},{10,11... | collective-permute-start | bytes 2359304 | tf_op jit(solution)/shard_map/ppermute | solution.py:202
  121.7 3.4 %copy-start.3 = (f32[384,512]{1,0:T(8,128)S(1)}, f32[384,512]{1,0:T(8,128)}, u32[]{:S(2)}) copy-start(f32[384,512]{1,0:T(8,128)} %copy-done.2) | copy-start | bytes 2359300
  122.5 11.4 %collective-permute-start.16 = (f32[128,768]{1,0:T(8,128)}, f32[128,768]{1,0:T(8,128)S(1)}, u32[]{:S(2)}, u32[]{:S(2)}) collective-permute-start(f32[128,768]{1,0:T(8,128)} %dynamic-slice_bitcast_fusion.1), channel_id=1, source_target_pairs={{0,2},{1,3},{2,0},{3,1},{4,6},{5,7},{6,4},{7,5},{8,10},{9,11},{10,... | collective-permute-start | bytes 1179656 | tf_op jit(solution)/shard_map/ppermute | solution.py:202

commit v13 on v12

--- a/solution.py
+++ b/solution.py
@@ -222,27 +222,28 @@
     w_one = swap_z(weight, 1)
     og = [out_grad, og_one, og_side, og_both]
     acts_all = [acts, acts_one, acts_side, acts_both]
-    keep_0, send_0 = weight_grad_part(acts_all, og, block_mask, where, rows, 0, 1)
-    got_0 = swap_z(send_0, 2)
-    w_peer = [swap_x(after(weight, acts_side))]
-    keep_1, send_1 = weight_grad_part(
-        acts_all, og, block_mask, after(where, w_peer[0]), rows, 1, width // BS - 1
-    )
-    got_1 = swap_z(send_1, 2)
-    grad_w = jnp.concatenate([keep_0 + got_0, keep_1 + got_1], axis=1)
-    w_three = swap_z(after(w_two, keep_0), 1)
+    keeps, gots = [], []
+    for j in range(width // BS):
+        keep, send = weight_grad_part(acts_all, og, block_mask, where, rows, j, 1)
+        keeps.append(keep)
+        gots.append(swap_z(send, 2))
+    grad_w = jnp.concatenate([k + g for k, g in zip(keeps, gots)], axis=1)
+    w_three = swap_z(after(w_two, keeps[0]), 1)
     w_mine = [weight, w_one, w_two, w_three]
-    w_peer += [swap_x(after(w_one, got_0)), swap_x(after(w_two, keep_0))]
-    w_peer.append(swap_x(after(w_three, keep_1)))
+    x_own = swap_x(after(weight, acts_side))
+    x_one = swap_x(after(w_one, gots[0], x_own, keeps[1]))
+    x_two = swap_x(after(w_two, keeps[0]))
+    x_three = swap_x(after(w_three, keeps[2], x_two))
+    w_peer = [x_own, x_one, x_two, x_three]
 
     sums = forward_and_input(
-        acts, w_mine[:3], w_peer[:3], out_grad, block_mask, where, 0, None
+        acts, w_mine[:3], w_peer[:3], after(out_grad, gots[1]), block_mask, where, 0, None
     )
     outputs, gx = forward_and_input(
         acts, w_mine[3:], w_peer[3:], out_grad, block_mask, where, 3, sums
     )
 
-    by = after(gx, got_1).reshape(2, 2, tokens, depth // 4)
+    by = after(gx, gots[2]).reshape(2, 2, tokens, depth // 4)
     pair = lax.dynamic_index_in_dim(by, c, 1, keepdims=False) + swap_f(
         lax.dynamic_index_in_dim(by, 1 - c, 1, keepdims=False), 1
     )

time: 135 us -> 132 us (0.978)
  waiting for transfers between devices: 89 us -> 77.2 us
  starting transfers between devices: 20.2 us -> 23.3 us
  other arithmetic: 4.36 us -> 6.49 us
  local copies, waits for them, and re-layouts: 5.01 us -> 7.1 us
  Pallas kernels: 15.1 us -> 16.9 us
    ppermute x15 -> x16, waiting for transfers between devices: 80.4 us -> 67.5 us  [swap_dp(): return lax.ppermute(a, 'dp', [(d, d ^ bits) for d in range(dp)])]
    ppermute x15 -> x16, starting transfers between devices: 18.7 us -> 21.7 us  [swap_dp(): return lax.ppermute(a, 'dp', [(d, d ^ bits) for d in range(dp)])]
    unnamed x17 -> x27, local copies, waits for them, and re-layouts: 3.03 us -> 5.9 us
    pallas_call x2 -> x3, Pallas kernels: 5.76 us -> 7.59 us  [weight_grad_part(): pl.pallas_call(kernel, grid=(chunks,), out_shape=(jax.ShapeDtypeStruct((r...]
  transfers between devices with their start and end apart: 17 -> 18, of which waited for: 13 -> 10; matrix products, arithmetic and copies ran while one was open for 4% -> 5% of each run, Pallas kernels for 11% -> 13%
where the time goes in v13:
time: 132 us
  waiting for transfers between devices  77.2 us (58%)
  starting transfers between devices  23.3 us (18%)
  Pallas kernels  16.9 us (13%)
  local copies, waits for them, and re-layouts  7.1 us (5%)
  other arithmetic  6.49 us (5%)
    ppermute x16, waiting for transfers between devices, swap_dp(): return lax.ppermute(a, 'dp', [(d, d ^ bits) for d in range(dp)])  67.5 us
    ppermute x16, starting transfers between devices, swap_dp(): return lax.ppermute(a, 'dp', [(d, d ^ bits) for d in range(dp)])  21.7 us
    ppermute x2, waiting for transfers between devices, swap_f(): return lax.ppermute(a, 'fsdp', [(d, d ^ bit) for d in range(fsdp)])  9.64 us
    pallas_call x2, Pallas kernels, forward_and_input(): pl.pallas_call(kernel, grid=(width // BS,), out_shape=(jax.ShapeDtypeStru...  9.29 us
    pallas_call x3, Pallas kernels, weight_grad_part(): pl.pallas_call(kernel, grid=(chunks,), out_shape=(jax.ShapeDtypeStruct((r...  7.59 us
    unnamed x27, local copies, waits for them, and re-layouts  5.9 us
  transfers between devices with their start and end apart: 18, of which 10 were waited for; matrix products, arithmetic and copies ran while one was open for 5% of the time, Pallas kernels for 13%

profile of v13, /device:TPU:0, one launch (start us, length us, event | category | flops | bytes accessed | tf_op | source)
XLA Modules:
  0.0 131.8 jit_solution(9853133622832971592)
XLA Ops:
  0.6 3.0 %collective-permute-start.5 = (bf16[4,128,768]{2,1,0:T(8,128)(2,1)}, bf16[4,128,768]{2,1,0:T(8,128)(2,1)S(1)}, u32[]{:S(2)}, u32[]{:S(2)}) collective-permute-start(bf16[4,128,768]{2,1,0:T(8,128)(2,1)} %og_ref.2), channel_id=1, source_target_pairs={{0,4},{4,0},{8,12},{12,8},{16,20},{20,16},{24,28},{28,24},{1,5},{5... | collective-permute-start | bytes 2359304 | tf_op jit(solution)/shard_map/ppermute | solution.py:193
  3.6 1.6 %collective-permute-start.4 = (bf16[4,128,768]{2,1,0:T(8,128)(2,1)}, bf16[4,128,768]{2,1,0:T(8,128)(2,1)S(1)}, u32[]{:S(2)}, u32[]{:S(2)}) collective-permute-start(bf16[4,128,768]{2,1,0:T(8,128)(2,1)} %og_ref.2), channel_id=1, source_target_pairs={{0,8},{4,12},{8,0},{12,4},{16,24},{20,28},{24,16},{28,20},{1,9},{5... | collective-permute-start | bytes 2359304 | tf_op jit(solution)/shard_map/ppermute | solution.py:193
  5.2 1.0 dynamic-slice_bitcast_fusion.3
  6.3 0.8 pad_maximum_fusion.1
  7.1 0.4 collective-permute-start.1
  7.5 0.7 pad_maximum_fusion.2
  8.2 0.1 collective-permute-start.2
  8.3 13.9 %collective-permute-done.5.refs_6_ = bf16[4,128,768]{2,1,0:T(8,128)(2,1)S(1)} collective-permute-done((bf16[4,128,768]{2,1,0:T(8,128)(2,1)}, bf16[4,128,768]{2,1,0:T(8,128)(2,1)S(1)}, u32[]{:S(2)}, u32[]{:S(2)}) %collective-permute-start.5) | collective-permute-done | bytes 786464 | tf_op jit(solution)/shard_map/ppermute | solution.py:193
  22.2 2.1 %collective-permute-done.4.refs_5_ = bf16[4,128,768]{2,1,0:T(8,128)(2,1)S(1)} collective-permute-done((bf16[4,128,768]{2,1,0:T(8,128)(2,1)}, bf16[4,128,768]{2,1,0:T(8,128)(2,1)S(1)}, u32[]{:S(2)}, u32[]{:S(2)}) %collective-permute-start.4) | collective-permute-done | bytes 786464 | tf_op jit(solution)/shard_map/ppermute | solution.py:193
  24.3 0.1 collective-permute-start.6
  24.4 3.0 %collective-permute-start = (bf16[384,768]{1,0:T(8,128)(2,1)}, bf16[384,768]{1,0:T(8,128)(2,1)}, u32[]{:S(2)}, u32[]{:S(2)}) collective-permute-start(bf16[384,768]{1,0:T(8,128)(2,1)} %rest_0_.1), channel_id=1, source_target_pairs={{0,16},{4,20},{8,24},{12,28},{16,0},{20,4},{24,8},{28,12},{1,17},{... | collective-permute-start | bytes 1769480 | tf_op jit(solution)/shard_map/ppermute | solution.py:193
  27.4 0.0 collective-permute-done.2.refs_2_
  27.4 11.6 %collective-permute-done.1.refs_1_ = bf16[2,128,768]{2,1,0:T(8,128)(2,1)S(1)} collective-permute-done((bf16[2,128,768]{2,1,0:T(8,128)(2,1)}, bf16[2,128,768]{2,1,0:T(8,128)(2,1)S(1)}, u32[]{:S(2)}, u32[]{:S(2)}) %collective-permute-start.1) | collective-permute-done | bytes 393248 | tf_op jit(solution)/shard_map/ppermute | solution.py:193
  39.1 0.7 pad_maximum_fusion.3
  39.8 0.0 collective-permute-start.3
  39.8 0.0 collective-permute-start.11
  39.8 2.0 %collective-permute-start.12 = (bf16[384,768]{1,0:T(8,128)(2,1)}, bf16[384,768]{1,0:T(8,128)(2,1)}, u32[]{:S(2)}, u32[]{:S(2)}) collective-permute-start(bf16[384,768]{1,0:T(8,128)(2,1)} %rest_0_.1), channel_id=1, source_target_pairs={{0,4},{4,0},{8,12},{12,8},{16,20},{20,16},{24,28},{28,24},{1,5},{5... | collective-permute-start | bytes 1769480 | tf_op jit(solution)/shard_map/ppermute | solution.py:193
  41.8 1.3 %copy.11.mask_ref = s32[4,12,12]{2,1,0:T(8,128)} copy(s32[4,12,12]{2,0,1:T(4,128)} %param.6) | data formatting | bytes 4608 | tf_op args[2]
  43.1 0.1 pad_add_fusion.where_ref
  43.2 4.7 %collective-permute-done.3.refs_3_ = bf16[128,768]{1,0:T(8,128)(2,1)} collective-permute-done((bf16[128,768]{1,0:T(8,128)(2,1)}, bf16[128,768]{1,0:T(8,128)(2,1)}, u32[]{:S(2)}, u32[]{:S(2)}) %collective-permute-start.3) | collective-permute-done | bytes 196640 | tf_op jit(solution)/shard_map/ppermute | solution.py:193
  47.9 0.0 collective-permute-done.6.refs_7_
  47.9 0.0 copy-done.1
  47.9 0.8 copy-done.2
  48.7 2.3 %weight_grad_part.3 = (f32[384,256]{1,0:T(8,128)S(1)}, f32[384,256]{1,0:T(8,128)S(1)}) custom-call(s32[4]{0:T(128)S(1)} %pad_add_fusion.where_ref, s32[4,12,12]{2,1,0:T(8,128)S(1)} %copy-done.2, bf16[128,3072]{1,0:T(8,128)(2,1)S(1)} %copy-done, bf16[2,128,768]{2,1,0:T(8,128)(2,1)S(1)} %collective-permute-done.1.refs_1_, ...), custom_call_target="tpu_custom_call" | custom-call | flops 805306368 | bytes 786432 | tf_op jit(solution)/shard_map/weight_grad_part/pallas_call | solution.py:84
  51.0 0.7 copy-done.5
  51.7 3.8 %collective-permute-start.13 = (f32[384,256]{1,0:T(8,128)S(1)}, f32[384,256]{1,0:T(8,128)S(1)}, u32[]{:S(2)}, u32[]{:S(2)}) collective-permute-start(f32[384,256]{1,0:T(8,128)S(1)} %get-tuple-element.30), channel_id=1, source_target_pairs={{0,16},{4,20},{8,24},{12,28},{16,0},{20,4},{24,8},{28,12},{1,17},{... | collective-permute-start | bytes 1179656 | tf_op jit(solution)/shard_map/ppermute | solution.py:193
  55.5 0.0 collective-permute-done.rest_2_
  55.5 0.6 collective-permute-start.8
  56.1 1.6 %collective-permute-start.7 = (bf16[384,768]{1,0:T(8,128)(2,1)}, bf16[384,768]{1,0:T(8,128)(2,1)}, u32[]{:S(2)}, u32[]{:S(2)}) collective-permute-start(bf16[384,768]{1,0:T(8,128)(2,1)} %collective-permute-done.rest_2_), channel_id=1, source_target_pairs={{0,8},{4,12},{8,0},{12,4},{16,24},{20,28},{24,16},{28,20},{1,9},{5... | collective-permute-start | bytes 1769480 | tf_op jit(solution)/shard_map/ppermute | solution.py:193
  57.6 3.0 %weight_grad_part.5 = (f32[384,256]{1,0:T(8,128)S(1)}, f32[384,256]{1,0:T(8,128)}) custom-call(s32[4]{0:T(128)S(1)} %pad_add_fusion.where_ref, s32[4,12,12]{2,1,0:T(8,128)S(1)} %copy-done.2, bf16[128,3072]{1,0:T(8,128)(2,1)S(1)} %copy-done, bf16[2,128,768]{2,1,0:T(8,128)(2,1)S(1)} %collective-permute-done.1.refs_1_, ...), custom_call_target="tpu_custom_call" | custom-call | flops 805306368 | bytes 786432 | tf_op jit(solution)/shard_map/weight_grad_part/pallas_call | solution.py:84
  60.7 0.7 copy-done.7
  61.4 6.6 %collective-permute-done.11.rest_1_ = bf16[384,768]{1,0:T(8,128)(2,1)} collective-permute-done((bf16[384,768]{1,0:T(8,128)(2,1)}, bf16[384,768]{1,0:T(8,128)(2,1)}, u32[]{:S(2)}, u32[]{:S(2)}) %collective-permute-start.11) | collective-permute-done | bytes 589856 | tf_op jit(solution)/shard_map/ppermute | solution.py:193
  68.0 0.0 collective-permute-done.12.rest_3_
  68.0 2.1 %collective-permute-done.13 = f32[384,256]{1,0:T(8,128)S(1)} collective-permute-done((f32[384,256]{1,0:T(8,128)S(1)}, f32[384,256]{1,0:T(8,128)S(1)}, u32[]{:S(2)}, u32[]{:S(2)}) %collective-permute-start.13) | collective-permute-done | bytes 393248 | tf_op jit(solution)/shard_map/ppermute | solution.py:193
  70.0 0.8 copy-done.11
  70.8 2.3 %collective-permute-start.14 = (bf16[384,768]{1,0:T(8,128)(2,1)}, bf16[384,768]{1,0:T(8,128)(2,1)}, u32[]{:S(2)}, u32[]{:S(2)}) collective-permute-start(bf16[384,768]{1,0:T(8,128)(2,1)} %collective-permute-done.11.rest_1_), channel_id=1, source_target_pairs={{0,4},{4,0},{8,12},{12,8},{16,20},{20,16},{24,28},{28,24},{1,5},{5... | collective-permute-start | bytes 1769480 | tf_op jit(solution)/shard_map/ppermute | solution.py:193
  73.1 1.6 %collective-permute-start.10 = (f32[384,256]{1,0:T(8,128)}, f32[384,256]{1,0:T(8,128)}, u32[]{:S(2)}, u32[]{:S(2)}) collective-permute-start(f32[384,256]{1,0:T(8,128)} %get-tuple-element.27), channel_id=1, source_target_pairs={{0,16},{4,20},{8,24},{12,28},{16,0},{20,4},{24,8},{28,12},{1,17},{... | collective-permute-start | bytes 1179656 | tf_op jit(solution)/shard_map/ppermute | solution.py:193
  74.7 0.8 copy-done.3
  75.4 2.3 %weight_grad_part.4 = (f32[384,256]{1,0:T(8,128)S(1)}, f32[384,256]{1,0:T(8,128)S(1)}) custom-call(s32[4]{0:T(128)S(1)} %pad_add_fusion.where_ref, s32[4,12,12]{2,1,0:T(8,128)S(1)} %copy-done.3, bf16[128,3072]{1,0:T(8,128)(2,1)S(1)} %copy-done, bf16[2,128,768]{2,1,0:T(8,128)(2,1)S(1)} %collective-permute-done.1.refs_1_, ...), custom_call_target="tpu_custom_call" | custom-call | flops 805306368 | bytes 786432 | tf_op jit(solution)/shard_map/weight_grad_part/pallas_call | solution.py:84
  77.7 0.0 copy-start.9
  77.7 0.7 copy-done.9
  78.5 1.3 %collective-permute-start.15 = (f32[384,256]{1,0:T(8,128)S(1)}, f32[384,256]{1,0:T(8,128)S(1)}, u32[]{:S(2)}, u32[]{:S(2)}) collective-permute-start(f32[384,256]{1,0:T(8,128)S(1)} %get-tuple-element.36), channel_id=1, source_target_pairs={{0,16},{4,20},{8,24},{12,28},{16,0},{20,4},{24,8},{28,12},{1,17},{... | collective-permute-start | bytes 1179656 | tf_op jit(solution)/shard_map/ppermute | solution.py:193
  79.8 22.3 %collective-permute-done.10 = f32[384,256]{1,0:T(8,128)} collective-permute-done((f32[384,256]{1,0:T(8,128)}, f32[384,256]{1,0:T(8,128)}, u32[]{:S(2)}, u32[]{:S(2)}) %collective-permute-start.10) | collective-permute-done | bytes 393248 | tf_op jit(solution)/shard_map/ppermute | solution.py:193
  102.1 0.0 collective-permute-done.8.rest_5_
  102.1 0.0 collective-permute-done.7.rest_0_
  102.1 0.3 collective-permute-start.9
  102.3 0.0 collective-permute-done.14.rest_4_
  102.4 5.4 %forward_and_input.2 = (f32[4,128,768]{2,1,0:T(8,128)S(1)}, f32[4,128,768]{2,1,0:T(8,128)S(1)}) custom-call(s32[4]{0:T(128)S(1)} %pad_add_fusion.where_ref, s32[4,12,12]{2,1,0:T(8,128)S(1)} %copy-done.4, bf16[128,3072]{1,0:T(8,128)(2,1)S(1)} %copy-done, bf16[4,128,768]{2,1,0:T(8,128)(2,1)S(1)} %copy-done.1, bf16[384,768]{1,0:T(8,128)(2,1)} %rest_0_.1, ...), custom_call_target="tpu_custom_call" | custom-call | flops 8153726976 | bytes 7077888 | tf_op jit(solution)/shard_map/forward_and_input/pallas_call | solution.py:153
  107.8 4.4 %collective-permute-done.9.rest_1_ = bf16[384,768]{1,0:T(8,128)(2,1)S(1)} collective-permute-done((bf16[384,768]{1,0:T(8,128)(2,1)}, bf16[384,768]{1,0:T(8,128)(2,1)S(1)}, u32[]{:S(2)}, u32[]{:S(2)}) %collective-permute-start.9) | collective-permute-done | bytes 589856 | tf_op jit(solution)/shard_map/ppermute | solution.py:193
  112.2 3.9 %forward_and_input.3 = (bf16[4,128,768]{2,1,0:T(8,128)(2,1)}, f32[4,128,768]{2,1,0:T(8,128)S(1)}) custom-call(s32[4]{0:T(128)S(1)} %pad_add_fusion.where_ref, s32[4,12,12]{2,1,0:T(8,128)S(1)} %copy-done.4, bf16[128,3072]{1,0:T(8,128)(2,1)S(1)} %copy-done, bf16[4,128,768]{2,1,0:T(8,128)(2,1)S(1)} %copy-done.1, ...), custom_call_target="tpu_custom_call" | custom-call | flops 2717908992 | bytes 2359296 | tf_op jit(solution)/shard_map/forward_and_input/pallas_call | solution.py:153
  116.0 0.0 collective-permute-done.15
  116.0 0.1 dynamic-slice_bitcast_fusion
  116.1 0.1 collective-permute-start.16
  116.2 2.4 %collective-permute-done.16 = f32[2,128,768]{2,1,0:T(8,128)} collective-permute-done((f32[2,128,768]{2,1,0:T(8,128)S(1)}, f32[2,128,768]{2,1,0:T(8,128)}, u32[]{:S(2)}, u32[]{:S(2)}) %collective-permute-start.16) | collective-permute-done | bytes 786464 | tf_op jit(solution)/shard_map/ppermute | solution.py:202
  118.6 1.2 bitcast_add_fusion
  119.8 0.0 copy-start.10
  119.8 1.6 %collective-permute-start.17 = (f32[128,768]{1,0:T(8,128)S(1)}, f32[128,768]{1,0:T(8,128)S(1)}, u32[]{:S(2)}, u32[]{:S(2)}) collective-permute-start(f32[128,768]{1,0:T(8,128)S(1)} %dynamic-slice_bitcast_fusion.1), channel_id=1, source_target_pairs={{0,2},{1,3},{2,0},{3,1},{4,6},{5,7},{6,4},{7,5},{8,10},{9,11},{10,... | collective-permute-start | bytes 1179656 | tf_op jit(solution)/shard_map/ppermute | solution.py:202
  121.4 1.1 add.72
  122.6 0.1 add.73
  122.6 0.0 copy-done.12
  122.7 0.1 add.71
  122.7 1.1 pad_maximum_fusion
  123.8 7.3 %collective-permute-done.17 = f32[128,768]{1,0:T(8,128)S(1)} collective-permute-done((f32[128,768]{1,0:T(8,128)S(1)}, f32[128,768]{1,0:T(8,128)S(1)}, u32[]{:S(2)}, u32[]{:S(2)}) %collective-permute-start.17) | collective-permute-done | bytes 393248 | tf_op jit(solution)/shard_map/ppermute | solution.py:202
  131.1 0.7 fusion
  (20 shorter events, 0.1 us)
Async XLA Ops:
  0.6 6.9 %copy-start = (bf16[128,3072]{1,0:T(8,128)(2,1)S(1)}, bf16[128,3072]{1,0:T(8,128)(2,1)}, u32[]{:S(2)}) copy-start(bf16[128,3072]{1,0:T(8,128)(2,1)} %acts_ref.3) | copy-start | bytes 2359300
  0.6 21.6 %collective-permute-start.5 = (bf16[4,128,768]{2,1,0:T(8,128)(2,1)}, bf16[4,128,768]{2,1,0:T(8,128)(2,1)S(1)}, u32[]{:S(2)}, u32[]{:S(2)}) collective-permute-start(bf16[4,128,768]{2,1,0:T(8,128)(2,1)} %og_ref.2), channel_id=1, source_target_pairs={{0,4},{4,0},{8,12},{12,8},{16,20},{20,16},{24,28},{28,24},{1,5},{5... | collective-permute-start | bytes 2359304 | tf_op jit(solution)/shard_map/ppermute | solution.py:193
  3.6 20.7 %collective-permute-start.4 = (bf16[4,128,768]{2,1,0:T(8,128)(2,1)}, bf16[4,128,768]{2,1,0:T(8,128)(2,1)S(1)}, u32[]{:S(2)}, u32[]{:S(2)}) collective-permute-start(bf16[4,128,768]{2,1,0:T(8,128)(2,1)} %og_ref.2), channel_id=1, source_target_pairs={{0,8},{4,12},{8,0},{12,4},{16,24},{20,28},{24,16},{28,20},{1,9},{5... | collective-permute-start | bytes 2359304 | tf_op jit(solution)/shard_map/ppermute | solution.py:193
  7.1 31.9 %collective-permute-start.1 = (bf16[2,128,768]{2,1,0:T(8,128)(2,1)}, bf16[2,128,768]{2,1,0:T(8,128)(2,1)S(1)}, u32[]{:S(2)}, u32[]{:S(2)}) collective-permute-start(bf16[2,128,768]{2,1,0:T(8,128)(2,1)} %pad_maximum_fusion.1), channel_id=1, source_target_pairs={{0,8},{4,12},{8,0},{12,4},{16,24},{20,28},{24,16},{28,20},{1,9},{5... | collective-permute-start | bytes 1179656 | tf_op jit(solution)/shard_map/ppermute | solution.py:193
  7.5 40.4 %copy-start.1 = (bf16[4,128,768]{2,1,0:T(8,128)(2,1)S(1)}, bf16[4,128,768]{2,1,0:T(8,128)(2,1)}, u32[]{:S(2)}) copy-start(bf16[4,128,768]{2,1,0:T(8,128)(2,1)} %og_ref.2) | copy-start | bytes 2359300
  8.2 19.2 %collective-permute-start.2 = (bf16[128,768]{1,0:T(8,128)(2,1)}, bf16[128,768]{1,0:T(8,128)(2,1)}, u32[]{:S(2)}, u32[]{:S(2)}) collective-permute-start(bf16[128,768]{1,0:T(8,128)(2,1)} %pad_maximum_fusion.2), channel_id=1, source_target_pairs={{0,4},{4,0},{8,12},{12,8},{16,20},{20,16},{24,28},{28,24},{1,5},{5... | collective-permute-start | bytes 589832 | tf_op jit(solution)/shard_map/ppermute | solution.py:193
  24.3 23.6 %collective-permute-start.6 = (bf16[4,128,768]{2,1,0:T(8,128)(2,1)S(1)}, bf16[4,128,768]{2,1,0:T(8,128)(2,1)}, u32[]{:S(2)}, u32[]{:S(2)}) collective-permute-start(bf16[4,128,768]{2,1,0:T(8,128)(2,1)S(1)} %collective-permute-done.4.refs_5_), channel_id=1, source_target_pairs={{0,4},{4,0},{8,12},{12,8},{16,20},{20,16},{24,28},{28,24},{1,5},{5... | collective-permute-start | bytes 2359304 | tf_op jit(solution)/shard_map/ppermute | solution.py:193
  24.4 31.1 %collective-permute-start = (bf16[384,768]{1,0:T(8,128)(2,1)}, bf16[384,768]{1,0:T(8,128)(2,1)}, u32[]{:S(2)}, u32[]{:S(2)}) collective-permute-start(bf16[384,768]{1,0:T(8,128)(2,1)} %rest_0_.1), channel_id=1, source_target_pairs={{0,16},{4,20},{8,24},{12,28},{16,0},{20,4},{24,8},{28,12},{1,17},{... | collective-permute-start | bytes 1769480 | tf_op jit(solution)/shard_map/ppermute | solution.py:193
  39.8 8.2 %collective-permute-start.3 = (bf16[128,768]{1,0:T(8,128)(2,1)}, bf16[128,768]{1,0:T(8,128)(2,1)}, u32[]{:S(2)}, u32[]{:S(2)}) collective-permute-start(bf16[128,768]{1,0:T(8,128)(2,1)} %pad_maximum_fusion.3), channel_id=1, source_target_pairs={{0,4},{4,0},{8,12},{12,8},{16,20},{20,16},{24,28},{28,24},{1,5},{5... | collective-permute-start | bytes 589832 | tf_op jit(solution)/shard_map/ppermute | solution.py:193
  39.8 28.2 %collective-permute-start.11 = (bf16[384,768]{1,0:T(8,128)(2,1)}, bf16[384,768]{1,0:T(8,128)(2,1)}, u32[]{:S(2)}, u32[]{:S(2)}) collective-permute-start(bf16[384,768]{1,0:T(8,128)(2,1)} %rest_0_.1), channel_id=1, source_target_pairs={{0,8},{4,12},{8,0},{12,4},{16,24},{20,28},{24,16},{28,20},{1,9},{5... | collective-permute-start | bytes 1769480 | tf_op jit(solution)/shard_map/ppermute | solution.py:193
  39.8 28.2 %collective-permute-start.12 = (bf16[384,768]{1,0:T(8,128)(2,1)}, bf16[384,768]{1,0:T(8,128)(2,1)}, u32[]{:S(2)}, u32[]{:S(2)}) collective-permute-start(bf16[384,768]{1,0:T(8,128)(2,1)} %rest_0_.1), channel_id=1, source_target_pairs={{0,4},{4,0},{8,12},{12,8},{16,20},{20,16},{24,28},{28,24},{1,5},{5... | collective-permute-start | bytes 1769480 | tf_op jit(solution)/shard_map/ppermute | solution.py:193
  47.9 0.8 copy-start.2
  51.0 0.7 copy-start.5
  51.7 18.3 %collective-permute-start.13 = (f32[384,256]{1,0:T(8,128)S(1)}, f32[384,256]{1,0:T(8,128)S(1)}, u32[]{:S(2)}, u32[]{:S(2)}) collective-permute-start(f32[384,256]{1,0:T(8,128)S(1)} %get-tuple-element.30), channel_id=1, source_target_pairs={{0,16},{4,20},{8,24},{12,28},{16,0},{20,4},{24,8},{28,12},{1,17},{... | collective-permute-start | bytes 1179656 | tf_op jit(solution)/shard_map/ppermute | solution.py:193
  55.5 46.6 %collective-permute-start.8 = (bf16[384,768]{1,0:T(8,128)(2,1)}, bf16[384,768]{1,0:T(8,128)(2,1)}, u32[]{:S(2)}, u32[]{:S(2)}) collective-permute-start(bf16[384,768]{1,0:T(8,128)(2,1)} %collective-permute-done.rest_2_), channel_id=1, source_target_pairs={{0,4},{4,0},{8,12},{12,8},{16,20},{20,16},{24,28},{28,24},{1,5},{5... | collective-permute-start | bytes 1769480 | tf_op jit(solution)/shard_map/ppermute | solution.py:193
  56.1 46.0 %collective-permute-start.7 = (bf16[384,768]{1,0:T(8,128)(2,1)}, bf16[384,768]{1,0:T(8,128)(2,1)}, u32[]{:S(2)}, u32[]{:S(2)}) collective-permute-start(bf16[384,768]{1,0:T(8,128)(2,1)} %collective-permute-done.rest_2_), channel_id=1, source_target_pairs={{0,8},{4,12},{8,0},{12,4},{16,24},{20,28},{24,16},{28,20},{1,9},{5... | collective-permute-start | bytes 1769480 | tf_op jit(solution)/shard_map/ppermute | solution.py:193
  60.7 0.7 copy-start.7
  70.0 0.8 copy-start.11
  70.8 31.5 %collective-permute-start.14 = (bf16[384,768]{1,0:T(8,128)(2,1)}, bf16[384,768]{1,0:T(8,128)(2,1)}, u32[]{:S(2)}, u32[]{:S(2)}) collective-permute-start(bf16[384,768]{1,0:T(8,128)(2,1)} %collective-permute-done.11.rest_1_), channel_id=1, source_target_pairs={{0,4},{4,0},{8,12},{12,8},{16,20},{20,16},{24,28},{28,24},{1,5},{5... | collective-permute-start | bytes 1769480 | tf_op jit(solution)/shard_map/ppermute | solution.py:193
  73.1 29.0 %collective-permute-start.10 = (f32[384,256]{1,0:T(8,128)}, f32[384,256]{1,0:T(8,128)}, u32[]{:S(2)}, u32[]{:S(2)}) collective-permute-start(f32[384,256]{1,0:T(8,128)} %get-tuple-element.27), channel_id=1, source_target_pairs={{0,16},{4,20},{8,24},{12,28},{16,0},{20,4},{24,8},{28,12},{1,17},{... | collective-permute-start | bytes 1179656 | tf_op jit(solution)/shard_map/ppermute | solution.py:193
  74.7 0.8 copy-start.3
  75.4 26.9 %copy-start.4 = (s32[4,12,12]{2,1,0:T(8,128)S(1)}, s32[4,12,12]{2,1,0:T(8,128)}, u32[]{:S(2)}) copy-start(s32[4,12,12]{2,1,0:T(8,128)} %copy.11.mask_ref) | copy-start | bytes 6916
  77.7 0.7 copy-start.9
  78.5 37.6 %collective-permute-start.15 = (f32[384,256]{1,0:T(8,128)S(1)}, f32[384,256]{1,0:T(8,128)S(1)}, u32[]{:S(2)}, u32[]{:S(2)}) collective-permute-start(f32[384,256]{1,0:T(8,128)S(1)} %get-tuple-element.36), channel_id=1, source_target_pairs={{0,16},{4,20},{8,24},{12,28},{16,0},{20,4},{24,8},{28,12},{1,17},{... | collective-permute-start | bytes 1179656 | tf_op jit(solution)/shard_map/ppermute | solution.py:193
  102.1 10.1 %collective-permute-start.9 = (bf16[384,768]{1,0:T(8,128)(2,1)}, bf16[384,768]{1,0:T(8,128)(2,1)S(1)}, u32[]{:S(2)}, u32[]{:S(2)}) collective-permute-start(bf16[384,768]{1,0:T(8,128)(2,1)} %collective-permute-done.7.rest_0_), channel_id=1, source_target_pairs={{0,4},{4,0},{8,12},{12,8},{16,20},{20,16},{24,28},{28,24},{1,5},{5... | collective-permute-start | bytes 1769480 | tf_op jit(solution)/shard_map/ppermute | solution.py:193
  116.1 2.5 %collective-permute-start.16 = (f32[2,128,768]{2,1,0:T(8,128)S(1)}, f32[2,128,768]{2,1,0:T(8,128)}, u32[]{:S(2)}, u32[]{:S(2)}) collective-permute-start(f32[2,128,768]{2,1,0:T(8,128)S(1)} %dynamic-slice_bitcast_fusion), channel_id=1, source_target_pairs={{0,1},{1,0},{2,3},{3,2},{4,5},{5,4},{6,7},{7,6},{8,9},{9,8},{10,11... | collective-permute-start | bytes 2359304 | tf_op jit(solution)/shard_map/ppermute | solution.py:202
  116.2 5.2 %copy-start.8 = (f32[384,256]{1,0:T(8,128)S(1)}, f32[384,256]{1,0:T(8,128)}, u32[]{:S(2)}) copy-start(f32[384,256]{1,0:T(8,128)} %copy-done.7) | copy-start | bytes 1179652
  119.8 2.8 %copy-start.10 = (f32[384,256]{1,0:T(8,128)S(1)}, f32[384,256]{1,0:T(8,128)}, u32[]{:S(2)}) copy-start(f32[384,256]{1,0:T(8,128)} %copy-done.9) | copy-start | bytes 1179652
  119.8 11.2 %collective-permute-start.17 = (f32[128,768]{1,0:T(8,128)S(1)}, f32[128,768]{1,0:T(8,128)S(1)}, u32[]{:S(2)}, u32[]{:S(2)}) collective-permute-start(f32[128,768]{1,0:T(8,128)S(1)} %dynamic-slice_bitcast_fusion.1), channel_id=1, source_target_pairs={{0,2},{1,3},{2,0},{3,1},{4,6},{5,7},{6,4},{7,5},{8,10},{9,11},{10,... | collective-permute-start | bytes 1179656 | tf_op jit(solution)/shard_map/ppermute | solution.py:202
  121.4 1.2 copy-start.6
  121.4 1.2 copy-start.12

commit v14 on v13

--- a/solution.py
+++ b/solution.py
@@ -237,13 +237,13 @@
     w_peer = [x_own, x_one, x_two, x_three]
 
     sums = forward_and_input(
-        acts, w_mine[:3], w_peer[:3], after(out_grad, gots[1]), block_mask, where, 0, None
+        acts, w_mine[:3], w_peer[:3], out_grad, block_mask, where, 0, None
     )
     outputs, gx = forward_and_input(
         acts, w_mine[3:], w_peer[3:], out_grad, block_mask, where, 3, sums
     )
 
-    by = after(gx, gots[2]).reshape(2, 2, tokens, depth // 4)
+    by = after(gx, gots[1], gots[2]).reshape(2, 2, tokens, depth // 4)
     pair = lax.dynamic_index_in_dim(by, c, 1, keepdims=False) + swap_f(
         lax.dynamic_index_in_dim(by, 1 - c, 1, keepdims=False), 1
     )

time: 132 us -> 124 us (0.939)
  waiting for transfers between devices: 77.2 us -> 65.1 us
  local copies, waits for them, and re-layouts: 7.1 us -> 10.3 us
  starting transfers between devices: 23.3 us -> 25.7 us
    ppermute x16, waiting for transfers between devices: 67.5 us -> 55.1 us  [swap_dp(): return lax.ppermute(a, 'dp', [(d, d ^ bits) for d in range(dp)])]
    ppermute x16, starting transfers between devices: 21.7 us -> 24.1 us  [swap_dp(): return lax.ppermute(a, 'dp', [(d, d ^ bits) for d in range(dp)])]
    unnamed x27 -> x37, local copies, waits for them, and re-layouts: 5.9 us -> 8.32 us
  transfers between devices with their start and end apart: 18 -> 18, of which waited for: 10 -> 11; matrix products, arithmetic and copies ran while one was open for 5% -> 5% of each run, Pallas kernels for 13% -> 13%
where the time goes in v14:
time: 124 us; the launch traced here: 123 us
  waiting for transfers between devices  65.1 us (52%)
  starting transfers between devices  25.7 us (21%)
  Pallas kernels  16.1 us (13%)
  local copies, waits for them, and re-layouts  10.3 us (8%)
  other arithmetic  5.43 us (4%)
    ppermute x16, waiting for transfers between devices, swap_dp(): return lax.ppermute(a, 'dp', [(d, d ^ bits) for d in range(dp)])  55.1 us
    ppermute x16, starting transfers between devices, swap_dp(): return lax.ppermute(a, 'dp', [(d, d ^ bits) for d in range(dp)])  24.1 us
    ppermute x2, waiting for transfers between devices, swap_f(): return lax.ppermute(a, 'fsdp', [(d, d ^ bit) for d in range(fsdp)])  10 us
    pallas_call x2, Pallas kernels, forward_and_input(): pl.pallas_call(kernel, grid=(width // BS,), out_shape=(jax.ShapeDtypeStru...  9.28 us
    unnamed x37, local copies, waits for them, and re-layouts  8.32 us
    pallas_call x3, Pallas kernels, weight_grad_part(): pl.pallas_call(kernel, grid=(chunks,), out_shape=(jax.ShapeDtypeStruct((r...  6.84 us
  transfers between devices with their start and end apart: 18, of which 11 were waited for; matrix products, arithmetic and copies ran while one was open for 5% of the time, Pallas kernels for 13%

profile of v14, /device:TPU:0, one launch (start us, length us, event | category | flops | bytes accessed | tf_op | source)
XLA Modules:
  0.0 123.4 jit_solution(16706772849725483030)
XLA Ops:
  0.6 3.0 %collective-permute-start.5 = (bf16[4,128,768]{2,1,0:T(8,128)(2,1)}, bf16[4,128,768]{2,1,0:T(8,128)(2,1)S(1)}, u32[]{:S(2)}, u32[]{:S(2)}) collective-permute-start(bf16[4,128,768]{2,1,0:T(8,128)(2,1)} %og_ref.3), channel_id=1, source_target_pairs={{0,4},{4,0},{8,12},{12,8},{16,20},{20,16},{24,28},{28,24},{1,5},{5... | collective-permute-start | bytes 2359304 | tf_op jit(solution)/shard_map/ppermute | solution.py:193
  3.6 1.6 %collective-permute-start.4 = (bf16[4,128,768]{2,1,0:T(8,128)(2,1)}, bf16[4,128,768]{2,1,0:T(8,128)(2,1)S(1)}, u32[]{:S(2)}, u32[]{:S(2)}) collective-permute-start(bf16[4,128,768]{2,1,0:T(8,128)(2,1)} %og_ref.3), channel_id=1, source_target_pairs={{0,8},{4,12},{8,0},{12,4},{16,24},{20,28},{24,16},{28,20},{1,9},{5... | collective-permute-start | bytes 2359304 | tf_op jit(solution)/shard_map/ppermute | solution.py:193
  5.2 1.0 dynamic-slice_bitcast_fusion.3
  6.3 0.8 pad_maximum_fusion.1
  7.1 0.4 collective-permute-start.1
  7.5 0.7 pad_maximum_fusion.2
  8.2 0.1 collective-permute-start.2
  8.3 13.9 %collective-permute-done.5.refs_6_ = bf16[4,128,768]{2,1,0:T(8,128)(2,1)S(1)} collective-permute-done((bf16[4,128,768]{2,1,0:T(8,128)(2,1)}, bf16[4,128,768]{2,1,0:T(8,128)(2,1)S(1)}, u32[]{:S(2)}, u32[]{:S(2)}) %collective-permute-start.5) | collective-permute-done | bytes 786464 | tf_op jit(solution)/shard_map/ppermute | solution.py:193
  22.2 2.1 %collective-permute-done.4.refs_5_ = bf16[4,128,768]{2,1,0:T(8,128)(2,1)S(1)} collective-permute-done((bf16[4,128,768]{2,1,0:T(8,128)(2,1)}, bf16[4,128,768]{2,1,0:T(8,128)(2,1)S(1)}, u32[]{:S(2)}, u32[]{:S(2)}) %collective-permute-start.4) | collective-permute-done | bytes 786464 | tf_op jit(solution)/shard_map/ppermute | solution.py:193
  24.3 0.1 collective-permute-start.6
  24.4 3.0 %collective-permute-start = (bf16[384,768]{1,0:T(8,128)(2,1)}, bf16[384,768]{1,0:T(8,128)(2,1)}, u32[]{:S(2)}, u32[]{:S(2)}) collective-permute-start(bf16[384,768]{1,0:T(8,128)(2,1)} %rest_0_.1), channel_id=1, source_target_pairs={{0,16},{4,20},{8,24},{12,28},{16,0},{20,4},{24,8},{28,12},{1,17},{... | collective-permute-start | bytes 1769480 | tf_op jit(solution)/shard_map/ppermute | solution.py:193
  27.4 0.0 collective-permute-done.2.refs_2_
  27.4 11.6 %collective-permute-done.1.refs_1_ = bf16[2,128,768]{2,1,0:T(8,128)(2,1)S(1)} collective-permute-done((bf16[2,128,768]{2,1,0:T(8,128)(2,1)}, bf16[2,128,768]{2,1,0:T(8,128)(2,1)S(1)}, u32[]{:S(2)}, u32[]{:S(2)}) %collective-permute-start.1) | collective-permute-done | bytes 393248 | tf_op jit(solution)/shard_map/ppermute | solution.py:193
  39.1 0.7 pad_maximum_fusion.3
  39.8 0.0 collective-permute-start.3
  39.8 0.0 collective-permute-start.10
  39.8 2.0 %collective-permute-start.11 = (bf16[384,768]{1,0:T(8,128)(2,1)}, bf16[384,768]{1,0:T(8,128)(2,1)}, u32[]{:S(2)}, u32[]{:S(2)}) collective-permute-start(bf16[384,768]{1,0:T(8,128)(2,1)} %rest_0_.1), channel_id=1, source_target_pairs={{0,4},{4,0},{8,12},{12,8},{16,20},{20,16},{24,28},{28,24},{1,5},{5... | collective-permute-start | bytes 1769480 | tf_op jit(solution)/shard_map/ppermute | solution.py:193
  41.8 1.4 %copy.11.mask_ref = s32[4,12,12]{2,1,0:T(8,128)} copy(s32[4,12,12]{2,0,1:T(4,128)} %param.6) | data formatting | bytes 4608 | tf_op args[2]
  43.1 0.1 pad_add_fusion.where_ref
  43.2 4.7 %collective-permute-done.3.refs_3_ = bf16[128,768]{1,0:T(8,128)(2,1)} collective-permute-done((bf16[128,768]{1,0:T(8,128)(2,1)}, bf16[128,768]{1,0:T(8,128)(2,1)}, u32[]{:S(2)}, u32[]{:S(2)}) %collective-permute-start.3) | collective-permute-done | bytes 196640 | tf_op jit(solution)/shard_map/ppermute | solution.py:193
  47.9 0.0 collective-permute-done.6.refs_7_
  47.9 0.8 copy-done.2
  48.7 2.3 %weight_grad_part.3 = (f32[384,256]{1,0:T(8,128)S(1)}, f32[384,256]{1,0:T(8,128)S(1)}) custom-call(s32[4]{0:T(128)S(1)} %pad_add_fusion.where_ref, s32[4,12,12]{2,1,0:T(8,128)S(1)} %copy-done.2, bf16[128,3072]{1,0:T(8,128)(2,1)S(1)} %copy-done, bf16[2,128,768]{2,1,0:T(8,128)(2,1)S(1)} %collective-permute-done.1.refs_1_, ...), custom_call_target="tpu_custom_call" | custom-call | flops 805306368 | bytes 786432 | tf_op jit(solution)/shard_map/weight_grad_part/pallas_call | solution.py:84
  51.0 0.7 copy-done.5
  51.7 3.8 %collective-permute-start.12 = (f32[384,256]{1,0:T(8,128)S(1)}, f32[384,256]{1,0:T(8,128)S(1)}, u32[]{:S(2)}, u32[]{:S(2)}) collective-permute-start(f32[384,256]{1,0:T(8,128)S(1)} %get-tuple-element.27), channel_id=1, source_target_pairs={{0,16},{4,20},{8,24},{12,28},{16,0},{20,4},{24,8},{28,12},{1,17},{... | collective-permute-start | bytes 1179656 | tf_op jit(solution)/shard_map/ppermute | solution.py:193
  55.5 0.6 collective-permute-start.8
  56.1 1.6 %collective-permute-start.7 = (bf16[384,768]{1,0:T(8,128)(2,1)}, bf16[384,768]{1,0:T(8,128)(2,1)}, u32[]{:S(2)}, u32[]{:S(2)}) collective-permute-start(bf16[384,768]{1,0:T(8,128)(2,1)} %collective-permute-done.rest_2_), channel_id=1, source_target_pairs={{0,8},{4,12},{8,0},{12,4},{16,24},{20,28},{24,16},{28,20},{1,9},{5... | collective-permute-start | bytes 1769480 | tf_op jit(solution)/shard_map/ppermute | solution.py:193
  57.6 2.3 %weight_grad_part.5 = (f32[384,256]{1,0:T(8,128)S(1)}, f32[384,256]{1,0:T(8,128)S(1)}) custom-call(s32[4]{0:T(128)S(1)} %pad_add_fusion.where_ref, s32[4,12,12]{2,1,0:T(8,128)S(1)} %copy-done.2, bf16[128,3072]{1,0:T(8,128)(2,1)S(1)} %copy-done, bf16[2,128,768]{2,1,0:T(8,128)(2,1)S(1)} %collective-permute-done.1.refs_1_, ...), custom_call_target="tpu_custom_call" | custom-call | flops 805306368 | bytes 786432 | tf_op jit(solution)/shard_map/weight_grad_part/pallas_call | solution.py:84
  59.9 0.8 copy-done.7
  60.7 0.8 copy-done.11
  61.4 6.5 %collective-permute-done.10.rest_1_ = bf16[384,768]{1,0:T(8,128)(2,1)} collective-permute-done((bf16[384,768]{1,0:T(8,128)(2,1)}, bf16[384,768]{1,0:T(8,128)(2,1)}, u32[]{:S(2)}, u32[]{:S(2)}) %collective-permute-start.10) | collective-permute-done | bytes 589856 | tf_op jit(solution)/shard_map/ppermute | solution.py:193
  68.0 2.1 %collective-permute-done.12 = f32[384,256]{1,0:T(8,128)S(1)} collective-permute-done((f32[384,256]{1,0:T(8,128)S(1)}, f32[384,256]{1,0:T(8,128)S(1)}, u32[]{:S(2)}, u32[]{:S(2)}) %collective-permute-start.12) | collective-permute-done | bytes 393248 | tf_op jit(solution)/shard_map/ppermute | solution.py:193
  70.0 0.8 copy-done.12
  70.8 2.3 %collective-permute-start.13 = (bf16[384,768]{1,0:T(8,128)(2,1)}, bf16[384,768]{1,0:T(8,128)(2,1)}, u32[]{:S(2)}, u32[]{:S(2)}) collective-permute-start(bf16[384,768]{1,0:T(8,128)(2,1)} %collective-permute-done.10.rest_1_), channel_id=1, source_target_pairs={{0,4},{4,0},{8,12},{12,8},{16,20},{20,16},{24,28},{28,24},{1,5},{5... | collective-permute-start | bytes 1769480 | tf_op jit(solution)/shard_map/ppermute | solution.py:193
  73.1 1.6 %collective-permute-start.14 = (f32[384,256]{1,0:T(8,128)}, f32[384,256]{1,0:T(8,128)S(1)}, u32[]{:S(2)}, u32[]{:S(2)}) collective-permute-start(f32[384,256]{1,0:T(8,128)} %copy-done.11), channel_id=1, source_target_pairs={{0,16},{4,20},{8,24},{12,28},{16,0},{20,4},{24,8},{28,12},{1,17},{... | collective-permute-start | bytes 1179656 | tf_op jit(solution)/shard_map/ppermute | solution.py:193
  74.7 0.8 copy-done.3
  75.4 2.3 %weight_grad_part.4 = (f32[384,256]{1,0:T(8,128)S(1)}, f32[384,256]{1,0:T(8,128)S(1)}) custom-call(s32[4]{0:T(128)S(1)} %pad_add_fusion.where_ref, s32[4,12,12]{2,1,0:T(8,128)S(1)} %copy-done.3, bf16[128,3072]{1,0:T(8,128)(2,1)S(1)} %copy-done, bf16[2,128,768]{2,1,0:T(8,128)(2,1)S(1)} %collective-permute-done.1.refs_1_, ...), custom_call_target="tpu_custom_call" | custom-call | flops 805306368 | bytes 786432 | tf_op jit(solution)/shard_map/weight_grad_part/pallas_call | solution.py:84
  77.7 0.0 copy-start.9
  77.7 0.7 copy-done.9
  78.5 1.3 %collective-permute-start.15 = (f32[384,256]{1,0:T(8,128)S(1)}, f32[384,256]{1,0:T(8,128)S(1)}, u32[]{:S(2)}, u32[]{:S(2)}) collective-permute-start(f32[384,256]{1,0:T(8,128)S(1)} %get-tuple-element.34), channel_id=1, source_target_pairs={{0,16},{4,20},{8,24},{12,28},{16,0},{20,4},{24,8},{28,12},{1,17},{... | collective-permute-start | bytes 1179656 | tf_op jit(solution)/shard_map/ppermute | solution.py:193
  79.8 7.6 %collective-permute-done.7.rest_0_ = bf16[384,768]{1,0:T(8,128)(2,1)} collective-permute-done((bf16[384,768]{1,0:T(8,128)(2,1)}, bf16[384,768]{1,0:T(8,128)(2,1)}, u32[]{:S(2)}, u32[]{:S(2)}) %collective-permute-start.7) | collective-permute-done | bytes 589856 | tf_op jit(solution)/shard_map/ppermute | solution.py:193
  87.5 2.8 %collective-permute-start.9 = (bf16[384,768]{1,0:T(8,128)(2,1)}, bf16[384,768]{1,0:T(8,128)(2,1)S(1)}, u32[]{:S(2)}, u32[]{:S(2)}) collective-permute-start(bf16[384,768]{1,0:T(8,128)(2,1)} %collective-permute-done.7.rest_0_), channel_id=1, source_target_pairs={{0,4},{4,0},{8,12},{12,8},{16,20},{20,16},{24,28},{28,24},{1,5},{5... | collective-permute-start | bytes 1769480 | tf_op jit(solution)/shard_map/ppermute | solution.py:193
  90.2 0.0 collective-permute-done.13.rest_4_
  90.2 5.4 %forward_and_input.2 = (f32[4,128,768]{2,1,0:T(8,128)S(1)}, f32[4,128,768]{2,1,0:T(8,128)S(1)}) custom-call(s32[4]{0:T(128)S(1)} %pad_add_fusion.where_ref, s32[4,12,12]{2,1,0:T(8,128)S(1)} %copy-done.4, bf16[128,3072]{1,0:T(8,128)(2,1)S(1)} %copy-done, bf16[4,128,768]{2,1,0:T(8,128)(2,1)S(1)} %copy-done.1, bf16[384,768]{1,0:T(8,128)(2,1)} %rest_0_.1, ...), custom_call_target="tpu_custom_call" | custom-call | flops 8153726976 | bytes 7077888 | tf_op jit(solution)/shard_map/forward_and_input/pallas_call | solution.py:153
  95.7 6.0 %collective-permute-done.9.rest_1_ = bf16[384,768]{1,0:T(8,128)(2,1)S(1)} collective-permute-done((bf16[384,768]{1,0:T(8,128)(2,1)}, bf16[384,768]{1,0:T(8,128)(2,1)S(1)}, u32[]{:S(2)}, u32[]{:S(2)}) %collective-permute-start.9) | collective-permute-done | bytes 589856 | tf_op jit(solution)/shard_map/ppermute | solution.py:193
  101.7 3.9 %forward_and_input.3 = (bf16[4,128,768]{2,1,0:T(8,128)(2,1)}, f32[4,128,768]{2,1,0:T(8,128)S(1)}) custom-call(s32[4]{0:T(128)S(1)} %pad_add_fusion.where_ref, s32[4,12,12]{2,1,0:T(8,128)S(1)} %copy-done.4, bf16[128,3072]{1,0:T(8,128)(2,1)S(1)} %copy-done, bf16[4,128,768]{2,1,0:T(8,128)(2,1)S(1)} %copy-done.1, ...), custom_call_target="tpu_custom_call" | custom-call | flops 2717908992 | bytes 2359296 | tf_op jit(solution)/shard_map/forward_and_input/pallas_call | solution.py:153
  105.6 0.6 collective-permute-done.15
  106.2 0.2 copy-done.14
  106.3 0.1 dynamic-slice_bitcast_fusion
  106.4 0.5 copy-done.16
  106.9 0.0 collective-permute-start.16
  106.9 2.4 %collective-permute-done.16 = f32[2,128,768]{2,1,0:T(8,128)} collective-permute-done((f32[2,128,768]{2,1,0:T(8,128)S(1)}, f32[2,128,768]{2,1,0:T(8,128)}, u32[]{:S(2)}, u32[]{:S(2)}) %collective-permute-start.16) | collective-permute-done | bytes 786464 | tf_op jit(solution)/shard_map/ppermute | solution.py:202
  109.3 1.2 bitcast_add_fusion
  110.5 0.0 copy-start.10
  110.6 0.8 dynamic-slice_bitcast_fusion.1
  111.3 1.5 %collective-permute-start.17 = (f32[128,768]{1,0:T(8,128)}, f32[128,768]{1,0:T(8,128)S(1)}, u32[]{:S(2)}, u32[]{:S(2)}) collective-permute-start(f32[128,768]{1,0:T(8,128)} %dynamic-slice_bitcast_fusion.1), channel_id=1, source_target_pairs={{0,2},{1,3},{2,0},{3,1},{4,6},{5,7},{6,4},{7,5},{8,10},{9,11},{10,... | collective-permute-start | bytes 1179656 | tf_op jit(solution)/shard_map/ppermute | solution.py:202
  112.9 0.1 add.72
  112.9 0.1 add.73
  113.0 0.9 copy-done.6
  113.8 0.1 copy-done.13
  114.0 0.1 add.71
  114.0 1.1 pad_maximum_fusion
  115.1 7.6 %collective-permute-done.17 = f32[128,768]{1,0:T(8,128)S(1)} collective-permute-done((f32[128,768]{1,0:T(8,128)}, f32[128,768]{1,0:T(8,128)S(1)}, u32[]{:S(2)}, u32[]{:S(2)}) %collective-permute-start.17) | collective-permute-done | bytes 393248 | tf_op jit(solution)/shard_map/ppermute | solution.py:202
  122.7 0.7 fusion
  (30 shorter events, 0.1 us)
Async XLA Ops:
  0.6 6.9 %copy-start = (bf16[128,3072]{1,0:T(8,128)(2,1)S(1)}, bf16[128,3072]{1,0:T(8,128)(2,1)}, u32[]{:S(2)}) copy-start(bf16[128,3072]{1,0:T(8,128)(2,1)} %acts_ref.3) | copy-start | bytes 2359300
  0.6 21.6 %collective-permute-start.5 = (bf16[4,128,768]{2,1,0:T(8,128)(2,1)}, bf16[4,128,768]{2,1,0:T(8,128)(2,1)S(1)}, u32[]{:S(2)}, u32[]{:S(2)}) collective-permute-start(bf16[4,128,768]{2,1,0:T(8,128)(2,1)} %og_ref.3), channel_id=1, source_target_pairs={{0,4},{4,0},{8,12},{12,8},{16,20},{20,16},{24,28},{28,24},{1,5},{5... | collective-permute-start | bytes 2359304 | tf_op jit(solution)/shard_map/ppermute | solution.py:193
  3.6 20.7 %collective-permute-start.4 = (bf16[4,128,768]{2,1,0:T(8,128)(2,1)}, bf16[4,128,768]{2,1,0:T(8,128)(2,1)S(1)}, u32[]{:S(2)}, u32[]{:S(2)}) collective-permute-start(bf16[4,128,768]{2,1,0:T(8,128)(2,1)} %og_ref.3), channel_id=1, source_target_pairs={{0,8},{4,12},{8,0},{12,4},{16,24},{20,28},{24,16},{28,20},{1,9},{5... | collective-permute-start | bytes 2359304 | tf_op jit(solution)/shard_map/ppermute | solution.py:193
  7.1 31.9 %collective-permute-start.1 = (bf16[2,128,768]{2,1,0:T(8,128)(2,1)}, bf16[2,128,768]{2,1,0:T(8,128)(2,1)S(1)}, u32[]{:S(2)}, u32[]{:S(2)}) collective-permute-start(bf16[2,128,768]{2,1,0:T(8,128)(2,1)} %pad_maximum_fusion.1), channel_id=1, source_target_pairs={{0,8},{4,12},{8,0},{12,4},{16,24},{20,28},{24,16},{28,20},{1,9},{5... | collective-permute-start | bytes 1179656 | tf_op jit(solution)/shard_map/ppermute | solution.py:193
  7.5 40.4 %copy-start.1 = (bf16[4,128,768]{2,1,0:T(8,128)(2,1)S(1)}, bf16[4,128,768]{2,1,0:T(8,128)(2,1)}, u32[]{:S(2)}) copy-start(bf16[4,128,768]{2,1,0:T(8,128)(2,1)} %og_ref.3) | copy-start | bytes 2359300
  8.2 19.2 %collective-permute-start.2 = (bf16[128,768]{1,0:T(8,128)(2,1)}, bf16[128,768]{1,0:T(8,128)(2,1)}, u32[]{:S(2)}, u32[]{:S(2)}) collective-permute-start(bf16[128,768]{1,0:T(8,128)(2,1)} %pad_maximum_fusion.2), channel_id=1, source_target_pairs={{0,4},{4,0},{8,12},{12,8},{16,20},{20,16},{24,28},{28,24},{1,5},{5... | collective-permute-start | bytes 589832 | tf_op jit(solution)/shard_map/ppermute | solution.py:193
  24.3 23.6 %collective-permute-start.6 = (bf16[4,128,768]{2,1,0:T(8,128)(2,1)S(1)}, bf16[4,128,768]{2,1,0:T(8,128)(2,1)}, u32[]{:S(2)}, u32[]{:S(2)}) collective-permute-start(bf16[4,128,768]{2,1,0:T(8,128)(2,1)S(1)} %collective-permute-done.4.refs_5_), channel_id=1, source_target_pairs={{0,4},{4,0},{8,12},{12,8},{16,20},{20,16},{24,28},{28,24},{1,5},{5... | collective-permute-start | bytes 2359304 | tf_op jit(solution)/shard_map/ppermute | solution.py:193
  24.4 31.1 %collective-permute-start = (bf16[384,768]{1,0:T(8,128)(2,1)}, bf16[384,768]{1,0:T(8,128)(2,1)}, u32[]{:S(2)}, u32[]{:S(2)}) collective-permute-start(bf16[384,768]{1,0:T(8,128)(2,1)} %rest_0_.1), channel_id=1, source_target_pairs={{0,16},{4,20},{8,24},{12,28},{16,0},{20,4},{24,8},{28,12},{1,17},{... | collective-permute-start | bytes 1769480 | tf_op jit(solution)/shard_map/ppermute | solution.py:193
  39.8 8.2 %collective-permute-start.3 = (bf16[128,768]{1,0:T(8,128)(2,1)}, bf16[128,768]{1,0:T(8,128)(2,1)}, u32[]{:S(2)}, u32[]{:S(2)}) collective-permute-start(bf16[128,768]{1,0:T(8,128)(2,1)} %pad_maximum_fusion.3), channel_id=1, source_target_pairs={{0,4},{4,0},{8,12},{12,8},{16,20},{20,16},{24,28},{28,24},{1,5},{5... | collective-permute-start | bytes 589832 | tf_op jit(solution)/shard_map/ppermute | solution.py:193
  39.8 28.2 %collective-permute-start.10 = (bf16[384,768]{1,0:T(8,128)(2,1)}, bf16[384,768]{1,0:T(8,128)(2,1)}, u32[]{:S(2)}, u32[]{:S(2)}) collective-permute-start(bf16[384,768]{1,0:T(8,128)(2,1)} %rest_0_.1), channel_id=1, source_target_pairs={{0,8},{4,12},{8,0},{12,4},{16,24},{20,28},{24,16},{28,20},{1,9},{5... | collective-permute-start | bytes 1769480 | tf_op jit(solution)/shard_map/ppermute | solution.py:193
  39.8 28.2 %collective-permute-start.11 = (bf16[384,768]{1,0:T(8,128)(2,1)}, bf16[384,768]{1,0:T(8,128)(2,1)}, u32[]{:S(2)}, u32[]{:S(2)}) collective-permute-start(bf16[384,768]{1,0:T(8,128)(2,1)} %rest_0_.1), channel_id=1, source_target_pairs={{0,4},{4,0},{8,12},{12,8},{16,20},{20,16},{24,28},{28,24},{1,5},{5... | collective-permute-start | bytes 1769480 | tf_op jit(solution)/shard_map/ppermute | solution.py:193
  47.9 0.8 copy-start.2
  51.0 0.7 copy-start.5
  51.7 18.3 %collective-permute-start.12 = (f32[384,256]{1,0:T(8,128)S(1)}, f32[384,256]{1,0:T(8,128)S(1)}, u32[]{:S(2)}, u32[]{:S(2)}) collective-permute-start(f32[384,256]{1,0:T(8,128)S(1)} %get-tuple-element.27), channel_id=1, source_target_pairs={{0,16},{4,20},{8,24},{12,28},{16,0},{20,4},{24,8},{28,12},{1,17},{... | collective-permute-start | bytes 1179656 | tf_op jit(solution)/shard_map/ppermute | solution.py:193
  55.5 24.3 %collective-permute-start.8 = (bf16[384,768]{1,0:T(8,128)(2,1)}, bf16[384,768]{1,0:T(8,128)(2,1)}, u32[]{:S(2)}, u32[]{:S(2)}) collective-permute-start(bf16[384,768]{1,0:T(8,128)(2,1)} %collective-permute-done.rest_2_), channel_id=1, source_target_pairs={{0,4},{4,0},{8,12},{12,8},{16,20},{20,16},{24,28},{28,24},{1,5},{5... | collective-permute-start | bytes 1769480 | tf_op jit(solution)/shard_map/ppermute | solution.py:193
  56.1 31.4 %collective-permute-start.7 = (bf16[384,768]{1,0:T(8,128)(2,1)}, bf16[384,768]{1,0:T(8,128)(2,1)}, u32[]{:S(2)}, u32[]{:S(2)}) collective-permute-start(bf16[384,768]{1,0:T(8,128)(2,1)} %collective-permute-done.rest_2_), channel_id=1, source_target_pairs={{0,8},{4,12},{8,0},{12,4},{16,24},{20,28},{24,16},{28,20},{1,9},{5... | collective-permute-start | bytes 1769480 | tf_op jit(solution)/shard_map/ppermute | solution.py:193
  59.9 0.8 copy-start.7
  60.7 0.8 copy-start.11
  70.0 0.8 copy-start.12
  70.8 19.4 %collective-permute-start.13 = (bf16[384,768]{1,0:T(8,128)(2,1)}, bf16[384,768]{1,0:T(8,128)(2,1)}, u32[]{:S(2)}, u32[]{:S(2)}) collective-permute-start(bf16[384,768]{1,0:T(8,128)(2,1)} %collective-permute-done.10.rest_1_), channel_id=1, source_target_pairs={{0,4},{4,0},{8,12},{12,8},{16,20},{20,16},{24,28},{28,24},{1,5},{5... | collective-permute-start | bytes 1769480 | tf_op jit(solution)/shard_map/ppermute | solution.py:193
  73.1 32.5 %collective-permute-start.14 = (f32[384,256]{1,0:T(8,128)}, f32[384,256]{1,0:T(8,128)S(1)}, u32[]{:S(2)}, u32[]{:S(2)}) collective-permute-start(f32[384,256]{1,0:T(8,128)} %copy-done.11), channel_id=1, source_target_pairs={{0,16},{4,20},{8,24},{12,28},{16,0},{20,4},{24,8},{28,12},{1,17},{... | collective-permute-start | bytes 1179656 | tf_op jit(solution)/shard_map/ppermute | solution.py:193
  74.7 0.8 copy-start.3
  75.4 14.8 %copy-start.4 = (s32[4,12,12]{2,1,0:T(8,128)S(1)}, s32[4,12,12]{2,1,0:T(8,128)}, u32[]{:S(2)}) copy-start(s32[4,12,12]{2,1,0:T(8,128)} %copy.11.mask_ref) | copy-start | bytes 6916
  77.7 0.7 copy-start.9
  78.5 27.7 %collective-permute-start.15 = (f32[384,256]{1,0:T(8,128)S(1)}, f32[384,256]{1,0:T(8,128)S(1)}, u32[]{:S(2)}, u32[]{:S(2)}) collective-permute-start(f32[384,256]{1,0:T(8,128)S(1)} %get-tuple-element.34), channel_id=1, source_target_pairs={{0,16},{4,20},{8,24},{12,28},{16,0},{20,4},{24,8},{28,12},{1,17},{... | collective-permute-start | bytes 1179656 | tf_op jit(solution)/shard_map/ppermute | solution.py:193
  87.5 14.2 %collective-permute-start.9 = (bf16[384,768]{1,0:T(8,128)(2,1)}, bf16[384,768]{1,0:T(8,128)(2,1)S(1)}, u32[]{:S(2)}, u32[]{:S(2)}) collective-permute-start(bf16[384,768]{1,0:T(8,128)(2,1)} %collective-permute-done.7.rest_0_), channel_id=1, source_target_pairs={{0,4},{4,0},{8,12},{12,8},{16,20},{20,16},{24,28},{28,24},{1,5},{5... | collective-permute-start | bytes 1769480 | tf_op jit(solution)/shard_map/ppermute | solution.py:193
  105.5 0.8 copy-start.14
  106.2 0.7 copy-start.16
  106.9 2.4 %collective-permute-start.16 = (f32[2,128,768]{2,1,0:T(8,128)S(1)}, f32[2,128,768]{2,1,0:T(8,128)}, u32[]{:S(2)}, u32[]{:S(2)}) collective-permute-start(f32[2,128,768]{2,1,0:T(8,128)S(1)} %dynamic-slice_bitcast_fusion), channel_id=1, source_target_pairs={{0,1},{1,0},{2,3},{3,2},{4,5},{5,4},{6,7},{7,6},{8,9},{9,8},{10,11... | collective-permute-start | bytes 2359304 | tf_op jit(solution)/shard_map/ppermute | solution.py:202
  106.9 6.0 %copy-start.8 = (f32[384,256]{1,0:T(8,128)S(1)}, f32[384,256]{1,0:T(8,128)}, u32[]{:S(2)}) copy-start(f32[384,256]{1,0:T(8,128)} %copy-done.7) | copy-start | bytes 1179652
  106.9 6.0 %copy-start.15 = (f32[384,256]{1,0:T(8,128)S(1)}, f32[384,256]{1,0:T(8,128)}, u32[]{:S(2)}) copy-start(f32[384,256]{1,0:T(8,128)} %copy-done.14) | copy-start | bytes 1179652
  110.5 2.4 %copy-start.10 = (f32[384,256]{1,0:T(8,128)S(1)}, f32[384,256]{1,0:T(8,128)}, u32[]{:S(2)}) copy-start(f32[384,256]{1,0:T(8,128)} %copy-done.9) | copy-start | bytes 1179652
  110.5 2.4 %copy-start.17 = (f32[384,256]{1,0:T(8,128)S(1)}, f32[384,256]{1,0:T(8,128)}, u32[]{:S(2)}) copy-start(f32[384,256]{1,0:T(8,128)} %copy-done.16) | copy-start | bytes 1179652
  111.3 11.4 %collective-permute-start.17 = (f32[128,768]{1,0:T(8,128)}, f32[128,768]{1,0:T(8,128)S(1)}, u32[]{:S(2)}, u32[]{:S(2)}) collective-permute-start(f32[128,768]{1,0:T(8,128)} %dynamic-slice_bitcast_fusion.1), channel_id=1, source_target_pairs={{0,2},{1,3},{2,0},{3,1},{4,6},{5,7},{6,4},{7,5},{8,10},{9,11},{10,... | collective-permute-start | bytes 1179656 | tf_op jit(solution)/shard_map/ppermute | solution.py:202
  112.8 1.0 copy-start.6
  112.9 1.1 copy-start.13

commit v15 on v14

--- a/solution.py
+++ b/solution.py
@@ -98,27 +98,35 @@
     )(where, block_mask, *acts, *og)
 
 
-def forward_and_input(acts, w_mine, w_peer, og, block_mask, where, first, before):
+def forward_and_input(acts, w_mine, w_peer, og, block_mask, where, first, out_before=None, gx_before=None):
     nsub, tokens, width = og.shape
     depth = acts.shape[1]
     nz = len(w_mine)
     owners = depth // (2 * w_mine[0].shape[0])
+    started = out_before is None and gx_before is None
+    outs = started or out_before is not None
+    gxs = started or gx_before is not None
     rows = w_mine[0].shape[0]
     per = rows // LANES
     two = BS // LANES
 
     def kernel(where_ref, mask_ref, acts_ref, og_ref, *rest):
         w_refs, rest = rest[: 2 * nz], rest[2 * nz :]
-        out_ref, gx_ref, acc, hilo = rest[-4:]
+        acc, hilo = rest[-2:]
+        out_ref = rest[-3 - gxs]
+        gx_ref = rest[-3]
         z, x = where_ref[0], where_ref[1]
         step = pl.program_id(0)
         col = where_ref[2] + step
 
-        @pl.when(step == 0)
-        def _():
-            gx_ref[...] = rest[1][...] if before else jnp.zeros_like(gx_ref)
-
-        acc[...] = rest[0][...] if before else jnp.zeros_like(acc)
+        if gxs:
+
+            @pl.when(step == 0)
+            def _():
+                gx_ref[...] = jnp.zeros_like(gx_ref) if started else rest[0][...]
+
+        if outs:
+            acc[...] = jnp.zeros_like(acc) if started else rest[0][...]
         for k in range(nz):
             owner = z ^ (first + k)
             tiles = []
@@ -130,20 +138,24 @@
                 block = owner * (2 * per // two) + b
                 w = jnp.concatenate(tiles[b * two : (b + 1) * two])
                 cols = pl.ds(pl.multiple_of(block * BS, BS), BS)
+                if outs:
+                    prod = jnp.dot(acts_ref[:, cols], w, preferred_element_type=F32)
+                    for s in range(nsub):
+                        acc[s] += mask_ref[s, block, col].astype(F32) * prod
+                if not gxs:
+                    continue
                 total = jnp.zeros((tokens, BS), F32)
                 for s in range(nsub):
                     total = total + mask_ref[s, block, col].astype(F32) * og_ref[s].astype(F32)
                 hi = total.astype(BF16)
                 hilo[:tokens] = hi
                 hilo[tokens:] = (total - hi.astype(F32)).astype(BF16)
-                prod = jnp.dot(acts_ref[:, cols], w, preferred_element_type=F32)
-                for s in range(nsub):
-                    acc[s] += mask_ref[s, block, col].astype(F32) * prod
                 both = lax.dot_general(
                     hilo[...], w, (((1,), (1,)), ((), ())), preferred_element_type=F32
                 )
                 gx_ref[owner, :, b * BS : (b + 1) * BS] += both[:tokens] + both[tokens:]
-        out_ref[...] = acc[...].astype(out_ref.dtype)
+        if outs:
+            out_ref[...] = acc[...].astype(out_ref.dtype)
 
     smem = pl.BlockSpec(memory_space=pltpu.SMEM)
     by_col = pl.BlockSpec((nsub, tokens, BS), lambda j: (0, 0, j))
@@ -153,14 +165,12 @@
     return pl.pallas_call(
         kernel,
         grid=(width // BS,),
-        out_shape=(
-            jax.ShapeDtypeStruct((nsub, tokens, width), BF16 if before else F32),
-            jax.ShapeDtypeStruct(by_owner, F32),
-        ),
+        out_shape=[jax.ShapeDtypeStruct((nsub, tokens, width), F32 if started else BF16)] * outs
+        + [jax.ShapeDtypeStruct(by_owner, F32)] * gxs,
         in_specs=[smem, smem, whole, by_col]
         + [pl.BlockSpec((rows, BS), lambda j: (0, j))] * (2 * nz)
-        + ([by_col, gx_spec] if before else []),
-        out_specs=(by_col, gx_spec),
+        + ([] if started else [by_col] * outs + [gx_spec] * gxs),
+        out_specs=[by_col] * outs + [gx_spec] * gxs,
         scratch_shapes=[
             pltpu.VMEM((nsub, tokens, BS), F32),
             pltpu.VMEM((2 * tokens, BS), BF16),
@@ -172,7 +182,7 @@
             transcendentals=0,
         ),
         name="forward_and_input",
-    )(where, block_mask, acts, og, *w_mine, *w_peer, *(before or ()))
+    )(where, block_mask, acts, og, *w_mine, *w_peer, *[a for a in (out_before, gx_before) if a is not None])
 
 
 def on_device(acts, weight, block_mask, out_grad):
@@ -223,8 +233,8 @@
     og = [out_grad, og_one, og_side, og_both]
     acts_all = [acts, acts_one, acts_side, acts_both]
     keeps, gots = [], []
-    for j in range(width // BS):
-        keep, send = weight_grad_part(acts_all, og, block_mask, where, rows, j, 1)
+    for j, count in ((0, 1), (1, width // BS - 1)):
+        keep, send = weight_grad_part(acts_all, og, block_mask, where, rows, j, count)
         keeps.append(keep)
         gots.append(swap_z(send, 2))
     grad_w = jnp.concatenate([k + g for k, g in zip(keeps, gots)], axis=1)
@@ -233,17 +243,15 @@
     x_own = swap_x(after(weight, acts_side))
     x_one = swap_x(after(w_one, gots[0], x_own, keeps[1]))
     x_two = swap_x(after(w_two, keeps[0]))
-    x_three = swap_x(after(w_three, keeps[2], x_two))
+    x_three = swap_x(after(w_three, keeps[1], x_two))
     w_peer = [x_own, x_one, x_two, x_three]
 
-    sums = forward_and_input(
-        acts, w_mine[:3], w_peer[:3], out_grad, block_mask, where, 0, None
-    )
-    outputs, gx = forward_and_input(
-        acts, w_mine[3:], w_peer[3:], out_grad, block_mask, where, 3, sums
-    )
-
-    by = after(gx, gots[1], gots[2]).reshape(2, 2, tokens, depth // 4)
+    part, gx = forward_and_input(acts, w_mine[:3], w_peer[:3], out_grad, block_mask, where, 0)
+    last = (acts, w_mine[3:], w_peer[3:], out_grad, block_mask, where, 3)
+    (gx,) = forward_and_input(*last, gx_before=gx)
+    (outputs,) = forward_and_input(*last, out_before=part)
+
+    by = after(gx, gots[1]).reshape(2, 2, tokens, depth // 4)
     pair = lax.dynamic_index_in_dim(by, c, 1, keepdims=False) + swap_f(
         lax.dynamic_index_in_dim(by, 1 - c, 1, keepdims=False), 1
     )

time: 124 us -> 124 us (level)
  waiting for transfers between devices: 65.1 us -> 71.8 us
  starting transfers between devices: 25.7 us -> 20.3 us
  local copies, waits for them, and re-layouts: 10.3 us -> 7.22 us
  Pallas kernels: 16.1 us -> 17.6 us
    ppermute x16 -> x15, waiting for transfers between devices: 55.1 us -> 66.4 us  [swap_dp(): return lax.ppermute(a, 'dp', [(d, d ^ bits) for d in range(dp)])]
    ppermute x16 -> x15, starting transfers between devices: 24.1 us -> 18.7 us  [swap_dp(): return lax.ppermute(a, 'dp', [(d, d ^ bits) for d in range(dp)])]
    ppermute x2, waiting for transfers between devices: 10 us -> 5.43 us  [swap_f(): return lax.ppermute(a, 'fsdp', [(d, d ^ bit) for d in range(fsdp)])]
    unnamed x37 -> x31, local copies, waits for them, and re-layouts: 8.32 us -> 5.12 us
    pallas_call x2 -> x3, Pallas kernels: 9.28 us -> 11.8 us  [forward_and_input(): pl.pallas_call(kernel, grid=(width // BS,), out_shape=[jax.ShapeDtypeStru...]
    add x3 -> x2, other arithmetic: 0.15 us -> 2.39 us  [on_device(): grad_w = jnp.concatenate([k + g for k, g in zip(keeps, gots)], axis=1)]
    pallas_call x3 -> x2, Pallas kernels: 6.84 us -> 5.75 us  [weight_grad_part(): pl.pallas_call(kernel, grid=(chunks,), out_shape=(jax.ShapeDtypeStruct((r...]
  transfers between devices with their start and end apart: 18 -> 17, of which waited for: 11 -> 12; matrix products, arithmetic and copies ran while one was open for 5% -> 4% of each run, Pallas kernels for 13% -> 14%
where the time goes in v15:
time: 124 us; the launch traced here: 123 us
  waiting for transfers between devices  71.8 us (58%)
  starting transfers between devices  20.3 us (16%)
  Pallas kernels  17.6 us (14%)
  local copies, waits for them, and re-layouts  7.22 us (6%)
  other arithmetic  5.57 us (4%)
    ppermute x15, waiting for transfers between devices, swap_dp(): return lax.ppermute(a, 'dp', [(d, d ^ bits) for d in range(dp)])  66.4 us
    ppermute x15, starting transfers between devices, swap_dp(): return lax.ppermute(a, 'dp', [(d, d ^ bits) for d in range(dp)])  18.7 us
    pallas_call x3, Pallas kernels, forward_and_input(): pl.pallas_call(kernel, grid=(width // BS,), out_shape=[jax.ShapeDtypeStru...  11.8 us
    pallas_call x2, Pallas kernels, weight_grad_part(): pl.pallas_call(kernel, grid=(chunks,), out_shape=(jax.ShapeDtypeStruct((r...  5.75 us
    ppermute x2, waiting for transfers between devices, swap_f(): return lax.ppermute(a, 'fsdp', [(d, d ^ bit) for d in range(fsdp)])  5.43 us
    unnamed x31, local copies, waits for them, and re-layouts  5.12 us
  transfers between devices with their start and end apart: 17, of which 12 were waited for; matrix products, arithmetic and copies ran while one was open for 4% of the time, Pallas kernels for 14%

profile of v15, /device:TPU:0, one launch (start us, length us, event | category | flops | bytes accessed | tf_op | source)
XLA Modules:
  0.0 123.2 jit_solution(12504643510145406961)
XLA Ops:
  0.6 0.0 copy-start
  0.6 3.1 %collective-permute-start.4 = (bf16[4,128,768]{2,1,0:T(8,128)(2,1)}, bf16[4,128,768]{2,1,0:T(8,128)(2,1)S(1)}, u32[]{:S(2)}, u32[]{:S(2)}) collective-permute-start(bf16[4,128,768]{2,1,0:T(8,128)(2,1)} %og_ref.5), channel_id=1, source_target_pairs={{0,8},{4,12},{8,0},{12,4},{16,24},{20,28},{24,16},{28,20},{1,9},{5... | collective-permute-start | bytes 2359304 | tf_op jit(solution)/shard_map/ppermute | solution.py:203
  3.7 1.5 %collective-permute-start.5 = (bf16[4,128,768]{2,1,0:T(8,128)(2,1)}, bf16[4,128,768]{2,1,0:T(8,128)(2,1)}, u32[]{:S(2)}, u32[]{:S(2)}) collective-permute-start(bf16[4,128,768]{2,1,0:T(8,128)(2,1)} %og_ref.5), channel_id=1, source_target_pairs={{0,4},{4,0},{8,12},{12,8},{16,20},{20,16},{24,28},{28,24},{1,5},{5... | collective-permute-start | bytes 2359304 | tf_op jit(solution)/shard_map/ppermute | solution.py:203
  5.2 1.0 dynamic-slice_bitcast_fusion.3
  6.3 0.0 copy-start.1
  6.3 0.5 collective-permute-start.1
  6.8 0.0 copy-done
  6.9 0.2 collective-permute-start.2
  7.1 15.2 %collective-permute-done.4.refs_5_ = bf16[4,128,768]{2,1,0:T(8,128)(2,1)S(1)} collective-permute-done((bf16[4,128,768]{2,1,0:T(8,128)(2,1)}, bf16[4,128,768]{2,1,0:T(8,128)(2,1)S(1)}, u32[]{:S(2)}, u32[]{:S(2)}) %collective-permute-start.4) | collective-permute-done | bytes 786464 | tf_op jit(solution)/shard_map/ppermute | solution.py:203
  22.3 2.2 %collective-permute-done.5.refs_6_ = bf16[4,128,768]{2,1,0:T(8,128)(2,1)} collective-permute-done((bf16[4,128,768]{2,1,0:T(8,128)(2,1)}, bf16[4,128,768]{2,1,0:T(8,128)(2,1)}, u32[]{:S(2)}, u32[]{:S(2)}) %collective-permute-start.5) | collective-permute-done | bytes 786464 | tf_op jit(solution)/shard_map/ppermute | solution.py:203
  24.5 1.5 %collective-permute-start.6 = (bf16[4,128,768]{2,1,0:T(8,128)(2,1)S(1)}, bf16[4,128,768]{2,1,0:T(8,128)(2,1)}, u32[]{:S(2)}, u32[]{:S(2)}) collective-permute-start(bf16[4,128,768]{2,1,0:T(8,128)(2,1)S(1)} %collective-permute-done.4.refs_5_), channel_id=1, source_target_pairs={{0,4},{4,0},{8,12},{12,8},{16,20},{20,16},{24,28},{28,24},{1,5},{5... | collective-permute-start | bytes 2359304 | tf_op jit(solution)/shard_map/ppermute | solution.py:203
  26.0 2.6 %collective-permute-start = (bf16[384,768]{1,0:T(8,128)(2,1)}, bf16[384,768]{1,0:T(8,128)(2,1)}, u32[]{:S(2)}, u32[]{:S(2)}) collective-permute-start(bf16[384,768]{1,0:T(8,128)(2,1)} %rest_0_.1), channel_id=1, source_target_pairs={{0,16},{4,20},{8,24},{12,28},{16,0},{20,4},{24,8},{28,12},{1,17},{... | collective-permute-start | bytes 1769480 | tf_op jit(solution)/shard_map/ppermute | solution.py:203
  28.6 0.0 collective-permute-done.2.refs_2_
  28.6 6.8 %collective-permute-done.1.refs_1_ = bf16[2,128,768]{2,1,0:T(8,128)(2,1)S(1)} collective-permute-done((bf16[2,128,768]{2,1,0:T(8,128)(2,1)S(1)}, bf16[2,128,768]{2,1,0:T(8,128)(2,1)S(1)}, u32[]{:S(2)}, u32[]{:S(2)}) %collective-permute-start.1) | collective-permute-done | bytes 393248 | tf_op jit(solution)/shard_map/ppermute | solution.py:203
  35.6 2.7 %collective-permute-start.3 = (bf16[128,768]{1,0:T(8,128)(2,1)S(1)}, bf16[128,768]{1,0:T(8,128)(2,1)S(1)}, u32[]{:S(2)}, u32[]{:S(2)}) collective-permute-start(bf16[128,768]{1,0:T(8,128)(2,1)S(1)} %pad_maximum_fusion.3), channel_id=1, source_target_pairs={{0,4},{4,0},{8,12},{12,8},{16,20},{20,16},{24,28},{28,24},{1,5},{5... | collective-permute-start | bytes 589832 | tf_op jit(solution)/shard_map/ppermute | solution.py:203
  38.2 0.0 collective-permute-start.10
  38.2 0.2 collective-permute-start.11
  38.4 0.0 copy-done.14
  38.4 0.6 copy.10.mask_ref
  39.0 0.1 pad_add_fusion.where_ref
  39.1 10.6 %collective-permute-done.3.refs_3_ = bf16[128,768]{1,0:T(8,128)(2,1)S(1)} collective-permute-done((bf16[128,768]{1,0:T(8,128)(2,1)S(1)}, bf16[128,768]{1,0:T(8,128)(2,1)S(1)}, u32[]{:S(2)}, u32[]{:S(2)}) %collective-permute-start.3) | collective-permute-done | bytes 196640 | tf_op jit(solution)/shard_map/ppermute | solution.py:203
  49.7 0.0 collective-permute-done.6.refs_7_
  49.7 0.0 copy-done.1
  49.7 0.8 copy-done.4
  50.5 2.2 %weight_grad_part.2 = (f32[384,256]{1,0:T(8,128)S(1)}, f32[384,256]{1,0:T(8,128)S(1)}) custom-call(s32[4]{0:T(128)S(1)} %pad_add_fusion.where_ref, s32[4,12,12]{2,1,0:T(8,128)S(1)} %copy-done.4, bf16[128,3072]{1,0:T(8,128)(2,1)S(1)} %copy-done, bf16[2,128,768]{2,1,0:T(8,128)(2,1)S(1)} %collective-permute-done.1.refs_1_, ...), custom_call_target="tpu_custom_call" | custom-call | flops 805306368 | bytes 786432 | tf_op jit(solution)/shard_map/weight_grad_part/pallas_call | solution.py:84
  52.6 2.7 %collective-permute-start.12 = (f32[384,256]{1,0:T(8,128)S(1)}, f32[384,256]{1,0:T(8,128)}, u32[]{:S(2)}, u32[]{:S(2)}) collective-permute-start(f32[384,256]{1,0:T(8,128)S(1)} %get-tuple-element.23), channel_id=1, source_target_pairs={{0,16},{4,20},{8,24},{12,28},{16,0},{20,4},{24,8},{28,12},{1,17},{... | collective-permute-start | bytes 1179656 | tf_op jit(solution)/shard_map/ppermute | solution.py:203
  55.3 0.0 collective-permute-done.rest_2_
  55.3 1.5 %collective-permute-start.8 = (bf16[384,768]{1,0:T(8,128)(2,1)}, bf16[384,768]{1,0:T(8,128)(2,1)}, u32[]{:S(2)}, u32[]{:S(2)}) collective-permute-start(bf16[384,768]{1,0:T(8,128)(2,1)} %collective-permute-done.rest_2_), channel_id=1, source_target_pairs={{0,4},{4,0},{8,12},{12,8},{16,20},{20,16},{24,28},{28,24},{1,5},{5... | collective-permute-start | bytes 1769480 | tf_op jit(solution)/shard_map/ppermute | solution.py:203
  56.8 0.4 collective-permute-start.7
  57.3 3.6 %weight_grad_part.3 = (f32[384,512]{1,0:T(8,128)S(1)}, f32[384,512]{1,0:T(8,128)S(1)}) custom-call(s32[4]{0:T(128)S(1)} %pad_add_fusion.where_ref, s32[4,12,12]{2,1,0:T(8,128)S(1)} %copy-done.4, bf16[128,3072]{1,0:T(8,128)(2,1)S(1)} %copy-done, bf16[2,128,768]{2,1,0:T(8,128)(2,1)S(1)} %collective-permute-done.1.refs_1_, ...), custom_call_target="tpu_custom_call" | custom-call | flops 1610612736 | bytes 1572864 | tf_op jit(solution)/shard_map/weight_grad_part/pallas_call | solution.py:84
  60.8 0.0 copy-start.2
  60.8 0.9 copy-done.2
  61.7 0.9 copy-done.8
  62.6 4.2 %collective-permute-done.10.rest_1_ = bf16[384,768]{1,0:T(8,128)(2,1)} collective-permute-done((bf16[384,768]{1,0:T(8,128)(2,1)}, bf16[384,768]{1,0:T(8,128)(2,1)}, u32[]{:S(2)}, u32[]{:S(2)}) %collective-permute-start.10) | collective-permute-done | bytes 589856 | tf_op jit(solution)/shard_map/ppermute | solution.py:203
  66.8 0.0 collective-permute-done.11.rest_3_
  66.8 3.8 %collective-permute-done.12 = f32[384,256]{1,0:T(8,128)} collective-permute-done((f32[384,256]{1,0:T(8,128)S(1)}, f32[384,256]{1,0:T(8,128)}, u32[]{:S(2)}, u32[]{:S(2)}) %collective-permute-start.12) | collective-permute-done | bytes 393248 | tf_op jit(solution)/shard_map/ppermute | solution.py:203
  70.6 1.5 %collective-permute-start.13 = (bf16[384,768]{1,0:T(8,128)(2,1)}, bf16[384,768]{1,0:T(8,128)(2,1)S(1)}, u32[]{:S(2)}, u32[]{:S(2)}) collective-permute-start(bf16[384,768]{1,0:T(8,128)(2,1)} %collective-permute-done.10.rest_1_), channel_id=1, source_target_pairs={{0,4},{4,0},{8,12},{12,8},{16,20},{20,16},{24,28},{28,24},{1,5},{5... | collective-permute-start | bytes 1769480 | tf_op jit(solution)/shard_map/ppermute | solution.py:203
  72.1 0.0 collective-permute-start.14
  72.1 3.0 %collective-permute-done.8.rest_5_ = bf16[384,768]{1,0:T(8,128)(2,1)} collective-permute-done((bf16[384,768]{1,0:T(8,128)(2,1)}, bf16[384,768]{1,0:T(8,128)(2,1)}, u32[]{:S(2)}, u32[]{:S(2)}) %collective-permute-start.8) | collective-permute-done | bytes 589856 | tf_op jit(solution)/shard_map/ppermute | solution.py:203
  75.1 12.0 %collective-permute-done.7.rest_0_ = bf16[384,768]{1,0:T(8,128)(2,1)} collective-permute-done((bf16[384,768]{1,0:T(8,128)(2,1)}, bf16[384,768]{1,0:T(8,128)(2,1)}, u32[]{:S(2)}, u32[]{:S(2)}) %collective-permute-start.7) | collective-permute-done | bytes 589856 | tf_op jit(solution)/shard_map/ppermute | solution.py:203
  87.0 0.4 collective-permute-start.9
  87.4 0.0 collective-permute-done.13.rest_4_
  87.4 0.8 copy-done.5
  88.2 1.1 copy-done.9
  89.2 5.3 %forward_and_input.3 = (f32[4,128,768]{2,1,0:T(8,128)S(1)}, f32[4,128,768]{2,1,0:T(8,128)S(1)}) custom-call(s32[4]{0:T(128)S(1)} %pad_add_fusion.where_ref, s32[4,12,12]{2,1,0:T(8,128)S(1)} %copy-done.5, bf16[128,3072]{1,0:T(8,128)(2,1)S(1)} %copy-done, bf16[4,128,768]{2,1,0:T(8,128)(2,1)S(1)} %copy-done.1, bf16[384,768]{1,0:T(8,128)(2,1)S(1)} %copy-done.9, ...), custom_call_target="tpu_custom_call" | custom-call | flops 8153726976 | bytes 7077888 | tf_op jit(solution)/shard_map/forward_and_input/pallas_call | solution.py:165
  94.6 0.0 copy-start.12
  94.6 5.8 %collective-permute-done.9.rest_1_ = bf16[384,768]{1,0:T(8,128)(2,1)S(1)} collective-permute-done((bf16[384,768]{1,0:T(8,128)(2,1)}, bf16[384,768]{1,0:T(8,128)(2,1)S(1)}, u32[]{:S(2)}, u32[]{:S(2)}) %collective-permute-start.9) | collective-permute-done | bytes 589856 | tf_op jit(solution)/shard_map/ppermute | solution.py:203
  100.3 0.0 copy-done.6
  100.4 3.0 %forward_and_input.5 = f32[4,128,768]{2,1,0:T(8,128)S(1)} custom-call(s32[4]{0:T(128)S(1)} %pad_add_fusion.where_ref, s32[4,12,12]{2,1,0:T(8,128)S(1)} %copy-done.6, bf16[128,3072]{1,0:T(8,128)(2,1)S(1)} %copy-done, bf16[4,128,768]{2,1,0:T(8,128)(2,1)S(1)} %copy-done.1, bf16[384,768]{1,0:T(8,128)(2,1)} %collective-permute-done.7.rest_0_, ...), custom_call_target="tpu_custom_call" | custom-call | flops 2717908992 | bytes 2359296 | tf_op jit(solution)/shard_map/forward_and_input/pallas_call | solution.py:165
  103.3 2.8 %collective-permute-done.14 = f32[384,512]{1,0:T(8,128)} collective-permute-done((f32[384,512]{1,0:T(8,128)}, f32[384,512]{1,0:T(8,128)}, u32[]{:S(2)}, u32[]{:S(2)}) %collective-permute-start.14) | collective-permute-done | bytes 786464 | tf_op jit(solution)/shard_map/ppermute | solution.py:203
  106.1 0.9 dynamic-slice_bitcast_fusion
  107.1 0.0 collective-permute-start.15
  107.1 1.1 add.68
  108.2 0.1 copy-done.3
  108.3 1.3 %add.69 = f32[384,512]{1,0:T(8,128)S(1)} add(f32[384,512]{1,0:T(8,128)S(1)} %copy-done.3, f32[384,512]{1,0:T(8,128)} %collective-permute-done.14) | non-fusion elementwise | flops 196608 | bytes 2359296 | tf_op jit(solution)/shard_map/add | solution.py:240
  109.6 0.1 collective-permute-done.15
  109.7 1.2 bitcast_add_fusion
  110.9 0.0 copy-start.7
  111.0 1.6 %collective-permute-start.16 = (f32[128,768]{1,0:T(8,128)S(1)}, f32[128,768]{1,0:T(8,128)S(1)}, u32[]{:S(2)}, u32[]{:S(2)}) collective-permute-start(f32[128,768]{1,0:T(8,128)S(1)} %dynamic-slice_bitcast_fusion.1), channel_id=1, source_target_pairs={{0,2},{1,3},{2,0},{3,1},{4,6},{5,7},{6,4},{7,5},{8,10},{9,11},{10,... | collective-permute-start | bytes 1179656 | tf_op jit(solution)/shard_map/ppermute | solution.py:212
  112.6 1.1 pad_maximum_fusion
  113.7 0.0 copy-done.11
  113.7 3.5 %forward_and_input.4 = bf16[4,128,768]{2,1,0:T(8,128)(2,1)} custom-call(s32[4]{0:T(128)S(1)} %pad_add_fusion.where_ref, s32[4,12,12]{2,1,0:T(8,128)S(1)} %copy-done.7, bf16[128,3072]{1,0:T(8,128)(2,1)S(1)} %copy-done, bf16[4,128,768]{2,1,0:T(8,128)(2,1)S(1)} %copy-done.1, bf16[384,768]{1,0:T(8,128)(2,1)} %collective-permute-done.7.rest_0_, ...), custom_call_target="tpu_custom_call" | custom-call | flops 2717908992 | bytes 2359296 | tf_op jit(solution)/shard_map/forward_and_input/pallas_call | solution.py:165
  117.2 5.3 %collective-permute-done.16 = f32[128,768]{1,0:T(8,128)S(1)} collective-permute-done((f32[128,768]{1,0:T(8,128)S(1)}, f32[128,768]{1,0:T(8,128)S(1)}, u32[]{:S(2)}, u32[]{:S(2)}) %collective-permute-start.16) | collective-permute-done | bytes 393248 | tf_op jit(solution)/shard_map/ppermute | solution.py:212
  122.5 0.7 fusion
  (21 shorter events, 0.2 us)
Async XLA Ops:
  0.6 6.2 %copy-start = (bf16[128,3072]{1,0:T(8,128)(2,1)S(1)}, bf16[128,3072]{1,0:T(8,128)(2,1)}, u32[]{:S(2)}) copy-start(bf16[128,3072]{1,0:T(8,128)(2,1)} %acts_ref.5) | copy-start | bytes 2359300
  0.6 21.7 %collective-permute-start.4 = (bf16[4,128,768]{2,1,0:T(8,128)(2,1)}, bf16[4,128,768]{2,1,0:T(8,128)(2,1)S(1)}, u32[]{:S(2)}, u32[]{:S(2)}) collective-permute-start(bf16[4,128,768]{2,1,0:T(8,128)(2,1)} %og_ref.5), channel_id=1, source_target_pairs={{0,8},{4,12},{8,0},{12,4},{16,24},{20,28},{24,16},{28,20},{1,9},{5... | collective-permute-start | bytes 2359304 | tf_op jit(solution)/shard_map/ppermute | solution.py:203
  3.7 20.8 %collective-permute-start.5 = (bf16[4,128,768]{2,1,0:T(8,128)(2,1)}, bf16[4,128,768]{2,1,0:T(8,128)(2,1)}, u32[]{:S(2)}, u32[]{:S(2)}) collective-permute-start(bf16[4,128,768]{2,1,0:T(8,128)(2,1)} %og_ref.5), channel_id=1, source_target_pairs={{0,4},{4,0},{8,12},{12,8},{16,20},{20,16},{24,28},{28,24},{1,5},{5... | collective-permute-start | bytes 2359304 | tf_op jit(solution)/shard_map/ppermute | solution.py:203
  6.3 43.4 %copy-start.1 = (bf16[4,128,768]{2,1,0:T(8,128)(2,1)S(1)}, bf16[4,128,768]{2,1,0:T(8,128)(2,1)}, u32[]{:S(2)}) copy-start(bf16[4,128,768]{2,1,0:T(8,128)(2,1)} %og_ref.5) | copy-start | bytes 2359300
  6.3 29.1 %collective-permute-start.1 = (bf16[2,128,768]{2,1,0:T(8,128)(2,1)S(1)}, bf16[2,128,768]{2,1,0:T(8,128)(2,1)S(1)}, u32[]{:S(2)}, u32[]{:S(2)}) collective-permute-start(bf16[2,128,768]{2,1,0:T(8,128)(2,1)S(1)} %pad_maximum_fusion.1), channel_id=1, source_target_pairs={{0,8},{4,12},{8,0},{12,4},{16,24},{20,28},{24,16},{28,20},{1,9},{5... | collective-permute-start | bytes 1179656 | tf_op jit(solution)/shard_map/ppermute | solution.py:203
  6.9 21.7 %collective-permute-start.2 = (bf16[128,768]{1,0:T(8,128)(2,1)S(1)}, bf16[128,768]{1,0:T(8,128)(2,1)S(1)}, u32[]{:S(2)}, u32[]{:S(2)}) collective-permute-start(bf16[128,768]{1,0:T(8,128)(2,1)S(1)} %pad_maximum_fusion.2), channel_id=1, source_target_pairs={{0,4},{4,0},{8,12},{12,8},{16,20},{20,16},{24,28},{28,24},{1,5},{5... | collective-permute-start | bytes 589832 | tf_op jit(solution)/shard_map/ppermute | solution.py:203
  24.5 25.2 %collective-permute-start.6 = (bf16[4,128,768]{2,1,0:T(8,128)(2,1)S(1)}, bf16[4,128,768]{2,1,0:T(8,128)(2,1)}, u32[]{:S(2)}, u32[]{:S(2)}) collective-permute-start(bf16[4,128,768]{2,1,0:T(8,128)(2,1)S(1)} %collective-permute-done.4.refs_5_), channel_id=1, source_target_pairs={{0,4},{4,0},{8,12},{12,8},{16,20},{20,16},{24,28},{28,24},{1,5},{5... | collective-permute-start | bytes 2359304 | tf_op jit(solution)/shard_map/ppermute | solution.py:203
  26.0 29.3 %collective-permute-start = (bf16[384,768]{1,0:T(8,128)(2,1)}, bf16[384,768]{1,0:T(8,128)(2,1)}, u32[]{:S(2)}, u32[]{:S(2)}) collective-permute-start(bf16[384,768]{1,0:T(8,128)(2,1)} %rest_0_.1), channel_id=1, source_target_pairs={{0,16},{4,20},{8,24},{12,28},{16,0},{20,4},{24,8},{28,12},{1,17},{... | collective-permute-start | bytes 1769480 | tf_op jit(solution)/shard_map/ppermute | solution.py:203
  35.5 2.9 %copy-start.14 = (s32[4,12,12]{2,0,1:T(4,128)S(1)}, s32[4,12,12]{2,0,1:T(4,128)}, u32[]{:S(2)}) copy-start(s32[4,12,12]{2,0,1:T(4,128)} %param.6) | copy-start | bytes 6916
  35.6 14.1 %collective-permute-start.3 = (bf16[128,768]{1,0:T(8,128)(2,1)S(1)}, bf16[128,768]{1,0:T(8,128)(2,1)S(1)}, u32[]{:S(2)}, u32[]{:S(2)}) collective-permute-start(bf16[128,768]{1,0:T(8,128)(2,1)S(1)} %pad_maximum_fusion.3), channel_id=1, source_target_pairs={{0,4},{4,0},{8,12},{12,8},{16,20},{20,16},{24,28},{28,24},{1,5},{5... | collective-permute-start | bytes 589832 | tf_op jit(solution)/shard_map/ppermute | solution.py:203
  38.2 28.6 %collective-permute-start.10 = (bf16[384,768]{1,0:T(8,128)(2,1)}, bf16[384,768]{1,0:T(8,128)(2,1)}, u32[]{:S(2)}, u32[]{:S(2)}) collective-permute-start(bf16[384,768]{1,0:T(8,128)(2,1)} %rest_0_.1), channel_id=1, source_target_pairs={{0,8},{4,12},{8,0},{12,4},{16,24},{20,28},{24,16},{28,20},{1,9},{5... | collective-permute-start | bytes 1769480 | tf_op jit(solution)/shard_map/ppermute | solution.py:203
  38.2 28.6 %collective-permute-start.11 = (bf16[384,768]{1,0:T(8,128)(2,1)}, bf16[384,768]{1,0:T(8,128)(2,1)}, u32[]{:S(2)}, u32[]{:S(2)}) collective-permute-start(bf16[384,768]{1,0:T(8,128)(2,1)} %rest_0_.1), channel_id=1, source_target_pairs={{0,4},{4,0},{8,12},{12,8},{16,20},{20,16},{24,28},{28,24},{1,5},{5... | collective-permute-start | bytes 1769480 | tf_op jit(solution)/shard_map/ppermute | solution.py:203
  49.7 0.8 copy-start.4
  52.6 18.0 %collective-permute-start.12 = (f32[384,256]{1,0:T(8,128)S(1)}, f32[384,256]{1,0:T(8,128)}, u32[]{:S(2)}, u32[]{:S(2)}) collective-permute-start(f32[384,256]{1,0:T(8,128)S(1)} %get-tuple-element.23), channel_id=1, source_target_pairs={{0,16},{4,20},{8,24},{12,28},{16,0},{20,4},{24,8},{28,12},{1,17},{... | collective-permute-start | bytes 1179656 | tf_op jit(solution)/shard_map/ppermute | solution.py:203
  55.3 19.8 %collective-permute-start.8 = (bf16[384,768]{1,0:T(8,128)(2,1)}, bf16[384,768]{1,0:T(8,128)(2,1)}, u32[]{:S(2)}, u32[]{:S(2)}) collective-permute-start(bf16[384,768]{1,0:T(8,128)(2,1)} %collective-permute-done.rest_2_), channel_id=1, source_target_pairs={{0,4},{4,0},{8,12},{12,8},{16,20},{20,16},{24,28},{28,24},{1,5},{5... | collective-permute-start | bytes 1769480 | tf_op jit(solution)/shard_map/ppermute | solution.py:203
  56.8 30.2 %collective-permute-start.7 = (bf16[384,768]{1,0:T(8,128)(2,1)}, bf16[384,768]{1,0:T(8,128)(2,1)}, u32[]{:S(2)}, u32[]{:S(2)}) collective-permute-start(bf16[384,768]{1,0:T(8,128)(2,1)} %collective-permute-done.rest_2_), channel_id=1, source_target_pairs={{0,8},{4,12},{8,0},{12,4},{16,24},{20,28},{24,16},{28,20},{1,9},{5... | collective-permute-start | bytes 1769480 | tf_op jit(solution)/shard_map/ppermute | solution.py:203
  60.8 0.9 copy-start.2
  61.7 0.9 copy-start.8
  70.6 16.8 %collective-permute-start.13 = (bf16[384,768]{1,0:T(8,128)(2,1)}, bf16[384,768]{1,0:T(8,128)(2,1)S(1)}, u32[]{:S(2)}, u32[]{:S(2)}) collective-permute-start(bf16[384,768]{1,0:T(8,128)(2,1)} %collective-permute-done.10.rest_1_), channel_id=1, source_target_pairs={{0,4},{4,0},{8,12},{12,8},{16,20},{20,16},{24,28},{28,24},{1,5},{5... | collective-permute-start | bytes 1769480 | tf_op jit(solution)/shard_map/ppermute | solution.py:203
  72.1 34.0 %collective-permute-start.14 = (f32[384,512]{1,0:T(8,128)}, f32[384,512]{1,0:T(8,128)}, u32[]{:S(2)}, u32[]{:S(2)}) collective-permute-start(f32[384,512]{1,0:T(8,128)} %copy-done.8), channel_id=1, source_target_pairs={{0,16},{4,20},{8,24},{12,28},{16,0},{20,4},{24,8},{28,12},{1,17},{... | collective-permute-start | bytes 2359304 | tf_op jit(solution)/shard_map/ppermute | solution.py:203
  87.0 13.3 %collective-permute-start.9 = (bf16[384,768]{1,0:T(8,128)(2,1)}, bf16[384,768]{1,0:T(8,128)(2,1)S(1)}, u32[]{:S(2)}, u32[]{:S(2)}) collective-permute-start(bf16[384,768]{1,0:T(8,128)(2,1)} %collective-permute-done.7.rest_0_), channel_id=1, source_target_pairs={{0,4},{4,0},{8,12},{12,8},{16,20},{20,16},{24,28},{28,24},{1,5},{5... | collective-permute-start | bytes 1769480 | tf_op jit(solution)/shard_map/ppermute | solution.py:203
  87.4 0.8 copy-start.5
  88.2 1.1 copy-start.9
  89.2 11.1 %copy-start.6 = (s32[4,12,12]{2,1,0:T(8,128)S(1)}, s32[4,12,12]{2,1,0:T(8,128)}, u32[]{:S(2)}) copy-start(s32[4,12,12]{2,1,0:T(8,128)} %copy.10.mask_ref) | copy-start | bytes 6916
  94.6 8.8 %copy-start.12 = (f32[4,128,768]{2,1,0:T(8,128)}, f32[4,128,768]{2,1,0:T(8,128)S(1)}, u32[]{:S(2)}) copy-start(f32[4,128,768]{2,1,0:T(8,128)S(1)} %get-tuple-element.25.rest_2_) | copy-start | bytes 4718596
  100.3 3.0 %copy-start.10 = (bf16[384,768]{1,0:T(8,128)(2,1)}, bf16[384,768]{1,0:T(8,128)(2,1)S(1)}, u32[]{:S(2)}) copy-start(bf16[384,768]{1,0:T(8,128)(2,1)S(1)} %collective-permute-done.9.rest_1_) | copy-start | bytes 1769476
  107.1 2.6 %collective-permute-start.15 = (f32[2,128,768]{2,1,0:T(8,128)}, f32[2,128,768]{2,1,0:T(8,128)}, u32[]{:S(2)}, u32[]{:S(2)}) collective-permute-start(f32[2,128,768]{2,1,0:T(8,128)} %dynamic-slice_bitcast_fusion), channel_id=1, source_target_pairs={{0,1},{1,0},{2,3},{3,2},{4,5},{5,4},{6,7},{7,6},{8,9},{9,8},{10,11... | collective-permute-start | bytes 2359304 | tf_op jit(solution)/shard_map/ppermute | solution.py:212
  107.1 1.3 %copy-start.3 = (f32[384,512]{1,0:T(8,128)S(1)}, f32[384,512]{1,0:T(8,128)}, u32[]{:S(2)}) copy-start(f32[384,512]{1,0:T(8,128)} %copy-done.2) | copy-start | bytes 2359300
  110.9 2.8 %copy-start.7 = (s32[4,12,12]{2,1,0:T(8,128)S(1)}, s32[4,12,12]{2,1,0:T(8,128)}, u32[]{:S(2)}) copy-start(s32[4,12,12]{2,1,0:T(8,128)} %copy.10.mask_ref) | copy-start | bytes 6916
  110.9 2.7 %copy-start.11 = (bf16[384,768]{1,0:T(8,128)(2,1)S(1)}, bf16[384,768]{1,0:T(8,128)(2,1)}, u32[]{:S(2)}) copy-start(bf16[384,768]{1,0:T(8,128)(2,1)} %copy-done.10) | copy-start | bytes 1769476
  110.9 2.7 %copy-start.13 = (f32[4,128,768]{2,1,0:T(8,128)S(1)}, f32[4,128,768]{2,1,0:T(8,128)}, u32[]{:S(2)}) copy-start(f32[4,128,768]{2,1,0:T(8,128)} %copy-done.12) | copy-start | bytes 4718596
  111.0 11.5 %collective-permute-start.16 = (f32[128,768]{1,0:T(8,128)S(1)}, f32[128,768]{1,0:T(8,128)S(1)}, u32[]{:S(2)}, u32[]{:S(2)}) collective-permute-start(f32[128,768]{1,0:T(8,128)S(1)} %dynamic-slice_bitcast_fusion.1), channel_id=1, source_target_pairs={{0,2},{1,3},{2,0},{3,1},{4,6},{5,7},{6,4},{7,5},{8,10},{9,11},{10,... | collective-permute-start | bytes 1179656 | tf_op jit(solution)/shard_map/ppermute | solution.py:212

commit v16 on v15

--- a/solution.py
+++ b/solution.py
@@ -251,10 +251,11 @@
     (gx,) = forward_and_input(*last, gx_before=gx)
     (outputs,) = forward_and_input(*last, out_before=part)
 
-    by = after(gx, gots[1]).reshape(2, 2, tokens, depth // 4)
+    by = gx.reshape(2, 2, tokens, depth // 4)
     pair = lax.dynamic_index_in_dim(by, c, 1, keepdims=False) + swap_f(
         lax.dynamic_index_in_dim(by, 1 - c, 1, keepdims=False), 1
     )
+    pair = after(pair, gots[1])
     grad_x = lax.dynamic_index_in_dim(pair, y, 0, keepdims=False) + swap_f(
         lax.dynamic_index_in_dim(pair, 1 - y, 0, keepdims=False), 2
     )

time: 124 us -> 121 us (0.976)
  waiting for transfers between devices: 71.8 us -> 69.1 us
    ppermute x15, waiting for transfers between devices: 66.4 us -> 64.3 us  [swap_dp(): return lax.ppermute(a, 'dp', [(d, d ^ bits) for d in range(dp)])]
  transfers between devices with their start and end apart: 17 -> 17, of which waited for: 12 -> 11; matrix products, arithmetic and copies ran while one was open for 4% -> 5% of each run, Pallas kernels for 14% -> 15%
where the time goes in v16:
time: 121 us; the launch traced here: 120 us
  waiting for transfers between devices  69.1 us (57%)
  starting transfers between devices  20.3 us (17%)
  Pallas kernels  17.6 us (15%)
  local copies, waits for them, and re-layouts  7.1 us (6%)
  other arithmetic  5.57 us (5%)
    ppermute x15, waiting for transfers between devices, swap_dp(): return lax.ppermute(a, 'dp', [(d, d ^ bits) for d in range(dp)])  64.3 us
    ppermute x15, starting transfers between devices, swap_dp(): return lax.ppermute(a, 'dp', [(d, d ^ bits) for d in range(dp)])  18.7 us
    pallas_call x3, Pallas kernels, forward_and_input(): pl.pallas_call(kernel, grid=(width // BS,), out_shape=[jax.ShapeDtypeStru...  11.8 us
    pallas_call x2, Pallas kernels, weight_grad_part(): pl.pallas_call(kernel, grid=(chunks,), out_shape=(jax.ShapeDtypeStruct((r...  5.75 us
    unnamed x31, local copies, waits for them, and re-layouts  4.99 us
    ppermute x2, waiting for transfers between devices, swap_f(): return lax.ppermute(a, 'fsdp', [(d, d ^ bit) for d in range(fsdp)])  4.8 us
  transfers between devices with their start and end apart: 17, of which 11 were waited for; matrix products, arithmetic and copies ran while one was open for 5% of the time, Pallas kernels for 15%

profile of v16, /device:TPU:0, one launch (start us, length us, event | category | flops | bytes accessed | tf_op | source)
XLA Modules:
  0.0 120.4 jit_solution(4222583034591776171)
XLA Ops:
  0.6 0.0 copy-start
  0.6 3.1 %collective-permute-start.4 = (bf16[4,128,768]{2,1,0:T(8,128)(2,1)}, bf16[4,128,768]{2,1,0:T(8,128)(2,1)S(1)}, u32[]{:S(2)}, u32[]{:S(2)}) collective-permute-start(bf16[4,128,768]{2,1,0:T(8,128)(2,1)} %og_ref.5), channel_id=1, source_target_pairs={{0,8},{4,12},{8,0},{12,4},{16,24},{20,28},{24,16},{28,20},{1,9},{5... | collective-permute-start | bytes 2359304 | tf_op jit(solution)/shard_map/ppermute | solution.py:203
  3.7 1.5 %collective-permute-start.5 = (bf16[4,128,768]{2,1,0:T(8,128)(2,1)}, bf16[4,128,768]{2,1,0:T(8,128)(2,1)}, u32[]{:S(2)}, u32[]{:S(2)}) collective-permute-start(bf16[4,128,768]{2,1,0:T(8,128)(2,1)} %og_ref.5), channel_id=1, source_target_pairs={{0,4},{4,0},{8,12},{12,8},{16,20},{20,16},{24,28},{28,24},{1,5},{5... | collective-permute-start | bytes 2359304 | tf_op jit(solution)/shard_map/ppermute | solution.py:203
  5.2 1.0 dynamic-slice_bitcast_fusion.3
  6.3 0.0 copy-start.1
  6.3 0.5 collective-permute-start.1
  6.8 0.0 copy-done
  6.9 0.2 collective-permute-start.2
  7.1 15.2 %collective-permute-done.4.refs_5_ = bf16[4,128,768]{2,1,0:T(8,128)(2,1)S(1)} collective-permute-done((bf16[4,128,768]{2,1,0:T(8,128)(2,1)}, bf16[4,128,768]{2,1,0:T(8,128)(2,1)S(1)}, u32[]{:S(2)}, u32[]{:S(2)}) %collective-permute-start.4) | collective-permute-done | bytes 786464 | tf_op jit(solution)/shard_map/ppermute | solution.py:203
  22.3 2.2 %collective-permute-done.5.refs_6_ = bf16[4,128,768]{2,1,0:T(8,128)(2,1)} collective-permute-done((bf16[4,128,768]{2,1,0:T(8,128)(2,1)}, bf16[4,128,768]{2,1,0:T(8,128)(2,1)}, u32[]{:S(2)}, u32[]{:S(2)}) %collective-permute-start.5) | collective-permute-done | bytes 786464 | tf_op jit(solution)/shard_map/ppermute | solution.py:203
  24.5 1.5 %collective-permute-start.6 = (bf16[4,128,768]{2,1,0:T(8,128)(2,1)S(1)}, bf16[4,128,768]{2,1,0:T(8,128)(2,1)}, u32[]{:S(2)}, u32[]{:S(2)}) collective-permute-start(bf16[4,128,768]{2,1,0:T(8,128)(2,1)S(1)} %collective-permute-done.4.refs_5_), channel_id=1, source_target_pairs={{0,4},{4,0},{8,12},{12,8},{16,20},{20,16},{24,28},{28,24},{1,5},{5... | collective-permute-start | bytes 2359304 | tf_op jit(solution)/shard_map/ppermute | solution.py:203
  26.0 2.6 %collective-permute-start = (bf16[384,768]{1,0:T(8,128)(2,1)}, bf16[384,768]{1,0:T(8,128)(2,1)}, u32[]{:S(2)}, u32[]{:S(2)}) collective-permute-start(bf16[384,768]{1,0:T(8,128)(2,1)} %rest_0_.1), channel_id=1, source_target_pairs={{0,16},{4,20},{8,24},{12,28},{16,0},{20,4},{24,8},{28,12},{1,17},{... | collective-permute-start | bytes 1769480 | tf_op jit(solution)/shard_map/ppermute | solution.py:203
  28.6 0.0 collective-permute-done.2.refs_2_
  28.6 6.8 %collective-permute-done.1.refs_1_ = bf16[2,128,768]{2,1,0:T(8,128)(2,1)S(1)} collective-permute-done((bf16[2,128,768]{2,1,0:T(8,128)(2,1)S(1)}, bf16[2,128,768]{2,1,0:T(8,128)(2,1)S(1)}, u32[]{:S(2)}, u32[]{:S(2)}) %collective-permute-start.1) | collective-permute-done | bytes 393248 | tf_op jit(solution)/shard_map/ppermute | solution.py:203
  35.6 2.7 %collective-permute-start.3 = (bf16[128,768]{1,0:T(8,128)(2,1)S(1)}, bf16[128,768]{1,0:T(8,128)(2,1)S(1)}, u32[]{:S(2)}, u32[]{:S(2)}) collective-permute-start(bf16[128,768]{1,0:T(8,128)(2,1)S(1)} %pad_maximum_fusion.3), channel_id=1, source_target_pairs={{0,4},{4,0},{8,12},{12,8},{16,20},{20,16},{24,28},{28,24},{1,5},{5... | collective-permute-start | bytes 589832 | tf_op jit(solution)/shard_map/ppermute | solution.py:203
  38.2 0.0 collective-permute-start.10
  38.2 0.2 collective-permute-start.11
  38.4 0.0 copy-done.14
  38.4 0.6 copy.10.mask_ref
  39.0 0.1 pad_add_fusion.where_ref
  39.1 10.6 %collective-permute-done.3.refs_3_ = bf16[128,768]{1,0:T(8,128)(2,1)S(1)} collective-permute-done((bf16[128,768]{1,0:T(8,128)(2,1)S(1)}, bf16[128,768]{1,0:T(8,128)(2,1)S(1)}, u32[]{:S(2)}, u32[]{:S(2)}) %collective-permute-start.3) | collective-permute-done | bytes 196640 | tf_op jit(solution)/shard_map/ppermute | solution.py:203
  49.7 0.0 collective-permute-done.6.refs_7_
  49.7 0.0 copy-done.1
  49.7 0.8 copy-done.4
  50.5 2.2 %weight_grad_part.2 = (f32[384,256]{1,0:T(8,128)S(1)}, f32[384,256]{1,0:T(8,128)S(1)}) custom-call(s32[4]{0:T(128)S(1)} %pad_add_fusion.where_ref, s32[4,12,12]{2,1,0:T(8,128)S(1)} %copy-done.4, bf16[128,3072]{1,0:T(8,128)(2,1)S(1)} %copy-done, bf16[2,128,768]{2,1,0:T(8,128)(2,1)S(1)} %collective-permute-done.1.refs_1_, ...), custom_call_target="tpu_custom_call" | custom-call | flops 805306368 | bytes 786432 | tf_op jit(solution)/shard_map/weight_grad_part/pallas_call | solution.py:84
  52.6 2.7 %collective-permute-start.12 = (f32[384,256]{1,0:T(8,128)S(1)}, f32[384,256]{1,0:T(8,128)}, u32[]{:S(2)}, u32[]{:S(2)}) collective-permute-start(f32[384,256]{1,0:T(8,128)S(1)} %get-tuple-element.23), channel_id=1, source_target_pairs={{0,16},{4,20},{8,24},{12,28},{16,0},{20,4},{24,8},{28,12},{1,17},{... | collective-permute-start | bytes 1179656 | tf_op jit(solution)/shard_map/ppermute | solution.py:203
  55.3 0.0 collective-permute-done.rest_2_
  55.3 1.5 %collective-permute-start.8 = (bf16[384,768]{1,0:T(8,128)(2,1)}, bf16[384,768]{1,0:T(8,128)(2,1)}, u32[]{:S(2)}, u32[]{:S(2)}) collective-permute-start(bf16[384,768]{1,0:T(8,128)(2,1)} %collective-permute-done.rest_2_), channel_id=1, source_target_pairs={{0,4},{4,0},{8,12},{12,8},{16,20},{20,16},{24,28},{28,24},{1,5},{5... | collective-permute-start | bytes 1769480 | tf_op jit(solution)/shard_map/ppermute | solution.py:203
  56.8 0.4 collective-permute-start.7
  57.3 3.6 %weight_grad_part.3 = (f32[384,512]{1,0:T(8,128)S(1)}, f32[384,512]{1,0:T(8,128)S(1)}) custom-call(s32[4]{0:T(128)S(1)} %pad_add_fusion.where_ref, s32[4,12,12]{2,1,0:T(8,128)S(1)} %copy-done.4, bf16[128,3072]{1,0:T(8,128)(2,1)S(1)} %copy-done, bf16[2,128,768]{2,1,0:T(8,128)(2,1)S(1)} %collective-permute-done.1.refs_1_, ...), custom_call_target="tpu_custom_call" | custom-call | flops 1610612736 | bytes 1572864 | tf_op jit(solution)/shard_map/weight_grad_part/pallas_call | solution.py:84
  60.8 0.0 copy-start.2
  60.8 0.9 copy-done.2
  61.7 0.9 copy-done.8
  62.6 4.2 %collective-permute-done.10.rest_1_ = bf16[384,768]{1,0:T(8,128)(2,1)} collective-permute-done((bf16[384,768]{1,0:T(8,128)(2,1)}, bf16[384,768]{1,0:T(8,128)(2,1)}, u32[]{:S(2)}, u32[]{:S(2)}) %collective-permute-start.10) | collective-permute-done | bytes 589856 | tf_op jit(solution)/shard_map/ppermute | solution.py:203
  66.8 0.0 collective-permute-done.11.rest_3_
  66.8 3.8 %collective-permute-done.12 = f32[384,256]{1,0:T(8,128)} collective-permute-done((f32[384,256]{1,0:T(8,128)S(1)}, f32[384,256]{1,0:T(8,128)}, u32[]{:S(2)}, u32[]{:S(2)}) %collective-permute-start.12) | collective-permute-done | bytes 393248 | tf_op jit(solution)/shard_map/ppermute | solution.py:203
  70.6 1.5 %collective-permute-start.13 = (bf16[384,768]{1,0:T(8,128)(2,1)}, bf16[384,768]{1,0:T(8,128)(2,1)S(1)}, u32[]{:S(2)}, u32[]{:S(2)}) collective-permute-start(bf16[384,768]{1,0:T(8,128)(2,1)} %collective-permute-done.10.rest_1_), channel_id=1, source_target_pairs={{0,4},{4,0},{8,12},{12,8},{16,20},{20,16},{24,28},{28,24},{1,5},{5... | collective-permute-start | bytes 1769480 | tf_op jit(solution)/shard_map/ppermute | solution.py:203
  72.1 0.0 collective-permute-start.14
  72.1 3.0 %collective-permute-done.8.rest_5_ = bf16[384,768]{1,0:T(8,128)(2,1)} collective-permute-done((bf16[384,768]{1,0:T(8,128)(2,1)}, bf16[384,768]{1,0:T(8,128)(2,1)}, u32[]{:S(2)}, u32[]{:S(2)}) %collective-permute-start.8) | collective-permute-done | bytes 589856 | tf_op jit(solution)/shard_map/ppermute | solution.py:203
  75.1 12.0 %collective-permute-done.7.rest_0_ = bf16[384,768]{1,0:T(8,128)(2,1)} collective-permute-done((bf16[384,768]{1,0:T(8,128)(2,1)}, bf16[384,768]{1,0:T(8,128)(2,1)}, u32[]{:S(2)}, u32[]{:S(2)}) %collective-permute-start.7) | collective-permute-done | bytes 589856 | tf_op jit(solution)/shard_map/ppermute | solution.py:203
  87.0 0.4 collective-permute-start.9
  87.4 0.0 collective-permute-done.13.rest_4_
  87.4 0.8 copy-done.5
  88.2 1.1 copy-done.9
  89.2 5.3 %forward_and_input.3 = (f32[4,128,768]{2,1,0:T(8,128)S(1)}, f32[4,128,768]{2,1,0:T(8,128)S(1)}) custom-call(s32[4]{0:T(128)S(1)} %pad_add_fusion.where_ref, s32[4,12,12]{2,1,0:T(8,128)S(1)} %copy-done.5, bf16[128,3072]{1,0:T(8,128)(2,1)S(1)} %copy-done, bf16[4,128,768]{2,1,0:T(8,128)(2,1)S(1)} %copy-done.1, bf16[384,768]{1,0:T(8,128)(2,1)S(1)} %copy-done.9, ...), custom_call_target="tpu_custom_call" | custom-call | flops 8153726976 | bytes 7077888 | tf_op jit(solution)/shard_map/forward_and_input/pallas_call | solution.py:165
  94.6 0.0 copy-start.12
  94.6 5.8 %collective-permute-done.9.rest_1_ = bf16[384,768]{1,0:T(8,128)(2,1)S(1)} collective-permute-done((bf16[384,768]{1,0:T(8,128)(2,1)}, bf16[384,768]{1,0:T(8,128)(2,1)S(1)}, u32[]{:S(2)}, u32[]{:S(2)}) %collective-permute-start.9) | collective-permute-done | bytes 589856 | tf_op jit(solution)/shard_map/ppermute | solution.py:203
  100.4 3.0 %forward_and_input.5 = f32[4,128,768]{2,1,0:T(8,128)S(1)} custom-call(s32[4]{0:T(128)S(1)} %pad_add_fusion.where_ref, s32[4,12,12]{2,1,0:T(8,128)S(1)} %copy-done.6, bf16[128,3072]{1,0:T(8,128)(2,1)S(1)} %copy-done, bf16[4,128,768]{2,1,0:T(8,128)(2,1)S(1)} %copy-done.1, bf16[384,768]{1,0:T(8,128)(2,1)} %collective-permute-done.7.rest_0_, ...), custom_call_target="tpu_custom_call" | custom-call | flops 2717908992 | bytes 2359296 | tf_op jit(solution)/shard_map/forward_and_input/pallas_call | solution.py:165
  103.3 0.9 dynamic-slice_bitcast_fusion
  104.3 0.0 collective-permute-start.15
  104.3 1.1 add.68
  105.4 0.7 collective-permute-done.14
  106.1 0.0 copy-done.3
  106.1 1.3 %add.69 = f32[384,512]{1,0:T(8,128)S(1)} add(f32[384,512]{1,0:T(8,128)S(1)} %copy-done.3, f32[384,512]{1,0:T(8,128)} %collective-permute-done.14) | non-fusion elementwise | flops 196608 | bytes 2359296 | tf_op jit(solution)/shard_map/add | solution.py:240
  107.4 0.0 collective-permute-done.15
  107.4 1.2 %bitcast_add_fusion = f32[2,128,768]{2,1,0:T(8,128)S(1)} fusion(f32[2,128,768]{2,1,0:T(8,128)} %collective-permute-done.15, f32[2,2,128,768]{3,2,1,0:T(8,128)S(1)} %bitcast.24, s32[]{:T(128)S(6)} %select_n.56), kind=kLoop, calls=%fused_computation.1 | loop fusion | flops 196608 | bytes 2359300 | tf_op jit(solution)/shard_map/add | solution.py:255
  108.6 0.0 copy-start.7
  108.7 0.0 copy-start.11
  108.7 0.0 copy-start.13
  108.7 1.6 %collective-permute-start.16 = (f32[128,768]{1,0:T(8,128)S(1)}, f32[128,768]{1,0:T(8,128)S(1)}, u32[]{:S(2)}, u32[]{:S(2)}) collective-permute-start(f32[128,768]{1,0:T(8,128)S(1)} %dynamic-slice_bitcast_fusion.1), channel_id=1, source_target_pairs={{0,2},{1,3},{2,0},{3,1},{4,6},{5,7},{6,4},{7,5},{8,10},{9,11},{10,... | collective-permute-start | bytes 1179656 | tf_op jit(solution)/shard_map/ppermute | solution.py:212
  110.3 1.1 pad_maximum_fusion
  111.4 3.5 %forward_and_input.4 = bf16[4,128,768]{2,1,0:T(8,128)(2,1)} custom-call(s32[4]{0:T(128)S(1)} %pad_add_fusion.where_ref, s32[4,12,12]{2,1,0:T(8,128)S(1)} %copy-done.7, bf16[128,3072]{1,0:T(8,128)(2,1)S(1)} %copy-done, bf16[4,128,768]{2,1,0:T(8,128)(2,1)S(1)} %copy-done.1, bf16[384,768]{1,0:T(8,128)(2,1)} %collective-permute-done.7.rest_0_, ...), custom_call_target="tpu_custom_call" | custom-call | flops 2717908992 | bytes 2359296 | tf_op jit(solution)/shard_map/forward_and_input/pallas_call | solution.py:165
  114.9 4.8 %collective-permute-done.16 = f32[128,768]{1,0:T(8,128)S(1)} collective-permute-done((f32[128,768]{1,0:T(8,128)S(1)}, f32[128,768]{1,0:T(8,128)S(1)}, u32[]{:S(2)}, u32[]{:S(2)}) %collective-permute-start.16) | collective-permute-done | bytes 393248 | tf_op jit(solution)/shard_map/ppermute | solution.py:212
  119.7 0.7 fusion
  (21 shorter events, 0.2 us)
Async XLA Ops:
  0.6 6.2 %copy-start = (bf16[128,3072]{1,0:T(8,128)(2,1)S(1)}, bf16[128,3072]{1,0:T(8,128)(2,1)}, u32[]{:S(2)}) copy-start(bf16[128,3072]{1,0:T(8,128)(2,1)} %acts_ref.5) | copy-start | bytes 2359300
  0.6 21.7 %collective-permute-start.4 = (bf16[4,128,768]{2,1,0:T(8,128)(2,1)}, bf16[4,128,768]{2,1,0:T(8,128)(2,1)S(1)}, u32[]{:S(2)}, u32[]{:S(2)}) collective-permute-start(bf16[4,128,768]{2,1,0:T(8,128)(2,1)} %og_ref.5), channel_id=1, source_target_pairs={{0,8},{4,12},{8,0},{12,4},{16,24},{20,28},{24,16},{28,20},{1,9},{5... | collective-permute-start | bytes 2359304 | tf_op jit(solution)/shard_map/ppermute | solution.py:203
  3.7 20.8 %collective-permute-start.5 = (bf16[4,128,768]{2,1,0:T(8,128)(2,1)}, bf16[4,128,768]{2,1,0:T(8,128)(2,1)}, u32[]{:S(2)}, u32[]{:S(2)}) collective-permute-start(bf16[4,128,768]{2,1,0:T(8,128)(2,1)} %og_ref.5), channel_id=1, source_target_pairs={{0,4},{4,0},{8,12},{12,8},{16,20},{20,16},{24,28},{28,24},{1,5},{5... | collective-permute-start | bytes 2359304 | tf_op jit(solution)/shard_map/ppermute | solution.py:203
  6.3 43.4 %copy-start.1 = (bf16[4,128,768]{2,1,0:T(8,128)(2,1)S(1)}, bf16[4,128,768]{2,1,0:T(8,128)(2,1)}, u32[]{:S(2)}) copy-start(bf16[4,128,768]{2,1,0:T(8,128)(2,1)} %og_ref.5) | copy-start | bytes 2359300
  6.3 29.1 %collective-permute-start.1 = (bf16[2,128,768]{2,1,0:T(8,128)(2,1)S(1)}, bf16[2,128,768]{2,1,0:T(8,128)(2,1)S(1)}, u32[]{:S(2)}, u32[]{:S(2)}) collective-permute-start(bf16[2,128,768]{2,1,0:T(8,128)(2,1)S(1)} %pad_maximum_fusion.1), channel_id=1, source_target_pairs={{0,8},{4,12},{8,0},{12,4},{16,24},{20,28},{24,16},{28,20},{1,9},{5... | collective-permute-start | bytes 1179656 | tf_op jit(solution)/shard_map/ppermute | solution.py:203
  6.9 21.7 %collective-permute-start.2 = (bf16[128,768]{1,0:T(8,128)(2,1)S(1)}, bf16[128,768]{1,0:T(8,128)(2,1)S(1)}, u32[]{:S(2)}, u32[]{:S(2)}) collective-permute-start(bf16[128,768]{1,0:T(8,128)(2,1)S(1)} %pad_maximum_fusion.2), channel_id=1, source_target_pairs={{0,4},{4,0},{8,12},{12,8},{16,20},{20,16},{24,28},{28,24},{1,5},{5... | collective-permute-start | bytes 589832 | tf_op jit(solution)/shard_map/ppermute | solution.py:203
  24.5 25.2 %collective-permute-start.6 = (bf16[4,128,768]{2,1,0:T(8,128)(2,1)S(1)}, bf16[4,128,768]{2,1,0:T(8,128)(2,1)}, u32[]{:S(2)}, u32[]{:S(2)}) collective-permute-start(bf16[4,128,768]{2,1,0:T(8,128)(2,1)S(1)} %collective-permute-done.4.refs_5_), channel_id=1, source_target_pairs={{0,4},{4,0},{8,12},{12,8},{16,20},{20,16},{24,28},{28,24},{1,5},{5... | collective-permute-start | bytes 2359304 | tf_op jit(solution)/shard_map/ppermute | solution.py:203
  26.0 29.3 %collective-permute-start = (bf16[384,768]{1,0:T(8,128)(2,1)}, bf16[384,768]{1,0:T(8,128)(2,1)}, u32[]{:S(2)}, u32[]{:S(2)}) collective-permute-start(bf16[384,768]{1,0:T(8,128)(2,1)} %rest_0_.1), channel_id=1, source_target_pairs={{0,16},{4,20},{8,24},{12,28},{16,0},{20,4},{24,8},{28,12},{1,17},{... | collective-permute-start | bytes 1769480 | tf_op jit(solution)/shard_map/ppermute | solution.py:203
  35.5 2.9 %copy-start.14 = (s32[4,12,12]{2,0,1:T(4,128)S(1)}, s32[4,12,12]{2,0,1:T(4,128)}, u32[]{:S(2)}) copy-start(s32[4,12,12]{2,0,1:T(4,128)} %param.6) | copy-start | bytes 6916
  35.6 14.1 %collective-permute-start.3 = (bf16[128,768]{1,0:T(8,128)(2,1)S(1)}, bf16[128,768]{1,0:T(8,128)(2,1)S(1)}, u32[]{:S(2)}, u32[]{:S(2)}) collective-permute-start(bf16[128,768]{1,0:T(8,128)(2,1)S(1)} %pad_maximum_fusion.3), channel_id=1, source_target_pairs={{0,4},{4,0},{8,12},{12,8},{16,20},{20,16},{24,28},{28,24},{1,5},{5... | collective-permute-start | bytes 589832 | tf_op jit(solution)/shard_map/ppermute | solution.py:203
  38.2 28.6 %collective-permute-start.10 = (bf16[384,768]{1,0:T(8,128)(2,1)}, bf16[384,768]{1,0:T(8,128)(2,1)}, u32[]{:S(2)}, u32[]{:S(2)}) collective-permute-start(bf16[384,768]{1,0:T(8,128)(2,1)} %rest_0_.1), channel_id=1, source_target_pairs={{0,8},{4,12},{8,0},{12,4},{16,24},{20,28},{24,16},{28,20},{1,9},{5... | collective-permute-start | bytes 1769480 | tf_op jit(solution)/shard_map/ppermute | solution.py:203
  38.2 28.6 %collective-permute-start.11 = (bf16[384,768]{1,0:T(8,128)(2,1)}, bf16[384,768]{1,0:T(8,128)(2,1)}, u32[]{:S(2)}, u32[]{:S(2)}) collective-permute-start(bf16[384,768]{1,0:T(8,128)(2,1)} %rest_0_.1), channel_id=1, source_target_pairs={{0,4},{4,0},{8,12},{12,8},{16,20},{20,16},{24,28},{28,24},{1,5},{5... | collective-permute-start | bytes 1769480 | tf_op jit(solution)/shard_map/ppermute | solution.py:203
  49.7 0.8 copy-start.4
  52.6 18.0 %collective-permute-start.12 = (f32[384,256]{1,0:T(8,128)S(1)}, f32[384,256]{1,0:T(8,128)}, u32[]{:S(2)}, u32[]{:S(2)}) collective-permute-start(f32[384,256]{1,0:T(8,128)S(1)} %get-tuple-element.23), channel_id=1, source_target_pairs={{0,16},{4,20},{8,24},{12,28},{16,0},{20,4},{24,8},{28,12},{1,17},{... | collective-permute-start | bytes 1179656 | tf_op jit(solution)/shard_map/ppermute | solution.py:203
  55.3 19.8 %collective-permute-start.8 = (bf16[384,768]{1,0:T(8,128)(2,1)}, bf16[384,768]{1,0:T(8,128)(2,1)}, u32[]{:S(2)}, u32[]{:S(2)}) collective-permute-start(bf16[384,768]{1,0:T(8,128)(2,1)} %collective-permute-done.rest_2_), channel_id=1, source_target_pairs={{0,4},{4,0},{8,12},{12,8},{16,20},{20,16},{24,28},{28,24},{1,5},{5... | collective-permute-start | bytes 1769480 | tf_op jit(solution)/shard_map/ppermute | solution.py:203
  56.8 30.2 %collective-permute-start.7 = (bf16[384,768]{1,0:T(8,128)(2,1)}, bf16[384,768]{1,0:T(8,128)(2,1)}, u32[]{:S(2)}, u32[]{:S(2)}) collective-permute-start(bf16[384,768]{1,0:T(8,128)(2,1)} %collective-permute-done.rest_2_), channel_id=1, source_target_pairs={{0,8},{4,12},{8,0},{12,4},{16,24},{20,28},{24,16},{28,20},{1,9},{5... | collective-permute-start | bytes 1769480 | tf_op jit(solution)/shard_map/ppermute | solution.py:203
  60.8 0.9 copy-start.2
  61.7 0.9 copy-start.8
  70.6 16.8 %collective-permute-start.13 = (bf16[384,768]{1,0:T(8,128)(2,1)}, bf16[384,768]{1,0:T(8,128)(2,1)S(1)}, u32[]{:S(2)}, u32[]{:S(2)}) collective-permute-start(bf16[384,768]{1,0:T(8,128)(2,1)} %collective-permute-done.10.rest_1_), channel_id=1, source_target_pairs={{0,4},{4,0},{8,12},{12,8},{16,20},{20,16},{24,28},{28,24},{1,5},{5... | collective-permute-start | bytes 1769480 | tf_op jit(solution)/shard_map/ppermute | solution.py:203
  72.1 34.0 %collective-permute-start.14 = (f32[384,512]{1,0:T(8,128)}, f32[384,512]{1,0:T(8,128)}, u32[]{:S(2)}, u32[]{:S(2)}) collective-permute-start(f32[384,512]{1,0:T(8,128)} %copy-done.8), channel_id=1, source_target_pairs={{0,16},{4,20},{8,24},{12,28},{16,0},{20,4},{24,8},{28,12},{1,17},{... | collective-permute-start | bytes 2359304 | tf_op jit(solution)/shard_map/ppermute | solution.py:203
  87.0 13.3 %collective-permute-start.9 = (bf16[384,768]{1,0:T(8,128)(2,1)}, bf16[384,768]{1,0:T(8,128)(2,1)S(1)}, u32[]{:S(2)}, u32[]{:S(2)}) collective-permute-start(bf16[384,768]{1,0:T(8,128)(2,1)} %collective-permute-done.7.rest_0_), channel_id=1, source_target_pairs={{0,4},{4,0},{8,12},{12,8},{16,20},{20,16},{24,28},{28,24},{1,5},{5... | collective-permute-start | bytes 1769480 | tf_op jit(solution)/shard_map/ppermute | solution.py:203
  87.4 0.8 copy-start.5
  88.2 1.1 copy-start.9
  89.2 11.1 %copy-start.6 = (s32[4,12,12]{2,1,0:T(8,128)S(1)}, s32[4,12,12]{2,1,0:T(8,128)}, u32[]{:S(2)}) copy-start(s32[4,12,12]{2,1,0:T(8,128)} %copy.10.mask_ref) | copy-start | bytes 6916
  94.6 8.8 %copy-start.12 = (f32[4,128,768]{2,1,0:T(8,128)}, f32[4,128,768]{2,1,0:T(8,128)S(1)}, u32[]{:S(2)}) copy-start(f32[4,128,768]{2,1,0:T(8,128)S(1)} %get-tuple-element.25.rest_2_) | copy-start | bytes 4718596
  100.3 3.0 %copy-start.10 = (bf16[384,768]{1,0:T(8,128)(2,1)}, bf16[384,768]{1,0:T(8,128)(2,1)S(1)}, u32[]{:S(2)}) copy-start(bf16[384,768]{1,0:T(8,128)(2,1)S(1)} %collective-permute-done.9.rest_1_) | copy-start | bytes 1769476
  104.3 3.1 %collective-permute-start.15 = (f32[2,128,768]{2,1,0:T(8,128)}, f32[2,128,768]{2,1,0:T(8,128)}, u32[]{:S(2)}, u32[]{:S(2)}) collective-permute-start(f32[2,128,768]{2,1,0:T(8,128)} %dynamic-slice_bitcast_fusion), channel_id=1, source_target_pairs={{0,1},{1,0},{2,3},{3,2},{4,5},{5,4},{6,7},{7,6},{8,9},{9,8},{10,11... | collective-permute-start | bytes 2359304 | tf_op jit(solution)/shard_map/ppermute | solution.py:212
  104.3 1.9 %copy-start.3 = (f32[384,512]{1,0:T(8,128)S(1)}, f32[384,512]{1,0:T(8,128)}, u32[]{:S(2)}) copy-start(f32[384,512]{1,0:T(8,128)} %copy-done.2) | copy-start | bytes 2359300
  108.6 2.8 %copy-start.7 = (s32[4,12,12]{2,1,0:T(8,128)S(1)}, s32[4,12,12]{2,1,0:T(8,128)}, u32[]{:S(2)}) copy-start(s32[4,12,12]{2,1,0:T(8,128)} %copy.10.mask_ref) | copy-start | bytes 6916
  108.7 2.7 %copy-start.11 = (bf16[384,768]{1,0:T(8,128)(2,1)S(1)}, bf16[384,768]{1,0:T(8,128)(2,1)}, u32[]{:S(2)}) copy-start(bf16[384,768]{1,0:T(8,128)(2,1)} %copy-done.10) | copy-start | bytes 1769476
  108.7 2.7 %copy-start.13 = (f32[4,128,768]{2,1,0:T(8,128)S(1)}, f32[4,128,768]{2,1,0:T(8,128)}, u32[]{:S(2)}) copy-start(f32[4,128,768]{2,1,0:T(8,128)} %copy-done.12) | copy-start | bytes 4718596
  108.7 11.0 %collective-permute-start.16 = (f32[128,768]{1,0:T(8,128)S(1)}, f32[128,768]{1,0:T(8,128)S(1)}, u32[]{:S(2)}, u32[]{:S(2)}) collective-permute-start(f32[128,768]{1,0:T(8,128)S(1)} %dynamic-slice_bitcast_fusion.1), channel_id=1, source_target_pairs={{0,2},{1,3},{2,0},{3,1},{4,6},{5,7},{6,4},{7,5},{8,10},{9,11},{10,... | collective-permute-start | bytes 1179656 | tf_op jit(solution)/shard_map/ppermute | solution.py:212

commit v17 on v16

--- a/solution.py
+++ b/solution.py
@@ -10,8 +10,8 @@
 LANES = 128
 F32 = jnp.float32
 BF16 = jnp.bfloat16
-PART_VMEM = 16 * 1024 * 1024
-FORWARD_VMEM = 28 * 1024 * 1024
+PART_VMEM = 48 * 1024 * 1024
+FORWARD_VMEM = 48 * 1024 * 1024
 
 
 def plain(acts, weight, block_mask, out_grad):

time: 121 us -> 123 us (1.017)
  local copies, waits for them, and re-layouts: 7.1 us -> 8.83 us
  waiting for transfers between devices: 69.1 us -> 67.7 us
    ppermute x15, waiting for transfers between devices: 64.3 us -> 62.3 us  [swap_dp(): return lax.ppermute(a, 'dp', [(d, d ^ bits) for d in range(dp)])]
    unnamed x31 -> x33, local copies, waits for them, and re-layouts: 4.99 us -> 6.73 us
    pallas_call x3, Pallas kernels: 11.8 us -> 13.1 us  [forward_and_input(): pl.pallas_call(kernel, grid=(width // BS,), out_shape=[jax.ShapeDtypeStru...]
where the time goes in v17:
time: 123 us; the launch traced here: 122 us
  waiting for transfers between devices  67.7 us (55%)
  starting transfers between devices  20.3 us (17%)
  Pallas kernels  18.8 us (15%)
  local copies, waits for them, and re-layouts  8.83 us (7%)
  other arithmetic  5.57 us (5%)
    ppermute x15, waiting for transfers between devices, swap_dp(): return lax.ppermute(a, 'dp', [(d, d ^ bits) for d in range(dp)])  62.3 us
    ppermute x15, starting transfers between devices, swap_dp(): return lax.ppermute(a, 'dp', [(d, d ^ bits) for d in range(dp)])  18.7 us
    pallas_call x3, Pallas kernels, forward_and_input(): pl.pallas_call(kernel, grid=(width // BS,), out_shape=[jax.ShapeDtypeStru...  13.1 us
    unnamed x33, local copies, waits for them, and re-layouts  6.73 us
    pallas_call x2, Pallas kernels, weight_grad_part(): pl.pallas_call(kernel, grid=(chunks,), out_shape=(jax.ShapeDtypeStruct((r...  5.75 us
    ppermute x2, waiting for transfers between devices, swap_f(): return lax.ppermute(a, 'fsdp', [(d, d ^ bit) for d in range(fsdp)])  5.42 us
  transfers between devices with their start and end apart: 17, of which 11 were waited for; matrix products, arithmetic and copies ran while one was open for 5% of the time, Pallas kernels for 15%

profile of v17, /device:TPU:0, one launch (start us, length us, event | category | flops | bytes accessed | tf_op | source)
XLA Modules:
  0.0 122.0 jit_solution(11697849940270325136)
XLA Ops:
  0.6 0.0 copy-start
  0.6 3.1 %collective-permute-start.4 = (bf16[4,128,768]{2,1,0:T(8,128)(2,1)}, bf16[4,128,768]{2,1,0:T(8,128)(2,1)S(1)}, u32[]{:S(2)}, u32[]{:S(2)}) collective-permute-start(bf16[4,128,768]{2,1,0:T(8,128)(2,1)} %og_ref.5), channel_id=1, source_target_pairs={{0,8},{4,12},{8,0},{12,4},{16,24},{20,28},{24,16},{28,20},{1,9},{5... | collective-permute-start | bytes 2359304 | tf_op jit(solution)/shard_map/ppermute | solution.py:203
  3.7 1.5 %collective-permute-start.5 = (bf16[4,128,768]{2,1,0:T(8,128)(2,1)}, bf16[4,128,768]{2,1,0:T(8,128)(2,1)}, u32[]{:S(2)}, u32[]{:S(2)}) collective-permute-start(bf16[4,128,768]{2,1,0:T(8,128)(2,1)} %og_ref.5), channel_id=1, source_target_pairs={{0,4},{4,0},{8,12},{12,8},{16,20},{20,16},{24,28},{28,24},{1,5},{5... | collective-permute-start | bytes 2359304 | tf_op jit(solution)/shard_map/ppermute | solution.py:203
  5.2 1.0 dynamic-slice_bitcast_fusion.3
  6.3 0.0 copy-start.1
  6.3 0.5 collective-permute-start.1
  6.8 0.0 copy-done
  6.9 0.2 collective-permute-start.2
  7.1 15.2 %collective-permute-done.4.refs_5_ = bf16[4,128,768]{2,1,0:T(8,128)(2,1)S(1)} collective-permute-done((bf16[4,128,768]{2,1,0:T(8,128)(2,1)}, bf16[4,128,768]{2,1,0:T(8,128)(2,1)S(1)}, u32[]{:S(2)}, u32[]{:S(2)}) %collective-permute-start.4) | collective-permute-done | bytes 786464 | tf_op jit(solution)/shard_map/ppermute | solution.py:203
  22.3 2.2 %collective-permute-done.5.refs_6_ = bf16[4,128,768]{2,1,0:T(8,128)(2,1)} collective-permute-done((bf16[4,128,768]{2,1,0:T(8,128)(2,1)}, bf16[4,128,768]{2,1,0:T(8,128)(2,1)}, u32[]{:S(2)}, u32[]{:S(2)}) %collective-permute-start.5) | collective-permute-done | bytes 786464 | tf_op jit(solution)/shard_map/ppermute | solution.py:203
  24.5 1.5 %collective-permute-start.6 = (bf16[4,128,768]{2,1,0:T(8,128)(2,1)S(1)}, bf16[4,128,768]{2,1,0:T(8,128)(2,1)}, u32[]{:S(2)}, u32[]{:S(2)}) collective-permute-start(bf16[4,128,768]{2,1,0:T(8,128)(2,1)S(1)} %collective-permute-done.4.refs_5_), channel_id=1, source_target_pairs={{0,4},{4,0},{8,12},{12,8},{16,20},{20,16},{24,28},{28,24},{1,5},{5... | collective-permute-start | bytes 2359304 | tf_op jit(solution)/shard_map/ppermute | solution.py:203
  26.0 2.6 %collective-permute-start = (bf16[384,768]{1,0:T(8,128)(2,1)}, bf16[384,768]{1,0:T(8,128)(2,1)}, u32[]{:S(2)}, u32[]{:S(2)}) collective-permute-start(bf16[384,768]{1,0:T(8,128)(2,1)} %rest_0_.1), channel_id=1, source_target_pairs={{0,16},{4,20},{8,24},{12,28},{16,0},{20,4},{24,8},{28,12},{1,17},{... | collective-permute-start | bytes 1769480 | tf_op jit(solution)/shard_map/ppermute | solution.py:203
  28.6 0.0 collective-permute-done.2.refs_2_
  28.6 6.8 %collective-permute-done.1.refs_1_ = bf16[2,128,768]{2,1,0:T(8,128)(2,1)S(1)} collective-permute-done((bf16[2,128,768]{2,1,0:T(8,128)(2,1)S(1)}, bf16[2,128,768]{2,1,0:T(8,128)(2,1)S(1)}, u32[]{:S(2)}, u32[]{:S(2)}) %collective-permute-start.1) | collective-permute-done | bytes 393248 | tf_op jit(solution)/shard_map/ppermute | solution.py:203
  35.6 2.7 %collective-permute-start.3 = (bf16[128,768]{1,0:T(8,128)(2,1)S(1)}, bf16[128,768]{1,0:T(8,128)(2,1)S(1)}, u32[]{:S(2)}, u32[]{:S(2)}) collective-permute-start(bf16[128,768]{1,0:T(8,128)(2,1)S(1)} %pad_maximum_fusion.3), channel_id=1, source_target_pairs={{0,4},{4,0},{8,12},{12,8},{16,20},{20,16},{24,28},{28,24},{1,5},{5... | collective-permute-start | bytes 589832 | tf_op jit(solution)/shard_map/ppermute | solution.py:203
  38.2 0.0 collective-permute-start.10
  38.2 0.2 collective-permute-start.11
  38.4 0.0 copy-done.15
  38.4 0.6 copy.10.mask_ref
  39.0 0.1 pad_add_fusion.where_ref
  39.1 10.6 %collective-permute-done.3.refs_3_ = bf16[128,768]{1,0:T(8,128)(2,1)S(1)} collective-permute-done((bf16[128,768]{1,0:T(8,128)(2,1)S(1)}, bf16[128,768]{1,0:T(8,128)(2,1)S(1)}, u32[]{:S(2)}, u32[]{:S(2)}) %collective-permute-start.3) | collective-permute-done | bytes 196640 | tf_op jit(solution)/shard_map/ppermute | solution.py:203
  49.7 0.0 collective-permute-done.6.refs_7_
  49.7 0.0 copy-done.1
  49.7 0.8 copy-done.4
  50.5 2.2 %weight_grad_part.2 = (f32[384,256]{1,0:T(8,128)S(1)}, f32[384,256]{1,0:T(8,128)S(1)}) custom-call(s32[4]{0:T(128)S(1)} %pad_add_fusion.where_ref, s32[4,12,12]{2,1,0:T(8,128)S(1)} %copy-done.4, bf16[128,3072]{1,0:T(8,128)(2,1)S(1)} %copy-done, bf16[2,128,768]{2,1,0:T(8,128)(2,1)S(1)} %collective-permute-done.1.refs_1_, ...), custom_call_target="tpu_custom_call" | custom-call | flops 805306368 | bytes 786432 | tf_op jit(solution)/shard_map/weight_grad_part/pallas_call | solution.py:84
  52.6 2.7 %collective-permute-start.12 = (f32[384,256]{1,0:T(8,128)S(1)}, f32[384,256]{1,0:T(8,128)}, u32[]{:S(2)}, u32[]{:S(2)}) collective-permute-start(f32[384,256]{1,0:T(8,128)S(1)} %get-tuple-element.23), channel_id=1, source_target_pairs={{0,16},{4,20},{8,24},{12,28},{16,0},{20,4},{24,8},{28,12},{1,17},{... | collective-permute-start | bytes 1179656 | tf_op jit(solution)/shard_map/ppermute | solution.py:203
  55.3 0.0 collective-permute-done.rest_2_
  55.3 1.5 %collective-permute-start.8 = (bf16[384,768]{1,0:T(8,128)(2,1)}, bf16[384,768]{1,0:T(8,128)(2,1)}, u32[]{:S(2)}, u32[]{:S(2)}) collective-permute-start(bf16[384,768]{1,0:T(8,128)(2,1)} %collective-permute-done.rest_2_), channel_id=1, source_target_pairs={{0,4},{4,0},{8,12},{12,8},{16,20},{20,16},{24,28},{28,24},{1,5},{5... | collective-permute-start | bytes 1769480 | tf_op jit(solution)/shard_map/ppermute | solution.py:203
  56.8 0.4 collective-permute-start.7
  57.3 3.6 %weight_grad_part.3 = (f32[384,512]{1,0:T(8,128)S(1)}, f32[384,512]{1,0:T(8,128)S(1)}) custom-call(s32[4]{0:T(128)S(1)} %pad_add_fusion.where_ref, s32[4,12,12]{2,1,0:T(8,128)S(1)} %copy-done.5, bf16[128,3072]{1,0:T(8,128)(2,1)S(1)} %copy-done, bf16[2,128,768]{2,1,0:T(8,128)(2,1)S(1)} %collective-permute-done.1.refs_1_, ...), custom_call_target="tpu_custom_call" | custom-call | flops 1610612736 | bytes 1572864 | tf_op jit(solution)/shard_map/weight_grad_part/pallas_call | solution.py:84
  60.8 0.0 copy-start.2
  60.8 0.9 copy-done.2
  61.7 0.9 copy-done.9
  62.6 4.2 %collective-permute-done.10.rest_1_ = bf16[384,768]{1,0:T(8,128)(2,1)} collective-permute-done((bf16[384,768]{1,0:T(8,128)(2,1)}, bf16[384,768]{1,0:T(8,128)(2,1)}, u32[]{:S(2)}, u32[]{:S(2)}) %collective-permute-start.10) | collective-permute-done | bytes 589856 | tf_op jit(solution)/shard_map/ppermute | solution.py:203
  66.8 0.0 collective-permute-done.11.rest_3_
  66.8 3.8 %collective-permute-done.12 = f32[384,256]{1,0:T(8,128)} collective-permute-done((f32[384,256]{1,0:T(8,128)S(1)}, f32[384,256]{1,0:T(8,128)}, u32[]{:S(2)}, u32[]{:S(2)}) %collective-permute-start.12) | collective-permute-done | bytes 393248 | tf_op jit(solution)/shard_map/ppermute | solution.py:203
  70.6 1.5 %collective-permute-start.13 = (bf16[384,768]{1,0:T(8,128)(2,1)}, bf16[384,768]{1,0:T(8,128)(2,1)S(1)}, u32[]{:S(2)}, u32[]{:S(2)}) collective-permute-start(bf16[384,768]{1,0:T(8,128)(2,1)} %collective-permute-done.10.rest_1_), channel_id=1, source_target_pairs={{0,4},{4,0},{8,12},{12,8},{16,20},{20,16},{24,28},{28,24},{1,5},{5... | collective-permute-start | bytes 1769480 | tf_op jit(solution)/shard_map/ppermute | solution.py:203
  72.1 0.0 collective-permute-start.14
  72.1 3.0 %collective-permute-done.8.rest_5_ = bf16[384,768]{1,0:T(8,128)(2,1)} collective-permute-done((bf16[384,768]{1,0:T(8,128)(2,1)}, bf16[384,768]{1,0:T(8,128)(2,1)}, u32[]{:S(2)}, u32[]{:S(2)}) %collective-permute-start.8) | collective-permute-done | bytes 589856 | tf_op jit(solution)/shard_map/ppermute | solution.py:203
  75.1 12.0 %collective-permute-done.7.rest_0_ = bf16[384,768]{1,0:T(8,128)(2,1)} collective-permute-done((bf16[384,768]{1,0:T(8,128)(2,1)}, bf16[384,768]{1,0:T(8,128)(2,1)}, u32[]{:S(2)}, u32[]{:S(2)}) %collective-permute-start.7) | collective-permute-done | bytes 589856 | tf_op jit(solution)/shard_map/ppermute | solution.py:203
  87.0 0.4 collective-permute-start.9
  87.4 0.0 collective-permute-done.13.rest_4_
  87.4 0.8 copy-done.6
  88.2 1.1 copy-done.10
  89.2 6.6 %forward_and_input.3 = (f32[4,128,768]{2,1,0:T(8,128)}, f32[4,128,768]{2,1,0:T(8,128)}) custom-call(s32[4]{0:T(128)S(1)} %pad_add_fusion.where_ref, s32[4,12,12]{2,1,0:T(8,128)S(1)} %copy-done.6, bf16[128,3072]{1,0:T(8,128)(2,1)S(1)} %copy-done, bf16[4,128,768]{2,1,0:T(8,128)(2,1)S(1)} %copy-done.1, bf16[384,768]{1,0:T(8,128)(2,1)S(1)} %copy-done.10, ...), custom_call_target="tpu_custom_call" | custom-call | flops 8153726976 | bytes 7077888 | tf_op jit(solution)/shard_map/forward_and_input/pallas_call | solution.py:165
  95.9 4.5 %collective-permute-done.9.rest_1_ = bf16[384,768]{1,0:T(8,128)(2,1)S(1)} collective-permute-done((bf16[384,768]{1,0:T(8,128)(2,1)}, bf16[384,768]{1,0:T(8,128)(2,1)S(1)}, u32[]{:S(2)}, u32[]{:S(2)}) %collective-permute-start.9) | collective-permute-done | bytes 589856 | tf_op jit(solution)/shard_map/ppermute | solution.py:203
  100.3 1.6 %copy-done.13 = f32[4,128,768]{2,1,0:T(8,128)S(1)} copy-done((f32[4,128,768]{2,1,0:T(8,128)S(1)}, f32[4,128,768]{2,1,0:T(8,128)}, u32[]{:S(2)}) %copy-start.13) | copy-done | bytes 1572888
  102.0 2.9 %forward_and_input.5 = f32[4,128,768]{2,1,0:T(8,128)S(1)} custom-call(s32[4]{0:T(128)S(1)} %pad_add_fusion.where_ref, s32[4,12,12]{2,1,0:T(8,128)S(1)} %copy-done.7, bf16[128,3072]{1,0:T(8,128)(2,1)S(1)} %copy-done, bf16[4,128,768]{2,1,0:T(8,128)(2,1)S(1)} %copy-done.1, bf16[384,768]{1,0:T(8,128)(2,1)} %collective-permute-done.7.rest_0_, ...), custom_call_target="tpu_custom_call" | custom-call | flops 2717908992 | bytes 2359296 | tf_op jit(solution)/shard_map/forward_and_input/pallas_call | solution.py:165
  104.9 0.9 dynamic-slice_bitcast_fusion
  105.8 0.0 collective-permute-start.15
  105.8 1.1 add.68
  107.0 0.0 collective-permute-done.14
  107.0 0.1 copy-done.3
  107.1 1.3 %add.69 = f32[384,512]{1,0:T(8,128)S(1)} add(f32[384,512]{1,0:T(8,128)S(1)} %copy-done.3, f32[384,512]{1,0:T(8,128)} %collective-permute-done.14) | non-fusion elementwise | flops 196608 | bytes 2359296 | tf_op jit(solution)/shard_map/add | solution.py:240
  108.4 0.1 collective-permute-done.15
  108.5 1.2 bitcast_add_fusion
  109.7 0.0 copy-start.8
  109.8 1.6 %collective-permute-start.16 = (f32[128,768]{1,0:T(8,128)S(1)}, f32[128,768]{1,0:T(8,128)S(1)}, u32[]{:S(2)}, u32[]{:S(2)}) collective-permute-start(f32[128,768]{1,0:T(8,128)S(1)} %dynamic-slice_bitcast_fusion.1), channel_id=1, source_target_pairs={{0,2},{1,3},{2,0},{3,1},{4,6},{5,7},{6,4},{7,5},{8,10},{9,11},{10,... | collective-permute-start | bytes 1179656 | tf_op jit(solution)/shard_map/ppermute | solution.py:212
  111.3 1.1 pad_maximum_fusion
  112.4 0.0 copy-done.8
  112.4 0.0 copy-done.14
  112.4 3.5 %forward_and_input.4 = bf16[4,128,768]{2,1,0:T(8,128)(2,1)} custom-call(s32[4]{0:T(128)S(1)} %pad_add_fusion.where_ref, s32[4,12,12]{2,1,0:T(8,128)S(1)} %copy-done.8, bf16[128,3072]{1,0:T(8,128)(2,1)S(1)} %copy-done, bf16[4,128,768]{2,1,0:T(8,128)(2,1)S(1)} %copy-done.1, bf16[384,768]{1,0:T(8,128)(2,1)} %collective-permute-done.7.rest_0_, ...), custom_call_target="tpu_custom_call" | custom-call | flops 2717908992 | bytes 2359296 | tf_op jit(solution)/shard_map/forward_and_input/pallas_call | solution.py:165
  116.0 5.3 %collective-permute-done.16 = f32[128,768]{1,0:T(8,128)S(1)} collective-permute-done((f32[128,768]{1,0:T(8,128)S(1)}, f32[128,768]{1,0:T(8,128)S(1)}, u32[]{:S(2)}, u32[]{:S(2)}) %collective-permute-start.16) | collective-permute-done | bytes 393248 | tf_op jit(solution)/shard_map/ppermute | solution.py:212
  121.3 0.7 fusion
  (23 shorter events, 0.2 us)
Async XLA Ops:
  0.6 6.2 %copy-start = (bf16[128,3072]{1,0:T(8,128)(2,1)S(1)}, bf16[128,3072]{1,0:T(8,128)(2,1)}, u32[]{:S(2)}) copy-start(bf16[128,3072]{1,0:T(8,128)(2,1)} %acts_ref.5) | copy-start | bytes 2359300
  0.6 21.7 %collective-permute-start.4 = (bf16[4,128,768]{2,1,0:T(8,128)(2,1)}, bf16[4,128,768]{2,1,0:T(8,128)(2,1)S(1)}, u32[]{:S(2)}, u32[]{:S(2)}) collective-permute-start(bf16[4,128,768]{2,1,0:T(8,128)(2,1)} %og_ref.5), channel_id=1, source_target_pairs={{0,8},{4,12},{8,0},{12,4},{16,24},{20,28},{24,16},{28,20},{1,9},{5... | collective-permute-start | bytes 2359304 | tf_op jit(solution)/shard_map/ppermute | solution.py:203
  3.7 20.8 %collective-permute-start.5 = (bf16[4,128,768]{2,1,0:T(8,128)(2,1)}, bf16[4,128,768]{2,1,0:T(8,128)(2,1)}, u32[]{:S(2)}, u32[]{:S(2)}) collective-permute-start(bf16[4,128,768]{2,1,0:T(8,128)(2,1)} %og_ref.5), channel_id=1, source_target_pairs={{0,4},{4,0},{8,12},{12,8},{16,20},{20,16},{24,28},{28,24},{1,5},{5... | collective-permute-start | bytes 2359304 | tf_op jit(solution)/shard_map/ppermute | solution.py:203
  6.3 43.4 %copy-start.1 = (bf16[4,128,768]{2,1,0:T(8,128)(2,1)S(1)}, bf16[4,128,768]{2,1,0:T(8,128)(2,1)}, u32[]{:S(2)}) copy-start(bf16[4,128,768]{2,1,0:T(8,128)(2,1)} %og_ref.5) | copy-start | bytes 2359300
  6.3 29.1 %collective-permute-start.1 = (bf16[2,128,768]{2,1,0:T(8,128)(2,1)S(1)}, bf16[2,128,768]{2,1,0:T(8,128)(2,1)S(1)}, u32[]{:S(2)}, u32[]{:S(2)}) collective-permute-start(bf16[2,128,768]{2,1,0:T(8,128)(2,1)S(1)} %pad_maximum_fusion.1), channel_id=1, source_target_pairs={{0,8},{4,12},{8,0},{12,4},{16,24},{20,28},{24,16},{28,20},{1,9},{5... | collective-permute-start | bytes 1179656 | tf_op jit(solution)/shard_map/ppermute | solution.py:203
  6.9 21.7 %collective-permute-start.2 = (bf16[128,768]{1,0:T(8,128)(2,1)S(1)}, bf16[128,768]{1,0:T(8,128)(2,1)S(1)}, u32[]{:S(2)}, u32[]{:S(2)}) collective-permute-start(bf16[128,768]{1,0:T(8,128)(2,1)S(1)} %pad_maximum_fusion.2), channel_id=1, source_target_pairs={{0,4},{4,0},{8,12},{12,8},{16,20},{20,16},{24,28},{28,24},{1,5},{5... | collective-permute-start | bytes 589832 | tf_op jit(solution)/shard_map/ppermute | solution.py:203
  24.5 25.2 %collective-permute-start.6 = (bf16[4,128,768]{2,1,0:T(8,128)(2,1)S(1)}, bf16[4,128,768]{2,1,0:T(8,128)(2,1)}, u32[]{:S(2)}, u32[]{:S(2)}) collective-permute-start(bf16[4,128,768]{2,1,0:T(8,128)(2,1)S(1)} %collective-permute-done.4.refs_5_), channel_id=1, source_target_pairs={{0,4},{4,0},{8,12},{12,8},{16,20},{20,16},{24,28},{28,24},{1,5},{5... | collective-permute-start | bytes 2359304 | tf_op jit(solution)/shard_map/ppermute | solution.py:203
  26.0 29.3 %collective-permute-start = (bf16[384,768]{1,0:T(8,128)(2,1)}, bf16[384,768]{1,0:T(8,128)(2,1)}, u32[]{:S(2)}, u32[]{:S(2)}) collective-permute-start(bf16[384,768]{1,0:T(8,128)(2,1)} %rest_0_.1), channel_id=1, source_target_pairs={{0,16},{4,20},{8,24},{12,28},{16,0},{20,4},{24,8},{28,12},{1,17},{... | collective-permute-start | bytes 1769480 | tf_op jit(solution)/shard_map/ppermute | solution.py:203
  35.5 2.9 %copy-start.15 = (s32[4,12,12]{2,0,1:T(4,128)S(1)}, s32[4,12,12]{2,0,1:T(4,128)}, u32[]{:S(2)}) copy-start(s32[4,12,12]{2,0,1:T(4,128)} %param.6) | copy-start | bytes 6916
  35.6 14.1 %collective-permute-start.3 = (bf16[128,768]{1,0:T(8,128)(2,1)S(1)}, bf16[128,768]{1,0:T(8,128)(2,1)S(1)}, u32[]{:S(2)}, u32[]{:S(2)}) collective-permute-start(bf16[128,768]{1,0:T(8,128)(2,1)S(1)} %pad_maximum_fusion.3), channel_id=1, source_target_pairs={{0,4},{4,0},{8,12},{12,8},{16,20},{20,16},{24,28},{28,24},{1,5},{5... | collective-permute-start | bytes 589832 | tf_op jit(solution)/shard_map/ppermute | solution.py:203
  38.2 28.6 %collective-permute-start.10 = (bf16[384,768]{1,0:T(8,128)(2,1)}, bf16[384,768]{1,0:T(8,128)(2,1)}, u32[]{:S(2)}, u32[]{:S(2)}) collective-permute-start(bf16[384,768]{1,0:T(8,128)(2,1)} %rest_0_.1), channel_id=1, source_target_pairs={{0,8},{4,12},{8,0},{12,4},{16,24},{20,28},{24,16},{28,20},{1,9},{5... | collective-permute-start | bytes 1769480 | tf_op jit(solution)/shard_map/ppermute | solution.py:203
  38.2 28.6 %collective-permute-start.11 = (bf16[384,768]{1,0:T(8,128)(2,1)}, bf16[384,768]{1,0:T(8,128)(2,1)}, u32[]{:S(2)}, u32[]{:S(2)}) collective-permute-start(bf16[384,768]{1,0:T(8,128)(2,1)} %rest_0_.1), channel_id=1, source_target_pairs={{0,4},{4,0},{8,12},{12,8},{16,20},{20,16},{24,28},{28,24},{1,5},{5... | collective-permute-start | bytes 1769480 | tf_op jit(solution)/shard_map/ppermute | solution.py:203
  49.7 0.8 copy-start.4
  50.5 6.8 %copy-start.5 = (s32[4,12,12]{2,1,0:T(8,128)S(1)}, s32[4,12,12]{2,1,0:T(8,128)}, u32[]{:S(2)}) copy-start(s32[4,12,12]{2,1,0:T(8,128)} %copy.10.mask_ref) | copy-start | bytes 6916
  52.6 18.0 %collective-permute-start.12 = (f32[384,256]{1,0:T(8,128)S(1)}, f32[384,256]{1,0:T(8,128)}, u32[]{:S(2)}, u32[]{:S(2)}) collective-permute-start(f32[384,256]{1,0:T(8,128)S(1)} %get-tuple-element.23), channel_id=1, source_target_pairs={{0,16},{4,20},{8,24},{12,28},{16,0},{20,4},{24,8},{28,12},{1,17},{... | collective-permute-start | bytes 1179656 | tf_op jit(solution)/shard_map/ppermute | solution.py:203
  55.3 19.8 %collective-permute-start.8 = (bf16[384,768]{1,0:T(8,128)(2,1)}, bf16[384,768]{1,0:T(8,128)(2,1)}, u32[]{:S(2)}, u32[]{:S(2)}) collective-permute-start(bf16[384,768]{1,0:T(8,128)(2,1)} %collective-permute-done.rest_2_), channel_id=1, source_target_pairs={{0,4},{4,0},{8,12},{12,8},{16,20},{20,16},{24,28},{28,24},{1,5},{5... | collective-permute-start | bytes 1769480 | tf_op jit(solution)/shard_map/ppermute | solution.py:203
  56.8 30.2 %collective-permute-start.7 = (bf16[384,768]{1,0:T(8,128)(2,1)}, bf16[384,768]{1,0:T(8,128)(2,1)}, u32[]{:S(2)}, u32[]{:S(2)}) collective-permute-start(bf16[384,768]{1,0:T(8,128)(2,1)} %collective-permute-done.rest_2_), channel_id=1, source_target_pairs={{0,8},{4,12},{8,0},{12,4},{16,24},{20,28},{24,16},{28,20},{1,9},{5... | collective-permute-start | bytes 1769480 | tf_op jit(solution)/shard_map/ppermute | solution.py:203
  60.8 0.9 copy-start.2
  61.7 0.9 copy-start.9
  70.6 16.8 %collective-permute-start.13 = (bf16[384,768]{1,0:T(8,128)(2,1)}, bf16[384,768]{1,0:T(8,128)(2,1)S(1)}, u32[]{:S(2)}, u32[]{:S(2)}) collective-permute-start(bf16[384,768]{1,0:T(8,128)(2,1)} %collective-permute-done.10.rest_1_), channel_id=1, source_target_pairs={{0,4},{4,0},{8,12},{12,8},{16,20},{20,16},{24,28},{28,24},{1,5},{5... | collective-permute-start | bytes 1769480 | tf_op jit(solution)/shard_map/ppermute | solution.py:203
  72.1 34.9 %collective-permute-start.14 = (f32[384,512]{1,0:T(8,128)}, f32[384,512]{1,0:T(8,128)}, u32[]{:S(2)}, u32[]{:S(2)}) collective-permute-start(f32[384,512]{1,0:T(8,128)} %copy-done.9), channel_id=1, source_target_pairs={{0,16},{4,20},{8,24},{12,28},{16,0},{20,4},{24,8},{28,12},{1,17},{... | collective-permute-start | bytes 2359304 | tf_op jit(solution)/shard_map/ppermute | solution.py:203
  87.0 13.3 %collective-permute-start.9 = (bf16[384,768]{1,0:T(8,128)(2,1)}, bf16[384,768]{1,0:T(8,128)(2,1)S(1)}, u32[]{:S(2)}, u32[]{:S(2)}) collective-permute-start(bf16[384,768]{1,0:T(8,128)(2,1)} %collective-permute-done.7.rest_0_), channel_id=1, source_target_pairs={{0,4},{4,0},{8,12},{12,8},{16,20},{20,16},{24,28},{28,24},{1,5},{5... | collective-permute-start | bytes 1769480 | tf_op jit(solution)/shard_map/ppermute | solution.py:203
  87.4 0.8 copy-start.6
  88.2 1.1 copy-start.10
  89.2 11.1 %copy-start.7 = (s32[4,12,12]{2,1,0:T(8,128)S(1)}, s32[4,12,12]{2,1,0:T(8,128)}, u32[]{:S(2)}) copy-start(s32[4,12,12]{2,1,0:T(8,128)} %copy.10.mask_ref) | copy-start | bytes 6916
  100.3 4.6 %copy-start.11 = (bf16[384,768]{1,0:T(8,128)(2,1)}, bf16[384,768]{1,0:T(8,128)(2,1)S(1)}, u32[]{:S(2)}) copy-start(bf16[384,768]{1,0:T(8,128)(2,1)S(1)} %collective-permute-done.9.rest_1_) | copy-start | bytes 1769476
  100.3 1.6 %copy-start.13 = (f32[4,128,768]{2,1,0:T(8,128)S(1)}, f32[4,128,768]{2,1,0:T(8,128)}, u32[]{:S(2)}) copy-start(f32[4,128,768]{2,1,0:T(8,128)} %get-tuple-element.27.rest_2_) | copy-start | bytes 4718596
  105.8 2.6 %collective-permute-start.15 = (f32[2,128,768]{2,1,0:T(8,128)}, f32[2,128,768]{2,1,0:T(8,128)}, u32[]{:S(2)}, u32[]{:S(2)}) collective-permute-start(f32[2,128,768]{2,1,0:T(8,128)} %dynamic-slice_bitcast_fusion), channel_id=1, source_target_pairs={{0,1},{1,0},{2,3},{3,2},{4,5},{5,4},{6,7},{7,6},{8,9},{9,8},{10,11... | collective-permute-start | bytes 2359304 | tf_op jit(solution)/shard_map/ppermute | solution.py:212
  105.8 1.3 %copy-start.3 = (f32[384,512]{1,0:T(8,128)S(1)}, f32[384,512]{1,0:T(8,128)}, u32[]{:S(2)}) copy-start(f32[384,512]{1,0:T(8,128)} %copy-done.2) | copy-start | bytes 2359300
  109.7 2.8 %copy-start.8 = (s32[4,12,12]{2,1,0:T(8,128)S(1)}, s32[4,12,12]{2,1,0:T(8,128)}, u32[]{:S(2)}) copy-start(s32[4,12,12]{2,1,0:T(8,128)} %copy.10.mask_ref) | copy-start | bytes 6916
  109.7 2.8 %copy-start.12 = (bf16[384,768]{1,0:T(8,128)(2,1)S(1)}, bf16[384,768]{1,0:T(8,128)(2,1)}, u32[]{:S(2)}) copy-start(bf16[384,768]{1,0:T(8,128)(2,1)} %copy-done.11) | copy-start | bytes 1769476
  109.7 2.7 %copy-start.14 = (f32[4,128,768]{2,1,0:T(8,128)S(1)}, f32[4,128,768]{2,1,0:T(8,128)}, u32[]{:S(2)}) copy-start(f32[4,128,768]{2,1,0:T(8,128)} %get-tuple-element.25.rest_2_) | copy-start | bytes 4718596
  109.8 11.5 %collective-permute-start.16 = (f32[128,768]{1,0:T(8,128)S(1)}, f32[128,768]{1,0:T(8,128)S(1)}, u32[]{:S(2)}, u32[]{:S(2)}) collective-permute-start(f32[128,768]{1,0:T(8,128)S(1)} %dynamic-slice_bitcast_fusion.1), channel_id=1, source_target_pairs={{0,2},{1,3},{2,0},{3,1},{4,6},{5,7},{6,4},{7,5},{8,10},{9,11},{10,... | collective-permute-start | bytes 1179656 | tf_op jit(solution)/shard_map/ppermute | solution.py:212

commit v18 on v17

--- a/solution.py
+++ b/solution.py
@@ -10,8 +10,8 @@
 LANES = 128
 F32 = jnp.float32
 BF16 = jnp.bfloat16
-PART_VMEM = 48 * 1024 * 1024
-FORWARD_VMEM = 48 * 1024 * 1024
+PART_VMEM = 9 * 1024 * 1024
+FORWARD_VMEM = 17 * 1024 * 1024
 
 
 def plain(acts, weight, block_mask, out_grad):

time: 123 us -> 121 us (0.984)
  local copies, waits for them, and re-layouts: 8.83 us -> 7.1 us
  waiting for transfers between devices: 67.7 us -> 69.1 us
    ppermute x15, waiting for transfers between devices: 62.3 us -> 64.3 us  [swap_dp(): return lax.ppermute(a, 'dp', [(d, d ^ bits) for d in range(dp)])]
    unnamed x33 -> x31, local copies, waits for them, and re-layouts: 6.73 us -> 4.99 us
    pallas_call x3, Pallas kernels: 13.1 us -> 11.8 us  [forward_and_input(): pl.pallas_call(kernel, grid=(width // BS,), out_shape=[jax.ShapeDtypeStru...]
where the time goes in v18:
time: 121 us; the launch traced here: 120 us
  waiting for transfers between devices  69.1 us (57%)
  starting transfers between devices  20.3 us (17%)
  Pallas kernels  17.6 us (15%)
  local copies, waits for them, and re-layouts  7.1 us (6%)
  other arithmetic  5.57 us (5%)
    ppermute x15, waiting for transfers between devices, swap_dp(): return lax.ppermute(a, 'dp', [(d, d ^ bits) for d in range(dp)])  64.3 us
    ppermute x15, starting transfers between devices, swap_dp(): return lax.ppermute(a, 'dp', [(d, d ^ bits) for d in range(dp)])  18.7 us
    pallas_call x3, Pallas kernels, forward_and_input(): pl.pallas_call(kernel, grid=(width // BS,), out_shape=[jax.ShapeDtypeStru...  11.8 us
    pallas_call x2, Pallas kernels, weight_grad_part(): pl.pallas_call(kernel, grid=(chunks,), out_shape=(jax.ShapeDtypeStruct((r...  5.75 us
    unnamed x31, local copies, waits for them, and re-layouts  4.99 us
    ppermute x2, waiting for transfers between devices, swap_f(): return lax.ppermute(a, 'fsdp', [(d, d ^ bit) for d in range(fsdp)])  4.8 us
  transfers between devices with their start and end apart: 17, of which 11 were waited for; matrix products, arithmetic and copies ran while one was open for 5% of the time, Pallas kernels for 15%

profile of v18, /device:TPU:0, one launch (start us, length us, event | category | flops | bytes accessed | tf_op | source)
XLA Modules:
  0.0 120.4 jit_solution(9996991537407084225)
XLA Ops:
  0.6 0.0 copy-start
  0.6 3.1 %collective-permute-start.4 = (bf16[4,128,768]{2,1,0:T(8,128)(2,1)}, bf16[4,128,768]{2,1,0:T(8,128)(2,1)S(1)}, u32[]{:S(2)}, u32[]{:S(2)}) collective-permute-start(bf16[4,128,768]{2,1,0:T(8,128)(2,1)} %og_ref.5), channel_id=1, source_target_pairs={{0,8},{4,12},{8,0},{12,4},{16,24},{20,28},{24,16},{28,20},{1,9},{5... | collective-permute-start | bytes 2359304 | tf_op jit(solution)/shard_map/ppermute | solution.py:203
  3.7 1.5 %collective-permute-start.5 = (bf16[4,128,768]{2,1,0:T(8,128)(2,1)}, bf16[4,128,768]{2,1,0:T(8,128)(2,1)}, u32[]{:S(2)}, u32[]{:S(2)}) collective-permute-start(bf16[4,128,768]{2,1,0:T(8,128)(2,1)} %og_ref.5), channel_id=1, source_target_pairs={{0,4},{4,0},{8,12},{12,8},{16,20},{20,16},{24,28},{28,24},{1,5},{5... | collective-permute-start | bytes 2359304 | tf_op jit(solution)/shard_map/ppermute | solution.py:203
  5.2 1.0 dynamic-slice_bitcast_fusion.3
  6.3 0.0 copy-start.1
  6.3 0.5 collective-permute-start.1
  6.8 0.0 copy-done
  6.9 0.2 collective-permute-start.2
  7.1 15.2 %collective-permute-done.4.refs_5_ = bf16[4,128,768]{2,1,0:T(8,128)(2,1)S(1)} collective-permute-done((bf16[4,128,768]{2,1,0:T(8,128)(2,1)}, bf16[4,128,768]{2,1,0:T(8,128)(2,1)S(1)}, u32[]{:S(2)}, u32[]{:S(2)}) %collective-permute-start.4) | collective-permute-done | bytes 786464 | tf_op jit(solution)/shard_map/ppermute | solution.py:203
  22.3 2.2 %collective-permute-done.5.refs_6_ = bf16[4,128,768]{2,1,0:T(8,128)(2,1)} collective-permute-done((bf16[4,128,768]{2,1,0:T(8,128)(2,1)}, bf16[4,128,768]{2,1,0:T(8,128)(2,1)}, u32[]{:S(2)}, u32[]{:S(2)}) %collective-permute-start.5) | collective-permute-done | bytes 786464 | tf_op jit(solution)/shard_map/ppermute | solution.py:203
  24.5 1.5 %collective-permute-start.6 = (bf16[4,128,768]{2,1,0:T(8,128)(2,1)S(1)}, bf16[4,128,768]{2,1,0:T(8,128)(2,1)}, u32[]{:S(2)}, u32[]{:S(2)}) collective-permute-start(bf16[4,128,768]{2,1,0:T(8,128)(2,1)S(1)} %collective-permute-done.4.refs_5_), channel_id=1, source_target_pairs={{0,4},{4,0},{8,12},{12,8},{16,20},{20,16},{24,28},{28,24},{1,5},{5... | collective-permute-start | bytes 2359304 | tf_op jit(solution)/shard_map/ppermute | solution.py:203
  26.0 2.6 %collective-permute-start = (bf16[384,768]{1,0:T(8,128)(2,1)}, bf16[384,768]{1,0:T(8,128)(2,1)}, u32[]{:S(2)}, u32[]{:S(2)}) collective-permute-start(bf16[384,768]{1,0:T(8,128)(2,1)} %rest_0_.1), channel_id=1, source_target_pairs={{0,16},{4,20},{8,24},{12,28},{16,0},{20,4},{24,8},{28,12},{1,17},{... | collective-permute-start | bytes 1769480 | tf_op jit(solution)/shard_map/ppermute | solution.py:203
  28.6 0.0 collective-permute-done.2.refs_2_
  28.6 6.8 %collective-permute-done.1.refs_1_ = bf16[2,128,768]{2,1,0:T(8,128)(2,1)S(1)} collective-permute-done((bf16[2,128,768]{2,1,0:T(8,128)(2,1)S(1)}, bf16[2,128,768]{2,1,0:T(8,128)(2,1)S(1)}, u32[]{:S(2)}, u32[]{:S(2)}) %collective-permute-start.1) | collective-permute-done | bytes 393248 | tf_op jit(solution)/shard_map/ppermute | solution.py:203
  35.6 2.7 %collective-permute-start.3 = (bf16[128,768]{1,0:T(8,128)(2,1)S(1)}, bf16[128,768]{1,0:T(8,128)(2,1)S(1)}, u32[]{:S(2)}, u32[]{:S(2)}) collective-permute-start(bf16[128,768]{1,0:T(8,128)(2,1)S(1)} %pad_maximum_fusion.3), channel_id=1, source_target_pairs={{0,4},{4,0},{8,12},{12,8},{16,20},{20,16},{24,28},{28,24},{1,5},{5... | collective-permute-start | bytes 589832 | tf_op jit(solution)/shard_map/ppermute | solution.py:203
  38.2 0.0 collective-permute-start.10
  38.2 0.2 collective-permute-start.11
  38.4 0.0 copy-done.14
  38.4 0.6 copy.10.mask_ref
  39.0 0.1 pad_add_fusion.where_ref
  39.1 10.6 %collective-permute-done.3.refs_3_ = bf16[128,768]{1,0:T(8,128)(2,1)S(1)} collective-permute-done((bf16[128,768]{1,0:T(8,128)(2,1)S(1)}, bf16[128,768]{1,0:T(8,128)(2,1)S(1)}, u32[]{:S(2)}, u32[]{:S(2)}) %collective-permute-start.3) | collective-permute-done | bytes 196640 | tf_op jit(solution)/shard_map/ppermute | solution.py:203
  49.7 0.0 collective-permute-done.6.refs_7_
  49.7 0.0 copy-done.1
  49.7 0.8 copy-done.4
  50.5 2.2 %weight_grad_part.2 = (f32[384,256]{1,0:T(8,128)S(1)}, f32[384,256]{1,0:T(8,128)S(1)}) custom-call(s32[4]{0:T(128)S(1)} %pad_add_fusion.where_ref, s32[4,12,12]{2,1,0:T(8,128)S(1)} %copy-done.4, bf16[128,3072]{1,0:T(8,128)(2,1)S(1)} %copy-done, bf16[2,128,768]{2,1,0:T(8,128)(2,1)S(1)} %collective-permute-done.1.refs_1_, ...), custom_call_target="tpu_custom_call" | custom-call | flops 805306368 | bytes 786432 | tf_op jit(solution)/shard_map/weight_grad_part/pallas_call | solution.py:84
  52.6 2.7 %collective-permute-start.12 = (f32[384,256]{1,0:T(8,128)S(1)}, f32[384,256]{1,0:T(8,128)}, u32[]{:S(2)}, u32[]{:S(2)}) collective-permute-start(f32[384,256]{1,0:T(8,128)S(1)} %get-tuple-element.23), channel_id=1, source_target_pairs={{0,16},{4,20},{8,24},{12,28},{16,0},{20,4},{24,8},{28,12},{1,17},{... | collective-permute-start | bytes 1179656 | tf_op jit(solution)/shard_map/ppermute | solution.py:203
  55.3 0.0 collective-permute-done.rest_2_
  55.3 1.5 %collective-permute-start.8 = (bf16[384,768]{1,0:T(8,128)(2,1)}, bf16[384,768]{1,0:T(8,128)(2,1)}, u32[]{:S(2)}, u32[]{:S(2)}) collective-permute-start(bf16[384,768]{1,0:T(8,128)(2,1)} %collective-permute-done.rest_2_), channel_id=1, source_target_pairs={{0,4},{4,0},{8,12},{12,8},{16,20},{20,16},{24,28},{28,24},{1,5},{5... | collective-permute-start | bytes 1769480 | tf_op jit(solution)/shard_map/ppermute | solution.py:203
  56.8 0.4 collective-permute-start.7
  57.3 3.6 %weight_grad_part.3 = (f32[384,512]{1,0:T(8,128)S(1)}, f32[384,512]{1,0:T(8,128)S(1)}) custom-call(s32[4]{0:T(128)S(1)} %pad_add_fusion.where_ref, s32[4,12,12]{2,1,0:T(8,128)S(1)} %copy-done.4, bf16[128,3072]{1,0:T(8,128)(2,1)S(1)} %copy-done, bf16[2,128,768]{2,1,0:T(8,128)(2,1)S(1)} %collective-permute-done.1.refs_1_, ...), custom_call_target="tpu_custom_call" | custom-call | flops 1610612736 | bytes 1572864 | tf_op jit(solution)/shard_map/weight_grad_part/pallas_call | solution.py:84
  60.8 0.0 copy-start.2
  60.8 0.9 copy-done.2
  61.7 0.9 copy-done.8
  62.6 4.2 %collective-permute-done.10.rest_1_ = bf16[384,768]{1,0:T(8,128)(2,1)} collective-permute-done((bf16[384,768]{1,0:T(8,128)(2,1)}, bf16[384,768]{1,0:T(8,128)(2,1)}, u32[]{:S(2)}, u32[]{:S(2)}) %collective-permute-start.10) | collective-permute-done | bytes 589856 | tf_op jit(solution)/shard_map/ppermute | solution.py:203
  66.8 0.0 collective-permute-done.11.rest_3_
  66.8 3.8 %collective-permute-done.12 = f32[384,256]{1,0:T(8,128)} collective-permute-done((f32[384,256]{1,0:T(8,128)S(1)}, f32[384,256]{1,0:T(8,128)}, u32[]{:S(2)}, u32[]{:S(2)}) %collective-permute-start.12) | collective-permute-done | bytes 393248 | tf_op jit(solution)/shard_map/ppermute | solution.py:203
  70.6 1.5 %collective-permute-start.13 = (bf16[384,768]{1,0:T(8,128)(2,1)}, bf16[384,768]{1,0:T(8,128)(2,1)S(1)}, u32[]{:S(2)}, u32[]{:S(2)}) collective-permute-start(bf16[384,768]{1,0:T(8,128)(2,1)} %collective-permute-done.10.rest_1_), channel_id=1, source_target_pairs={{0,4},{4,0},{8,12},{12,8},{16,20},{20,16},{24,28},{28,24},{1,5},{5... | collective-permute-start | bytes 1769480 | tf_op jit(solution)/shard_map/ppermute | solution.py:203
  72.1 0.0 collective-permute-start.14
  72.1 3.0 %collective-permute-done.8.rest_5_ = bf16[384,768]{1,0:T(8,128)(2,1)} collective-permute-done((bf16[384,768]{1,0:T(8,128)(2,1)}, bf16[384,768]{1,0:T(8,128)(2,1)}, u32[]{:S(2)}, u32[]{:S(2)}) %collective-permute-start.8) | collective-permute-done | bytes 589856 | tf_op jit(solution)/shard_map/ppermute | solution.py:203
  75.1 12.0 %collective-permute-done.7.rest_0_ = bf16[384,768]{1,0:T(8,128)(2,1)} collective-permute-done((bf16[384,768]{1,0:T(8,128)(2,1)}, bf16[384,768]{1,0:T(8,128)(2,1)}, u32[]{:S(2)}, u32[]{:S(2)}) %collective-permute-start.7) | collective-permute-done | bytes 589856 | tf_op jit(solution)/shard_map/ppermute | solution.py:203
  87.0 0.4 collective-permute-start.9
  87.4 0.0 collective-permute-done.13.rest_4_
  87.4 0.8 copy-done.5
  88.2 1.1 copy-done.9
  89.2 5.3 %forward_and_input.3 = (f32[4,128,768]{2,1,0:T(8,128)S(1)}, f32[4,128,768]{2,1,0:T(8,128)S(1)}) custom-call(s32[4]{0:T(128)S(1)} %pad_add_fusion.where_ref, s32[4,12,12]{2,1,0:T(8,128)S(1)} %copy-done.5, bf16[128,3072]{1,0:T(8,128)(2,1)S(1)} %copy-done, bf16[4,128,768]{2,1,0:T(8,128)(2,1)S(1)} %copy-done.1, bf16[384,768]{1,0:T(8,128)(2,1)S(1)} %copy-done.9, ...), custom_call_target="tpu_custom_call" | custom-call | flops 8153726976 | bytes 7077888 | tf_op jit(solution)/shard_map/forward_and_input/pallas_call | solution.py:165
  94.6 0.0 copy-start.12
  94.6 5.8 %collective-permute-done.9.rest_1_ = bf16[384,768]{1,0:T(8,128)(2,1)S(1)} collective-permute-done((bf16[384,768]{1,0:T(8,128)(2,1)}, bf16[384,768]{1,0:T(8,128)(2,1)S(1)}, u32[]{:S(2)}, u32[]{:S(2)}) %collective-permute-start.9) | collective-permute-done | bytes 589856 | tf_op jit(solution)/shard_map/ppermute | solution.py:203
  100.4 3.0 %forward_and_input.5 = f32[4,128,768]{2,1,0:T(8,128)S(1)} custom-call(s32[4]{0:T(128)S(1)} %pad_add_fusion.where_ref, s32[4,12,12]{2,1,0:T(8,128)S(1)} %copy-done.6, bf16[128,3072]{1,0:T(8,128)(2,1)S(1)} %copy-done, bf16[4,128,768]{2,1,0:T(8,128)(2,1)S(1)} %copy-done.1, bf16[384,768]{1,0:T(8,128)(2,1)} %collective-permute-done.7.rest_0_, ...), custom_call_target="tpu_custom_call" | custom-call | flops 2717908992 | bytes 2359296 | tf_op jit(solution)/shard_map/forward_and_input/pallas_call | solution.py:165
  103.3 0.9 dynamic-slice_bitcast_fusion
  104.3 0.0 collective-permute-start.15
  104.3 1.1 add.68
  105.4 0.7 collective-permute-done.14
  106.1 0.0 copy-done.3
  106.1 1.3 %add.69 = f32[384,512]{1,0:T(8,128)S(1)} add(f32[384,512]{1,0:T(8,128)S(1)} %copy-done.3, f32[384,512]{1,0:T(8,128)} %collective-permute-done.14) | non-fusion elementwise | flops 196608 | bytes 2359296 | tf_op jit(solution)/shard_map/add | solution.py:240
  107.4 0.0 collective-permute-done.15
  107.4 1.2 %bitcast_add_fusion = f32[2,128,768]{2,1,0:T(8,128)S(1)} fusion(f32[2,128,768]{2,1,0:T(8,128)} %collective-permute-done.15, f32[2,2,128,768]{3,2,1,0:T(8,128)S(1)} %bitcast.24, s32[]{:T(128)S(6)} %select_n.56), kind=kLoop, calls=%fused_computation.1 | loop fusion | flops 196608 | bytes 2359300 | tf_op jit(solution)/shard_map/add | solution.py:255
  108.6 0.0 copy-start.7
  108.7 0.0 copy-start.11
  108.7 0.0 copy-start.13
  108.7 1.6 %collective-permute-start.16 = (f32[128,768]{1,0:T(8,128)S(1)}, f32[128,768]{1,0:T(8,128)S(1)}, u32[]{:S(2)}, u32[]{:S(2)}) collective-permute-start(f32[128,768]{1,0:T(8,128)S(1)} %dynamic-slice_bitcast_fusion.1), channel_id=1, source_target_pairs={{0,2},{1,3},{2,0},{3,1},{4,6},{5,7},{6,4},{7,5},{8,10},{9,11},{10,... | collective-permute-start | bytes 1179656 | tf_op jit(solution)/shard_map/ppermute | solution.py:212
  110.3 1.1 pad_maximum_fusion
  111.4 3.5 %forward_and_input.4 = bf16[4,128,768]{2,1,0:T(8,128)(2,1)} custom-call(s32[4]{0:T(128)S(1)} %pad_add_fusion.where_ref, s32[4,12,12]{2,1,0:T(8,128)S(1)} %copy-done.7, bf16[128,3072]{1,0:T(8,128)(2,1)S(1)} %copy-done, bf16[4,128,768]{2,1,0:T(8,128)(2,1)S(1)} %copy-done.1, bf16[384,768]{1,0:T(8,128)(2,1)} %collective-permute-done.7.rest_0_, ...), custom_call_target="tpu_custom_call" | custom-call | flops 2717908992 | bytes 2359296 | tf_op jit(solution)/shard_map/forward_and_input/pallas_call | solution.py:165
  114.9 4.8 %collective-permute-done.16 = f32[128,768]{1,0:T(8,128)S(1)} collective-permute-done((f32[128,768]{1,0:T(8,128)S(1)}, f32[128,768]{1,0:T(8,128)S(1)}, u32[]{:S(2)}, u32[]{:S(2)}) %collective-permute-start.16) | collective-permute-done | bytes 393248 | tf_op jit(solution)/shard_map/ppermute | solution.py:212
  119.7 0.7 fusion
  (21 shorter events, 0.2 us)
Async XLA Ops:
  0.6 6.2 %copy-start = (bf16[128,3072]{1,0:T(8,128)(2,1)S(1)}, bf16[128,3072]{1,0:T(8,128)(2,1)}, u32[]{:S(2)}) copy-start(bf16[128,3072]{1,0:T(8,128)(2,1)} %acts_ref.5) | copy-start | bytes 2359300
  0.6 21.7 %collective-permute-start.4 = (bf16[4,128,768]{2,1,0:T(8,128)(2,1)}, bf16[4,128,768]{2,1,0:T(8,128)(2,1)S(1)}, u32[]{:S(2)}, u32[]{:S(2)}) collective-permute-start(bf16[4,128,768]{2,1,0:T(8,128)(2,1)} %og_ref.5), channel_id=1, source_target_pairs={{0,8},{4,12},{8,0},{12,4},{16,24},{20,28},{24,16},{28,20},{1,9},{5... | collective-permute-start | bytes 2359304 | tf_op jit(solution)/shard_map/ppermute | solution.py:203
  3.7 20.8 %collective-permute-start.5 = (bf16[4,128,768]{2,1,0:T(8,128)(2,1)}, bf16[4,128,768]{2,1,0:T(8,128)(2,1)}, u32[]{:S(2)}, u32[]{:S(2)}) collective-permute-start(bf16[4,128,768]{2,1,0:T(8,128)(2,1)} %og_ref.5), channel_id=1, source_target_pairs={{0,4},{4,0},{8,12},{12,8},{16,20},{20,16},{24,28},{28,24},{1,5},{5... | collective-permute-start | bytes 2359304 | tf_op jit(solution)/shard_map/ppermute | solution.py:203
  6.3 43.4 %copy-start.1 = (bf16[4,128,768]{2,1,0:T(8,128)(2,1)S(1)}, bf16[4,128,768]{2,1,0:T(8,128)(2,1)}, u32[]{:S(2)}) copy-start(bf16[4,128,768]{2,1,0:T(8,128)(2,1)} %og_ref.5) | copy-start | bytes 2359300
  6.3 29.1 %collective-permute-start.1 = (bf16[2,128,768]{2,1,0:T(8,128)(2,1)S(1)}, bf16[2,128,768]{2,1,0:T(8,128)(2,1)S(1)}, u32[]{:S(2)}, u32[]{:S(2)}) collective-permute-start(bf16[2,128,768]{2,1,0:T(8,128)(2,1)S(1)} %pad_maximum_fusion.1), channel_id=1, source_target_pairs={{0,8},{4,12},{8,0},{12,4},{16,24},{20,28},{24,16},{28,20},{1,9},{5... | collective-permute-start | bytes 1179656 | tf_op jit(solution)/shard_map/ppermute | solution.py:203
  6.9 21.7 %collective-permute-start.2 = (bf16[128,768]{1,0:T(8,128)(2,1)S(1)}, bf16[128,768]{1,0:T(8,128)(2,1)S(1)}, u32[]{:S(2)}, u32[]{:S(2)}) collective-permute-start(bf16[128,768]{1,0:T(8,128)(2,1)S(1)} %pad_maximum_fusion.2), channel_id=1, source_target_pairs={{0,4},{4,0},{8,12},{12,8},{16,20},{20,16},{24,28},{28,24},{1,5},{5... | collective-permute-start | bytes 589832 | tf_op jit(solution)/shard_map/ppermute | solution.py:203
  24.5 25.2 %collective-permute-start.6 = (bf16[4,128,768]{2,1,0:T(8,128)(2,1)S(1)}, bf16[4,128,768]{2,1,0:T(8,128)(2,1)}, u32[]{:S(2)}, u32[]{:S(2)}) collective-permute-start(bf16[4,128,768]{2,1,0:T(8,128)(2,1)S(1)} %collective-permute-done.4.refs_5_), channel_id=1, source_target_pairs={{0,4},{4,0},{8,12},{12,8},{16,20},{20,16},{24,28},{28,24},{1,5},{5... | collective-permute-start | bytes 2359304 | tf_op jit(solution)/shard_map/ppermute | solution.py:203
  26.0 29.3 %collective-permute-start = (bf16[384,768]{1,0:T(8,128)(2,1)}, bf16[384,768]{1,0:T(8,128)(2,1)}, u32[]{:S(2)}, u32[]{:S(2)}) collective-permute-start(bf16[384,768]{1,0:T(8,128)(2,1)} %rest_0_.1), channel_id=1, source_target_pairs={{0,16},{4,20},{8,24},{12,28},{16,0},{20,4},{24,8},{28,12},{1,17},{... | collective-permute-start | bytes 1769480 | tf_op jit(solution)/shard_map/ppermute | solution.py:203
  35.5 2.9 %copy-start.14 = (s32[4,12,12]{2,0,1:T(4,128)S(1)}, s32[4,12,12]{2,0,1:T(4,128)}, u32[]{:S(2)}) copy-start(s32[4,12,12]{2,0,1:T(4,128)} %param.6) | copy-start | bytes 6916
  35.6 14.1 %collective-permute-start.3 = (bf16[128,768]{1,0:T(8,128)(2,1)S(1)}, bf16[128,768]{1,0:T(8,128)(2,1)S(1)}, u32[]{:S(2)}, u32[]{:S(2)}) collective-permute-start(bf16[128,768]{1,0:T(8,128)(2,1)S(1)} %pad_maximum_fusion.3), channel_id=1, source_target_pairs={{0,4},{4,0},{8,12},{12,8},{16,20},{20,16},{24,28},{28,24},{1,5},{5... | collective-permute-start | bytes 589832 | tf_op jit(solution)/shard_map/ppermute | solution.py:203
  38.2 28.6 %collective-permute-start.10 = (bf16[384,768]{1,0:T(8,128)(2,1)}, bf16[384,768]{1,0:T(8,128)(2,1)}, u32[]{:S(2)}, u32[]{:S(2)}) collective-permute-start(bf16[384,768]{1,0:T(8,128)(2,1)} %rest_0_.1), channel_id=1, source_target_pairs={{0,8},{4,12},{8,0},{12,4},{16,24},{20,28},{24,16},{28,20},{1,9},{5... | collective-permute-start | bytes 1769480 | tf_op jit(solution)/shard_map/ppermute | solution.py:203
  38.2 28.6 %collective-permute-start.11 = (bf16[384,768]{1,0:T(8,128)(2,1)}, bf16[384,768]{1,0:T(8,128)(2,1)}, u32[]{:S(2)}, u32[]{:S(2)}) collective-permute-start(bf16[384,768]{1,0:T(8,128)(2,1)} %rest_0_.1), channel_id=1, source_target_pairs={{0,4},{4,0},{8,12},{12,8},{16,20},{20,16},{24,28},{28,24},{1,5},{5... | collective-permute-start | bytes 1769480 | tf_op jit(solution)/shard_map/ppermute | solution.py:203
  49.7 0.8 copy-start.4
  52.6 18.0 %collective-permute-start.12 = (f32[384,256]{1,0:T(8,128)S(1)}, f32[384,256]{1,0:T(8,128)}, u32[]{:S(2)}, u32[]{:S(2)}) collective-permute-start(f32[384,256]{1,0:T(8,128)S(1)} %get-tuple-element.23), channel_id=1, source_target_pairs={{0,16},{4,20},{8,24},{12,28},{16,0},{20,4},{24,8},{28,12},{1,17},{... | collective-permute-start | bytes 1179656 | tf_op jit(solution)/shard_map/ppermute | solution.py:203
  55.3 19.8 %collective-permute-start.8 = (bf16[384,768]{1,0:T(8,128)(2,1)}, bf16[384,768]{1,0:T(8,128)(2,1)}, u32[]{:S(2)}, u32[]{:S(2)}) collective-permute-start(bf16[384,768]{1,0:T(8,128)(2,1)} %collective-permute-done.rest_2_), channel_id=1, source_target_pairs={{0,4},{4,0},{8,12},{12,8},{16,20},{20,16},{24,28},{28,24},{1,5},{5... | collective-permute-start | bytes 1769480 | tf_op jit(solution)/shard_map/ppermute | solution.py:203
  56.8 30.2 %collective-permute-start.7 = (bf16[384,768]{1,0:T(8,128)(2,1)}, bf16[384,768]{1,0:T(8,128)(2,1)}, u32[]{:S(2)}, u32[]{:S(2)}) collective-permute-start(bf16[384,768]{1,0:T(8,128)(2,1)} %collective-permute-done.rest_2_), channel_id=1, source_target_pairs={{0,8},{4,12},{8,0},{12,4},{16,24},{20,28},{24,16},{28,20},{1,9},{5... | collective-permute-start | bytes 1769480 | tf_op jit(solution)/shard_map/ppermute | solution.py:203
  60.8 0.9 copy-start.2
  61.7 0.9 copy-start.8
  70.6 16.8 %collective-permute-start.13 = (bf16[384,768]{1,0:T(8,128)(2,1)}, bf16[384,768]{1,0:T(8,128)(2,1)S(1)}, u32[]{:S(2)}, u32[]{:S(2)}) collective-permute-start(bf16[384,768]{1,0:T(8,128)(2,1)} %collective-permute-done.10.rest_1_), channel_id=1, source_target_pairs={{0,4},{4,0},{8,12},{12,8},{16,20},{20,16},{24,28},{28,24},{1,5},{5... | collective-permute-start | bytes 1769480 | tf_op jit(solution)/shard_map/ppermute | solution.py:203
  72.1 34.0 %collective-permute-start.14 = (f32[384,512]{1,0:T(8,128)}, f32[384,512]{1,0:T(8,128)}, u32[]{:S(2)}, u32[]{:S(2)}) collective-permute-start(f32[384,512]{1,0:T(8,128)} %copy-done.8), channel_id=1, source_target_pairs={{0,16},{4,20},{8,24},{12,28},{16,0},{20,4},{24,8},{28,12},{1,17},{... | collective-permute-start | bytes 2359304 | tf_op jit(solution)/shard_map/ppermute | solution.py:203
  87.0 13.3 %collective-permute-start.9 = (bf16[384,768]{1,0:T(8,128)(2,1)}, bf16[384,768]{1,0:T(8,128)(2,1)S(1)}, u32[]{:S(2)}, u32[]{:S(2)}) collective-permute-start(bf16[384,768]{1,0:T(8,128)(2,1)} %collective-permute-done.7.rest_0_), channel_id=1, source_target_pairs={{0,4},{4,0},{8,12},{12,8},{16,20},{20,16},{24,28},{28,24},{1,5},{5... | collective-permute-start | bytes 1769480 | tf_op jit(solution)/shard_map/ppermute | solution.py:203
  87.4 0.8 copy-start.5
  88.2 1.1 copy-start.9
  89.2 11.1 %copy-start.6 = (s32[4,12,12]{2,1,0:T(8,128)S(1)}, s32[4,12,12]{2,1,0:T(8,128)}, u32[]{:S(2)}) copy-start(s32[4,12,12]{2,1,0:T(8,128)} %copy.10.mask_ref) | copy-start | bytes 6916
  94.6 8.8 %copy-start.12 = (f32[4,128,768]{2,1,0:T(8,128)}, f32[4,128,768]{2,1,0:T(8,128)S(1)}, u32[]{:S(2)}) copy-start(f32[4,128,768]{2,1,0:T(8,128)S(1)} %get-tuple-element.25.rest_2_) | copy-start | bytes 4718596
  100.3 3.0 %copy-start.10 = (bf16[384,768]{1,0:T(8,128)(2,1)}, bf16[384,768]{1,0:T(8,128)(2,1)S(1)}, u32[]{:S(2)}) copy-start(bf16[384,768]{1,0:T(8,128)(2,1)S(1)} %collective-permute-done.9.rest_1_) | copy-start | bytes 1769476
  104.3 3.1 %collective-permute-start.15 = (f32[2,128,768]{2,1,0:T(8,128)}, f32[2,128,768]{2,1,0:T(8,128)}, u32[]{:S(2)}, u32[]{:S(2)}) collective-permute-start(f32[2,128,768]{2,1,0:T(8,128)} %dynamic-slice_bitcast_fusion), channel_id=1, source_target_pairs={{0,1},{1,0},{2,3},{3,2},{4,5},{5,4},{6,7},{7,6},{8,9},{9,8},{10,11... | collective-permute-start | bytes 2359304 | tf_op jit(solution)/shard_map/ppermute | solution.py:212
  104.3 1.9 %copy-start.3 = (f32[384,512]{1,0:T(8,128)S(1)}, f32[384,512]{1,0:T(8,128)}, u32[]{:S(2)}) copy-start(f32[384,512]{1,0:T(8,128)} %copy-done.2) | copy-start | bytes 2359300
  108.6 2.8 %copy-start.7 = (s32[4,12,12]{2,1,0:T(8,128)S(1)}, s32[4,12,12]{2,1,0:T(8,128)}, u32[]{:S(2)}) copy-start(s32[4,12,12]{2,1,0:T(8,128)} %copy.10.mask_ref) | copy-start | bytes 6916
  108.7 2.7 %copy-start.11 = (bf16[384,768]{1,0:T(8,128)(2,1)S(1)}, bf16[384,768]{1,0:T(8,128)(2,1)}, u32[]{:S(2)}) copy-start(bf16[384,768]{1,0:T(8,128)(2,1)} %copy-done.10) | copy-start | bytes 1769476
  108.7 2.7 %copy-start.13 = (f32[4,128,768]{2,1,0:T(8,128)S(1)}, f32[4,128,768]{2,1,0:T(8,128)}, u32[]{:S(2)}) copy-start(f32[4,128,768]{2,1,0:T(8,128)} %copy-done.12) | copy-start | bytes 4718596
  108.7 11.0 %collective-permute-start.16 = (f32[128,768]{1,0:T(8,128)S(1)}, f32[128,768]{1,0:T(8,128)S(1)}, u32[]{:S(2)}, u32[]{:S(2)}) collective-permute-start(f32[128,768]{1,0:T(8,128)S(1)} %dynamic-slice_bitcast_fusion.1), channel_id=1, source_target_pairs={{0,2},{1,3},{2,0},{3,1},{4,6},{5,7},{6,4},{7,5},{8,10},{9,11},{10,... | collective-permute-start | bytes 1179656 | tf_op jit(solution)/shard_map/ppermute | solution.py:212
